TPU v7x, 256 devices: a whole 4x4x8 slice. The times are simulated.
256 devices in a mesh: feat: 8 (over y, core), dom: 32 (over z, x).
Axes of the slice: x: 4, y: 4, z: 8, core: 2. Of those that a mesh axis runs over, the one named last changes fastest.
Arguments:
- features: bfloat16 [8, 4096, 4096], P(None, 'dom', 'feat'), may hold values from -6 to 6
- w_one: bfloat16 [4096, 1024], P('feat'), may hold values from -0.09375 to 0.09375
- w_two: bfloat16 [1024, 512], replicated, may hold values from -0.25 to 0.25
- neighbor: int32 [8, 4096, 10], P('feat', 'dom'), may hold values from 0 to 383
- degree: int32 [8, 4096], P('feat', 'dom'), may hold values from 1 to 10
- send_rows: int32 [8, 1024, 8], P('feat', 'dom'), may hold values from 0 to 127
- grad_out: bfloat16 [8, 4096, 512], P('feat', 'dom'), may hold values from -6 to 6
Outputs:
- out_two: bfloat16 [8, 4096, 512], P('feat', 'dom')
- grad_one: float32 [4096, 1024], P('feat')
- grad_two: float32 [1024, 512], replicated
All inputs are finite; a program needn't handle non-finite values.
Results may differ from a plain program's by a relative error of at most 0.015.
Values may be sent and summed in bfloat16 or wider, within the bound.
No kernel may reach another device: no remote copies, remote signals or barrier semaphores. Data moves between devices by JAX's collectives and lax.ppermute only.
A program may use at most 64 MiB of HBM per device.

v0:
```python
import math

import jax
import jax.numpy as jnp
from jax import lax
from jax.sharding import PartitionSpec as P


def trade(buffer):
    return lax.all_to_all(buffer, "dom", split_axis=0, concat_axis=0, tiled=True)


def on_device(features, w_one, w_two, neighbor, degree, send_rows, grad_out):
    groups, nodes, cols = features.shape
    width = w_two.shape[1]
    nbrs = neighbor[0]
    degs = degree[0]
    sends = send_rows[0]
    parts = lax.axis_size("dom")
    fan = nbrs.shape[1]
    slots = jnp.arange(fan, dtype=jnp.int32)
    weight = (slots[None, :] < degs[:, None]).astype(jnp.float32) / degs[:, None].astype(
        jnp.float32
    )
    flat = features.reshape(groups * nodes, cols)

    def spread(values):
        boxes = values[sends]
        recv = trade(boxes)
        table = jnp.concatenate([values, recv.reshape(-1, values.shape[1])], axis=0)
        gathered = table[nbrs]
        return jnp.sum(gathered.astype(jnp.float32) * weight[..., None], axis=1)

    def gather_back(grads):
        span = grads.shape[1]
        terms = (weight[..., None] * grads[:, None, :]).reshape(-1, span)
        table = jnp.zeros((nodes + sends.size, span), jnp.float32).at[nbrs.reshape(-1)].add(terms)
        local = table[:nodes]
        outgoing = table[nodes:].astype(jnp.bfloat16).reshape(parts, sends.shape[1], span)
        returned = trade(outgoing)
        home = (
            jnp.zeros((nodes, span), jnp.float32)
            .at[sends.reshape(-1)]
            .add(returned.reshape(-1, span).astype(jnp.float32))
        )
        return local + home

    rows = flat
    proj = lax.psum_scatter(
        jnp.dot(rows, w_one, preferred_element_type=jnp.float32),
        "feat",
        scatter_dimension=0,
        tiled=True,
    )
    p_self = proj[:, :width]
    p_near = proj[:, width:].astype(jnp.bfloat16)
    pre = p_self + spread(p_near)
    hidden = (pre * jax.nn.sigmoid(pre)).astype(jnp.bfloat16)
    agg = spread(hidden).astype(jnp.bfloat16)
    joined = jnp.concatenate([hidden, agg], axis=-1)
    out = jnp.dot(joined, w_two, preferred_element_type=jnp.float32).astype(jnp.bfloat16)
    grads = grad_out[0]
    two_sum = lax.dot_general(
        joined, grads, (((0,), (0,)), ((), ())), preferred_element_type=jnp.float32
    )
    dcat = lax.dot_general(
        grads, w_two, (((1,), (1,)), ((), ())), preferred_element_type=jnp.float32
    )
    d_hidden = dcat[:, :width] + gather_back(dcat[:, width:])
    sig = jax.nn.sigmoid(pre)
    d_pre = d_hidden * sig * (1.0 + pre * (1.0 - sig))
    d_near = gather_back(d_pre)
    d_proj = jnp.concatenate([d_pre, d_near], axis=-1).astype(jnp.bfloat16)
    rows = flat
    one_sum = lax.dot_general(
        rows,
        lax.all_gather(d_proj, "feat", axis=0, tiled=True),
        (((0,), (0,)), ((), ())),
        preferred_element_type=jnp.float32,
    )
    one_sum = lax.psum(one_sum.astype(jnp.bfloat16), "dom").astype(jnp.float32)
    two_sum = lax.psum(two_sum, ("feat", "dom"))
    scale = 1.0 / math.sqrt(groups * nodes * parts)
    return (out[None], one_sum * scale, two_sum * scale)


def solution(mesh):
    in_specs = (
        P(None, "dom", "feat"),
        P("feat", None),
        P(),
        P("feat", "dom", None),
        P("feat", "dom"),
        P("feat", "dom", None),
        P("feat", "dom", None),
    )
    out_specs = (P("feat", "dom", None), P("feat", None), P())
    return jax.shard_map(
        on_device, mesh=mesh, in_specs=in_specs, out_specs=out_specs, check_vma=False
    )
```

profile of v0, /device:TPU:32, one launch (start us, length us, event | category | flops | bytes accessed | tf_op | source)
XLA Modules:
  0.0 581.5 jit_solution(4482622993260259353)
XLA Ops:
  7.2 1.2 copy-done
  8.4 4.4 fusion.26
  12.8 0.7 copy-done.6
  13.5 0.1 copy.13
  13.6 0.1 reshape_squeeze.8
  13.7 0.3 copy-done.1
  14.0 0.5 fusion.20
  14.5 2.5 mul.73
  17.0 4.5 mul.74
  21.6 0.1 convert_divide_fusion
  21.7 0.1 div.23
  21.9 13.1 %scatter_custom_fusion = f32[384,512]{1,0:T(8,128)S(1)} fusion(s32[1280]{0:T(1024)S(1)} %fusion.22, f32[1280,512]{1,0:T(8,128)} %mul.74, f32[1280]{0:T(1024)S(1)} %div.23, f32[]{:T(128)} %constant.9.clone.1), kind=kCustom, calls=%fused_computation.12 | custom fusion | flops 1310720 | bytes 3416068 | tf_op jit(solution)/shard_map/scatter-add | solution.py:37
  34.9 0.7 fusion.14
  35.7 11.2 %all-to-all-start.2 = ((bf16[32,8,512]{2,1,0:T(8,128)(2,1)}), bf16[32,8,512]{2,1,0:T(8,128)(2,1)S(1)}, u32[]{:S(2)}, u32[]{:S(2)}) async-start(bf16[32,8,512]{2,1,0:T(8,128)(2,1)} %fusion.14), calls=%async_computation.3 | async-start | bytes 524288 | tf_op jit(solution)/shard_map/all_to_all | solution.py:10
  47.1 0.1 copy.12
  47.2 0.1 reshape.219
  47.3 8.7 %reduce-scatter.2.cloned.1.call-done = f32[128,1024]{1,0:T(8,128)} async-done(((f32[1024,1024]{1,0:T(8,128)}), f32[128,1024]{1,0:T(8,128)}) %reduce-scatter.2.cloned.1.call-update) | async-done | bytes 524304 | tf_op jit(solution)/shard_map/reduce_scatter | solution.py:49
  56.0 1.0 slice.65
  57.0 1.9 gather_fusion
  58.9 0.2 all-to-all-done.2
  59.0 10.0 %all-to-all-start = ((bf16[32,8,512]{2,1,0:T(8,128)(2,1)}), bf16[32,8,512]{2,1,0:T(8,128)(2,1)S(1)}, u32[]{:S(2)}, u32[]{:S(2)}) async-start(bf16[32,8,512]{2,1,0:T(8,128)(2,1)} %bitcast.2), calls=%async_computation.1 | async-start | bytes 524288 | tf_op jit(solution)/shard_map/all_to_all | solution.py:10
  69.3 2.4 scatter_custom_fusion.1
  71.7 8.1 %all-to-all-done = bf16[32,8,512]{2,1,0:T(8,128)(2,1)S(1)} async-done(((bf16[32,8,512]{2,1,0:T(8,128)(2,1)}), bf16[32,8,512]{2,1,0:T(8,128)(2,1)S(1)}, u32[]{:S(2)}, u32[]{:S(2)}) %all-to-all-start) | async-done | bytes 262176 | tf_op jit(solution)/shard_map/all_to_all | solution.py:10
  79.9 4.1 gather_fusion.1
  84.0 2.1 reshape.277
  86.1 3.2 multiply_reduce_fusion.1
  89.3 0.1 fusion.25
  89.5 2.5 mul.79
  92.0 4.5 mul.80
  96.5 13.1 %scatter_custom_fusion.2 = f32[384,512]{1,0:T(8,128)S(1)} fusion(s32[1280]{0:T(1024)S(1)} %fusion.22, f32[1280,512]{1,0:T(8,128)} %mul.80, f32[1280]{0:T(1024)S(1)} %div.23, f32[]{:T(128)} %constant.9.clone.1), kind=kCustom, calls=%fused_computation.10 | custom fusion | flops 1310720 | bytes 3416068 | tf_op jit(solution)/shard_map/scatter-add | solution.py:37
  109.6 0.7 fusion.15
  110.3 4.6 all-to-all-start.3
  115.0 10.7 %all-to-all-done.3 = bf16[32,8,512]{2,1,0:T(8,128)(2,1)S(1)} async-done(((bf16[32,8,512]{2,1,0:T(8,128)(2,1)}), bf16[32,8,512]{2,1,0:T(8,128)(2,1)S(1)}, u32[]{:S(2)}, u32[]{:S(2)}) %all-to-all-start.3) | async-done | bytes 262176 | tf_op jit(solution)/shard_map/all_to_all | solution.py:10
  125.7 2.2 scatter_custom_fusion.3
  128.0 0.7 pad_maximum_fusion.3
  128.8 1.2 gather_fusion.2
  129.9 15.2 %all_to_all.20 = bf16[32,8,512]{2,1,0:T(8,128)(2,1)S(1)} all-to-all(bf16[32,8,512]{2,1,0:T(8,128)(2,1)S(1)} %bitcast.50), channel_id=1, replica_groups=mesh['feat'=8,'dom'=32] {'dom'}, dimensions={0} | all-to-all | bytes 524288 | tf_op jit(solution)/shard_map/all_to_all | solution.py:10
  145.1 4.1 gather_fusion.3
  149.2 2.1 reshape.278
  151.3 3.3 multiply_reduce_fusion
  154.6 1.8 fusion.18
  156.5 3.9 fusion.4
  160.4 1.0 fusion.7
  161.4 256.9 %all-reduce.5.cloned.1.call-done = f32[1024,512]{1,0:T(8,128)} async-done(((f32[1024,512]{1,0:T(8,128)}), f32[1024,512]{1,0:T(8,128)}) %all-reduce.5.cloned.1.call-update) | async-done | bytes 2097168 | tf_op jit(solution)/shard_map/psum | solution.py:82
  418.3 3.2 broadcast_multiply_fusion
  421.5 150.1 %all-reduce.3.cloned.1.call-done = bf16[512,1024]{0,1:T(8,128)(2,1)} async-done(((bf16[512,1024]{0,1:T(8,128)(2,1)}), bf16[512,1024]{0,1:T(8,128)(2,1)}) %all-reduce.3.cloned.1.call-update) | async-done | bytes 1048592 | tf_op jit(solution)/shard_map/psum | solution.py:81
  571.6 1.5 convert_multiply_fusion
  573.1 1.8 copy.15
  (41 shorter events, 0.8 us)
Async XLA Ops:
  7.2 1.2 copy-start
  7.2 48.8 %reduce-scatter.2.cloned.1.call-start = ((), (), s32[]{:S(2)}) async-start(), calls=%async_computation.5 | async-start | bytes 4718592 | tf_op jit(solution)/shard_map/reduce_scatter | solution.py:49
  12.8 0.7 copy-start.6
  12.8 1.2 copy-start.1
  12.8 1.2 copy-start.3
  17.0 4.5 copy-start.8
  21.6 25.3 %copy-start.7 = (s32[1,32,8]{1,2,0:T(8,128)S(1)}, s32[1,32,8]{1,2,0:T(8,128)}, u32[]{:S(2)}) copy-start(s32[1,32,8]{1,2,0:T(8,128)} %param.12) | copy-start | bytes 3076
  35.7 23.4 %all-to-all-start.2 = ((bf16[32,8,512]{2,1,0:T(8,128)(2,1)}), bf16[32,8,512]{2,1,0:T(8,128)(2,1)S(1)}, u32[]{:S(2)}, u32[]{:S(2)}) async-start(bf16[32,8,512]{2,1,0:T(8,128)(2,1)} %fusion.14), calls=%async_computation.3 | async-start | bytes 524288 | tf_op jit(solution)/shard_map/all_to_all | solution.py:10
  59.0 20.8 %all-to-all-start = ((bf16[32,8,512]{2,1,0:T(8,128)(2,1)}), bf16[32,8,512]{2,1,0:T(8,128)(2,1)S(1)}, u32[]{:S(2)}, u32[]{:S(2)}) async-start(bf16[32,8,512]{2,1,0:T(8,128)(2,1)} %bitcast.2), calls=%async_computation.1 | async-start | bytes 524288 | tf_op jit(solution)/shard_map/all_to_all | solution.py:10
  86.1 3.3 copy-start.5
  110.3 15.4 %all-to-all-start.3 = ((bf16[32,8,512]{2,1,0:T(8,128)(2,1)}), bf16[32,8,512]{2,1,0:T(8,128)(2,1)S(1)}, u32[]{:S(2)}, u32[]{:S(2)}) async-start(bf16[32,8,512]{2,1,0:T(8,128)(2,1)} %fusion.15), calls=%async_computation.4 | async-start | bytes 524288 | tf_op jit(solution)/shard_map/all_to_all | solution.py:10
  114.9 41.6 %all-gather.2.cloned.1.call-start = ((), (), s32[]{:S(2)}) async-start(), calls=%async_computation.6 | async-start | bytes 2359296 | tf_op jit(solution)/shard_map/all_gather | solution.py:77
  128.7 289.6 %all-reduce.5.cloned.1.call-start = ((), (), s32[]{:S(2)}) async-start(), calls=%async_computation.8 | async-start | bytes 4194304 | tf_op jit(solution)/shard_map/psum | solution.py:82
  151.3 3.3 copy-start.4
  156.4 4.0 copy-start.2
  156.4 415.2 %all-reduce.3.cloned.1.call-start = ((), (), s32[]{:S(2)}) async-start(), calls=%async_computation.7 | async-start | bytes 2097152 | tf_op jit(solution)/shard_map/psum | solution.py:81
Sparse Core Ops, SparseCore 0:
  12.9 43.0 reduce-scatter.1
  128.8 24.2 all-gather.1
  159.1 259.2 all-reduce.4
  422.2 149.3 all-reduce.2
where the time goes:
time: 583 us; the launch traced here: 581 us
  waiting for transfers between devices  435 us (75%)
  other arithmetic  43.1 us (7%)
  local copies, waits for them, and re-layouts  36.9 us (6%)
  starting transfers between devices  25.9 us (4%)
  blocking collectives  15.2 us (3%)
  between operations  14.1 us (2%)
  matrix products  11.5 us (2%)
    psum x1, waiting for transfers between devices, on_device(): two_sum = lax.psum(two_sum, ('feat', 'dom'))  257 us
    psum x1, waiting for transfers between devices, on_device(): one_sum = lax.psum(one_sum.astype(jnp.bfloat16), 'dom').astype(jnp.float32)  150 us
    scatter-add x2, other arithmetic, gather_back(): jnp.zeros((nodes + sends.size, span), jnp.float32).at[nbrs.reshape(-1)]  26.1 us
    all_to_all x3, starting transfers between devices, trade(): lax.all_to_all(buffer, 'dom', split_axis=0, concat_axis=0, tiled=True)  25.8 us
    all_to_all x3, waiting for transfers between devices, trade(): lax.all_to_all(buffer, 'dom', split_axis=0, concat_axis=0, tiled=True)  19 us
    all_to_all x1, blocking collectives, trade(): lax.all_to_all(buffer, 'dom', split_axis=0, concat_axis=0, tiled=True)  15.2 us
    mul x4, local copies, waits for them, and re-layouts, gather_back(): terms = (weight[..., None] * grads[:, None, :]).reshape(-1, span)  14 us
  transfers between devices with their start and end apart: 7, of which 6 were waited for; matrix products, arithmetic and copies ran while one was open for 8% of the time, Pallas kernels for 0%

commit v1 on v0

v1 whole, which is shorter than its diff:
```python
import math

import jax
import jax.numpy as jnp
from jax import lax
from jax.experimental import pallas as pl
from jax.experimental.pallas import tpu as pltpu
from jax.sharding import PartitionSpec as P

F32 = jnp.float32
BF16 = jnp.bfloat16
CHIPS = 4
NT = (((1,), (1,)), ((), ()))
TN = (((0,), (0,)), ((), ()))


def step(core):
    return 1 if core == 0 else -1


FORWARD = [(y * 2 + c, (y + step(c)) % CHIPS * 2 + c) for y in range(CHIPS) for c in range(2)]
BACKWARD = [(y * 2 + c, (y - step(c)) % CHIPS * 2 + c) for y in range(CHIPS) for c in range(2)]
SWAP = [(i, i ^ 1) for i in range(2 * CHIPS)]


def mm(a, b, dims=(((1,), (0,)), ((), ()))):
    return lax.dot_general(a, b, dims, preferred_element_type=F32)


def whole(name, body, outs, *args):
    return pl.pallas_call(body, out_shape=outs, name=name)(*args)


def shape(dims, kind=BF16):
    return jax.ShapeDtypeStruct(dims, kind)


def trade(boxes):
    return lax.all_to_all(boxes, "dom", split_axis=0, concat_axis=0, tiled=True)


def tables_body(nbr_t, nbr, deg_row, deg_col, send_col, send_row, give, take, own, own_t):
    nodes = nbr.shape[0]
    fan = nbr.shape[1]
    span = give.shape[0]

    def entries(axis, dims):
        r = lax.broadcasted_iota(jnp.int32, dims, axis)
        return nodes + (r // 16) * 8 + r % 16, r % 16

    down, down_j = entries(0, (span, nodes))
    down = jnp.where(down_j < 8, down, -2)
    side, side_j = entries(1, (nodes, span))
    side = jnp.where(side_j >= 8, side - 8, -2)
    row = lax.broadcasted_iota(jnp.int32, (nodes, nodes), 0)
    col = lax.broadcasted_iota(jnp.int32, (nodes, nodes), 1)
    give_sum = jnp.zeros((span, nodes), F32)
    take_sum = jnp.zeros((nodes, span), F32)
    own_sum = jnp.zeros((nodes, nodes), F32)
    own_t_sum = jnp.zeros((nodes, nodes), F32)
    for s in range(fan):
        as_row = jnp.where(s < deg_row[...], nbr_t[s : s + 1, :], -1)
        as_col = jnp.where(s < deg_col[...], nbr[:, s : s + 1], -1)
        give_sum += jnp.where(down == as_row, 1.0, 0.0)
        take_sum += jnp.where(side == as_col, 1.0, 0.0)
        own_sum += jnp.where(col == as_col, 1.0, 0.0)
        own_t_sum += jnp.where(row == as_row, 1.0, 0.0)
    give[:, :nodes] = give_sum.astype(BF16)
    node_lane = lax.broadcasted_iota(jnp.int32, (span, nodes), 1)
    give[:, nodes:] = jnp.where(node_lane == send_col[...], 1.0, 0.0).astype(BF16)
    take[:nodes, :] = take_sum.astype(BF16)
    node_row = lax.broadcasted_iota(jnp.int32, (nodes, span), 0)
    take[nodes:, :] = jnp.where(node_row == send_row[...], 1.0, 0.0).astype(BF16)
    own[...] = own_sum.astype(BF16)
    own_t[...] = own_t_sum.astype(BF16)


def project(order, flat, w_one, kind):
    groups, nodes, cols = flat.shape
    width = w_one.shape[1]
    picks = order.shape[0]

    def body(order_ref, rows, w, out):
        out[0] = mm(rows[0], w[...]).astype(kind)

    return pl.pallas_call(
        body,
        out_shape=shape((picks, nodes, width), kind),
        grid_spec=pltpu.PrefetchScalarGridSpec(
            num_scalar_prefetch=1,
            grid=(picks,),
            in_specs=[
                pl.BlockSpec((1, nodes, cols), lambda i, o: (o[i], 0, 0)),
                pl.BlockSpec((cols, width), lambda i, o: (0, 0)),
            ],
            out_specs=pl.BlockSpec((1, nodes, width), lambda i, o: (i, 0, 0)),
        ),
        name="project",
        cost_estimate=pl.CostEstimate(
            flops=2 * picks * nodes * cols * width,
            bytes_accessed=2 * picks * nodes * (cols + width),
            transcendentals=0,
        ),
    )(order, flat, w_one)


def forward_body(part, got, near, far, grads, inv, give, p_self, p_near, boxes):
    width = grads.shape[1]
    total = (
        part[...] + got[...].astype(F32) + near[...].astype(F32) + far[...].astype(F32)
    )
    p_self[...] = total[:, :width]
    mine = total[:, width:].astype(BF16)
    p_near[...] = mine
    scaled = (grads[...].astype(F32) * inv[...]).astype(BF16)
    boxes[...] = mm(give[...], jnp.concatenate([scaled, mine], axis=0)).astype(BF16)


def middle_body(
    recv, p_self, p_near, grads, inv, w_two, give, take, own, own_t,
    boxes, d_pre_out, near_local, hidden_out, back_out,
):
    nodes, width = grads.shape
    both = mm(take[...], recv[...])
    grad = grads[...]
    scaled = (grad.astype(F32) * inv[...]).astype(BF16)
    pre = p_self[...] + inv[...] * (both[:nodes] + mm(own[...], p_near[...]))
    back = (both[nodes:] + mm(own_t[...], scaled)).astype(BF16)
    back_out[...] = back
    d_hidden = mm(grad, w_two[:width, :], NT) + mm(back, w_two[width:, :], NT)
    sig = jax.nn.sigmoid(pre)
    hidden = (pre * sig).astype(BF16)
    hidden_out[...] = hidden
    d_pre = d_hidden * sig * (1.0 + pre * (1.0 - sig))
    d_pre_out[...] = d_pre.astype(BF16)
    term = (d_pre * inv[...]).astype(BF16)
    boxes[...] = mm(give[...], jnp.concatenate([term, hidden], axis=0)).astype(BF16)
    near_local[...] = mm(own_t[...], term)


def near_body(recv, near_local, take, out):
    out[...] = (near_local[...] + mm(take[...], recv[...])).astype(BF16)


def out_body(recv, hidden, inv, take, own, w_two, out):
    width = hidden.shape[1]
    agg = (inv[...] * (mm(take[...], recv[...]) + mm(own[...], hidden[...]))).astype(BF16)
    out[...] = (mm(hidden[...], w_two[:width, :]) + mm(agg, w_two[width:, :])).astype(BF16)


def two_body(hidden, grads, back, out):
    width = hidden.shape[1]
    out[:width, :] = mm(hidden[...], grads[...], TN)
    out[width:, :] = mm(hidden[...], back[...], TN)


def weight_grad(name, order, flat, mine, other, *extra, finish, out):
    groups, nodes, cols = flat.shape
    width = mine.shape[2]
    half = groups // 2

    def body(order_ref, rows, a, b, *rest):
        acc = rest[-1]
        i = pl.program_id(0)

        @pl.when(i == 0)
        def _():
            acc[...] = jnp.zeros_like(acc)

        @pl.when(i < half)
        def _():
            acc[...] += mm(rows[0], a[0], TN)

        @pl.when(i >= half)
        def _():
            acc[...] += mm(rows[0], b[0], TN)

        @pl.when(i == groups - 1)
        def _():
            finish(acc, *rest[:-1])

    fixed = [pl.BlockSpec(e.shape, lambda i, o, n=e.ndim: (0,) * n) for e in extra]
    return pl.pallas_call(
        body,
        out_shape=out,
        grid_spec=pltpu.PrefetchScalarGridSpec(
            num_scalar_prefetch=1,
            grid=(groups,),
            in_specs=[
                pl.BlockSpec((1, nodes, cols), lambda i, o: (o[i], 0, 0)),
                pl.BlockSpec((1, nodes, width), lambda i, o: (jnp.minimum(i, half - 1), 0, 0)),
                pl.BlockSpec((1, nodes, width), lambda i, o: (jnp.maximum(i - half, 0), 0, 0)),
                *fixed,
            ],
            out_specs=pl.BlockSpec(out.shape, lambda i, o, n=len(out.shape): (0,) * n),
            scratch_shapes=[pltpu.VMEM((cols, width), F32)],
        ),
        name=name,
        cost_estimate=pl.CostEstimate(
            flops=2 * groups * nodes * cols * width,
            bytes_accessed=2 * groups * nodes * (cols + width),
            transcendentals=0,
        ),
    )(order, flat, mine, other, *extra)


def self_finish(acc, out):
    out[...] = acc[...].astype(BF16)


def near_finish(acc, first, out):
    parts, rows, width = out.shape
    half = rows // 2
    out[:, :half, :] = first[...].reshape(parts, half, width)
    out[:, half:, :] = acc[...].astype(BF16).reshape(parts, half, width)


def sum_body(scale, recv, out):
    total = recv[0].astype(F32)
    for k in range(1, recv.shape[0]):
        total += recv[k].astype(F32)
    out[...] = jnp.broadcast_to((total * scale).astype(BF16)[None], out.shape)


def on_device(features, w_one, w_two, neighbor, degree, send_rows, grad_out):
    groups, nodes, cols = features.shape
    width = w_two.shape[1]
    parts = lax.axis_size("dom")
    feat = lax.axis_index("feat")
    y, core = feat // 2, feat % 2
    turn = 1 - 2 * core
    nbr = neighbor[0]
    deg = degree[0]
    sends = send_rows[0]
    kmax = sends.shape[1]
    grads = grad_out[0]
    scale = 1.0 / math.sqrt(groups * nodes * parts)

    def group_ids(offsets, on_core):
        return jnp.stack([(y + o + CHIPS) % CHIPS * 2 + on_core for o in offsets])

    theirs = project(group_ids([2, turn, -turn, 0], 1 - core), features, w_one, BF16)
    got = lax.ppermute(theirs, "feat", SWAP)
    mine = project(group_ids([2, -turn, turn, 0], core), features, w_one, F32)

    inv = (1.0 / deg.astype(F32))[:, None]
    blank = jnp.full_like(sends, -1)
    send_col = jnp.concatenate([blank, sends], axis=1).reshape(-1, 1)
    send_row = jnp.concatenate([sends, blank], axis=1).reshape(1, -1)
    span = 2 * sends.size
    give, take, own, own_t = whole(
        "tables",
        tables_body,
        (
            shape((span, 2 * nodes)),
            shape((2 * nodes, span)),
            shape((nodes, nodes)),
            shape((nodes, nodes)),
        ),
        nbr.T, nbr, deg[None, :], deg[:, None], send_col, send_row,
    )

    def sent(k):
        return mine[k] + got[k].astype(F32)

    relay = lax.ppermute(sent(0).astype(BF16), "feat", FORWARD)
    near = lax.ppermute(sent(1).astype(BF16), "feat", BACKWARD)
    far = lax.ppermute((sent(2) + relay.astype(F32)).astype(BF16), "feat", FORWARD)
    p_self, p_near, boxes = whole(
        "forward",
        forward_body,
        (shape((nodes, width), F32), shape((nodes, width)), shape((span, width))),
        mine[3], got[3], near, far, grads, inv, give,
    )
    recv = trade(boxes.reshape(parts, 2 * kmax, width)).reshape(span, width)
    boxes, d_pre, near_local, hidden, back = whole(
        "middle",
        middle_body,
        (
            shape((span, width)),
            shape((nodes, width)),
            shape((nodes, width), F32),
            shape((nodes, width)),
            shape((nodes, width)),
        ),
        recv, p_self, p_near, grads, inv, w_two, give, take, own, own_t,
    )
    recv = trade(boxes.reshape(parts, 2 * kmax, width)).reshape(span, width)

    two_sum = whole("two_sum", two_body, shape((2 * width, width), F32), hidden, grads, back)
    two_sum = lax.psum_scatter(two_sum, "feat", scatter_dimension=0, tiled=True)
    two_sum = lax.psum(two_sum, "dom")
    two_sum = lax.all_gather(two_sum * scale, "feat", axis=0, tiled=True)

    def gather(block):
        one = lax.ppermute(block, "feat", FORWARD)
        two = lax.ppermute(block, "feat", BACKWARD)
        three = lax.ppermute(one, "feat", FORWARD)
        held = jnp.stack([block, one, two, three])
        return held, lax.ppermute(held, "feat", SWAP)

    order = jnp.concatenate(
        [group_ids([0, -turn, turn, 2], core), group_ids([0, turn, -turn, 2], 1 - core)]
    )
    first = weight_grad(
        "self_grad", order, features, *gather(d_pre), finish=self_finish, out=shape((cols, width))
    )
    d_near = whole(
        "near", near_body, shape((nodes, width)), recv, near_local, take[nodes:, :]
    )
    out = whole(
        "out", out_body, shape((nodes, width)), recv, hidden, inv, take[:nodes, :], own, w_two
    )
    rows = 2 * cols // parts
    terms = weight_grad(
        "near_grad", order, features, *gather(d_near), first,
        finish=near_finish, out=shape((parts, rows, width)),
    )
    terms = trade(terms)
    chunk = whole(
        "sum", lambda recv, out: sum_body(scale, recv, out), shape((parts, rows, width)), terms
    )
    full = trade(chunk).astype(F32)
    one_sum = jnp.concatenate([full[:, : rows // 2], full[:, rows // 2 :]], axis=2)
    return out[None], one_sum.reshape(cols, 2 * width), two_sum


def solution(mesh):
    in_specs = (
        P(None, "dom", "feat"),
        P("feat", None),
        P(),
        P("feat", "dom", None),
        P("feat", "dom"),
        P("feat", "dom", None),
        P("feat", "dom", None),
    )
    out_specs = (P("feat", "dom", None), P("feat", None), P())
    return jax.shard_map(
        on_device, mesh=mesh, in_specs=in_specs, out_specs=out_specs, check_vma=False
    )
```

time: 583 us -> 337 us (0.58)
  waiting for transfers between devices: 435 us -> 195 us
  Pallas kernels: 0 us -> 44.6 us
  other arithmetic: 43.1 us -> 9.52 us
  local copies, waits for them, and re-layouts: 36.9 us -> 12.7 us
  blocking collectives: 15.2 us -> 28.2 us
  matrix products: 11.5 us -> 0 us
    psum x2 -> x1, waiting for transfers between devices: 407 us -> 146 us  [on_device(): two_sum = lax.psum(two_sum, 'dom')]
    pallas_call x0 -> x11, Pallas kernels: none -> 44.6 us  [the longest x7 19.4 us: whole(): return pl.pallas_call(body, out_shape=outs, name=name)(*args)]
    scatter-add x4 -> x0, other arithmetic: 30.8 us -> none  [the longest x2 26.1 us: gather_back(): jnp.zeros((nodes + sends.size, span), jnp.float32).at[nbrs.reshape(-1)]]
    all_to_all x3, waiting for transfers between devices: 19 us -> 36.9 us  [trade(): return lax.all_to_all(boxes, 'dom', split_axis=0, concat_axis=0, tiled=True)]
    mul x4 -> x0, local copies, waits for them, and re-layouts: 14 us -> none  [gather_back(): terms = (weight[..., None] * grads[:, None, :]).reshape(-1, span)]
    all_to_all x1, blocking collectives: 15.2 us -> 28.2 us  [trade(): return lax.all_to_all(boxes, 'dom', split_axis=0, concat_axis=0, tiled=True)]
    ppermute x0 -> x12, starting transfers between devices: none -> 11.8 us  [the longest x2 6.47 us: gather(): two = lax.ppermute(block, 'feat', BACKWARD)]
    dot_general x5 -> x0, matrix products: 11.5 us -> none  [the longest x1 4.4 us: on_device(): jnp.dot(rows, w_one, preferred_element_type=jnp.float32)]
  transfers between devices with their start and end apart: 7 -> 18, of which waited for: 6 -> 7; matrix products, arithmetic and copies ran while one was open for 8% -> 4% of each run, Pallas kernels for 0% -> 9%
where the time goes in v1:
time: 337 us; the launch traced here: 335 us
  waiting for transfers between devices  195 us (58%)
  Pallas kernels  44.6 us (13%)
  starting transfers between devices  30.9 us (9%)
  blocking collectives  28.2 us (8%)
  between operations  14 us (4%)
  local copies, waits for them, and re-layouts  12.7 us (4%)
  other arithmetic  9.52 us (3%)
    psum x1, waiting for transfers between devices, on_device(): two_sum = lax.psum(two_sum, 'dom')  146 us
    all_to_all x3, waiting for transfers between devices, trade(): return lax.all_to_all(boxes, 'dom', split_axis=0, concat_axis=0, tiled=True)  36.9 us
    all_to_all x1, blocking collectives, trade(): return lax.all_to_all(boxes, 'dom', split_axis=0, concat_axis=0, tiled=True)  28.2 us
    pallas_call x7, Pallas kernels, whole(): return pl.pallas_call(body, out_shape=outs, name=name)(*args)  19.4 us
    all_to_all x3, starting transfers between devices, trade(): return lax.all_to_all(boxes, 'dom', split_axis=0, concat_axis=0, tiled=True)  19 us
    pallas_call x2, Pallas kernels, weight_grad(): pl.pallas_call(body, out_shape=out, grid_spec=pltpu.PrefetchScalarGridSpe...  15.2 us
    pallas_call x2, Pallas kernels, project(): pl.pallas_call(body, out_shape=shape((picks, nodes, width), kind), grid_s...  10.1 us
    unnamed x31, local copies, waits for them, and re-layouts  8.09 us
  transfers between devices with their start and end apart: 18, of which 7 were waited for; matrix products, arithmetic and copies ran while one was open for 4% of the time, Pallas kernels for 9%

profile of v1, /device:TPU:32, one launch (start us, length us, event | category | flops | bytes accessed | tf_op | source)
XLA Modules:
  0.0 334.5 jit_solution(12073299712450248318)
XLA Ops:
  7.3 0.6 pad_add_fusion.1.order_ref
  7.9 4.9 %project.3 = bf16[4,128,1024]{2,1,0:T(8,128)(2,1)} custom-call(s32[4]{0:T(128)} %pad_add_fusion.1.order_ref, bf16[8,128,512]{2,1,0:T(8,128)(2,1)} %rows.7, bf16[512,1024]{1,0:T(8,128)(2,1)} %w.3), custom_call_target="tpu_custom_call" | custom-call | flops 536870912 | bytes 1572864 | tf_op jit(solution)/shard_map/project/pallas_call | solution.py:86
  13.4 5.1 %project.2 = f32[4,128,1024]{2,1,0:T(8,128)} custom-call(s32[4]{0:T(128)} %pad_add_fusion.order_ref, bf16[8,128,512]{2,1,0:T(8,128)(2,1)} %rows.7, bf16[512,1024]{1,0:T(8,128)(2,1)} %w.3), custom_call_target="tpu_custom_call" | custom-call | flops 536870912 | bytes 1572864 | tf_op jit(solution)/shard_map/project/pallas_call | solution.py:86
  18.6 2.4 fusion.6
  21.0 1.6 collective-permute-start.2
  22.7 0.6 convert_divide_fusion.inv
  23.4 1.7 collective-permute-start.1
  25.0 3.5 %collective-permute-done.2 = bf16[128,1024]{1,0:T(8,128)(2,1)S(1)} collective-permute-done((bf16[128,1024]{1,0:T(8,128)(2,1)S(1)}, bf16[128,1024]{1,0:T(8,128)(2,1)S(1)}, u32[]{:S(2)}, u32[]{:S(2)}) %collective-permute-start.2) | collective-permute-done | bytes 262176 | tf_op jit(solution)/shard_map/ppermute | solution.py:266
  28.5 1.1 fusion.3
  29.7 1.9 collective-permute-start.3
  31.6 0.6 copy.27
  32.2 0.7 copy.17
  33.0 0.7 reshape.49.send_row
  33.6 0.9 reshape.55.send_col
  34.5 2.9 tables.1
  37.4 0.7 slice_bitcast_fusion.1.got
  38.1 0.7 copy-done.8
  38.9 2.7 forward.1
  41.6 28.2 %all_to_all.20 = bf16[32,16,512]{2,1,0:T(8,128)(2,1)} all-to-all(bf16[32,16,512]{2,1,0:T(8,128)(2,1)} %bitcast.51), channel_id=1, replica_groups=mesh['feat'=8,'dom'=32] {'dom'}, dimensions={0} | all-to-all | bytes 1048576 | tf_op jit(solution)/shard_map/all_to_all | solution.py:39
  69.8 3.6 %middle.1 = (bf16[512,512]{1,0:T(8,128)(2,1)}, bf16[128,512]{1,0:T(8,128)(2,1)}, f32[128,512]{1,0:T(8,128)}, bf16[128,512]{1,0:T(8,128)(2,1)}, bf16[128,512]{1,0:T(8,128)(2,1)}) custom-call(bf16[512,512]{1,0:T(8,128)(2,1)} %bitcast.47, f32[128,512]{1,0:T(8,128)} %get-tuple-element.17.p_self, bf16[128,512]{1,0:T(8,128)(2,1)} %get-tuple-element.18.p_near, ...), custom_call_target="tpu_custom_call" | custom-call | tf_op jit(solution)/shard_map/middle/pallas_call | solution.py:31
  73.4 2.8 two_sum.1
  76.3 6.5 %all-to-all-start.1 = ((bf16[32,16,512]{2,1,0:T(8,128)(2,1)}), bf16[32,16,512]{2,1,0:T(8,128)(2,1)S(1)}, u32[]{:S(2)}, u32[]{:S(2)}) async-start(bf16[32,16,512]{2,1,0:T(8,128)(2,1)} %bitcast.21), calls=%async_computation.1 | async-start | bytes 1048576 | tf_op jit(solution)/shard_map/all_to_all | solution.py:39
  82.9 0.7 fusion.8
  83.6 16.8 %all-to-all-done.1 = bf16[32,16,512]{2,1,0:T(8,128)(2,1)S(1)} async-done(((bf16[32,16,512]{2,1,0:T(8,128)(2,1)}), bf16[32,16,512]{2,1,0:T(8,128)(2,1)S(1)}, u32[]{:S(2)}, u32[]{:S(2)}) %all-to-all-start.1) | async-done | bytes 524320 | tf_op jit(solution)/shard_map/all_to_all | solution.py:39
  100.4 0.8 copy-done
  101.2 2.0 near.1
  103.3 3.2 collective-permute-start.9
  106.5 3.2 collective-permute-start.5
  109.8 1.8 collective-permute-done.4
  111.6 1.4 collective-permute-done.10
  113.2 4.6 %collective-permute-done.6 = bf16[128,512]{1,0:T(8,128)(2,1)S(1)} collective-permute-done((bf16[128,512]{1,0:T(8,128)(2,1)S(1)}, bf16[128,512]{1,0:T(8,128)(2,1)S(1)}, u32[]{:S(2)}, u32[]{:S(2)}) %collective-permute-start.6) | collective-permute-done | bytes 131104 | tf_op jit(solution)/shard_map/ppermute | solution.py:298
  117.7 1.0 pad_maximum_fusion.1.a
  118.8 0.6 concatenate.14.order_ref
  119.4 0.8 copy-done.6
  120.2 7.4 %self_grad.1.rest_0_ = bf16[512,512]{1,0:T(8,128)(2,1)} custom-call(s32[8]{0:T(128)} %concatenate.14.order_ref, bf16[8,128,512]{2,1,0:T(8,128)(2,1)} %rows.7, bf16[4,128,512]{2,1,0:T(8,128)(2,1)} %copy-done.2, bf16[4,128,512]{2,1,0:T(8,128)(2,1)} %copy-done.6), custom_call_target="tpu_custom_call" | custom-call | flops 536870912 | bytes 2097152 | tf_op jit(solution)/shard_map/self_grad/pallas_call | solution.py:183
  127.6 0.8 copy-done.7
  128.4 7.8 %near_grad.1 = bf16[32,32,512]{2,1,0:T(8,128)(2,1)} custom-call(s32[8]{0:T(128)} %concatenate.14.order_ref, bf16[8,128,512]{2,1,0:T(8,128)(2,1)} %rows.7, bf16[4,128,512]{2,1,0:T(8,128)(2,1)} %copy-done.3, bf16[4,128,512]{2,1,0:T(8,128)(2,1)} %copy-done.7, bf16[512,512]{1,0:T(8,128)(2,1)} %self_grad.1.rest_0_), custom_call_target="tpu_custom_call" | custom-call | flops 536870912 | bytes 2097152 | tf_op jit(solution)/shard_map/near_grad/pallas_call | solution.py:183
  136.2 5.8 %all-to-all-start.2 = ((bf16[32,32,512]{2,1,0:T(8,128)(2,1)}), bf16[32,32,512]{2,1,0:T(8,128)(2,1)S(1)}, u32[]{:S(2)}, u32[]{:S(2)}) async-start(bf16[32,32,512]{2,1,0:T(8,128)(2,1)} %near_grad.1), calls=%async_computation.2 | async-start | bytes 2097152 | tf_op jit(solution)/shard_map/all_to_all | solution.py:39
  142.1 0.7 all-reduce.4.cloned.1.call-update
  142.8 145.6 %all-reduce.4.cloned.1.call-done = f32[128,512]{1,0:T(8,128)} async-done(((f32[128,512]{1,0:T(8,128)}), f32[128,512]{1,0:T(8,128)}) %all-reduce.4.cloned.1.call-update) | async-done | bytes 262160 | tf_op jit(solution)/shard_map/psum | solution.py:292
  288.4 1.7 broadcast_multiply_fusion
  290.1 1.0 copy-done.1
  291.1 2.4 sum.1
  293.5 6.7 %all-to-all-start.3 = ((bf16[32,32,512]{2,1,0:T(8,128)(2,1)}), bf16[32,32,512]{2,1,0:T(8,128)(2,1)S(1)}, u32[]{:S(2)}, u32[]{:S(2)}) async-start(bf16[32,32,512]{2,1,0:T(8,128)(2,1)} %sum.1), calls=%async_computation.3 | async-start | bytes 2097152 | tf_op jit(solution)/shard_map/all_to_all | solution.py:39
  300.2 2.9 out.1
  303.1 20.1 %all-to-all-done.3 = bf16[32,32,512]{2,1,0:T(8,128)(2,1)S(1)} async-done(((bf16[32,32,512]{2,1,0:T(8,128)(2,1)}), bf16[32,32,512]{2,1,0:T(8,128)(2,1)S(1)}, u32[]{:S(2)}, u32[]{:S(2)}) %all-to-all-start.3) | async-done | bytes 1048608 | tf_op jit(solution)/shard_map/all_to_all | solution.py:39
  323.5 1.5 pad_maximum_fusion
  324.9 3.1 copy.30
  (52 shorter events, 1.8 us)
Async XLA Ops:
  7.2 134.9 %reduce-scatter.2.cloned.1.call-start = ((), (), s32[]{:S(2)}) async-start(), calls=%async_computation.5 | async-start | bytes 2359296 | tf_op jit(solution)/shard_map/reduce_scatter | solution.py:291
  12.8 5.7 %collective-permute-start = (bf16[4,128,1024]{2,1,0:T(8,128)(2,1)}, bf16[4,128,1024]{2,1,0:T(8,128)(2,1)S(1)}, u32[]{:S(2)}, u32[]{:S(2)}) collective-permute-start(bf16[4,128,1024]{2,1,0:T(8,128)(2,1)} %project.3), channel_id=1, source_target_pairs={{0,32},{32,0},{64,96},{96,64},{128,160},{160,128},{192,224},{224,1... | collective-permute-start | bytes 3145736 | tf_op jit(solution)/shard_map/ppermute | solution.py:243
  18.5 4.0 %copy-start.12 = (s32[1,32,8]{1,2,0:T(8,128)S(1)}, s32[1,32,8]{1,2,0:T(8,128)}, u32[]{:S(2)}) copy-start(s32[1,32,8]{1,2,0:T(8,128)} %param.12) | copy-start | bytes 3076
  18.6 4.1 %copy-start.13 = (s32[1,128]{1,0:T(1,128)S(1)}, s32[1,128]{1,0:T(1,128)}, u32[]{:S(2)}) copy-start(s32[1,128]{1,0:T(1,128)} %deg_row.1) | copy-start | bytes 1540
  18.6 13.1 %copy-start.11 = (s32[1,128,10]{1,0,2:T(1,128)S(1)}, s32[1,128,10]{1,0,2:T(1,128)}, u32[]{:S(2)}) copy-start(s32[1,128,10]{1,0,2:T(1,128)} %param.10) | copy-start | bytes 15364
  21.0 7.6 %collective-permute-start.2 = (bf16[128,1024]{1,0:T(8,128)(2,1)S(1)}, bf16[128,1024]{1,0:T(8,128)(2,1)S(1)}, u32[]{:S(2)}, u32[]{:S(2)}) collective-permute-start(bf16[128,1024]{1,0:T(8,128)(2,1)S(1)} %get-tuple-element.27), channel_id=1, source_target_pairs={{0,64},{32,224},{64,128},{96,32},{128,192},{160,96},{192,0},{224,1... | collective-permute-start | bytes 786440 | tf_op jit(solution)/shard_map/ppermute | solution.py:266
  22.7 11.8 %copy-start.5 = (s32[128,1]{1,0:T(8,128)}, s32[128,1]{1,0:T(8,128)S(1)}, u32[]{:S(2)}) copy-start(s32[128,1]{1,0:T(8,128)S(1)} %copy.16.deg_col) | copy-start | bytes 1540
  23.4 14.7 %collective-permute-start.1 = (bf16[128,1024]{1,0:T(8,128)(2,1)S(1)}, bf16[128,1024]{1,0:T(8,128)(2,1)S(1)}, u32[]{:S(2)}, u32[]{:S(2)}) collective-permute-start(bf16[128,1024]{1,0:T(8,128)(2,1)S(1)} %get-tuple-element.28), channel_id=1, source_target_pairs={{0,192},{32,96},{64,0},{96,160},{128,64},{160,224},{192,128},{224,... | collective-permute-start | bytes 786440 | tf_op jit(solution)/shard_map/ppermute | solution.py:267
  29.7 8.4 %collective-permute-start.3 = (bf16[128,1024]{1,0:T(8,128)(2,1)S(1)}, bf16[128,1024]{1,0:T(8,128)(2,1)S(1)}, u32[]{:S(2)}, u32[]{:S(2)}) collective-permute-start(bf16[128,1024]{1,0:T(8,128)(2,1)S(1)} %fusion.3), channel_id=1, source_target_pairs={{0,64},{32,224},{64,128},{96,32},{128,192},{160,96},{192,0},{224,1... | collective-permute-start | bytes 786440 | tf_op jit(solution)/shard_map/ppermute | solution.py:268
  38.1 0.7 copy-start.8
  38.1 0.8 copy-start.9
  76.2 6.5 %copy-start.10 = (bf16[128,512]{1,0:T(8,128)(2,1)S(1)}, bf16[128,512]{1,0:T(8,128)(2,1)}, u32[]{:S(2)}) copy-start(bf16[128,512]{1,0:T(8,128)(2,1)} %get-tuple-element.25) | copy-start | bytes 393220
  76.2 6.6 %copy-start.4 = (bf16[256,512]{1,0:T(8,128)(2,1)S(1)}, bf16[256,512]{1,0:T(8,128)(2,1)}, u32[]{:S(2)}) copy-start(bf16[256,512]{1,0:T(8,128)(2,1)} %get-tuple-element.19.take) | copy-start | bytes 786436
  76.3 24.2 %all-to-all-start.1 = ((bf16[32,16,512]{2,1,0:T(8,128)(2,1)}), bf16[32,16,512]{2,1,0:T(8,128)(2,1)S(1)}, u32[]{:S(2)}, u32[]{:S(2)}) async-start(bf16[32,16,512]{2,1,0:T(8,128)(2,1)} %bitcast.21), calls=%async_computation.1 | async-start | bytes 1048576 | tf_op jit(solution)/shard_map/all_to_all | solution.py:39
  82.8 23.7 %collective-permute-start.8 = (bf16[128,512]{1,0:T(8,128)(2,1)S(1)}, bf16[128,512]{1,0:T(8,128)(2,1)S(1)}, u32[]{:S(2)}, u32[]{:S(2)}) collective-permute-start(bf16[128,512]{1,0:T(8,128)(2,1)S(1)} %copy-done.10), channel_id=1, source_target_pairs={{0,64},{32,224},{64,128},{96,32},{128,192},{160,96},{192,0},{224,1... | collective-permute-start | bytes 393224 | tf_op jit(solution)/shard_map/ppermute | solution.py:296
  100.4 0.8 copy-start
  103.3 8.3 %collective-permute-start.4 = (bf16[128,512]{1,0:T(8,128)(2,1)}, bf16[128,512]{1,0:T(8,128)(2,1)S(1)}, u32[]{:S(2)}, u32[]{:S(2)}) collective-permute-start(bf16[128,512]{1,0:T(8,128)(2,1)} %near.1), channel_id=1, source_target_pairs={{0,64},{32,224},{64,128},{96,32},{128,192},{160,96},{192,0},{224,1... | collective-permute-start | bytes 393224 | tf_op jit(solution)/shard_map/ppermute | solution.py:296
  103.3 8.3 %collective-permute-start.9 = (bf16[128,512]{1,0:T(8,128)(2,1)S(1)}, bf16[128,512]{1,0:T(8,128)(2,1)S(1)}, u32[]{:S(2)}, u32[]{:S(2)}) collective-permute-start(bf16[128,512]{1,0:T(8,128)(2,1)S(1)} %copy-done.10), channel_id=1, source_target_pairs={{0,192},{32,96},{64,0},{96,160},{128,64},{160,224},{192,128},{224,... | collective-permute-start | bytes 393224 | tf_op jit(solution)/shard_map/ppermute | solution.py:297
  106.5 6.4 %collective-permute-start.10 = (bf16[128,512]{1,0:T(8,128)(2,1)S(1)}, bf16[128,512]{1,0:T(8,128)(2,1)S(1)}, u32[]{:S(2)}, u32[]{:S(2)}) collective-permute-start(bf16[128,512]{1,0:T(8,128)(2,1)S(1)} %collective-permute-done.8), channel_id=1, source_target_pairs={{0,64},{32,224},{64,128},{96,32},{128,192},{160,96},{192,0},{224,1... | collective-permute-start | bytes 393224 | tf_op jit(solution)/shard_map/ppermute | solution.py:298
  106.5 6.6 %collective-permute-start.5 = (bf16[128,512]{1,0:T(8,128)(2,1)}, bf16[128,512]{1,0:T(8,128)(2,1)S(1)}, u32[]{:S(2)}, u32[]{:S(2)}) collective-permute-start(bf16[128,512]{1,0:T(8,128)(2,1)} %near.1), channel_id=1, source_target_pairs={{0,192},{32,96},{64,0},{96,160},{128,64},{160,224},{192,128},{224,... | collective-permute-start | bytes 393224 | tf_op jit(solution)/shard_map/ppermute | solution.py:297
  111.6 6.2 %collective-permute-start.6 = (bf16[128,512]{1,0:T(8,128)(2,1)S(1)}, bf16[128,512]{1,0:T(8,128)(2,1)S(1)}, u32[]{:S(2)}, u32[]{:S(2)}) collective-permute-start(bf16[128,512]{1,0:T(8,128)(2,1)S(1)} %collective-permute-done.4), channel_id=1, source_target_pairs={{0,64},{32,224},{64,128},{96,32},{128,192},{160,96},{192,0},{224,1... | collective-permute-start | bytes 393224 | tf_op jit(solution)/shard_map/ppermute | solution.py:298
  113.0 6.4 %copy-start.2 = (bf16[4,128,512]{2,1,0:T(8,128)(2,1)}, bf16[4,128,512]{2,1,0:T(8,128)(2,1)S(1)}, u32[]{:S(2)}) copy-start(bf16[4,128,512]{2,1,0:T(8,128)(2,1)S(1)} %pad_maximum_fusion.2.a) | copy-start | bytes 1572868
  113.0 6.4 %collective-permute-start.11 = (bf16[4,128,512]{2,1,0:T(8,128)(2,1)S(1)}, bf16[4,128,512]{2,1,0:T(8,128)(2,1)S(1)}, u32[]{:S(2)}, u32[]{:S(2)}) collective-permute-start(bf16[4,128,512]{2,1,0:T(8,128)(2,1)S(1)} %pad_maximum_fusion.2.a), channel_id=1, source_target_pairs={{0,32},{32,0},{64,96},{96,64},{128,160},{160,128},{192,224},{224,1... | collective-permute-start | bytes 1572872 | tf_op jit(solution)/shard_map/ppermute | solution.py:300
  118.7 8.9 %copy-start.3 = (bf16[4,128,512]{2,1,0:T(8,128)(2,1)}, bf16[4,128,512]{2,1,0:T(8,128)(2,1)S(1)}, u32[]{:S(2)}) copy-start(bf16[4,128,512]{2,1,0:T(8,128)(2,1)S(1)} %pad_maximum_fusion.1.a) | copy-start | bytes 1572868
  118.7 8.9 %collective-permute-start.7 = (bf16[4,128,512]{2,1,0:T(8,128)(2,1)S(1)}, bf16[4,128,512]{2,1,0:T(8,128)(2,1)S(1)}, u32[]{:S(2)}, u32[]{:S(2)}) collective-permute-start(bf16[4,128,512]{2,1,0:T(8,128)(2,1)S(1)} %pad_maximum_fusion.1.a), channel_id=1, source_target_pairs={{0,32},{32,0},{64,96},{96,64},{128,160},{160,128},{192,224},{224,1... | collective-permute-start | bytes 1572872 | tf_op jit(solution)/shard_map/ppermute | solution.py:300
  119.4 0.8 copy-start.6
  127.6 0.8 copy-start.7
  136.2 153.9 %all-to-all-start.2 = ((bf16[32,32,512]{2,1,0:T(8,128)(2,1)}), bf16[32,32,512]{2,1,0:T(8,128)(2,1)S(1)}, u32[]{:S(2)}, u32[]{:S(2)}) async-start(bf16[32,32,512]{2,1,0:T(8,128)(2,1)} %near_grad.1), calls=%async_computation.2 | async-start | bytes 2097152 | tf_op jit(solution)/shard_map/all_to_all | solution.py:39
  142.0 146.4 %all-reduce.4.cloned.1.call-start = ((), (), s32[]{:S(2)}) async-start(), calls=%async_computation.6 | async-start | bytes 524288 | tf_op jit(solution)/shard_map/psum | solution.py:292
  142.8 182.2 %all-gather.2.cloned.1.call-start = ((), (), s32[]{:S(2)}) async-start(), calls=%async_computation.7 | async-start | bytes 2359296 | tf_op jit(solution)/shard_map/all_gather | solution.py:293
  290.1 1.0 copy-start.1
  293.5 29.7 %all-to-all-start.3 = ((bf16[32,32,512]{2,1,0:T(8,128)(2,1)}), bf16[32,32,512]{2,1,0:T(8,128)(2,1)S(1)}, u32[]{:S(2)}, u32[]{:S(2)}) async-start(bf16[32,32,512]{2,1,0:T(8,128)(2,1)} %sum.1), calls=%async_computation.3 | async-start | bytes 2097152 | tf_op jit(solution)/shard_map/all_to_all | solution.py:39
Sparse Core Ops, SparseCore 0:
  76.4 34.5 reduce-scatter.1
  146.3 142.0 all-reduce.3
  290.3 25.6 all-gather.1

commit v2 on v1

--- a/solution.py
+++ b/solution.py
@@ -75,33 +75,39 @@
     own_t[...] = own_t_sum.astype(BF16)
 
 
-def project(order, flat, w_one, kind):
+def places(offsets, other):
+    feat = lax.axis_index("feat")
+    y, core = feat // 2, feat % 2
+    turn = 1 - 2 * core
+    held = 1 - core if other else core
+    return [(y + CHIPS + o * (turn if t else 1)) % CHIPS * 2 + held for o, t in offsets]
+
+
+SUM_MINE = ((2, False), (-1, True), (1, True), (0, False))
+SUM_OTHER = ((2, False), (1, True), (-1, True), (0, False))
+GET_MINE = ((0, False), (-1, True), (1, True), (2, False))
+GET_OTHER = ((0, False), (1, True), (-1, True), (2, False))
+
+
+def project(flat, w_one, other, kind):
     groups, nodes, cols = flat.shape
     width = w_one.shape[1]
-    picks = order.shape[0]
-
-    def body(order_ref, rows, w, out):
-        out[0] = mm(rows[0], w[...]).astype(kind)
+
+    def body(rows, w, out):
+        ids = places(SUM_OTHER if other else SUM_MINE, other)
+        picked = jnp.concatenate([rows[g] for g in ids], axis=0)
+        out[...] = mm(picked, w[...]).astype(kind).reshape(out.shape)
 
     return pl.pallas_call(
         body,
-        out_shape=shape((picks, nodes, width), kind),
-        grid_spec=pltpu.PrefetchScalarGridSpec(
-            num_scalar_prefetch=1,
-            grid=(picks,),
-            in_specs=[
-                pl.BlockSpec((1, nodes, cols), lambda i, o: (o[i], 0, 0)),
-                pl.BlockSpec((cols, width), lambda i, o: (0, 0)),
-            ],
-            out_specs=pl.BlockSpec((1, nodes, width), lambda i, o: (i, 0, 0)),
-        ),
+        out_shape=shape((CHIPS, nodes, width), kind),
         name="project",
         cost_estimate=pl.CostEstimate(
-            flops=2 * picks * nodes * cols * width,
-            bytes_accessed=2 * picks * nodes * (cols + width),
+            flops=2 * CHIPS * nodes * cols * width,
+            bytes_accessed=2 * (groups * nodes * cols + cols * width),
             transcendentals=0,
         ),
-    )(order, flat, w_one)
+    )(flat, w_one)
 
 
 def forward_body(part, got, near, far, grads, inv, give, p_self, p_near, boxes):
@@ -148,71 +154,68 @@
     out[...] = (mm(hidden[...], w_two[:width, :]) + mm(agg, w_two[width:, :])).astype(BF16)
 
 
-def two_body(hidden, grads, back, out):
+def two_body(hidden, grads, back, mine, theirs):
     width = hidden.shape[1]
-    out[:width, :] = mm(hidden[...], grads[...], TN)
-    out[width:, :] = mm(hidden[...], back[...], TN)
-
-
-def weight_grad(name, order, flat, mine, other, *extra, finish, out):
+    nodes = mine.shape[1]
+    both = jnp.concatenate([grads[...], back[...]], axis=1)
+    pair = mm(hidden[...], both, TN)
+    total = jnp.concatenate([pair[:, :width], pair[:, width:]], axis=0)
+    total = total.reshape(2 * CHIPS, nodes, width)
+
+    def run(scratch):
+        scratch[...] = total
+        for k, g in enumerate(places(SUM_MINE, False)):
+            mine[k] = scratch[g]
+        for k, g in enumerate(places(SUM_OTHER, True)):
+            theirs[k] = scratch[g].astype(BF16)
+
+    pl.run_scoped(run, pltpu.VMEM(total.shape, F32))
+
+
+def mix_body(mine, got, block, ahead, behind):
+    ahead[0] = block[...]
+    behind[0] = block[...]
+    ahead[1] = (mine[0] + got[0].astype(F32)).astype(BF16)
+    behind[1] = (mine[1] + got[1].astype(F32)).astype(BF16)
+
+
+def pass_body(mine, got, relay, ahead):
+    ahead[0] = relay[0]
+    ahead[1] = (mine[2] + got[2].astype(F32) + relay[1].astype(F32)).astype(BF16)
+
+
+def turn_body(flat, out):
     groups, nodes, cols = flat.shape
-    width = mine.shape[2]
-    half = groups // 2
-
-    def body(order_ref, rows, a, b, *rest):
-        acc = rest[-1]
-        i = pl.program_id(0)
-
-        @pl.when(i == 0)
-        def _():
-            acc[...] = jnp.zeros_like(acc)
-
-        @pl.when(i < half)
-        def _():
-            acc[...] += mm(rows[0], a[0], TN)
-
-        @pl.when(i >= half)
-        def _():
-            acc[...] += mm(rows[0], b[0], TN)
-
-        @pl.when(i == groups - 1)
-        def _():
-            finish(acc, *rest[:-1])
-
-    fixed = [pl.BlockSpec(e.shape, lambda i, o, n=e.ndim: (0,) * n) for e in extra]
-    return pl.pallas_call(
-        body,
-        out_shape=out,
-        grid_spec=pltpu.PrefetchScalarGridSpec(
-            num_scalar_prefetch=1,
-            grid=(groups,),
-            in_specs=[
-                pl.BlockSpec((1, nodes, cols), lambda i, o: (o[i], 0, 0)),
-                pl.BlockSpec((1, nodes, width), lambda i, o: (jnp.minimum(i, half - 1), 0, 0)),
-                pl.BlockSpec((1, nodes, width), lambda i, o: (jnp.maximum(i - half, 0), 0, 0)),
-                *fixed,
-            ],
-            out_specs=pl.BlockSpec(out.shape, lambda i, o, n=len(out.shape): (0,) * n),
-            scratch_shapes=[pltpu.VMEM((cols, width), F32)],
-        ),
-        name=name,
-        cost_estimate=pl.CostEstimate(
-            flops=2 * groups * nodes * cols * width,
-            bytes_accessed=2 * groups * nodes * (cols + width),
-            transcendentals=0,
-        ),
-    )(order, flat, mine, other, *extra)
-
-
-def self_finish(acc, out):
-    out[...] = acc[...].astype(BF16)
-
-
-def near_finish(acc, first, out):
+    for g in range(groups):
+        out[:, g * nodes : (g + 1) * nodes] = flat[g].T
+
+
+def grad_of(flat_t, blocks, other, stack):
+    for g, block in zip(places(GET_MINE, False), blocks):
+        stack[g] = block
+    for k, g in enumerate(places(GET_OTHER, True)):
+        stack[g] = other[k]
+    groups, nodes, width = stack.shape
+    return mm(flat_t[...], stack[...].reshape(groups * nodes, width))
+
+
+def self_body(flat_t, b0, b1, b2, b3, other, out, stack):
+    out[...] = grad_of(flat_t, (b0[...], b1[0], b2[0], b3[0]), other, stack).astype(BF16)
+
+
+def near_grad_body(flat_t, b0, b1, b2, b3, other, first, mine, got, near, far, out, stack):
     parts, rows, width = out.shape
-    half = rows // 2
-    out[:, :half, :] = first[...].reshape(parts, half, width)
-    out[:, half:, :] = acc[...].astype(BF16).reshape(parts, half, width)
+    part = rows // 9 * 2
+    total = grad_of(flat_t, (b0[...], b1[...], b2[...], b3[...]), other, stack).astype(BF16)
+    for k in range(2):
+        cut = slice(k * width, (k + 1) * width)
+        out[:, k * part : (k + 1) * part, :] = first[:, cut].reshape(parts, part, width)
+        out[:, (k + 2) * part : (k + 3) * part, :] = total[:, cut].reshape(parts, part, width)
+    two = mine[3] + got[3].astype(F32) + near[1].astype(F32) + far[1].astype(F32)
+    half = parts // 2
+    for k in range(2):
+        cut = two[:, k * width : (k + 1) * width].astype(BF16)
+        out[k * half : (k + 1) * half, 4 * part :, :] = cut.reshape(half, part // 2, width)
 
 
 def sum_body(scale, recv, out):
@@ -222,13 +225,30 @@
     out[...] = jnp.broadcast_to((total * scale).astype(BF16)[None], out.shape)
 
 
+def spread_body(full, out):
+    parts, rows, width = full.shape
+    part = out.shape[0] // parts
+    for k in range(4):
+        piece = full[:, k * part : (k + 1) * part, :].astype(F32)
+        out[:, k * width : (k + 1) * width] = piece.reshape(parts * part, width)
+
+
+def join_body(b0, b1, b2, b3, other, out):
+    nodes = b0.shape[0]
+
+    def put(g, block):
+        out[pl.ds(pl.multiple_of(g * nodes, nodes), nodes), :] = block.astype(F32)
+
+    for g, block in zip(places(GET_MINE, False), (b0, b1, b2, b3)):
+        put(g, block[...])
+    for k, g in enumerate(places(GET_OTHER, True)):
+        put(g, other[k])
+
+
 def on_device(features, w_one, w_two, neighbor, degree, send_rows, grad_out):
     groups, nodes, cols = features.shape
     width = w_two.shape[1]
     parts = lax.axis_size("dom")
-    feat = lax.axis_index("feat")
-    y, core = feat // 2, feat % 2
-    turn = 1 - 2 * core
     nbr = neighbor[0]
     deg = degree[0]
     sends = send_rows[0]
@@ -236,12 +256,17 @@
     grads = grad_out[0]
     scale = 1.0 / math.sqrt(groups * nodes * parts)
 
-    def group_ids(offsets, on_core):
-        return jnp.stack([(y + o + CHIPS) % CHIPS * 2 + on_core for o in offsets])
-
-    theirs = project(group_ids([2, turn, -turn, 0], 1 - core), features, w_one, BF16)
-    got = lax.ppermute(theirs, "feat", SWAP)
-    mine = project(group_ids([2, -turn, turn, 0], core), features, w_one, F32)
+    def forward(block):
+        return lax.ppermute(block, "feat", FORWARD)
+
+    def backward(block):
+        return lax.ppermute(block, "feat", BACKWARD)
+
+    def swap(block):
+        return lax.ppermute(block, "feat", SWAP)
+
+    got = swap(project(features, w_one, True, BF16))
+    mine = project(features, w_one, False, F32)
 
     inv = (1.0 / deg.astype(F32))[:, None]
     blank = jnp.full_like(sends, -1)
@@ -259,13 +284,14 @@
         ),
         nbr.T, nbr, deg[None, :], deg[:, None], send_col, send_row,
     )
+    flat_t = whole("turn", turn_body, shape((cols, groups * nodes)), features)
 
     def sent(k):
         return mine[k] + got[k].astype(F32)
 
-    relay = lax.ppermute(sent(0).astype(BF16), "feat", FORWARD)
-    near = lax.ppermute(sent(1).astype(BF16), "feat", BACKWARD)
-    far = lax.ppermute((sent(2) + relay.astype(F32)).astype(BF16), "feat", FORWARD)
+    relay = forward(sent(0).astype(BF16))
+    near = backward(sent(1).astype(BF16))
+    far = forward((sent(2) + relay.astype(F32)).astype(BF16))
     p_self, p_near, boxes = whole(
         "forward",
         forward_body,
@@ -287,42 +313,55 @@
     )
     recv = trade(boxes.reshape(parts, 2 * kmax, width)).reshape(span, width)
 
-    two_sum = whole("two_sum", two_body, shape((2 * width, width), F32), hidden, grads, back)
-    two_sum = lax.psum_scatter(two_sum, "feat", scatter_dimension=0, tiled=True)
-    two_sum = lax.psum(two_sum, "dom")
-    two_sum = lax.all_gather(two_sum * scale, "feat", axis=0, tiled=True)
+    block = 2 * width // groups
+    mine, theirs = whole(
+        "two_sum",
+        two_body,
+        (shape((CHIPS, block, width), F32), shape((CHIPS, block, width))),
+        hidden, grads, back,
+    )
+    got = swap(theirs)
+    pair = shape((2, nodes, width))
+    ahead, behind = whole("mix", mix_body, (pair, pair), mine, got, d_pre)
+    relay = forward(ahead)
+    near = backward(behind)
+    far = forward(whole("pass", pass_body, pair, mine, got, relay))
+    other = swap(jnp.stack([d_pre, relay[0], near[0], far[0]]))
+    stack = [pltpu.VMEM((groups, nodes, width), BF16)]
+    first = pl.pallas_call(
+        self_body, out_shape=shape((cols, width)), scratch_shapes=stack, name="self_grad"
+    )(flat_t, d_pre, relay, near, far, other)
+
+    d_near = whole("near", near_body, shape((nodes, width)), recv, near_local, take[nodes:, :])
 
     def gather(block):
-        one = lax.ppermute(block, "feat", FORWARD)
-        two = lax.ppermute(block, "feat", BACKWARD)
-        three = lax.ppermute(one, "feat", FORWARD)
-        held = jnp.stack([block, one, two, three])
-        return held, lax.ppermute(held, "feat", SWAP)
-
-    order = jnp.concatenate(
-        [group_ids([0, -turn, turn, 2], core), group_ids([0, turn, -turn, 2], 1 - core)]
-    )
-    first = weight_grad(
-        "self_grad", order, features, *gather(d_pre), finish=self_finish, out=shape((cols, width))
-    )
-    d_near = whole(
-        "near", near_body, shape((nodes, width)), recv, near_local, take[nodes:, :]
-    )
+        one = forward(block)
+        two = backward(block)
+        three = forward(one)
+        return block, one, two, three, swap(jnp.stack([block, one, two, three]))
+
+    rows = 9 * cols // parts // 2
+    terms = pl.pallas_call(
+        near_grad_body,
+        out_shape=shape((parts, rows, width // 2)),
+        scratch_shapes=stack,
+        name="near_grad",
+    )(flat_t, *gather(d_near), first, mine, got, near, far)
+    terms = trade(terms)
     out = whole(
         "out", out_body, shape((nodes, width)), recv, hidden, inv, take[:nodes, :], own, w_two
     )
-    rows = 2 * cols // parts
-    terms = weight_grad(
-        "near_grad", order, features, *gather(d_near), first,
-        finish=near_finish, out=shape((parts, rows, width)),
-    )
-    terms = trade(terms)
-    chunk = whole(
-        "sum", lambda recv, out: sum_body(scale, recv, out), shape((parts, rows, width)), terms
-    )
-    full = trade(chunk).astype(F32)
-    one_sum = jnp.concatenate([full[:, : rows // 2], full[:, rows // 2 :]], axis=2)
-    return out[None], one_sum.reshape(cols, 2 * width), two_sum
+    full = trade(
+        whole("sum", lambda recv, out: sum_body(scale, recv, out), shape(terms.shape), terms)
+    )
+    tail = full[:, 8 * rows // 9 :, :]
+    half = parts // 2
+    chunk = jnp.concatenate(
+        [tail[:half].reshape(block, -1), tail[half:].reshape(block, -1)], axis=1
+    )
+    two = whole("join", join_body, shape((2 * width, width), F32), *gather(chunk))
+    one = whole("spread", spread_body, shape((cols, 2 * width), F32), full)
+    return out[None], one, two
 
 
 def solution(mesh):

time: 337 us -> 225 us (0.67)
  waiting for transfers between devices: 195 us -> 29.5 us
  blocking collectives: 28.2 us -> 107 us
  between operations: 14 us -> 0.92 us
  starting transfers between devices: 30.9 us -> 21.8 us
  other arithmetic: 9.52 us -> 5.35 us
    psum x1 -> x0, waiting for transfers between devices: 146 us -> none  [on_device(): two_sum = lax.psum(two_sum, 'dom')]
    all_to_all x1 -> x3, blocking collectives: 28.2 us -> 107 us  [trade(): return lax.all_to_all(boxes, 'dom', split_axis=0, concat_axis=0, tiled=True)]
    all_to_all x3 -> x1, waiting for transfers between devices: 36.9 us -> 0.54 us  [trade(): return lax.all_to_all(boxes, 'dom', split_axis=0, concat_axis=0, tiled=True)]
    ppermute x12 -> x17, waiting for transfers between devices: 11.3 us -> 28.9 us  [the longest x8 28.4 us: forward(): return lax.ppermute(block, 'feat', FORWARD)]
    all_to_all x3 -> x1, starting transfers between devices: 19 us -> 5.64 us  [trade(): return lax.all_to_all(boxes, 'dom', split_axis=0, concat_axis=0, tiled=True)]
    pallas_call x7 -> x12, Pallas kernels: 19.4 us -> 31.8 us  [whole(): return pl.pallas_call(body, out_shape=outs, name=name)(*args)]
    pallas_call x4, Pallas kernels: 25.3 us -> 14.3 us  [the longest x2 6.8 us: project(): pl.pallas_call(body, out_shape=shape((CHIPS, nodes, width), kind), name='...]
    ppermute x12 -> x17, starting transfers between devices: 11.8 us -> 16.2 us  [the longest x4 11.4 us: backward(): return lax.ppermute(block, 'feat', BACKWARD)]
  transfers between devices with their start and end apart: 18 -> 18, of which waited for: 7 -> 9; matrix products, arithmetic and copies ran while one was open for 4% -> 3% of each run, Pallas kernels for 9% -> 11%
where the time goes in v2:
time: 225 us; the launch traced here: 221 us
  blocking collectives  107 us (48%)
  Pallas kernels  46 us (20%)
  waiting for transfers between devices  29.5 us (13%)
  starting transfers between devices  21.8 us (10%)
  local copies, waits for them, and re-layouts  10.1 us (4%)
  other arithmetic  5.35 us (2%)
    all_to_all x3, blocking collectives, trade(): return lax.all_to_all(boxes, 'dom', split_axis=0, concat_axis=0, tiled=True)  107 us
    pallas_call x12, Pallas kernels, whole(): return pl.pallas_call(body, out_shape=outs, name=name)(*args)  31.8 us
    ppermute x8, waiting for transfers between devices, forward(): return lax.ppermute(block, 'feat', FORWARD)  28.4 us
    ppermute x4, starting transfers between devices, backward(): return lax.ppermute(block, 'feat', BACKWARD)  11.4 us
    pallas_call x2, Pallas kernels, project(): pl.pallas_call(body, out_shape=shape((CHIPS, nodes, width), kind), name='...  6.8 us
    unnamed x50, local copies, waits for them, and re-layouts  6.35 us
    all_to_all x1, starting transfers between devices, trade(): return lax.all_to_all(boxes, 'dom', split_axis=0, concat_axis=0, tiled=True)  5.64 us
  transfers between devices with their start and end apart: 18, of which 9 were waited for; matrix products, arithmetic and copies ran while one was open for 3% of the time, Pallas kernels for 11%

profile of v2, /device:TPU:32, one launch (start us, length us, event | category | flops | bytes accessed | tf_op | source)
XLA Modules:
  0.0 220.9 jit_solution(3303394395335560875)
XLA Ops:
  0.6 3.2 %project.3 = bf16[4,128,1024]{2,1,0:T(8,128)(2,1)} custom-call(bf16[8,128,512]{2,1,0:T(8,128)(2,1)} %flat.1, bf16[512,1024]{1,0:T(8,128)(2,1)} %w.3), custom_call_target="tpu_custom_call" | custom-call | flops 536870912 | bytes 2097152 | tf_op jit(solution)/shard_map/project/pallas_call | solution.py:101
  3.9 3.6 %project.2 = f32[4,128,1024]{2,1,0:T(8,128)} custom-call(bf16[8,128,512]{2,1,0:T(8,128)(2,1)} %flat.1, bf16[512,1024]{1,0:T(8,128)(2,1)} %w.3), custom_call_target="tpu_custom_call" | custom-call | flops 536870912 | bytes 2097152 | tf_op jit(solution)/shard_map/project/pallas_call | solution.py:101
  7.4 2.4 %fusion.6 = (bf16[128,1024]{1,0:T(8,128)(2,1)S(1)}, bf16[128,1024]{1,0:T(8,128)(2,1)S(1)}, f32[128,1024]{1,0:T(8,128)}) fusion(f32[4,128,1024]{2,1,0:T(8,128)} %project.2, bf16[4,128,1024]{2,1,0:T(8,128)(2,1)S(1)} %collective-permute-done), kind=kLoop, calls=%fused_computation.13 | loop fusion | flops 786432 | bytes 3145728 | tf_op jit(solution)/shard_map/convert_element_type | solution.py:292
  9.8 1.6 collective-permute-start.2
  12.3 1.7 collective-permute-start.1
  13.9 3.5 %collective-permute-done.2 = bf16[128,1024]{1,0:T(8,128)(2,1)S(1)} collective-permute-done((bf16[128,1024]{1,0:T(8,128)(2,1)S(1)}, bf16[128,1024]{1,0:T(8,128)(2,1)S(1)}, u32[]{:S(2)}, u32[]{:S(2)}) %collective-permute-start.2) | collective-permute-done | bytes 262176 | tf_op jit(solution)/shard_map/ppermute | solution.py:260
  17.4 1.1 fusion.3
  18.6 1.9 collective-permute-start.3
  21.1 0.7 copy.17
  21.8 0.9 reshape.59.send_col
  22.7 0.7 reshape.52.send_row
  23.4 2.9 %tables.1 = (bf16[512,256]{1,0:T(8,128)(2,1)}, bf16[256,512]{1,0:T(8,128)(2,1)}, bf16[128,128]{1,0:T(8,128)(2,1)}, bf16[128,128]{1,0:T(8,128)(2,1)}) custom-call(s32[10,128]{1,0:T(8,128)} %bitcast.59, s32[128,10]{1,0:T(8,128)} %bitcast.57, s32[1,128]{1,0:T(1,128)} %deg_row.1, s32[128,1]{1,0:T(8,128)} %copy-done.8, s32[512,1]{1,0:T(8,128)} %reshape.59.send_col, ...), custom_call_target="tpu_custom_call" | custom-call | tf_op jit(solution)/shard_map/tables/pallas_call | solution.py:31
  26.2 0.7 slice_bitcast_fusion.1.got
  27.0 0.7 copy-done.19
  27.7 2.7 %forward.1 = (f32[128,512]{1,0:T(8,128)}, bf16[128,512]{1,0:T(8,128)(2,1)}, bf16[512,512]{1,0:T(8,128)(2,1)}) custom-call(f32[128,1024]{1,0:T(8,128)} %get-tuple-element.37.part, bf16[128,1024]{1,0:T(8,128)(2,1)} %slice_bitcast_fusion.1.got, bf16[128,1024]{1,0:T(8,128)(2,1)} %copy-done.19, bf16[128,1024]{1,0:T(8,128)(2,1)} %copy-done.20, ...), custom_call_target="tpu_custom_call" | custom-call | tf_op jit(solution)/shard_map/forward/pallas_call | solution.py:31
  30.4 28.2 %all_to_all.20 = bf16[32,16,512]{2,1,0:T(8,128)(2,1)} all-to-all(bf16[32,16,512]{2,1,0:T(8,128)(2,1)} %bitcast.50), channel_id=1, replica_groups=mesh['feat'=8,'dom'=32] {'dom'}, dimensions={0} | all-to-all | bytes 1048576 | tf_op jit(solution)/shard_map/all_to_all | solution.py:39
  58.7 3.7 %middle.1 = (bf16[512,512]{1,0:T(8,128)(2,1)}, bf16[128,512]{1,0:T(8,128)(2,1)}, f32[128,512]{1,0:T(8,128)}, bf16[128,512]{1,0:T(8,128)(2,1)}, bf16[128,512]{1,0:T(8,128)(2,1)}) custom-call(bf16[512,512]{1,0:T(8,128)(2,1)} %bitcast.43, f32[128,512]{1,0:T(8,128)} %get-tuple-element.21.p_self, bf16[128,512]{1,0:T(8,128)(2,1)} %get-tuple-element.22.p_near, ...), custom_call_target="tpu_custom_call" | custom-call | tf_op jit(solution)/shard_map/middle/pallas_call | solution.py:31
  62.3 2.9 %two_sum.1 = (f32[4,128,512]{2,1,0:T(8,128)}, bf16[4,128,512]{2,1,0:T(8,128)(2,1)}) custom-call(bf16[128,512]{1,0:T(8,128)(2,1)} %get-tuple-element.27.hidden, bf16[128,512]{1,0:T(8,128)(2,1)} %bitcast.46, bf16[128,512]{1,0:T(8,128)(2,1)} %get-tuple-element.30.back), custom_call_target="tpu_custom_call" | custom-call | tf_op jit(solution)/shard_map/two_sum/pallas_call | solution.py:31
  65.2 1.0 collective-permute-start.8
  66.3 5.6 %all-to-all-start.1 = ((bf16[32,16,512]{2,1,0:T(8,128)(2,1)}), bf16[32,16,512]{2,1,0:T(8,128)(2,1)S(1)}, u32[]{:S(2)}, u32[]{:S(2)}) async-start(bf16[32,16,512]{2,1,0:T(8,128)(2,1)} %bitcast.49), calls=%async_computation.1 | async-start | bytes 1048576 | tf_op jit(solution)/shard_map/all_to_all | solution.py:39
  71.9 0.8 copy-done.1
  72.7 2.2 mix.1
  74.9 3.2 %collective-permute-start.10 = (bf16[2,128,512]{2,1,0:T(8,128)(2,1)}, bf16[2,128,512]{2,1,0:T(8,128)(2,1)S(1)}, u32[]{:S(2)}, u32[]{:S(2)}) collective-permute-start(bf16[2,128,512]{2,1,0:T(8,128)(2,1)} %get-tuple-element.34), channel_id=1, source_target_pairs={{0,192},{32,96},{64,0},{96,160},{128,64},{160,224},{192,128},{224,... | collective-permute-start | bytes 786440 | tf_op jit(solution)/shard_map/ppermute | solution.py:263
  78.2 7.1 %collective-permute-done.9.relay.b1 = bf16[2,128,512]{2,1,0:T(8,128)(2,1)S(1)} collective-permute-done((bf16[2,128,512]{2,1,0:T(8,128)(2,1)}, bf16[2,128,512]{2,1,0:T(8,128)(2,1)S(1)}, u32[]{:S(2)}, u32[]{:S(2)}) %collective-permute-start.9) | collective-permute-done | bytes 262176 | tf_op jit(solution)/shard_map/ppermute | solution.py:260
  85.3 0.7 copy-done.5
  86.0 2.2 pass.1
  88.2 0.7 fusion.8
  89.4 0.8 copy-done.2
  90.2 2.0 near.1.b0
  92.3 3.2 %collective-permute-start.5 = (bf16[128,512]{1,0:T(8,128)(2,1)}, bf16[128,512]{1,0:T(8,128)(2,1)S(1)}, u32[]{:S(2)}, u32[]{:S(2)}) collective-permute-start(bf16[128,512]{1,0:T(8,128)(2,1)} %near.1.b0), channel_id=1, source_target_pairs={{0,192},{32,96},{64,0},{96,160},{128,64},{160,224},{192,128},{224,... | collective-permute-start | bytes 393224 | tf_op jit(solution)/shard_map/ppermute | solution.py:263
  95.5 3.3 %collective-permute-done.4.b1 = bf16[128,512]{1,0:T(8,128)(2,1)S(1)} collective-permute-done((bf16[128,512]{1,0:T(8,128)(2,1)}, bf16[128,512]{1,0:T(8,128)(2,1)S(1)}, u32[]{:S(2)}, u32[]{:S(2)}) %collective-permute-start.4) | collective-permute-done | bytes 131104 | tf_op jit(solution)/shard_map/ppermute | solution.py:260
  99.5 5.5 %collective-permute-done.6.b3 = bf16[128,512]{1,0:T(8,128)(2,1)S(1)} collective-permute-done((bf16[128,512]{1,0:T(8,128)(2,1)S(1)}, bf16[128,512]{1,0:T(8,128)(2,1)S(1)}, u32[]{:S(2)}, u32[]{:S(2)}) %collective-permute-start.6) | collective-permute-done | bytes 131104 | tf_op jit(solution)/shard_map/ppermute | solution.py:260
  105.0 1.0 pad_maximum_fusion
  106.1 2.6 %turn.1.flat_t = bf16[512,1024]{1,0:T(8,128)(2,1)} custom-call(bf16[8,128,512]{2,1,0:T(8,128)(2,1)} %flat.1), custom_call_target="tpu_custom_call" | custom-call | tf_op jit(solution)/shard_map/turn/pallas_call | solution.py:31
  108.7 0.8 copy-done.11
  109.5 3.3 %self_grad.1.first = bf16[512,512]{1,0:T(8,128)(2,1)} custom-call(bf16[512,1024]{1,0:T(8,128)(2,1)} %turn.1.flat_t, bf16[128,512]{1,0:T(8,128)(2,1)} %get-tuple-element.29.block.b0, bf16[2,128,512]{2,1,0:T(8,128)(2,1)} %copy-done.5, bf16[2,128,512]{2,1,0:T(8,128)(2,1)} %copy-done.3, bf16[2,128,512]{2,1,0:T(8,128)(2,1)} %copy-done.4, ...), custom_call_target="tpu_custom_call" | custom-call | tf_op jit(solution)/shard_map/self_grad/pallas_call | solution.py:331
  112.7 0.8 copy-done.9
  113.6 4.2 %near_grad.1 = bf16[32,72,256]{2,1,0:T(8,128)(2,1)} custom-call(bf16[512,1024]{1,0:T(8,128)(2,1)} %turn.1.flat_t, bf16[128,512]{1,0:T(8,128)(2,1)} %near.1.b0, bf16[128,512]{1,0:T(8,128)(2,1)} %copy-done.13, bf16[128,512]{1,0:T(8,128)(2,1)} %copy-done.14, bf16[128,512]{1,0:T(8,128)(2,1)} %copy-done.15, bf16[4,128,512]{2,1,0:T(8,128)(2,1)} %copy-done.9, ...), custom_call_target="tpu_custom_call" | custom-call | tf_op jit(solution)/shard_map/near_grad/pallas_call | solution.py:344
  117.8 42.4 %all_to_all.21.recv = bf16[32,72,256]{2,1,0:T(8,128)(2,1)} all-to-all(bf16[32,72,256]{2,1,0:T(8,128)(2,1)} %near_grad.1), channel_id=1, replica_groups=mesh['feat'=8,'dom'=32] {'dom'}, dimensions={0} | all-to-all | bytes 2359296 | tf_op jit(solution)/shard_map/all_to_all | solution.py:39
  160.2 2.5 %sum.1 = bf16[32,72,256]{2,1,0:T(8,128)(2,1)} custom-call(bf16[32,72,256]{2,1,0:T(8,128)(2,1)} %all_to_all.21.recv), custom_call_target="tpu_custom_call" | custom-call | tf_op jit(solution)/shard_map/sum/pallas_call | solution.py:31
  162.6 36.5 %all_to_all.22.full = bf16[32,72,256]{2,1,0:T(8,128)(2,1)S(1)} all-to-all(bf16[32,72,256]{2,1,0:T(8,128)(2,1)} %sum.1), channel_id=1, replica_groups=mesh['feat'=8,'dom'=32] {'dom'}, dimensions={0} | all-to-all | bytes 2359296 | tf_op jit(solution)/shard_map/all_to_all | solution.py:39
  199.3 3.2 %collective-permute-start.14 = (bf16[128,512]{1,0:T(8,128)(2,1)S(1)}, bf16[128,512]{1,0:T(8,128)(2,1)S(1)}, u32[]{:S(2)}, u32[]{:S(2)}) collective-permute-start(bf16[128,512]{1,0:T(8,128)(2,1)S(1)} %get-tuple-element.43.b0), channel_id=1, source_target_pairs={{0,192},{32,96},{64,0},{96,160},{128,64},{160,224},{192,128},{224,... | collective-permute-start | bytes 393224 | tf_op jit(solution)/shard_map/ppermute | solution.py:263
  202.5 2.9 %collective-permute-done.13.b1 = bf16[128,512]{1,0:T(8,128)(2,1)S(1)} collective-permute-done((bf16[128,512]{1,0:T(8,128)(2,1)S(1)}, bf16[128,512]{1,0:T(8,128)(2,1)S(1)}, u32[]{:S(2)}, u32[]{:S(2)}) %collective-permute-start.13) | collective-permute-done | bytes 131104 | tf_op jit(solution)/shard_map/ppermute | solution.py:260
  205.5 6.1 %collective-permute-done.15.b3 = bf16[128,512]{1,0:T(8,128)(2,1)S(1)} collective-permute-done((bf16[128,512]{1,0:T(8,128)(2,1)S(1)}, bf16[128,512]{1,0:T(8,128)(2,1)S(1)}, u32[]{:S(2)}, u32[]{:S(2)}) %collective-permute-start.15) | collective-permute-done | bytes 131104 | tf_op jit(solution)/shard_map/ppermute | solution.py:260
  211.8 2.7 %out.1 = bf16[128,512]{1,0:T(8,128)(2,1)} custom-call(bf16[512,512]{1,0:T(8,128)(2,1)} %bitcast.42, bf16[128,512]{1,0:T(8,128)(2,1)} %get-tuple-element.27.hidden, f32[128,1]{1,0:T(8,128)} %convert_divide_fusion.inv, bf16[128,512]{1,0:T(8,128)(2,1)} %get-tuple-element.41.take, bf16[128,128]{1,0:T(8,128)(2,1)} %get-tuple-element.24.own, bf16[1024,512]{1,0:T(8,128)(2,1)} %w_two.3), custom_call_target="tpu_custom_call" | custom-call | tf_op jit(solution)/shard_map/out/pallas_call | solution.py:31
  214.5 2.7 %spread.1 = f32[512,1024]{1,0:T(8,128)} custom-call(bf16[32,72,256]{2,1,0:T(8,128)(2,1)} %copy-done), custom_call_target="tpu_custom_call" | custom-call | tf_op jit(solution)/shard_map/spread/pallas_call | solution.py:31
  217.3 0.8 copy-done.12
  218.1 2.8 %join.1 = f32[1024,512]{1,0:T(8,128)} custom-call(bf16[128,512]{1,0:T(8,128)(2,1)} %copy-done.10, bf16[128,512]{1,0:T(8,128)(2,1)} %copy-done.16, bf16[128,512]{1,0:T(8,128)(2,1)} %copy-done.17, bf16[128,512]{1,0:T(8,128)(2,1)} %copy-done.18, bf16[4,128,512]{2,1,0:T(8,128)(2,1)} %copy-done.12), custom_call_target="tpu_custom_call" | custom-call | tf_op jit(solution)/shard_map/join/pallas_call | solution.py:31
  (76 shorter events, 3.3 us)
Async XLA Ops:
  3.9 3.6 %collective-permute-start = (bf16[4,128,1024]{2,1,0:T(8,128)(2,1)}, bf16[4,128,1024]{2,1,0:T(8,128)(2,1)S(1)}, u32[]{:S(2)}, u32[]{:S(2)}) collective-permute-start(bf16[4,128,1024]{2,1,0:T(8,128)(2,1)} %project.3), channel_id=1, source_target_pairs={{0,32},{32,0},{64,96},{96,64},{128,160},{160,128},{192,224},{224,1... | collective-permute-start | bytes 3145736 | tf_op jit(solution)/shard_map/ppermute | solution.py:266
  7.4 4.0 %copy-start.23 = (s32[1,128]{1,0:T(1,128)S(1)}, s32[1,128]{1,0:T(1,128)}, u32[]{:S(2)}) copy-start(s32[1,128]{1,0:T(1,128)} %deg_row.1) | copy-start | bytes 1540
  7.4 4.1 %copy-start.22 = (s32[1,32,8]{1,2,0:T(8,128)S(1)}, s32[1,32,8]{1,2,0:T(8,128)}, u32[]{:S(2)}) copy-start(s32[1,32,8]{1,2,0:T(8,128)} %param.12) | copy-start | bytes 3076
  7.4 13.1 %copy-start.21 = (s32[1,128,10]{1,0,2:T(1,128)S(1)}, s32[1,128,10]{1,0,2:T(1,128)}, u32[]{:S(2)}) copy-start(s32[1,128,10]{1,0,2:T(1,128)} %param.10) | copy-start | bytes 15364
  9.8 7.6 %collective-permute-start.2 = (bf16[128,1024]{1,0:T(8,128)(2,1)S(1)}, bf16[128,1024]{1,0:T(8,128)(2,1)S(1)}, u32[]{:S(2)}, u32[]{:S(2)}) collective-permute-start(bf16[128,1024]{1,0:T(8,128)(2,1)S(1)} %get-tuple-element.35), channel_id=1, source_target_pairs={{0,64},{32,224},{64,128},{96,32},{128,192},{160,96},{192,0},{224,1... | collective-permute-start | bytes 786440 | tf_op jit(solution)/shard_map/ppermute | solution.py:260
  11.5 11.8 %copy-start.8 = (s32[128,1]{1,0:T(8,128)}, s32[128,1]{1,0:T(8,128)S(1)}, u32[]{:S(2)}) copy-start(s32[128,1]{1,0:T(8,128)S(1)} %copy.16.deg_col) | copy-start | bytes 1540
  12.3 14.7 %collective-permute-start.1 = (bf16[128,1024]{1,0:T(8,128)(2,1)S(1)}, bf16[128,1024]{1,0:T(8,128)(2,1)S(1)}, u32[]{:S(2)}, u32[]{:S(2)}) collective-permute-start(bf16[128,1024]{1,0:T(8,128)(2,1)S(1)} %get-tuple-element.36), channel_id=1, source_target_pairs={{0,192},{32,96},{64,0},{96,160},{128,64},{160,224},{192,128},{224,... | collective-permute-start | bytes 786440 | tf_op jit(solution)/shard_map/ppermute | solution.py:263
  18.6 8.4 %collective-permute-start.3 = (bf16[128,1024]{1,0:T(8,128)(2,1)S(1)}, bf16[128,1024]{1,0:T(8,128)(2,1)S(1)}, u32[]{:S(2)}, u32[]{:S(2)}) collective-permute-start(bf16[128,1024]{1,0:T(8,128)(2,1)S(1)} %fusion.3), channel_id=1, source_target_pairs={{0,64},{32,224},{64,128},{96,32},{128,192},{160,96},{192,0},{224,1... | collective-permute-start | bytes 786440 | tf_op jit(solution)/shard_map/ppermute | solution.py:260
  26.9 0.7 copy-start.19
  27.0 0.8 copy-start.20
  65.2 6.7 %collective-permute-start.8 = (bf16[4,128,512]{2,1,0:T(8,128)(2,1)}, bf16[4,128,512]{2,1,0:T(8,128)(2,1)S(1)}, u32[]{:S(2)}, u32[]{:S(2)}) collective-permute-start(bf16[4,128,512]{2,1,0:T(8,128)(2,1)} %get-tuple-element.32), channel_id=1, source_target_pairs={{0,32},{32,0},{64,96},{96,64},{128,160},{160,128},{192,224},{224,1... | collective-permute-start | bytes 1572872 | tf_op jit(solution)/shard_map/ppermute | solution.py:266
  66.3 23.2 %all-to-all-start.1 = ((bf16[32,16,512]{2,1,0:T(8,128)(2,1)}), bf16[32,16,512]{2,1,0:T(8,128)(2,1)S(1)}, u32[]{:S(2)}, u32[]{:S(2)}) async-start(bf16[32,16,512]{2,1,0:T(8,128)(2,1)} %bitcast.49), calls=%async_computation.1 | async-start | bytes 1048576 | tf_op jit(solution)/shard_map/all_to_all | solution.py:39
  71.9 16.3 %copy-start.7 = (bf16[256,512]{1,0:T(8,128)(2,1)S(1)}, bf16[256,512]{1,0:T(8,128)(2,1)}, u32[]{:S(2)}) copy-start(bf16[256,512]{1,0:T(8,128)(2,1)} %get-tuple-element.23.take) | copy-start | bytes 786436
  71.9 0.8 copy-start.1
  74.9 10.3 %collective-permute-start.9 = (bf16[2,128,512]{2,1,0:T(8,128)(2,1)}, bf16[2,128,512]{2,1,0:T(8,128)(2,1)S(1)}, u32[]{:S(2)}, u32[]{:S(2)}) collective-permute-start(bf16[2,128,512]{2,1,0:T(8,128)(2,1)} %get-tuple-element.33), channel_id=1, source_target_pairs={{0,64},{32,224},{64,128},{96,32},{128,192},{160,96},{192,0},{224,1... | collective-permute-start | bytes 786440 | tf_op jit(solution)/shard_map/ppermute | solution.py:260
  74.9 23.9 %copy-start.6 = (bf16[128,512]{1,0:T(8,128)(2,1)S(1)}, bf16[128,512]{1,0:T(8,128)(2,1)}, u32[]{:S(2)}) copy-start(bf16[128,512]{1,0:T(8,128)(2,1)} %get-tuple-element.29.block.b0) | copy-start | bytes 393220
  74.9 23.8 %collective-permute-start.10 = (bf16[2,128,512]{2,1,0:T(8,128)(2,1)}, bf16[2,128,512]{2,1,0:T(8,128)(2,1)S(1)}, u32[]{:S(2)}, u32[]{:S(2)}) collective-permute-start(bf16[2,128,512]{2,1,0:T(8,128)(2,1)} %get-tuple-element.34), channel_id=1, source_target_pairs={{0,192},{32,96},{64,0},{96,160},{128,64},{160,224},{192,128},{224,... | collective-permute-start | bytes 786440 | tf_op jit(solution)/shard_map/ppermute | solution.py:263
  85.3 0.7 copy-start.5
  88.2 10.7 %slice-start = ((bf16[2,128,512]{2,1,0:T(8,128)(2,1)}), bf16[1,128,512]{2,1,0:T(8,128)(2,1)S(1)}, s32[]{:S(2)}) async-start(bf16[2,128,512]{2,1,0:T(8,128)(2,1)} %copy-done.5), calls=%async_computation.4 | async-start | bytes 262144 | tf_op jit(solution)/shard_map/slice | solution.py:329
  88.2 10.6 %collective-permute-start.11 = (bf16[2,128,512]{2,1,0:T(8,128)(2,1)}, bf16[2,128,512]{2,1,0:T(8,128)(2,1)S(1)}, u32[]{:S(2)}, u32[]{:S(2)}) collective-permute-start(bf16[2,128,512]{2,1,0:T(8,128)(2,1)} %pass.1), channel_id=1, source_target_pairs={{0,64},{32,224},{64,128},{96,32},{128,192},{160,96},{192,0},{224,1... | collective-permute-start | bytes 786440 | tf_op jit(solution)/shard_map/ppermute | solution.py:260
  89.4 0.8 copy-start.2
  92.3 6.5 %collective-permute-start.4 = (bf16[128,512]{1,0:T(8,128)(2,1)}, bf16[128,512]{1,0:T(8,128)(2,1)S(1)}, u32[]{:S(2)}, u32[]{:S(2)}) collective-permute-start(bf16[128,512]{1,0:T(8,128)(2,1)} %near.1.b0), channel_id=1, source_target_pairs={{0,64},{32,224},{64,128},{96,32},{128,192},{160,96},{192,0},{224,1... | collective-permute-start | bytes 393224 | tf_op jit(solution)/shard_map/ppermute | solution.py:260
  92.3 7.2 %collective-permute-start.5 = (bf16[128,512]{1,0:T(8,128)(2,1)}, bf16[128,512]{1,0:T(8,128)(2,1)S(1)}, u32[]{:S(2)}, u32[]{:S(2)}) collective-permute-start(bf16[128,512]{1,0:T(8,128)(2,1)} %near.1.b0), channel_id=1, source_target_pairs={{0,192},{32,96},{64,0},{96,160},{128,64},{160,224},{192,128},{224,... | collective-permute-start | bytes 393224 | tf_op jit(solution)/shard_map/ppermute | solution.py:263
  98.8 9.9 %copy-start.13 = (bf16[128,512]{1,0:T(8,128)(2,1)}, bf16[128,512]{1,0:T(8,128)(2,1)S(1)}, u32[]{:S(2)}) copy-start(bf16[128,512]{1,0:T(8,128)(2,1)S(1)} %collective-permute-done.4.b1) | copy-start | bytes 393220
  98.8 6.2 %collective-permute-start.6 = (bf16[128,512]{1,0:T(8,128)(2,1)S(1)}, bf16[128,512]{1,0:T(8,128)(2,1)S(1)}, u32[]{:S(2)}, u32[]{:S(2)}) collective-permute-start(bf16[128,512]{1,0:T(8,128)(2,1)S(1)} %collective-permute-done.4.b1), channel_id=1, source_target_pairs={{0,64},{32,224},{64,128},{96,32},{128,192},{160,96},{192,0},{224,1... | collective-permute-start | bytes 393224 | tf_op jit(solution)/shard_map/ppermute | solution.py:260
  98.8 9.9 %copy-start.3 = (bf16[2,128,512]{2,1,0:T(8,128)(2,1)}, bf16[2,128,512]{2,1,0:T(8,128)(2,1)S(1)}, u32[]{:S(2)}) copy-start(bf16[2,128,512]{2,1,0:T(8,128)(2,1)S(1)} %collective-permute-done.10.b2.near) | copy-start | bytes 786436
  98.8 9.8 %copy-start.4 = (bf16[2,128,512]{2,1,0:T(8,128)(2,1)}, bf16[2,128,512]{2,1,0:T(8,128)(2,1)S(1)}, u32[]{:S(2)}) copy-start(bf16[2,128,512]{2,1,0:T(8,128)(2,1)S(1)} %collective-permute-done.11.b3.far) | copy-start | bytes 786436
  99.0 9.7 %collective-permute-start.12 = (bf16[4,128,512]{2,1,0:T(8,128)(2,1)S(1)}, bf16[4,128,512]{2,1,0:T(8,128)(2,1)S(1)}, u32[]{:S(2)}, u32[]{:S(2)}) collective-permute-start(bf16[4,128,512]{2,1,0:T(8,128)(2,1)S(1)} %pad_maximum_fusion.1), channel_id=1, source_target_pairs={{0,32},{32,0},{64,96},{96,64},{128,160},{160,128},{192,224},{224,1... | collective-permute-start | bytes 1572872 | tf_op jit(solution)/shard_map/ppermute | solution.py:266
  99.5 13.3 %copy-start.14 = (bf16[128,512]{1,0:T(8,128)(2,1)}, bf16[128,512]{1,0:T(8,128)(2,1)S(1)}, u32[]{:S(2)}) copy-start(bf16[128,512]{1,0:T(8,128)(2,1)S(1)} %collective-permute-done.5.b2) | copy-start | bytes 393220
  105.0 7.8 %copy-start.15 = (bf16[128,512]{1,0:T(8,128)(2,1)}, bf16[128,512]{1,0:T(8,128)(2,1)S(1)}, u32[]{:S(2)}) copy-start(bf16[128,512]{1,0:T(8,128)(2,1)S(1)} %collective-permute-done.6.b3) | copy-start | bytes 393220
  106.0 6.8 %collective-permute-start.7 = (bf16[4,128,512]{2,1,0:T(8,128)(2,1)S(1)}, bf16[4,128,512]{2,1,0:T(8,128)(2,1)S(1)}, u32[]{:S(2)}, u32[]{:S(2)}) collective-permute-start(bf16[4,128,512]{2,1,0:T(8,128)(2,1)S(1)} %pad_maximum_fusion), channel_id=1, source_target_pairs={{0,32},{32,0},{64,96},{96,64},{128,160},{160,128},{192,224},{224,1... | collective-permute-start | bytes 1572872 | tf_op jit(solution)/shard_map/ppermute | solution.py:266
  108.7 0.8 copy-start.11
  112.7 0.8 copy-start.9
  199.1 15.4 %copy-start = (bf16[32,72,256]{2,1,0:T(8,128)(2,1)}, bf16[32,72,256]{2,1,0:T(8,128)(2,1)S(1)}, u32[]{:S(2)}) copy-start(bf16[32,72,256]{2,1,0:T(8,128)(2,1)S(1)} %all_to_all.22.full) | copy-start | bytes 3538948
  199.2 18.1 %copy-start.10 = (bf16[128,512]{1,0:T(8,128)(2,1)}, bf16[128,512]{1,0:T(8,128)(2,1)S(1)}, u32[]{:S(2)}) copy-start(bf16[128,512]{1,0:T(8,128)(2,1)S(1)} %get-tuple-element.43.b0) | copy-start | bytes 393220
  199.2 6.3 %collective-permute-start.13 = (bf16[128,512]{1,0:T(8,128)(2,1)S(1)}, bf16[128,512]{1,0:T(8,128)(2,1)S(1)}, u32[]{:S(2)}, u32[]{:S(2)}) collective-permute-start(bf16[128,512]{1,0:T(8,128)(2,1)S(1)} %get-tuple-element.43.b0), channel_id=1, source_target_pairs={{0,64},{32,224},{64,128},{96,32},{128,192},{160,96},{192,0},{224,1... | collective-permute-start | bytes 393224 | tf_op jit(solution)/shard_map/ppermute | solution.py:260
  199.3 6.2 %collective-permute-start.14 = (bf16[128,512]{1,0:T(8,128)(2,1)S(1)}, bf16[128,512]{1,0:T(8,128)(2,1)S(1)}, u32[]{:S(2)}, u32[]{:S(2)}) collective-permute-start(bf16[128,512]{1,0:T(8,128)(2,1)S(1)} %get-tuple-element.43.b0), channel_id=1, source_target_pairs={{0,192},{32,96},{64,0},{96,160},{128,64},{160,224},{192,128},{224,... | collective-permute-start | bytes 393224 | tf_op jit(solution)/shard_map/ppermute | solution.py:263
  205.5 11.8 %copy-start.16 = (bf16[128,512]{1,0:T(8,128)(2,1)}, bf16[128,512]{1,0:T(8,128)(2,1)S(1)}, u32[]{:S(2)}) copy-start(bf16[128,512]{1,0:T(8,128)(2,1)S(1)} %collective-permute-done.13.b1) | copy-start | bytes 393220
  205.5 6.2 %collective-permute-start.15 = (bf16[128,512]{1,0:T(8,128)(2,1)S(1)}, bf16[128,512]{1,0:T(8,128)(2,1)S(1)}, u32[]{:S(2)}, u32[]{:S(2)}) collective-permute-start(bf16[128,512]{1,0:T(8,128)(2,1)S(1)} %collective-permute-done.13.b1), channel_id=1, source_target_pairs={{0,64},{32,224},{64,128},{96,32},{128,192},{160,96},{192,0},{224,1... | collective-permute-start | bytes 393224 | tf_op jit(solution)/shard_map/ppermute | solution.py:260
  205.5 11.8 %copy-start.17 = (bf16[128,512]{1,0:T(8,128)(2,1)}, bf16[128,512]{1,0:T(8,128)(2,1)S(1)}, u32[]{:S(2)}) copy-start(bf16[128,512]{1,0:T(8,128)(2,1)S(1)} %collective-permute-done.14.b2) | copy-start | bytes 393220
  211.6 5.6 %copy-start.18 = (bf16[128,512]{1,0:T(8,128)(2,1)}, bf16[128,512]{1,0:T(8,128)(2,1)S(1)}, u32[]{:S(2)}) copy-start(bf16[128,512]{1,0:T(8,128)(2,1)S(1)} %collective-permute-done.15.b3) | copy-start | bytes 393220
  211.7 5.6 %collective-permute-start.16 = (bf16[4,128,512]{2,1,0:T(8,128)(2,1)S(1)}, bf16[4,128,512]{2,1,0:T(8,128)(2,1)S(1)}, u32[]{:S(2)}, u32[]{:S(2)}) collective-permute-start(bf16[4,128,512]{2,1,0:T(8,128)(2,1)S(1)} %pad_maximum_fusion.2), channel_id=1, source_target_pairs={{0,32},{32,0},{64,96},{96,64},{128,160},{160,128},{192,224},{224,1... | collective-permute-start | bytes 1572872 | tf_op jit(solution)/shard_map/ppermute | solution.py:266
  217.3 0.8 copy-start.12

commit v3 on v2

v3 whole, which is shorter than its diff:
```python
import math

import jax
import jax.numpy as jnp
from jax import lax
from jax.experimental import pallas as pl
from jax.experimental.pallas import tpu as pltpu
from jax.sharding import PartitionSpec as P

F32 = jnp.float32
BF16 = jnp.bfloat16
CHIPS = 4
NT = (((1,), (1,)), ((), ()))
TN = (((0,), (0,)), ((), ()))


def step(core):
    return 1 if core == 0 else -1


def along_y(sign):
    return [
        (y * 2 + c, (y + sign * step(c)) % CHIPS * 2 + c) for y in range(CHIPS) for c in range(2)
    ]


def along_x(sign, parts, feats):
    def device(f, z, x):
        return f * parts + z * CHIPS + x % CHIPS

    return [
        (device(f, z, x), device(f, z, x + sign * step(f % 2)))
        for f in range(feats)
        for z in range(parts // CHIPS)
        for x in range(CHIPS)
    ]


SWAP = [(i, i ^ 1) for i in range(2 * CHIPS)]


def mm(a, b, dims=(((1,), (0,)), ((), ()))):
    return lax.dot_general(a, b, dims, preferred_element_type=F32)


def whole(name, body, outs, *args, flops=0, scratch=()):
    every = list(args) + list(outs if isinstance(outs, tuple) else (outs,))
    moved = sum(math.prod(e.shape) * jnp.dtype(e.dtype).itemsize for e in every)
    return pl.pallas_call(
        body,
        out_shape=outs,
        scratch_shapes=scratch,
        name=name,
        cost_estimate=pl.CostEstimate(
            flops=flops, bytes_accessed=moved + (4 << 20), transcendentals=0
        ),
    )(*args)


def shape(dims, kind=BF16):
    return jax.ShapeDtypeStruct(dims, kind)


def trade(boxes, groups=None):
    return lax.all_to_all(
        boxes, "dom", split_axis=0, concat_axis=0, axis_index_groups=groups, tiled=True
    )


def tables_body(
    nbr_t, nbr, deg_row, deg_col, send_col, send_row, two_col, two_row, flat,
    give, take, own, own_t, back, home, pick, mean, flat_t,
):
    nodes = nbr.shape[0]
    fan = nbr.shape[1]
    span = give.shape[0]
    half = span // 2

    def entries(axis, dims):
        r = lax.broadcasted_iota(jnp.int32, dims, axis)
        return nodes + (r // 16) * 8 + r % 16, r % 16

    down, down_j = entries(0, (span, nodes))
    down = jnp.where(down_j < 8, down, -2)
    side, side_j = entries(1, (nodes, span))
    side = jnp.where(side_j >= 8, side - 8, -2)
    row = lax.broadcasted_iota(jnp.int32, (nodes + half, nodes), 0)
    col = lax.broadcasted_iota(jnp.int32, (nodes, nodes + half), 1)
    give_sum = jnp.zeros((span, nodes), F32)
    take_sum = jnp.zeros((nodes, span), F32)
    by_col = jnp.zeros((nodes, nodes + half), F32)
    by_row = jnp.zeros((nodes + half, nodes), F32)
    for s in range(fan):
        as_row = jnp.where(s < deg_row[...], nbr_t[s : s + 1, :], -1)
        as_col = jnp.where(s < deg_col[...], nbr[:, s : s + 1], -1)
        give_sum += jnp.where(down == as_row, 1.0, 0.0)
        take_sum += jnp.where(side == as_col, 1.0, 0.0)
        by_col += jnp.where(col == as_col, 1.0, 0.0)
        by_row += jnp.where(row == as_row, 1.0, 0.0)

    def lane(rows):
        return lax.broadcasted_iota(jnp.int32, (rows, nodes), 1)

    def sub(cols):
        return lax.broadcasted_iota(jnp.int32, (nodes, cols), 0)

    give[:, :nodes] = give_sum.astype(BF16)
    give[:, nodes:] = jnp.where(lane(span) == two_col[...], 1.0, 0.0).astype(BF16)
    take[:nodes, :] = take_sum.astype(BF16)
    take[nodes:, :] = jnp.where(sub(span) == two_row[...], 1.0, 0.0).astype(BF16)
    own[...] = by_col[:, :nodes].astype(BF16)
    mean[...] = by_col[:, nodes:].astype(BF16)
    own_t[...] = by_row[:nodes].astype(BF16)
    back[...] = by_row[nodes:].astype(BF16)
    pick[...] = jnp.where(lane(half) == send_col[...], 1.0, 0.0).astype(BF16)
    home[...] = jnp.where(sub(half) == send_row[...], 1.0, 0.0).astype(BF16)
    for g in range(flat.shape[0]):
        flat_t[:, g * nodes : (g + 1) * nodes] = flat[g].T


def ring_place(at, turn, offset):
    o, turned = offset
    return (at + CHIPS + o * (turn if turned else 1)) % CHIPS


def places(offsets, other):
    feat = lax.axis_index("feat")
    y, core = feat // 2, feat % 2
    held = 1 - core if other else core
    return [ring_place(y, 1 - 2 * core, o) * 2 + held for o in offsets]


def places_x(offsets):
    core = lax.axis_index("feat") % 2
    x = lax.axis_index("dom") % CHIPS
    return [ring_place(x, 1 - 2 * core, o) for o in offsets]


SUM_MINE = ((2, False), (-1, True), (1, True), (0, False))
SUM_OTHER = ((2, False), (1, True), (-1, True), (0, False))
GET_MINE = ((0, False), (-1, True), (1, True), (2, False))
GET_OTHER = ((0, False), (1, True), (-1, True), (2, False))


def project(flat, w_one, other):
    groups, nodes, cols = flat.shape
    width = w_one.shape[1]
    cut = width // 4

    def body(rows, w, out):
        ids = places(SUM_OTHER if other else SUM_MINE, other)
        picked = jnp.concatenate([rows[g] for g in ids], axis=0)
        out[...] = mm(picked, w[...]).astype(BF16).reshape(out.shape)

    return pl.pallas_call(
        body,
        out_shape=shape((CHIPS, nodes, width)),
        grid=(width // cut,),
        in_specs=[
            pl.BlockSpec(flat.shape, lambda i: (0, 0, 0)),
            pl.BlockSpec((cols, cut), lambda i: (0, i)),
        ],
        out_specs=pl.BlockSpec((CHIPS, nodes, cut), lambda i: (0, 0, i)),
        name="project",
        cost_estimate=pl.CostEstimate(
            flops=2 * CHIPS * nodes * cols * width,
            bytes_accessed=2 * (groups * nodes * cols + 2 * cols * width) + (4 << 20),
            transcendentals=0,
        ),
    )(flat, w_one)


def add(*terms):
    total = terms[0].astype(F32)
    for term in terms[1:]:
        total += term.astype(F32)
    return total


def send_body(mine, got, ahead, behind):
    ahead[...] = add(mine[0], got[0]).astype(BF16)
    behind[...] = add(mine[1], got[1]).astype(BF16)


def relay_body(mine, got, relay, ahead):
    ahead[...] = add(mine[2], got[2], relay[...]).astype(BF16)


def forward_body(part, got, near, far, grads, inv, give, p_self, p_near, boxes):
    width = grads.shape[1]
    total = add(part[3], got[3], near[...], far[...])
    p_self[...] = total[:, :width]
    mine = total[:, width:].astype(BF16)
    p_near[...] = mine
    scaled = (grads[...].astype(F32) * inv[...]).astype(BF16)
    boxes[...] = mm(give[...], jnp.concatenate([scaled, mine], axis=0)).astype(BF16)


def middle_body(
    recv, p_self, p_near, grads, inv, w_two, take, own, own_t, back_t,
    boxes, d_pre_out, term_out, hidden_out, back_out,
):
    nodes, width = grads.shape
    both = mm(take[...], recv[...])
    grad = grads[...]
    scaled = (grad.astype(F32) * inv[...]).astype(BF16)
    pre = p_self[...] + inv[...] * (both[:nodes] + mm(own[...], p_near[...]))
    back = (both[nodes:] + mm(own_t[...], scaled)).astype(BF16)
    back_out[...] = back
    d_hidden = mm(grad, w_two[:width, :], NT) + mm(back, w_two[width:, :], NT)
    sig = jax.nn.sigmoid(pre)
    hidden_out[...] = (pre * sig).astype(BF16)
    d_pre = d_hidden * sig * (1.0 + pre * (1.0 - sig))
    d_pre_out[...] = d_pre.astype(BF16)
    term = (d_pre * inv[...]).astype(BF16)
    term_out[...] = term
    boxes[...] = mm(back_t[...], term).astype(BF16)


def near_body(recv, term, own_t, home, out):
    out[...] = (mm(own_t[...], term[...]) + mm(home[...], recv[...])).astype(BF16)


def out_body(recv, hidden, inv, mean, own, w_two, out):
    width = hidden.shape[1]
    parts, rows, cut = recv.shape
    rows = rows // 3
    got = jnp.concatenate(
        [recv[:, k * rows : (k + 1) * rows, :].reshape(parts * rows, cut) for k in range(2)],
        axis=1,
    )
    agg = (inv[...] * (mm(mean[...], got) + mm(own[...], hidden[...]))).astype(BF16)
    out[...] = (mm(hidden[...], w_two[:width, :]) + mm(agg, w_two[width:, :])).astype(BF16)


def two_body(hidden, grads, back, mine, theirs, scratch):
    width = hidden.shape[1]
    both = jnp.concatenate([grads[...], back[...]], axis=1)
    pair = mm(hidden[...], both, TN)
    half = scratch.shape[0] // 2
    for k in range(2):
        piece = pair[:, k * width : (k + 1) * width]
        scratch[k * half : (k + 1) * half] = piece.reshape(half, -1, width)
    for k, g in enumerate(places(SUM_MINE, False)):
        mine[k] = scratch[g]
    for k, g in enumerate(places(SUM_OTHER, True)):
        theirs[k] = scratch[g].astype(BF16)


def mix_body(mine, got, block, ahead, behind):
    ahead[0] = block[...]
    behind[0] = block[...]
    ahead[1] = add(mine[0], got[0]).astype(BF16)
    behind[1] = add(mine[1], got[1]).astype(BF16)


def pass_body(mine, got, relay, ahead):
    ahead[0] = relay[0]
    ahead[1] = add(mine[2], got[2], relay[1]).astype(BF16)


def pack_body(pick, hidden, mine, got, near, far, out):
    parts, rows, cut = out.shape
    rows = rows // 3
    boxes = mm(pick[...], hidden[...]).astype(BF16)
    for k in range(2):
        piece = boxes[:, k * cut : (k + 1) * cut].reshape(parts, rows, cut)
        out[:, k * rows : (k + 1) * rows, :] = piece
    two = add(mine[3], got[3], near[1], far[1]).astype(BF16)
    half = parts // 2
    for k in range(2):
        piece = two[:, k * cut : (k + 1) * cut].reshape(half, rows, cut)
        out[k * half : (k + 1) * half, 2 * rows :, :] = piece


def two_sum_body(scale, recv, out):
    parts, rows, cut = recv.shape
    out[...] = (add(*[recv[k, 2 * rows // 3 :, :] for k in range(parts)]) * scale).astype(BF16)


def grad_of(flat_t, blocks, other, stack):
    for g, block in zip(places(GET_MINE, False), blocks):
        stack[g] = block
    for k, g in enumerate(places(GET_OTHER, True)):
        stack[g] = other[k]
    groups, nodes, width = stack.shape
    return mm(flat_t[...], stack[...].reshape(groups * nodes, width))


def self_body(flat_t, b0, b1, b2, b3, other, out, stack):
    out[...] = grad_of(flat_t, (b0[...], b1[0], b2[0], b3[0]), other, stack).astype(BF16)


def near_grad_body(
    flat_t, b0, b1, b2, b3, other, first, chunk, ahead, behind, third, own, stack, total
):
    width = first.shape[1]
    total[:, :width] = first[...]
    blocks = (b0[...], b1[...], b2[...], b3[...])
    total[:, width:] = grad_of(flat_t, blocks, other, stack).astype(BF16)
    rows = own.shape[0]
    for x, target in zip(places_x(SUM_MINE), (ahead, behind, third, own)):
        target[:rows, :] = total[pl.ds(pl.multiple_of(x * rows, rows), rows), :]
    for target in (ahead, behind):
        target[rows:, :] = jnp.zeros_like(target[rows:, :])
        target[rows:, : chunk.shape[1]] = chunk[...]


def x_relay_body(third, relay, out):
    rows = third.shape[0]
    out[:rows, :] = add(third[...], relay[:rows, :]).astype(BF16)
    out[rows:, :] = relay[rows:, :]


def x_sum_body(own, relay, near, far, chunk, out):
    rows = own.shape[0]
    parts, deep, _ = out.shape
    cut = chunk.shape[1]
    tail = chunk.shape[0]
    total = add(own[...], near[:rows, :], far[:rows, :]).astype(BF16)
    out[:, : deep - tail, :] = total.reshape(parts, deep - tail, -1)
    held = [chunk[...], relay[rows:, :cut], near[rows:, :cut], far[rows:, :cut]]
    both = jnp.concatenate(held, axis=1)
    out[:, deep - tail :, :] = jnp.broadcast_to(both[None], (parts, *both.shape))


def z_sum_body(scale, recv, out, chunk, scratch):
    parts, deep, _ = recv.shape
    rows = out.shape[1]
    tail = deep - rows
    total = (add(*[recv[k, :rows, :] for k in range(parts)]) * scale).astype(BF16)
    out[...] = jnp.broadcast_to(total[None], out.shape)
    cut = scratch.shape[1] // 2
    half = parts // 2
    for k, x in enumerate(places_x(GET_MINE)):
        for z in range(parts):
            at = pl.multiple_of((z % half * CHIPS + x) * tail, tail)
            side = slice(z // half * cut, (z // half + 1) * cut)
            piece = recv[z, rows:, k * cut : (k + 1) * cut]
            scratch[pl.ds(at, tail), side] = piece.astype(F32)
    chunk[...] = scratch[...].astype(BF16)


def spread_body(b0, b1, b2, b3, out):
    rows = b0.shape[0]
    for x, block in zip(places_x(GET_MINE), (b0, b1, b2, b3)):
        out[pl.ds(pl.multiple_of(x * rows, rows), rows), :] = block[...].astype(F32)


def join_body(b0, b1, b2, b3, other, out):
    nodes = b0.shape[0]

    def put(g, block):
        out[pl.ds(pl.multiple_of(g * nodes, nodes), nodes), :] = block.astype(F32)

    for g, block in zip(places(GET_MINE, False), (b0, b1, b2, b3)):
        put(g, block[...])
    for k, g in enumerate(places(GET_OTHER, True)):
        put(g, other[k])


def on_device(features, w_one, w_two, neighbor, degree, send_rows, grad_out):
    groups, nodes, cols = features.shape
    width = w_two.shape[1]
    parts = lax.axis_size("dom")
    deep = parts // CHIPS
    nbr = neighbor[0]
    deg = degree[0]
    sends = send_rows[0]
    kmax = sends.shape[1]
    half = sends.size
    span = 2 * half
    grads = grad_out[0]
    scale = 1.0 / math.sqrt(groups * nodes * parts)
    y_ahead, y_behind = along_y(1), along_y(-1)
    x_ahead, x_behind = along_x(1, parts, groups), along_x(-1, parts, groups)
    lines = [[z * CHIPS + x for z in range(deep)] for x in range(CHIPS)]

    def forward(block):
        return lax.ppermute(block, "feat", y_ahead)

    def backward(block):
        return lax.ppermute(block, "feat", y_behind)

    def swap(block):
        return lax.ppermute(block, "feat", SWAP)

    def x_forward(block):
        return lax.ppermute(block, ("feat", "dom"), x_ahead)

    def x_backward(block):
        return lax.ppermute(block, ("feat", "dom"), x_behind)

    def gather(block, after=None):
        one = forward(block)
        two = backward(block)
        three = forward(one)
        held = jnp.stack([block, one, two, three])
        if after is not None:
            held, after = lax.optimization_barrier((held, after))
        return (block, one, two, three, swap(held)), after

    got = swap(project(features, w_one, True))
    mine = project(features, w_one, False)

    inv = (1.0 / deg.astype(F32))[:, None]
    blank = jnp.full_like(sends, -1)
    two_col = jnp.concatenate([blank, sends], axis=1).reshape(-1, 1)
    two_row = jnp.concatenate([sends, blank], axis=1).reshape(1, -1)
    give, take, own, own_t, back_t, home, pick, mean, flat_t = whole(
        "tables",
        tables_body,
        (
            shape((span, 2 * nodes)),
            shape((2 * nodes, span)),
            shape((nodes, nodes)),
            shape((nodes, nodes)),
            shape((half, nodes)),
            shape((nodes, half)),
            shape((half, nodes)),
            shape((nodes, half)),
            shape((cols, groups * nodes)),
        ),
        nbr.T, nbr, deg[None, :], deg[:, None], sends.reshape(-1, 1), sends.reshape(1, -1),
        two_col, two_row, features,
    )

    rows = shape((nodes, 2 * width))
    ahead, behind = whole("send", send_body, (rows, rows), mine, got)
    relay = forward(ahead)
    near = backward(behind)
    far = forward(whole("relay", relay_body, rows, mine, got, relay))
    p_self, p_near, boxes = whole(
        "forward",
        forward_body,
        (shape((nodes, width), F32), shape((nodes, width)), shape((span, width))),
        mine, got, near, far, grads, inv, give,
    )
    recv = trade(boxes.reshape(parts, 2 * kmax, width)).reshape(span, width)
    block = shape((nodes, width))
    boxes, d_pre, term, hidden, back = whole(
        "middle",
        middle_body,
        (shape((half, width)), block, block, block, block),
        recv, p_self, p_near, grads, inv, w_two, take, own, own_t, back_t,
    )
    recv = trade(boxes.reshape(parts, kmax, width)).reshape(half, width)

    rows = 2 * width // groups
    mine, theirs = whole(
        "two_sum",
        two_body,
        (shape((CHIPS, rows, width), F32), shape((CHIPS, rows, width))),
        hidden, grads, back,
        scratch=[pltpu.VMEM((groups, rows, width), F32)],
    )
    got = swap(theirs)
    pair = shape((2, nodes, width))
    ahead, behind = whole("mix", mix_body, (pair, pair), mine, got, d_pre)
    relay = forward(ahead)
    near = backward(behind)
    far = forward(whole("pass", pass_body, pair, mine, got, relay))
    other = swap(jnp.stack([d_pre, relay[0], near[0], far[0]]))
    stack = pltpu.VMEM((groups, nodes, width), BF16)
    first = whole(
        "self_grad", self_body, shape((cols, width)), flat_t, d_pre, relay, near, far, other,
        scratch=[stack], flops=2 * groups * nodes * cols * width,
    )
    packed = whole(
        "pack", pack_body, shape((parts, 3 * kmax, width // 2)),
        pick, hidden, mine, got, near, far,
    )

    d_near = whole("near", near_body, block, recv, term, own_t, home)
    gathered, first = gather(d_near, first)
    packed = trade(packed)
    out = whole("out", out_body, block, packed, hidden, inv, mean, own, w_two)
    chunk = whole(
        "two_scale",
        lambda recv, out: two_sum_body(scale, recv, out),
        shape((kmax, width // 2)),
        packed,
    )

    rows = cols // CHIPS
    message = shape((rows + kmax, 2 * width))
    plain = shape((rows, 2 * width))
    ahead, behind, third, mine = whole(
        "near_grad",
        near_grad_body,
        (message, message, plain, plain),
        flat_t, *gathered, first, chunk,
        scratch=[stack, pltpu.VMEM((cols, 2 * width), BF16)],
        flops=2 * groups * nodes * cols * width,
    )
    relay = x_forward(ahead)
    near = x_backward(behind)
    far = x_forward(whole("x_relay", x_relay_body, message, third, relay))
    terms = whole(
        "x_sum",
        x_sum_body,
        shape((deep, rows // deep + kmax, 2 * width)),
        mine, relay, near, far, chunk,
    )
    terms = trade(terms, lines)
    total, chunk = whole(
        "z_sum",
        lambda *refs: z_sum_body(scale, *refs),
        (shape((deep, rows // deep, 2 * width)), block),
        terms,
        scratch=[pltpu.VMEM((nodes, width), F32)],
    )
    total = trade(total, lines).reshape(rows, 2 * width)
    relay = x_forward(total)
    near = x_backward(total)
    far = x_forward(relay)
    two = whole("join", join_body, shape((2 * width, width), F32), *gather(chunk)[0])
    one = whole("spread", spread_body, shape((cols, 2 * width), F32), total, relay, near, far)
    return out[None], one, two


def solution(mesh):
    in_specs = (
        P(None, "dom", "feat"),
        P("feat", None),
        P(),
        P("feat", "dom", None),
        P("feat", "dom"),
        P("feat", "dom", None),
        P("feat", "dom", None),
    )
    out_specs = (P("feat", "dom", None), P("feat", None), P())
    return jax.shard_map(
        on_device, mesh=mesh, in_specs=in_specs, out_specs=out_specs, check_vma=False
    )
```

time: 225 us -> 226 us (level); the launches traced: 221 us -> 224 us
  blocking collectives: 107 us -> 43.8 us
  waiting for transfers between devices: 29.5 us -> 65 us
  starting transfers between devices: 21.8 us -> 37.9 us
  Pallas kernels: 46 us -> 57.8 us
  local copies, waits for them, and re-layouts: 10.1 us -> 16.2 us
  other arithmetic: 5.35 us -> 2.64 us
    all_to_all x3 -> x2, blocking collectives: 107 us -> 43.8 us  [trade(): lax.all_to_all(boxes, 'dom', split_axis=0, concat_axis=0, axis_index_grou...]
    ppermute x12 -> x18, waiting for transfers between devices: 28.9 us -> 46.2 us  [the longest x8 25.6 us: forward(): return lax.ppermute(block, 'feat', y_ahead)]
    all_to_all x1 -> x3, waiting for transfers between devices: 0.54 us -> 17.1 us  [trade(): lax.all_to_all(boxes, 'dom', split_axis=0, concat_axis=0, axis_index_grou...]
    pallas_call x16 -> x21, Pallas kernels: 46 us -> 57.8 us  [the longest x19 49.2 us: whole(): pl.pallas_call(body, out_shape=outs, scratch_shapes=scratch, name=name, c...]
    all_to_all x1 -> x3, starting transfers between devices: 5.64 us -> 14.7 us  [trade(): lax.all_to_all(boxes, 'dom', split_axis=0, concat_axis=0, axis_index_grou...]
    ppermute x12 -> x18, starting transfers between devices: 14.9 us -> 21.3 us  [the longest x4 10.1 us: backward(): return lax.ppermute(block, 'feat', y_behind)]
    unnamed x50 -> x65, local copies, waits for them, and re-layouts: 6.35 us -> 10.9 us
    convert_element_type x2 -> x0, other arithmetic: 3.54 us -> none  [the longest x1 2.4 us: on_device(): relay = forward(sent(0).astype(BF16))]
  transfers between devices with their start and end apart: 18 -> 26, of which waited for: 9 -> 13; matrix products, arithmetic and copies ran while one was open for 3% -> 4% of each run, Pallas kernels for 11% -> 13%
where the time goes in v3:
time: 226 us; the launch traced here: 224 us
  waiting for transfers between devices  65 us (29%)
  Pallas kernels  57.8 us (26%)
  blocking collectives  43.8 us (19%)
  starting transfers between devices  37.9 us (17%)
  local copies, waits for them, and re-layouts  16.2 us (7%)
  other arithmetic  2.64 us (1%)
    pallas_call x19, Pallas kernels, whole(): pl.pallas_call(body, out_shape=outs, scratch_shapes=scratch, name=name, c...  49.2 us
    all_to_all x2, blocking collectives, trade(): lax.all_to_all(boxes, 'dom', split_axis=0, concat_axis=0, axis_index_grou...  43.8 us
    ppermute x8, waiting for transfers between devices, forward(): return lax.ppermute(block, 'feat', y_ahead)  25.6 us
    ppermute x4, waiting for transfers between devices, x_forward(): return lax.ppermute(block, ('feat', 'dom'), x_ahead)  20.6 us
    all_to_all x3, waiting for transfers between devices, trade(): lax.all_to_all(boxes, 'dom', split_axis=0, concat_axis=0, axis_index_grou...  17.1 us
    all_to_all x3, starting transfers between devices, trade(): lax.all_to_all(boxes, 'dom', split_axis=0, concat_axis=0, axis_index_grou...  14.7 us
    unnamed x65, local copies, waits for them, and re-layouts  10.9 us
    ppermute x4, starting transfers between devices, backward(): return lax.ppermute(block, 'feat', y_behind)  10.1 us
  transfers between devices with their start and end apart: 26, of which 13 were waited for; matrix products, arithmetic and copies ran while one was open for 4% of the time, Pallas kernels for 13%

profile of v3, /device:TPU:32, one launch (start us, length us, event | category | flops | bytes accessed | tf_op | source)
XLA Modules:
  0.0 224.3 jit_solution(13463162434759816435)
XLA Ops:
  0.6 4.3 %project.3 = bf16[4,128,1024]{2,1,0:T(8,128)(2,1)} custom-call(bf16[8,128,512]{2,1,0:T(8,128)(2,1)} %rows.3, bf16[512,1024]{1,0:T(8,128)(2,1)} %w.3), custom_call_target="tpu_custom_call" | custom-call | flops 536870912 | bytes 7340032 | tf_op jit(solution)/shard_map/project/pallas_call | solution.py:155
  4.9 4.3 %project.2.mine.part = bf16[4,128,1024]{2,1,0:T(8,128)(2,1)} custom-call(bf16[8,128,512]{2,1,0:T(8,128)(2,1)} %rows.3, bf16[512,1024]{1,0:T(8,128)(2,1)} %w.3), custom_call_target="tpu_custom_call" | custom-call | flops 536870912 | bytes 7340032 | tf_op jit(solution)/shard_map/project/pallas_call | solution.py:155
  10.3 2.4 %send.1 = (bf16[128,1024]{1,0:T(8,128)(2,1)}, bf16[128,1024]{1,0:T(8,128)(2,1)}) custom-call(bf16[4,128,1024]{2,1,0:T(8,128)(2,1)} %project.2.mine.part, bf16[4,128,1024]{2,1,0:T(8,128)(2,1)} %copy-done), custom_call_target="tpu_custom_call" | custom-call | bytes 6815744 | tf_op jit(solution)/shard_map/send/pallas_call | solution.py:49
  12.6 1.6 collective-permute-start.2
  14.3 1.7 collective-permute-start.1
  16.0 4.9 %collective-permute-done.2.relay = bf16[128,1024]{1,0:T(8,128)(2,1)S(1)} collective-permute-done((bf16[128,1024]{1,0:T(8,128)(2,1)}, bf16[128,1024]{1,0:T(8,128)(2,1)S(1)}, u32[]{:S(2)}, u32[]{:S(2)}) %collective-permute-start.2) | collective-permute-done | bytes 262176 | tf_op jit(solution)/shard_map/ppermute | solution.py:380
  21.5 2.4 %relay.1 = bf16[128,1024]{1,0:T(8,128)(2,1)} custom-call(bf16[4,128,1024]{2,1,0:T(8,128)(2,1)} %project.2.mine.part, bf16[4,128,1024]{2,1,0:T(8,128)(2,1)} %copy-done, bf16[128,1024]{1,0:T(8,128)(2,1)} %copy-done.27), custom_call_target="tpu_custom_call" | custom-call | bytes 6815744 | tf_op jit(solution)/shard_map/relay/pallas_call | solution.py:49
  23.9 1.8 collective-permute-start.3
  30.9 4.2 %tables.1 = (bf16[512,256]{1,0:T(8,128)(2,1)}, bf16[256,512]{1,0:T(8,128)(2,1)}, bf16[128,128]{1,0:T(8,128)(2,1)}, bf16[128,128]{1,0:T(8,128)(2,1)}, bf16[256,12...) custom-call(s32[10,128]{1,0:T(8,128)} %bitcast.43, ...), custom_call_target="tpu_custom_call" | custom-call | bytes 7160832 | tf_op jit(solution)/shard_map/tables/pallas_call | solution.py:49
  35.0 1.5 convert_divide_fusion.inv
  37.3 3.1 %forward.1 = (f32[128,512]{1,0:T(8,128)}, bf16[128,512]{1,0:T(8,128)(2,1)}, bf16[512,512]{1,0:T(8,128)(2,1)}) custom-call(bf16[4,128,1024]{2,1,0:T(8,128)(2,1)} %project.2.mine.part, bf16[4,128,1024]{2,1,0:T(8,128)(2,1)} %copy-done, bf16[128,1024]{1,0:T(8,128)(2,1)} %copy-done.22, bf16[128,1024]{1,0:T(8,128)(2,1)} %copy-done.23, bf16[128,512]{1,0:T(8,128)(2,1)} %bitcast.24, ...), custom_call_target="tpu_custom_call" | custom-call | bytes 8126976 | tf_op jit(solution)/shard_map/forward/pallas_call | solution.py:49
  40.4 28.0 %all_to_all.25 = bf16[32,16,512]{2,1,0:T(8,128)(2,1)} all-to-all(bf16[32,16,512]{2,1,0:T(8,128)(2,1)} %bitcast.33), channel_id=1, replica_groups=mesh['feat'=8,'dom'=32] {'dom'}, dimensions={0} | all-to-all | bytes 1048576 | tf_op jit(solution)/shard_map/all_to_all | solution.py:65
  68.4 3.3 %middle.1 = (bf16[256,512]{1,0:T(8,128)(2,1)}, bf16[128,512]{1,0:T(8,128)(2,1)}, bf16[128,512]{1,0:T(8,128)(2,1)}, bf16[128,512]{1,0:T(8,128)(2,1)}, bf16[128,512]{1,0:T(8,128)(2,1)}) custom-call(bf16[512,512]{1,0:T(8,128)(2,1)} %bitcast.23, f32[128,512]{1,0:T(8,128)} %get-tuple-element.39.p_self, bf16[128,512]{1,0:T(8,128)(2,1)} %get-tuple-element.40.p_near, ...), custom_call_target="tpu_custom_call" | custom-call | bytes 7471616 | tf_op jit(solution)/shard_map/middle/pallas_call | solution.py:49
  71.7 2.7 %two_sum.1 = (f32[4,128,512]{2,1,0:T(8,128)}, bf16[4,128,512]{2,1,0:T(8,128)(2,1)}) custom-call(bf16[128,512]{1,0:T(8,128)(2,1)} %get-tuple-element.45.hidden, bf16[128,512]{1,0:T(8,128)(2,1)} %bitcast.26, bf16[128,512]{1,0:T(8,128)(2,1)} %get-tuple-element.46.back), custom_call_target="tpu_custom_call" | custom-call | bytes 6160384 | tf_op jit(solution)/shard_map/two_sum/pallas_call | solution.py:49
  74.4 1.7 collective-permute-start.4
  76.1 1.7 collective-permute-done.4.got
  78.7 2.2 mix.1
  81.0 3.1 %collective-permute-start.5 = (bf16[2,128,512]{2,1,0:T(8,128)(2,1)}, bf16[2,128,512]{2,1,0:T(8,128)(2,1)S(1)}, u32[]{:S(2)}, u32[]{:S(2)}) collective-permute-start(bf16[2,128,512]{2,1,0:T(8,128)(2,1)} %get-tuple-element.50), channel_id=1, source_target_pairs={{0,192},{32,96},{64,0},{96,160},{128,64},{160,224},{192,128},{224,... | collective-permute-start | bytes 786440 | tf_op jit(solution)/shard_map/ppermute | solution.py:383
  84.1 6.6 %collective-permute-done.6.relay.b1 = bf16[2,128,512]{2,1,0:T(8,128)(2,1)S(1)} collective-permute-done((bf16[2,128,512]{2,1,0:T(8,128)(2,1)}, bf16[2,128,512]{2,1,0:T(8,128)(2,1)S(1)}, u32[]{:S(2)}, u32[]{:S(2)}) %collective-permute-start.6) | collective-permute-done | bytes 262176 | tf_op jit(solution)/shard_map/ppermute | solution.py:380
  91.5 2.2 pass.1
  93.7 5.2 %all-to-all-start.2 = ((bf16[32,8,512]{2,1,0:T(8,128)(2,1)}), bf16[32,8,512]{2,1,0:T(8,128)(2,1)S(1)}, u32[]{:S(2)}, u32[]{:S(2)}) async-start(bf16[32,8,512]{2,1,0:T(8,128)(2,1)} %bitcast.9), calls=%async_computation.2 | async-start | bytes 524288 | tf_op jit(solution)/shard_map/all_to_all | solution.py:65
  99.9 1.6 collective-permute-done.7.far.b3
  101.7 8.8 %all-to-all-done.2 = bf16[32,8,512]{2,1,0:T(8,128)(2,1)S(1)} async-done(((bf16[32,8,512]{2,1,0:T(8,128)(2,1)}), bf16[32,8,512]{2,1,0:T(8,128)(2,1)S(1)}, u32[]{:S(2)}, u32[]{:S(2)}) %all-to-all-start.2) | async-done | bytes 262176 | tf_op jit(solution)/shard_map/all_to_all | solution.py:65
  111.2 1.9 near.1.b0
  114.0 2.3 %collective-permute-start.9 = (bf16[128,512]{1,0:T(8,128)(2,1)}, bf16[128,512]{1,0:T(8,128)(2,1)S(1)}, u32[]{:S(2)}, u32[]{:S(2)}) collective-permute-start(bf16[128,512]{1,0:T(8,128)(2,1)} %near.1.b0), channel_id=1, source_target_pairs={{0,192},{32,96},{64,0},{96,160},{128,64},{160,224},{192,128},{224,... | collective-permute-start | bytes 393224 | tf_op jit(solution)/shard_map/ppermute | solution.py:383
  116.3 3.2 %collective-permute-done.8.b1 = bf16[128,512]{1,0:T(8,128)(2,1)S(1)} collective-permute-done((bf16[128,512]{1,0:T(8,128)(2,1)}, bf16[128,512]{1,0:T(8,128)(2,1)S(1)}, u32[]{:S(2)}, u32[]{:S(2)}) %collective-permute-start.8) | collective-permute-done | bytes 131104 | tf_op jit(solution)/shard_map/ppermute | solution.py:380
  119.5 2.6 %pack.1 = bf16[32,24,256]{2,1,0:T(8,128)(2,1)} custom-call(bf16[256,128]{1,0:T(8,128)(2,1)} %get-tuple-element.34.pick, bf16[128,512]{1,0:T(8,128)(2,1)} %get-tuple-element.45.hidden, f32[4,128,512]{2,1,0:T(8,128)} %get-tuple-element.47.mine, bf16[4,128,512]{2,1,0:T(8,128)(2,1)} %copy-done.1, bf16[2,128,512]{2,1,0:T(8,128)(2,1)} %copy-done.4, ...), custom_call_target="tpu_custom_call" | custom-call | bytes 6881280 | tf_op jit(solution)/shard_map/pack/pallas_call | solution.py:49
  122.1 4.7 %all-to-all-start.1 = ((bf16[32,24,256]{2,1,0:T(8,128)(2,1)}), bf16[32,24,256]{2,1,0:T(8,128)(2,1)S(1)}, u32[]{:S(2)}, u32[]{:S(2)}) async-start(bf16[32,24,256]{2,1,0:T(8,128)(2,1)} %pack.1), calls=%async_computation.1 | async-start | bytes 786432 | tf_op jit(solution)/shard_map/all_to_all | solution.py:65
  127.8 3.3 %self_grad.1.first = bf16[512,512]{1,0:T(8,128)(2,1)} custom-call(bf16[512,1024]{1,0:T(8,128)(2,1)} %get-tuple-element.53.flat_t, bf16[128,512]{1,0:T(8,128)(2,1)} %get-tuple-element.49.block.b0, bf16[2,128,512]{2,1,0:T(8,128)(2,1)} %copy-done.3, bf16[2,128,512]{2,1,0:T(8,128)(2,1)} %copy-done.4, bf16[2,128,512]{2,1,0:T(8,128)(2,1)} %copy-done.5, ...), custom_call_target="tpu_custom_call" | custom-call | flops 536870912 | bytes 7208960 | tf_op jit(solution)/shard_map/self_grad/pallas_call | solution.py:49
  131.0 8.3 %all-to-all-done.1.recv = bf16[32,24,256]{2,1,0:T(8,128)(2,1)S(1)} async-done(((bf16[32,24,256]{2,1,0:T(8,128)(2,1)}), bf16[32,24,256]{2,1,0:T(8,128)(2,1)S(1)}, u32[]{:S(2)}, u32[]{:S(2)}) %all-to-all-start.1) | async-done | bytes 393248 | tf_op jit(solution)/shard_map/all_to_all | solution.py:65
  140.1 1.6 two_scale.1.chunk
  142.5 3.6 %near_grad.1 = (bf16[136,1024]{1,0:T(8,128)(2,1)}, bf16[136,1024]{1,0:T(8,128)(2,1)}, bf16[128,1024]{1,0:T(8,128)(2,1)}, bf16[128,1024]{1,0:T(8,128)(2,1)}) custom-call(bf16[512,1024]{1,0:T(8,128)(2,1)} %get-tuple-element.53.flat_t, bf16[128,512]{1,0:T(8,128)(2,1)} %near.1.b0, bf16[128,512]{1,0:T(8,128)(2,1)} %copy-done.14, bf16[128,512]{1,0:T(8,128)(2,1)} %copy-done.15, ...), custom_call_target="tpu_custom_call" | custom-call | flops 536870912 | bytes 7901184 | tf_op jit(solution)/shard_map/near_grad/pallas_call | solution.py:49
  146.5 2.7 %collective-permute-start.14 = (bf16[136,1024]{1,0:T(8,128)(2,1)}, bf16[136,1024]{1,0:T(8,128)(2,1)S(1)}, u32[]{:S(2)}, u32[]{:S(2)}) collective-permute-start(bf16[136,1024]{1,0:T(8,128)(2,1)} %get-tuple-element.61), channel_id=1, source_target_pairs={{0,3},{1,0},{2,1},{3,2},{4,7},{5,4},{6,5},{7,6},{8,11},{9,8},{10,9... | collective-permute-start | bytes 835592 | tf_op jit(solution)/shard_map/ppermute | solution.py:392
  149.3 4.7 %collective-permute-done.13.relay = bf16[136,1024]{1,0:T(8,128)(2,1)S(1)} collective-permute-done((bf16[136,1024]{1,0:T(8,128)(2,1)}, bf16[136,1024]{1,0:T(8,128)(2,1)S(1)}, u32[]{:S(2)}, u32[]{:S(2)}) %collective-permute-start.13) | collective-permute-done | bytes 278560 | tf_op jit(solution)/shard_map/ppermute | solution.py:389
  154.7 1.8 x_relay.1
  156.5 8.0 %collective-permute-done.15.far = bf16[136,1024]{1,0:T(8,128)(2,1)S(1)} collective-permute-done((bf16[136,1024]{1,0:T(8,128)(2,1)}, bf16[136,1024]{1,0:T(8,128)(2,1)S(1)}, u32[]{:S(2)}, u32[]{:S(2)}) %collective-permute-start.15) | collective-permute-done | bytes 278560 | tf_op jit(solution)/shard_map/ppermute | solution.py:389
  165.2 2.0 x_sum.1
  167.3 15.8 %all_to_all.26.refs_0_ = bf16[8,24,1024]{2,1,0:T(8,128)(2,1)} all-to-all(bf16[8,24,1024]{2,1,0:T(8,128)(2,1)} %x_sum.1), channel_id=1, replica_groups={{0,4,8,12,16,20,24,28},{1,5,9,13,17,21,25,29},{2,6,10,14,18,22,26,30},{..., dimensions={0} | all-to-all | bytes 786432 | tf_op jit(solution)/shard_map/all_to_all | solution.py:65
  183.1 1.8 z_sum.1
  184.9 4.8 %all-to-all-start.4 = ((bf16[8,16,1024]{2,1,0:T(8,128)(2,1)}), bf16[8,16,1024]{2,1,0:T(8,128)(2,1)S(1)}, u32[]{:S(2)}, u32[]{:S(2)}) async-start(bf16[8,16,1024]{2,1,0:T(8,128)(2,1)} %get-tuple-element.63), calls=%async_computation.4 | async-start | bytes 524288 | tf_op jit(solution)/shard_map/all_to_all | solution.py:65
  190.0 3.0 %collective-permute-start.20 = (bf16[128,512]{1,0:T(8,128)(2,1)}, bf16[128,512]{1,0:T(8,128)(2,1)S(1)}, u32[]{:S(2)}, u32[]{:S(2)}) collective-permute-start(bf16[128,512]{1,0:T(8,128)(2,1)} %get-tuple-element.64.b0), channel_id=1, source_target_pairs={{0,192},{32,96},{64,0},{96,160},{128,64},{160,224},{192,128},{224,... | collective-permute-start | bytes 393224 | tf_op jit(solution)/shard_map/ppermute | solution.py:383
  192.9 3.2 %collective-permute-done.19.b1 = bf16[128,512]{1,0:T(8,128)(2,1)S(1)} collective-permute-done((bf16[128,512]{1,0:T(8,128)(2,1)}, bf16[128,512]{1,0:T(8,128)(2,1)S(1)}, u32[]{:S(2)}, u32[]{:S(2)}) %collective-permute-start.19) | collective-permute-done | bytes 131104 | tf_op jit(solution)/shard_map/ppermute | solution.py:380
  196.1 6.2 %collective-permute-done.21.b3 = bf16[128,512]{1,0:T(8,128)(2,1)S(1)} collective-permute-done((bf16[128,512]{1,0:T(8,128)(2,1)S(1)}, bf16[128,512]{1,0:T(8,128)(2,1)S(1)}, u32[]{:S(2)}, u32[]{:S(2)}) %collective-permute-start.21) | collective-permute-done | bytes 131104 | tf_op jit(solution)/shard_map/ppermute | solution.py:380
  203.5 3.2 %collective-permute-start.17 = (bf16[128,1024]{1,0:T(8,128)(2,1)S(1)}, bf16[128,1024]{1,0:T(8,128)(2,1)S(1)}, u32[]{:S(2)}, u32[]{:S(2)}) collective-permute-start(bf16[128,1024]{1,0:T(8,128)(2,1)S(1)} %bitcast.30), channel_id=1, source_target_pairs={{0,3},{1,0},{2,1},{3,2},{4,7},{5,4},{6,5},{7,6},{8,11},{9,8},{10,9... | collective-permute-start | bytes 786440 | tf_op jit(solution)/shard_map/ppermute | solution.py:392
  206.7 6.7 %collective-permute-done.16.b1 = bf16[128,1024]{1,0:T(8,128)(2,1)S(1)} collective-permute-done((bf16[128,1024]{1,0:T(8,128)(2,1)S(1)}, bf16[128,1024]{1,0:T(8,128)(2,1)S(1)}, u32[]{:S(2)}, u32[]{:S(2)}) %collective-permute-start.16) | collective-permute-done | bytes 262176 | tf_op jit(solution)/shard_map/ppermute | solution.py:389
  213.4 2.7 %out.1 = bf16[128,512]{1,0:T(8,128)(2,1)} custom-call(bf16[32,24,256]{2,1,0:T(8,128)(2,1)} %copy-done.2, bf16[128,512]{1,0:T(8,128)(2,1)} %get-tuple-element.45.hidden, f32[128,1]{1,0:T(8,128)} %convert_divide_fusion.inv, bf16[128,256]{1,0:T(8,128)(2,1)} %get-tuple-element.52.mean, bf16[128,128]{1,0:T(8,128)(2,1)} %get-tuple-element.42.own, ...), custom_call_target="tpu_custom_call" | custom-call | bytes 5997056 | tf_op jit(solution)/shard_map/out/pallas_call | solution.py:49
  216.9 2.8 %join.1 = f32[1024,512]{1,0:T(8,128)} custom-call(bf16[128,512]{1,0:T(8,128)(2,1)} %get-tuple-element.64.b0, bf16[128,512]{1,0:T(8,128)(2,1)} %copy-done.16, bf16[128,512]{1,0:T(8,128)(2,1)} %copy-done.17, bf16[128,512]{1,0:T(8,128)(2,1)} %copy-done.19, bf16[4,128,512]{2,1,0:T(8,128)(2,1)} %copy-done.13), custom_call_target="tpu_custom_call" | custom-call | bytes 7340032 | tf_op jit(solution)/shard_map/join/pallas_call | solution.py:49
  221.7 2.7 %spread.1 = f32[512,1024]{1,0:T(8,128)} custom-call(bf16[128,1024]{1,0:T(8,128)(2,1)} %bitcast.31, bf16[128,1024]{1,0:T(8,128)(2,1)} %copy-done.24, bf16[128,1024]{1,0:T(8,128)(2,1)} %copy-done.25, bf16[128,1024]{1,0:T(8,128)(2,1)} %copy-done.26), custom_call_target="tpu_custom_call" | custom-call | bytes 7340032 | tf_op jit(solution)/shard_map/spread/pallas_call | solution.py:49
  (106 shorter events, 20.8 us)
Async XLA Ops:
  4.9 9.3 %copy-start.29 = (s32[1,32,8]{1,2,0:T(8,128)S(1)}, s32[1,32,8]{1,2,0:T(8,128)}, u32[]{:S(2)}) copy-start(s32[1,32,8]{1,2,0:T(8,128)} %param.12) | copy-start | bytes 3076
  4.9 4.3 %collective-permute-start = (bf16[4,128,1024]{2,1,0:T(8,128)(2,1)}, bf16[4,128,1024]{2,1,0:T(8,128)(2,1)S(1)}, u32[]{:S(2)}, u32[]{:S(2)}) collective-permute-start(bf16[4,128,1024]{2,1,0:T(8,128)(2,1)} %project.3), channel_id=1, source_target_pairs={{0,32},{32,0},{64,96},{96,64},{128,160},{160,128},{192,224},{224,1... | collective-permute-start | bytes 3145736 | tf_op jit(solution)/shard_map/ppermute | solution.py:386
  9.2 16.5 %copy-start.28 = (s32[1,128,10]{1,0,2:T(1,128)S(1)}, s32[1,128,10]{1,0,2:T(1,128)}, u32[]{:S(2)}) copy-start(s32[1,128,10]{1,0,2:T(1,128)} %param.10) | copy-start | bytes 15364
  9.2 19.4 %copy-start.30 = (s32[1,128]{1,0:T(1,128)S(1)}, s32[1,128]{1,0:T(1,128)}, u32[]{:S(2)}) copy-start(s32[1,128]{1,0:T(1,128)} %deg_row.1) | copy-start | bytes 1540
  9.2 1.0 copy-start
  12.6 8.2 %collective-permute-start.2 = (bf16[128,1024]{1,0:T(8,128)(2,1)}, bf16[128,1024]{1,0:T(8,128)(2,1)S(1)}, u32[]{:S(2)}, u32[]{:S(2)}) collective-permute-start(bf16[128,1024]{1,0:T(8,128)(2,1)} %get-tuple-element.36), channel_id=1, source_target_pairs={{0,64},{32,224},{64,128},{96,32},{128,192},{160,96},{192,0},{224,1... | collective-permute-start | bytes 786440 | tf_op jit(solution)/shard_map/ppermute | solution.py:380
  14.3 22.2 %collective-permute-start.1 = (bf16[128,1024]{1,0:T(8,128)(2,1)}, bf16[128,1024]{1,0:T(8,128)(2,1)S(1)}, u32[]{:S(2)}, u32[]{:S(2)}) collective-permute-start(bf16[128,1024]{1,0:T(8,128)(2,1)} %get-tuple-element.35), channel_id=1, source_target_pairs={{0,192},{32,96},{64,0},{96,160},{128,64},{160,224},{192,128},{224,... | collective-permute-start | bytes 786440 | tf_op jit(solution)/shard_map/ppermute | solution.py:383
  23.9 12.6 %collective-permute-start.3 = (bf16[128,1024]{1,0:T(8,128)(2,1)}, bf16[128,1024]{1,0:T(8,128)(2,1)S(1)}, u32[]{:S(2)}, u32[]{:S(2)}) collective-permute-start(bf16[128,1024]{1,0:T(8,128)(2,1)} %relay.1), channel_id=1, source_target_pairs={{0,64},{32,224},{64,128},{96,32},{128,192},{160,96},{192,0},{224,1... | collective-permute-start | bytes 786440 | tf_op jit(solution)/shard_map/ppermute | solution.py:380
  74.4 3.5 %collective-permute-start.4 = (bf16[4,128,512]{2,1,0:T(8,128)(2,1)}, bf16[4,128,512]{2,1,0:T(8,128)(2,1)S(1)}, u32[]{:S(2)}, u32[]{:S(2)}) collective-permute-start(bf16[4,128,512]{2,1,0:T(8,128)(2,1)} %get-tuple-element.48), channel_id=1, source_target_pairs={{0,32},{32,0},{64,96},{96,64},{128,160},{160,128},{192,224},{224,1... | collective-permute-start | bytes 1572872 | tf_op jit(solution)/shard_map/ppermute | solution.py:386
  77.9 0.8 copy-start.1
  80.9 20.6 %copy-start.7 = (bf16[128,512]{1,0:T(8,128)(2,1)S(1)}, bf16[128,512]{1,0:T(8,128)(2,1)}, u32[]{:S(2)}) copy-start(bf16[128,512]{1,0:T(8,128)(2,1)} %get-tuple-element.49.block.b0) | copy-start | bytes 393220
  80.9 9.9 %collective-permute-start.6 = (bf16[2,128,512]{2,1,0:T(8,128)(2,1)}, bf16[2,128,512]{2,1,0:T(8,128)(2,1)S(1)}, u32[]{:S(2)}, u32[]{:S(2)}) collective-permute-start(bf16[2,128,512]{2,1,0:T(8,128)(2,1)} %get-tuple-element.51), channel_id=1, source_target_pairs={{0,64},{32,224},{64,128},{96,32},{128,192},{160,96},{192,0},{224,1... | collective-permute-start | bytes 786440 | tf_op jit(solution)/shard_map/ppermute | solution.py:380
  81.0 18.8 %collective-permute-start.5 = (bf16[2,128,512]{2,1,0:T(8,128)(2,1)}, bf16[2,128,512]{2,1,0:T(8,128)(2,1)S(1)}, u32[]{:S(2)}, u32[]{:S(2)}) collective-permute-start(bf16[2,128,512]{2,1,0:T(8,128)(2,1)} %get-tuple-element.50), channel_id=1, source_target_pairs={{0,192},{32,96},{64,0},{96,160},{128,64},{160,224},{192,128},{224,... | collective-permute-start | bytes 786440 | tf_op jit(solution)/shard_map/ppermute | solution.py:383
  93.7 7.8 %collective-permute-start.7 = (bf16[2,128,512]{2,1,0:T(8,128)(2,1)}, bf16[2,128,512]{2,1,0:T(8,128)(2,1)S(1)}, u32[]{:S(2)}, u32[]{:S(2)}) collective-permute-start(bf16[2,128,512]{2,1,0:T(8,128)(2,1)} %pass.1), channel_id=1, source_target_pairs={{0,64},{32,224},{64,128},{96,32},{128,192},{160,96},{192,0},{224,1... | collective-permute-start | bytes 786440 | tf_op jit(solution)/shard_map/ppermute | solution.py:380
  93.7 16.8 %all-to-all-start.2 = ((bf16[32,8,512]{2,1,0:T(8,128)(2,1)}), bf16[32,8,512]{2,1,0:T(8,128)(2,1)S(1)}, u32[]{:S(2)}, u32[]{:S(2)}) async-start(bf16[32,8,512]{2,1,0:T(8,128)(2,1)} %bitcast.9), calls=%async_computation.2 | async-start | bytes 524288 | tf_op jit(solution)/shard_map/all_to_all | solution.py:65
  99.8 19.7 %copy-start.4 = (bf16[2,128,512]{2,1,0:T(8,128)(2,1)}, bf16[2,128,512]{2,1,0:T(8,128)(2,1)S(1)}, u32[]{:S(2)}) copy-start(bf16[2,128,512]{2,1,0:T(8,128)(2,1)S(1)} %collective-permute-done.5.near.b2) | copy-start | bytes 786436
  101.5 18.0 %copy-start.5 = (bf16[2,128,512]{2,1,0:T(8,128)(2,1)}, bf16[2,128,512]{2,1,0:T(8,128)(2,1)S(1)}, u32[]{:S(2)}) copy-start(bf16[2,128,512]{2,1,0:T(8,128)(2,1)S(1)} %collective-permute-done.7.far.b3) | copy-start | bytes 786436
  101.6 25.4 %collective-permute-start.11 = (bf16[4,128,512]{2,1,0:T(8,128)(2,1)S(1)}, bf16[4,128,512]{2,1,0:T(8,128)(2,1)S(1)}, u32[]{:S(2)}, u32[]{:S(2)}) collective-permute-start(bf16[4,128,512]{2,1,0:T(8,128)(2,1)S(1)} %pad_maximum_fusion.1), channel_id=1, source_target_pairs={{0,32},{32,0},{64,96},{96,64},{128,160},{160,128},{192,224},{224,1... | collective-permute-start | bytes 1572872 | tf_op jit(solution)/shard_map/ppermute | solution.py:386
  113.1 13.8 %copy-start.6 = (bf16[128,512]{1,0:T(8,128)(2,1)S(1)}, bf16[128,512]{1,0:T(8,128)(2,1)}, u32[]{:S(2)}) copy-start(bf16[128,512]{1,0:T(8,128)(2,1)} %near.1.b0) | copy-start | bytes 393220
  113.1 6.4 %collective-permute-start.8 = (bf16[128,512]{1,0:T(8,128)(2,1)}, bf16[128,512]{1,0:T(8,128)(2,1)S(1)}, u32[]{:S(2)}, u32[]{:S(2)}) collective-permute-start(bf16[128,512]{1,0:T(8,128)(2,1)} %near.1.b0), channel_id=1, source_target_pairs={{0,64},{32,224},{64,128},{96,32},{128,192},{160,96},{192,0},{224,1... | collective-permute-start | bytes 393224 | tf_op jit(solution)/shard_map/ppermute | solution.py:380
  114.0 12.8 %collective-permute-start.9 = (bf16[128,512]{1,0:T(8,128)(2,1)}, bf16[128,512]{1,0:T(8,128)(2,1)S(1)}, u32[]{:S(2)}, u32[]{:S(2)}) collective-permute-start(bf16[128,512]{1,0:T(8,128)(2,1)} %near.1.b0), channel_id=1, source_target_pairs={{0,192},{32,96},{64,0},{96,160},{128,64},{160,224},{192,128},{224,... | collective-permute-start | bytes 393224 | tf_op jit(solution)/shard_map/ppermute | solution.py:383
  119.5 7.4 %copy-start.14 = (bf16[128,512]{1,0:T(8,128)(2,1)}, bf16[128,512]{1,0:T(8,128)(2,1)S(1)}, u32[]{:S(2)}) copy-start(bf16[128,512]{1,0:T(8,128)(2,1)S(1)} %collective-permute-done.8.b1) | copy-start | bytes 393220
  119.5 7.3 %collective-permute-start.10 = (bf16[128,512]{1,0:T(8,128)(2,1)S(1)}, bf16[128,512]{1,0:T(8,128)(2,1)S(1)}, u32[]{:S(2)}, u32[]{:S(2)}) collective-permute-start(bf16[128,512]{1,0:T(8,128)(2,1)S(1)} %collective-permute-done.8.b1), channel_id=1, source_target_pairs={{0,64},{32,224},{64,128},{96,32},{128,192},{160,96},{192,0},{224,1... | collective-permute-start | bytes 393224 | tf_op jit(solution)/shard_map/ppermute | solution.py:380
  122.1 17.2 %all-to-all-start.1 = ((bf16[32,24,256]{2,1,0:T(8,128)(2,1)}), bf16[32,24,256]{2,1,0:T(8,128)(2,1)S(1)}, u32[]{:S(2)}, u32[]{:S(2)}) async-start(bf16[32,24,256]{2,1,0:T(8,128)(2,1)} %pack.1), calls=%async_computation.1 | async-start | bytes 786432 | tf_op jit(solution)/shard_map/all_to_all | solution.py:65
  126.8 14.9 %copy-start.15 = (bf16[128,512]{1,0:T(8,128)(2,1)}, bf16[128,512]{1,0:T(8,128)(2,1)S(1)}, u32[]{:S(2)}) copy-start(bf16[128,512]{1,0:T(8,128)(2,1)S(1)} %collective-permute-done.9.b2) | copy-start | bytes 393220
  126.8 14.8 %copy-start.18 = (bf16[128,512]{1,0:T(8,128)(2,1)}, bf16[128,512]{1,0:T(8,128)(2,1)S(1)}, u32[]{:S(2)}) copy-start(bf16[128,512]{1,0:T(8,128)(2,1)S(1)} %collective-permute-done.10.b3) | copy-start | bytes 393220
  127.0 0.8 copy-start.12
  131.0 10.6 %collective-permute-start.12 = (bf16[4,128,512]{2,1,0:T(8,128)(2,1)S(1)}, bf16[4,128,512]{2,1,0:T(8,128)(2,1)S(1)}, u32[]{:S(2)}, u32[]{:S(2)}) collective-permute-start(bf16[4,128,512]{2,1,0:T(8,128)(2,1)S(1)} %pad_maximum_fusion), channel_id=1, source_target_pairs={{0,32},{32,0},{64,96},{96,64},{128,160},{160,128},{192,224},{224,1... | collective-permute-start | bytes 1572872 | tf_op jit(solution)/shard_map/ppermute | solution.py:386
  141.7 0.8 copy-start.11
  146.1 8.0 %collective-permute-start.13 = (bf16[136,1024]{1,0:T(8,128)(2,1)}, bf16[136,1024]{1,0:T(8,128)(2,1)S(1)}, u32[]{:S(2)}, u32[]{:S(2)}) collective-permute-start(bf16[136,1024]{1,0:T(8,128)(2,1)} %get-tuple-element.60), channel_id=1, source_target_pairs={{0,1},{1,2},{2,3},{3,0},{4,5},{5,6},{6,7},{7,4},{8,9},{9,10},{10,1... | collective-permute-start | bytes 835592 | tf_op jit(solution)/shard_map/ppermute | solution.py:389
  146.5 10.0 %collective-permute-start.14 = (bf16[136,1024]{1,0:T(8,128)(2,1)}, bf16[136,1024]{1,0:T(8,128)(2,1)S(1)}, u32[]{:S(2)}, u32[]{:S(2)}) collective-permute-start(bf16[136,1024]{1,0:T(8,128)(2,1)} %get-tuple-element.61), channel_id=1, source_target_pairs={{0,3},{1,0},{2,1},{3,2},{4,7},{5,4},{6,5},{7,6},{8,11},{9,8},{10,9... | collective-permute-start | bytes 835592 | tf_op jit(solution)/shard_map/ppermute | solution.py:392
  156.5 8.0 %collective-permute-start.15 = (bf16[136,1024]{1,0:T(8,128)(2,1)}, bf16[136,1024]{1,0:T(8,128)(2,1)S(1)}, u32[]{:S(2)}, u32[]{:S(2)}) collective-permute-start(bf16[136,1024]{1,0:T(8,128)(2,1)} %x_relay.1), channel_id=1, source_target_pairs={{0,1},{1,2},{2,3},{3,0},{4,5},{5,6},{6,7},{7,4},{8,9},{9,10},{10,1... | collective-permute-start | bytes 835592 | tf_op jit(solution)/shard_map/ppermute | solution.py:389
  156.5 8.0 %copy-start.20 = (bf16[136,1024]{1,0:T(8,128)(2,1)}, bf16[136,1024]{1,0:T(8,128)(2,1)S(1)}, u32[]{:S(2)}) copy-start(bf16[136,1024]{1,0:T(8,128)(2,1)S(1)} %collective-permute-done.14.near) | copy-start | bytes 835588
  184.9 18.5 %all-to-all-start.4 = ((bf16[8,16,1024]{2,1,0:T(8,128)(2,1)}), bf16[8,16,1024]{2,1,0:T(8,128)(2,1)S(1)}, u32[]{:S(2)}, u32[]{:S(2)}) async-start(bf16[8,16,1024]{2,1,0:T(8,128)(2,1)} %get-tuple-element.63), calls=%async_computation.4 | async-start | bytes 524288 | tf_op jit(solution)/shard_map/all_to_all | solution.py:65
  189.7 6.4 %collective-permute-start.19 = (bf16[128,512]{1,0:T(8,128)(2,1)}, bf16[128,512]{1,0:T(8,128)(2,1)S(1)}, u32[]{:S(2)}, u32[]{:S(2)}) collective-permute-start(bf16[128,512]{1,0:T(8,128)(2,1)} %get-tuple-element.64.b0), channel_id=1, source_target_pairs={{0,64},{32,224},{64,128},{96,32},{128,192},{160,96},{192,0},{224,1... | collective-permute-start | bytes 393224 | tf_op jit(solution)/shard_map/ppermute | solution.py:380
  190.0 6.1 %collective-permute-start.20 = (bf16[128,512]{1,0:T(8,128)(2,1)}, bf16[128,512]{1,0:T(8,128)(2,1)S(1)}, u32[]{:S(2)}, u32[]{:S(2)}) collective-permute-start(bf16[128,512]{1,0:T(8,128)(2,1)} %get-tuple-element.64.b0), channel_id=1, source_target_pairs={{0,192},{32,96},{64,0},{96,160},{128,64},{160,224},{192,128},{224,... | collective-permute-start | bytes 393224 | tf_op jit(solution)/shard_map/ppermute | solution.py:383
  196.1 20.0 %copy-start.16 = (bf16[128,512]{1,0:T(8,128)(2,1)}, bf16[128,512]{1,0:T(8,128)(2,1)S(1)}, u32[]{:S(2)}) copy-start(bf16[128,512]{1,0:T(8,128)(2,1)S(1)} %collective-permute-done.19.b1) | copy-start | bytes 393220
  196.1 6.2 %collective-permute-start.21 = (bf16[128,512]{1,0:T(8,128)(2,1)S(1)}, bf16[128,512]{1,0:T(8,128)(2,1)S(1)}, u32[]{:S(2)}, u32[]{:S(2)}) collective-permute-start(bf16[128,512]{1,0:T(8,128)(2,1)S(1)} %collective-permute-done.19.b1), channel_id=1, source_target_pairs={{0,64},{32,224},{64,128},{96,32},{128,192},{160,96},{192,0},{224,1... | collective-permute-start | bytes 393224 | tf_op jit(solution)/shard_map/ppermute | solution.py:380
  196.1 20.0 %copy-start.17 = (bf16[128,512]{1,0:T(8,128)(2,1)}, bf16[128,512]{1,0:T(8,128)(2,1)S(1)}, u32[]{:S(2)}) copy-start(bf16[128,512]{1,0:T(8,128)(2,1)S(1)} %collective-permute-done.20.b2) | copy-start | bytes 393220
  202.3 13.8 %copy-start.19 = (bf16[128,512]{1,0:T(8,128)(2,1)}, bf16[128,512]{1,0:T(8,128)(2,1)S(1)}, u32[]{:S(2)}) copy-start(bf16[128,512]{1,0:T(8,128)(2,1)S(1)} %collective-permute-done.21.b3) | copy-start | bytes 393220
  203.3 12.8 %collective-permute-start.22 = (bf16[4,128,512]{2,1,0:T(8,128)(2,1)S(1)}, bf16[4,128,512]{2,1,0:T(8,128)(2,1)S(1)}, u32[]{:S(2)}, u32[]{:S(2)}) collective-permute-start(bf16[4,128,512]{2,1,0:T(8,128)(2,1)S(1)} %pad_maximum_fusion.2), channel_id=1, source_target_pairs={{0,32},{32,0},{64,96},{96,64},{128,160},{160,128},{192,224},{224,1... | collective-permute-start | bytes 1572872 | tf_op jit(solution)/shard_map/ppermute | solution.py:386
  203.4 16.3 %copy-start.9 = (bf16[8,16,1024]{2,1,0:T(8,128)(2,1)}, bf16[8,16,1024]{2,1,0:T(8,128)(2,1)S(1)}, u32[]{:S(2)}) copy-start(bf16[8,16,1024]{2,1,0:T(8,128)(2,1)S(1)} %all-to-all-done.4) | copy-start | bytes 786436
  203.4 10.0 %collective-permute-start.16 = (bf16[128,1024]{1,0:T(8,128)(2,1)S(1)}, bf16[128,1024]{1,0:T(8,128)(2,1)S(1)}, u32[]{:S(2)}, u32[]{:S(2)}) collective-permute-start(bf16[128,1024]{1,0:T(8,128)(2,1)S(1)} %bitcast.29), channel_id=1, source_target_pairs={{0,1},{1,2},{2,3},{3,0},{4,5},{5,6},{6,7},{7,4},{8,9},{9,10},{10,1... | collective-permute-start | bytes 786440 | tf_op jit(solution)/shard_map/ppermute | solution.py:389
  203.5 16.2 %collective-permute-start.17 = (bf16[128,1024]{1,0:T(8,128)(2,1)S(1)}, bf16[128,1024]{1,0:T(8,128)(2,1)S(1)}, u32[]{:S(2)}, u32[]{:S(2)}) collective-permute-start(bf16[128,1024]{1,0:T(8,128)(2,1)S(1)} %bitcast.30), channel_id=1, source_target_pairs={{0,3},{1,0},{2,1},{3,2},{4,7},{5,4},{6,5},{7,6},{8,11},{9,8},{10,9... | collective-permute-start | bytes 786440 | tf_op jit(solution)/shard_map/ppermute | solution.py:392
  213.4 6.3 %copy-start.24 = (bf16[128,1024]{1,0:T(8,128)(2,1)}, bf16[128,1024]{1,0:T(8,128)(2,1)S(1)}, u32[]{:S(2)}) copy-start(bf16[128,1024]{1,0:T(8,128)(2,1)S(1)} %collective-permute-done.16.b1) | copy-start | bytes 786436
  213.4 7.6 %collective-permute-start.18 = (bf16[128,1024]{1,0:T(8,128)(2,1)S(1)}, bf16[128,1024]{1,0:T(8,128)(2,1)S(1)}, u32[]{:S(2)}, u32[]{:S(2)}) collective-permute-start(bf16[128,1024]{1,0:T(8,128)(2,1)S(1)} %collective-permute-done.16.b1), channel_id=1, source_target_pairs={{0,1},{1,2},{2,3},{3,0},{4,5},{5,6},{6,7},{7,4},{8,9},{9,10},{10,1... | collective-permute-start | bytes 786440 | tf_op jit(solution)/shard_map/ppermute | solution.py:389
  216.1 0.8 copy-start.13
  219.7 1.3 copy-start.25
  (9 other events, 6.5 us)

commit v4 on v0

v4 whole, which is shorter than its diff:
```python
import math

import jax
import jax.numpy as jnp
from jax import lax
from jax.experimental import pallas as pl
from jax.experimental.pallas import tpu as pltpu
from jax.sharding import PartitionSpec as P

F32 = jnp.float32
BF16 = jnp.bfloat16
CHIPS = 4
NT = (((1,), (1,)), ((), ()))
TN = (((0,), (0,)), ((), ()))


def step(core):
    return 1 if core == 0 else -1


def along_y(sign):
    return [
        (y * 2 + c, (y + sign * step(c)) % CHIPS * 2 + c) for y in range(CHIPS) for c in range(2)
    ]


def along_x(sign, parts, feats):
    def device(f, z, x):
        return f * parts + z * CHIPS + x % CHIPS

    return [
        (device(f, z, x), device(f, z, x + sign * step(f % 2)))
        for f in range(feats)
        for z in range(parts // CHIPS)
        for x in range(CHIPS)
    ]


SWAP = [(i, i ^ 1) for i in range(2 * CHIPS)]


def mm(a, b, dims=(((1,), (0,)), ((), ()))):
    return lax.dot_general(a, b, dims, preferred_element_type=F32)


def whole(name, body, outs, *args, scratch=()):
    return pl.pallas_call(body, out_shape=outs, scratch_shapes=scratch, name=name)(*args)


def shape(dims, kind=BF16):
    return jax.ShapeDtypeStruct(dims, kind)


def trade(boxes, groups=None):
    return lax.all_to_all(
        boxes, "dom", split_axis=0, concat_axis=0, axis_index_groups=groups, tiled=True
    )


def tables_body(nbr_t, deg, sends_t, give, take, own, own_t, inv):
    fan, nodes = nbr_t.shape
    kmax, parts = sends_t.shape
    span = 2 * kmax * parts
    r = lax.broadcasted_iota(jnp.int32, (span, nodes), 0)
    j = r % (2 * kmax)
    entry = nodes + r // (2 * kmax) * kmax + j
    leave = jnp.where(j < kmax, entry, -2)
    arrive = jnp.where(j >= kmax, entry - kmax, -2)
    row = lax.broadcasted_iota(jnp.int32, (nodes, nodes), 0)
    leave_sum = jnp.zeros((span, nodes), F32)
    arrive_sum = jnp.zeros((span, nodes), F32)
    own_sum = jnp.zeros((nodes, nodes), F32)
    for s in range(fan):
        used = jnp.where(s < deg[...], nbr_t[s : s + 1, :], -1)
        leave_sum += jnp.where(leave == used, 1.0, 0.0)
        arrive_sum += jnp.where(arrive == used, 1.0, 0.0)
        own_sum += jnp.where(row == used, 1.0, 0.0)
    own_t[...] = own_sum.astype(BF16)
    own[...] = own_sum.T.astype(BF16)
    part = lax.broadcasted_iota(jnp.int32, (parts, span), 0)
    lane = lax.broadcasted_iota(jnp.int32, (parts, span), 1)
    spread = jnp.where(lane // (2 * kmax) == part, 1.0, 0.0).astype(BF16)
    ids = mm(sends_t[...].astype(F32).astype(BF16), spread)
    slot = lax.broadcasted_iota(jnp.int32, (kmax, span), 0)
    at = lax.broadcasted_iota(jnp.int32, (kmax, span), 1) % (2 * kmax)
    back_id = jnp.sum(jnp.where(slot == at, ids + 1.0, 0.0), axis=0, keepdims=True) - 1.0
    pick_id = jnp.sum(jnp.where(slot + kmax == at, ids + 1.0, 0.0), axis=0, keepdims=True) - 1.0
    node = lax.broadcasted_iota(jnp.int32, (nodes, span), 0).astype(F32)
    home = jnp.where(node == back_id, 1.0, 0.0)
    pick = jnp.where(node == pick_id, 1.0, 0.0)
    give[:, :nodes] = leave_sum.astype(BF16)
    give[:, nodes:] = pick.T.astype(BF16)
    take[:nodes, :] = arrive_sum.T.astype(BF16)
    take[nodes:, :] = home.astype(BF16)
    inv[...] = jnp.broadcast_to(1.0 / deg[...].astype(F32), (nodes, nodes)).T


def turn_body(flat, out):
    groups, nodes, cols = flat.shape
    for g in range(groups):
        out[:, g * nodes : (g + 1) * nodes] = flat[g].T


def ring_place(at, turn, offset):
    o, turned = offset
    return (at + CHIPS + o * (turn if turned else 1)) % CHIPS


def places(offsets, other):
    feat = lax.axis_index("feat")
    y, core = feat // 2, feat % 2
    held = 1 - core if other else core
    return [ring_place(y, 1 - 2 * core, o) * 2 + held for o in offsets]


def places_x(offsets):
    core = lax.axis_index("feat") % 2
    x = lax.axis_index("dom") % CHIPS
    return [ring_place(x, 1 - 2 * core, o) for o in offsets]


SUM_MINE = ((2, False), (-1, True), (1, True), (0, False))
SUM_OTHER = ((2, False), (1, True), (-1, True), (0, False))
GET_MINE = ((0, False), (-1, True), (1, True), (2, False))
GET_OTHER = ((0, False), (1, True), (-1, True), (2, False))


def project(flat, w_one, other):
    groups, nodes, cols = flat.shape

    def body(rows, w, out):
        ids = places(SUM_OTHER if other else SUM_MINE, other)
        picked = jnp.concatenate([rows[g] for g in ids], axis=0)
        out[...] = mm(picked, w[...]).astype(BF16).reshape(out.shape)

    return whole("project", body, shape((CHIPS, nodes, w_one.shape[1])), flat, w_one)


def add(*terms):
    total = terms[0].astype(F32)
    for term in terms[1:]:
        total += term.astype(F32)
    return total


def forward_body(part, got, near, far, grads, inv, give, p_self, p_near, boxes):
    width = grads.shape[1]
    total = add(part[...], got[...], near[...], far[...])
    p_self[...] = total[:, :width]
    mine = total[:, width:].astype(BF16)
    p_near[...] = mine
    scaled = (grads[...].astype(F32) * inv[:, :1]).astype(BF16)
    boxes[...] = mm(give[...], jnp.concatenate([scaled, mine], axis=0)).astype(BF16)


def middle_body(
    recv, p_self, p_near, grads, inv, w_two, give, take, own, own_t,
    boxes, near_local, hidden_out, ahead, behind, third, mine, scratch,
):
    nodes, width = grads.shape
    scales = inv[:, :1]
    both = mm(take[...], recv[...])
    grad = grads[...]
    scaled = (grad.astype(F32) * scales).astype(BF16)
    pre = p_self[...] + scales * (both[:nodes] + mm(own[...], p_near[...]))
    back = (both[nodes:] + mm(own_t[...], scaled)).astype(BF16)
    d_hidden = mm(grad, w_two[:width, :], NT) + mm(back, w_two[width:, :], NT)
    sig = jax.nn.sigmoid(pre)
    hidden = (pre * sig).astype(BF16)
    hidden_out[...] = hidden
    d_pre = d_hidden * sig * (1.0 + pre * (1.0 - sig))
    term = (d_pre * scales).astype(BF16)
    boxes[...] = mm(give[...], jnp.concatenate([term, hidden], axis=0)).astype(BF16)
    near_local[...] = mm(own_t[...], term)
    half = scratch.shape[0] // 2
    for k, right in enumerate((grad, back)):
        piece = mm(hidden, right, TN).astype(BF16)
        scratch[k * half : (k + 1) * half] = piece.reshape(half, -1, width)
    ahead[0] = d_pre.astype(BF16)
    behind[0] = d_pre.astype(BF16)
    for k, other in enumerate((True, False)):
        away, back_to, on_to, here = places(SUM_MINE, other)
        ahead[1 + k] = scratch[away]
        behind[1 + k] = scratch[back_to]
        third[k] = scratch[on_to]
        mine[k] = scratch[here]


def near_body(recv, near_local, take, out):
    nodes = out.shape[0]
    out[...] = (near_local[...] + mm(take[nodes:, :], recv[...])).astype(BF16)


def out_body(recv, hidden, inv, take, own, w_two, out):
    nodes, width = hidden.shape
    total = mm(take[:nodes, :], recv[...]) + mm(own[...], hidden[...])
    agg = (inv[:, :1] * total).astype(BF16)
    out[...] = (mm(hidden[...], w_two[:width, :]) + mm(agg, w_two[width:, :])).astype(BF16)


def grad_of(flat_t, held, other, stack):
    for k, g in enumerate(places(GET_MINE, False)):
        stack[g] = held[k]
    for k, g in enumerate(places(GET_OTHER, True)):
        stack[g] = other[k]
    groups, nodes, width = stack.shape
    return mm(flat_t[...], stack[...].reshape(groups * nodes, width)).astype(BF16)


def self_body(flat_t, held, other, out, stack):
    out[...] = grad_of(flat_t, held, other, stack)


def near_grad_body(
    flat_t, held, other, first, two_mine, two_other, ahead, behind, third, own, stack, boxes
):
    width = first.shape[1]
    chips, deep, rows, cut = boxes.shape
    block = first.shape[0] // chips
    part = block // deep
    sides = (first[...], grad_of(flat_t, held, other, stack))
    two = add(two_mine[...], two_other[...]).astype(BF16)
    tail = rows - 4 * part
    slab = deep * tail
    for x in range(chips):
        for q in range(4):
            at = q % 2 * cut
            piece = sides[q // 2][x * block : (x + 1) * block, at : at + cut]
            boxes[x, :, q * part : (q + 1) * part, :] = piece.reshape(deep, part, cut)
        piece = two[x % 2 * slab : (x % 2 + 1) * slab, x // 2 * cut : (x // 2 + 1) * cut]
        boxes[x, :, 4 * part :, :] = piece.reshape(deep, tail, cut)
    for x, target in zip(places_x(SUM_MINE), (ahead, behind, third, own)):
        target[...] = boxes[x]


def chunk_body(b0, b1, b2, b3, out, scratch):
    deep, rows, cut = b0.shape
    chips, slab, _ = scratch.shape
    tail = slab // deep
    for x, block in zip(places_x(GET_MINE), (b0, b1, b2, b3)):
        scratch[x] = block[:, rows - tail :, :].reshape(slab, cut)
    for x in range(chips):
        at = x % 2 * slab
        out[at : at + slab, x // 2 * cut : (x // 2 + 1) * cut] = scratch[x]


def spread_body(b0, b1, b2, b3, out):
    deep, rows, cut = b0.shape
    block = out.shape[0] // CHIPS
    part = block // deep
    for x, held in zip(places_x(GET_MINE), (b0, b1, b2, b3)):
        at = pl.ds(pl.multiple_of(x * block, block), block)
        for q in range(4):
            piece = held[:, q * part : (q + 1) * part, :].astype(F32)
            out[at, q * cut : (q + 1) * cut] = piece.reshape(block, cut)


def join_body(held, other, out):
    nodes = held.shape[1]

    def put(g, block):
        out[pl.ds(pl.multiple_of(g * nodes, nodes), nodes), :] = block.astype(F32)

    for k, g in enumerate(places(GET_MINE, False)):
        put(g, held[k])
    for k, g in enumerate(places(GET_OTHER, True)):
        put(g, other[k])


def on_device(features, w_one, w_two, neighbor, degree, send_rows, grad_out):
    groups, nodes, cols = features.shape
    width = w_two.shape[1]
    parts = lax.axis_size("dom")
    deep = parts // CHIPS
    sends = send_rows[0]
    kmax = sends.shape[1]
    span = 2 * sends.size
    grads = grad_out[0]
    scale = 1.0 / math.sqrt(groups * nodes * parts)
    y_ahead, y_behind = along_y(1), along_y(-1)
    x_ahead, x_behind = along_x(1, parts, groups), along_x(-1, parts, groups)
    lines = [[z * CHIPS + x for z in range(deep)] for x in range(CHIPS)]

    def forward(block):
        return lax.ppermute(block, "feat", y_ahead)

    def backward(block):
        return lax.ppermute(block, "feat", y_behind)

    def swap(block):
        return lax.ppermute(block, "feat", SWAP)

    def x_forward(block):
        return lax.ppermute(block, ("feat", "dom"), x_ahead)

    def x_backward(block):
        return lax.ppermute(block, ("feat", "dom"), x_behind)

    def gather(block):
        one = forward(block)
        two = backward(block)
        return jnp.stack([block, one, two, forward(one)])

    got = swap(project(features, w_one, True))
    mine = project(features, w_one, False)
    give, take, own, own_t, inv = whole(
        "tables",
        tables_body,
        (
            shape((span, 2 * nodes)),
            shape((2 * nodes, span)),
            shape((nodes, nodes)),
            shape((nodes, nodes)),
            shape((nodes, nodes), F32),
        ),
        neighbor[0].T, degree, sends.T,
    )
    flat_t = whole("turn", turn_body, shape((cols, groups * nodes)), features)
    relay = forward(add(mine[0], got[0]).astype(BF16))
    near = backward(add(mine[1], got[1]).astype(BF16))
    far = forward(add(mine[2], got[2], relay).astype(BF16))
    block = shape((nodes, width))
    p_self, p_near, boxes = whole(
        "forward",
        forward_body,
        (shape((nodes, width), F32), block, shape((span, width))),
        mine[3], got[3], near, far, grads, inv, give,
    )
    recv = trade(boxes.reshape(parts, 2 * kmax, width)).reshape(span, width)
    rows = 2 * width // groups
    boxes, near_local, hidden, ahead, behind, third, mine = whole(
        "middle",
        middle_body,
        (
            shape((span, width)),
            shape((nodes, width), F32),
            block,
            shape((3, rows, width)),
            shape((3, rows, width)),
            shape((2, rows, width)),
            shape((2, rows, width)),
        ),
        recv, p_self, p_near, grads, inv, w_two, give, take, own, own_t,
        scratch=[pltpu.VMEM((groups, rows, width), BF16)],
    )
    recv = trade(boxes.reshape(parts, 2 * kmax, width)).reshape(span, width)

    relay = forward(ahead)
    near = backward(behind)
    far = forward(jnp.concatenate([relay[:1], add(third, relay[1:]).astype(BF16)]))
    sums = add(mine, near[1:], far[1:])
    held = jnp.stack([ahead[0], relay[0], near[0], far[0], sums[0].astype(BF16)])
    other = swap(held)
    stack = pltpu.VMEM((groups, nodes, width), BF16)
    first = whole("self_grad", self_body, shape((cols, width)), flat_t, held, other, scratch=[stack])
    two_mine, two_other = sums[1], other[4]

    d_near = whole("near", near_body, block, recv, near_local, take)
    held, first = lax.optimization_barrier((gather(d_near), first))
    other = swap(held)
    out = whole("out", out_body, block, recv, hidden, inv, take, own, w_two)

    lot = shape((deep, 9 * cols // parts // 2, width // 2))
    ahead, behind, third, mine = whole(
        "near_grad",
        near_grad_body,
        (lot, lot, lot, lot),
        flat_t, held, other, first, two_mine, two_other,
        scratch=[stack, pltpu.VMEM((CHIPS, *lot.shape), BF16)],
    )
    relay = x_forward(ahead)
    near = x_backward(behind)
    far = x_forward(add(third, relay).astype(BF16))
    terms = trade(add(mine, near, far).astype(BF16), lines)
    total = (jnp.sum(terms.astype(F32), axis=0) * scale).astype(BF16)
    total = trade(jnp.broadcast_to(total[None], terms.shape), lines)
    relay = x_forward(total)
    near = x_backward(total)
    lots = (total, relay, near, x_forward(relay))
    slab = 2 * width // groups // 2
    chunk = whole(
        "chunk", chunk_body, block, *lots, scratch=[pltpu.VMEM((CHIPS, slab, width // 2), BF16)]
    )
    held = gather(chunk)
    one = whole("spread", spread_body, shape((cols, 2 * width), F32), *lots)
    two = whole("join", join_body, shape((2 * width, width), F32), held, swap(held))
    return out[None], one, two


def solution(mesh):
    in_specs = (
        P(None, "dom", "feat"),
        P("feat", None),
        P(),
        P("feat", "dom", None),
        P("feat", "dom"),
        P("feat", "dom", None),
        P("feat", "dom", None),
    )
    out_specs = (P("feat", "dom", None), P("feat", None), P())
    return jax.shard_map(
        on_device, mesh=mesh, in_specs=in_specs, out_specs=out_specs, check_vma=False
    )
```

time: 583 us -> 216 us (0.37)
  waiting for transfers between devices: 435 us -> 73 us
  blocking collectives: 15.2 us -> 55.7 us
  Pallas kernels: 0 us -> 36.8 us
  other arithmetic: 43.1 us -> 6.66 us
  local copies, waits for them, and re-layouts: 36.9 us -> 11 us
  between operations: 14.1 us -> 0.9 us
  matrix products: 11.5 us -> 0 us
    psum x2 -> x0, waiting for transfers between devices: 407 us -> none  [the longest x1 257 us: on_device(): two_sum = lax.psum(two_sum, ('feat', 'dom'))]
    ppermute x0 -> x22, waiting for transfers between devices: none -> 61.7 us  [the longest x8 33.6 us: forward(): return lax.ppermute(block, 'feat', y_ahead)]
    all_to_all x1 -> x3, blocking collectives: 15.2 us -> 55.7 us  [trade(): lax.all_to_all(boxes, 'dom', split_axis=0, concat_axis=0, axis_index_grou...]
    pallas_call x0 -> x13, Pallas kernels: none -> 36.8 us  [whole(): pl.pallas_call(body, out_shape=outs, scratch_shapes=scratch, name=name)]
    scatter-add x4 -> x0, other arithmetic: 30.8 us -> none  [the longest x2 26.1 us: gather_back(): jnp.zeros((nodes + sends.size, span), jnp.float32).at[nbrs.reshape(-1)]]
    ppermute x0 -> x22, starting transfers between devices: none -> 21.7 us  [the longest x4 10.5 us: backward(): return lax.ppermute(block, 'feat', y_behind)]
    all_to_all x3 -> x1, starting transfers between devices: 25.8 us -> 6.11 us  [trade(): lax.all_to_all(boxes, 'dom', split_axis=0, concat_axis=0, axis_index_grou...]
    mul x4 -> x0, local copies, waits for them, and re-layouts: 14 us -> none  [gather_back(): terms = (weight[..., None] * grads[:, None, :]).reshape(-1, span)]
  transfers between devices with their start and end apart: 7 -> 23, of which waited for: 6 -> 14; matrix products, arithmetic and copies ran while one was open for 8% -> 5% of each run, Pallas kernels for 0% -> 7%
where the time goes in v4:
time: 216 us; the launch traced here: 212 us
  waiting for transfers between devices  73 us (34%)
  blocking collectives  55.7 us (26%)
  Pallas kernels  36.8 us (17%)
  starting transfers between devices  27.8 us (13%)
  local copies, waits for them, and re-layouts  11 us (5%)
  other arithmetic  6.66 us (3%)
    all_to_all x3, blocking collectives, trade(): lax.all_to_all(boxes, 'dom', split_axis=0, concat_axis=0, axis_index_grou...  55.7 us
    pallas_call x13, Pallas kernels, whole(): pl.pallas_call(body, out_shape=outs, scratch_shapes=scratch, name=name)  36.8 us
    ppermute x8, waiting for transfers between devices, forward(): return lax.ppermute(block, 'feat', y_ahead)  33.6 us
    ppermute x4, waiting for transfers between devices, x_forward(): return lax.ppermute(block, ('feat', 'dom'), x_ahead)  25.9 us
    all_to_all x1, waiting for transfers between devices, trade(): lax.all_to_all(boxes, 'dom', split_axis=0, concat_axis=0, axis_index_grou...  11.3 us
    ppermute x4, starting transfers between devices, backward(): return lax.ppermute(block, 'feat', y_behind)  10.5 us
    unnamed x36, local copies, waits for them, and re-layouts  6.25 us
    all_to_all x1, starting transfers between devices, trade(): lax.all_to_all(boxes, 'dom', split_axis=0, concat_axis=0, axis_index_grou...  6.11 us
  transfers between devices with their start and end apart: 23, of which 14 were waited for; matrix products, arithmetic and copies ran while one was open for 5% of the time, Pallas kernels for 7%

profile of v4, /device:TPU:32, one launch (start us, length us, event | category | flops | bytes accessed | tf_op | source)
XLA Modules:
  0.0 211.8 jit_solution(8700952236111308865)
XLA Ops:
  0.6 3.2 %project.3 = bf16[4,128,1024]{2,1,0:T(8,128)(2,1)} custom-call(bf16[8,128,512]{2,1,0:T(8,128)(2,1)} %flat.1, bf16[512,1024]{1,0:T(8,128)(2,1)} %w.3), custom_call_target="tpu_custom_call" | custom-call | tf_op jit(solution)/shard_map/project/pallas_call | solution.py:47
  3.9 3.2 %project.2 = bf16[4,128,1024]{2,1,0:T(8,128)(2,1)} custom-call(bf16[8,128,512]{2,1,0:T(8,128)(2,1)} %flat.1, bf16[512,1024]{1,0:T(8,128)(2,1)} %w.3), custom_call_target="tpu_custom_call" | custom-call | tf_op jit(solution)/shard_map/project/pallas_call | solution.py:47
  7.1 1.2 fusion.2
  8.3 1.7 collective-permute-start.2
  10.0 1.7 collective-permute-start.1
  11.6 4.8 %collective-permute-done.2 = bf16[128,1024]{1,0:T(8,128)(2,1)S(1)} collective-permute-done((bf16[128,1024]{1,0:T(8,128)(2,1)S(1)}, bf16[128,1024]{1,0:T(8,128)(2,1)S(1)}, u32[]{:S(2)}, u32[]{:S(2)}) %collective-permute-start.2) | collective-permute-done | bytes 262176 | tf_op jit(solution)/shard_map/ppermute | solution.py:285
  16.5 1.1 fusion
  17.5 1.8 collective-permute-start.3
  19.3 1.7 slice_bitcast_fusion.2.part
  21.6 2.0 tables.1
  24.4 1.7 collective-permute-done.3.far
  26.8 2.6 %forward.1 = (f32[128,512]{1,0:T(8,128)}, bf16[128,512]{1,0:T(8,128)(2,1)}, bf16[512,512]{1,0:T(8,128)(2,1)}) custom-call(bf16[128,1024]{1,0:T(8,128)(2,1)} %slice_bitcast_fusion.2.part, bf16[128,1024]{1,0:T(8,128)(2,1)} %slice_bitcast_fusion.1.got, bf16[128,1024]{1,0:T(8,128)(2,1)} %copy-done.13, bf16[128,1024]{1,0:T(8,128)(2,1)} %copy-done.14, ...), custom_call_target="tpu_custom_call" | custom-call | tf_op jit(solution)/shard_map/forward/pallas_call | solution.py:47
  29.4 29.0 %all_to_all.20 = bf16[32,16,512]{2,1,0:T(8,128)(2,1)} all-to-all(bf16[32,16,512]{2,1,0:T(8,128)(2,1)} %bitcast.41), channel_id=1, replica_groups=mesh['feat'=8,'dom'=32] {'dom'}, dimensions={0} | all-to-all | bytes 1048576 | tf_op jit(solution)/shard_map/all_to_all | solution.py:55
  58.4 4.1 %middle.1 = (bf16[512,512]{1,0:T(8,128)(2,1)}, f32[128,512]{1,0:T(8,128)}, bf16[128,512]{1,0:T(8,128)(2,1)}, bf16[3,128,512]{2,1,0:T(8,128)(2,1)}, bf16[3,128,51...) custom-call(bf16[512,512]{1,0:T(8,128)(2,1)} %bitcast.40, ...), custom_call_target="tpu_custom_call" | custom-call | tf_op jit(solution)/shard_map/middle/pallas_call | solution.py:47
  62.6 3.2 %collective-permute-start.8 = (bf16[3,128,512]{2,1,0:T(8,128)(2,1)}, bf16[3,128,512]{2,1,0:T(8,128)(2,1)S(1)}, u32[]{:S(2)}, u32[]{:S(2)}) collective-permute-start(bf16[3,128,512]{2,1,0:T(8,128)(2,1)} %get-tuple-element.36), channel_id=1, source_target_pairs={{0,192},{32,96},{64,0},{96,160},{128,64},{160,224},{192,128},{224,... | collective-permute-start | bytes 1179656 | tf_op jit(solution)/shard_map/ppermute | solution.py:288
  65.8 0.9 slice_dynamic-update-slice_fusion.2
  66.7 8.2 %collective-permute-done.7 = bf16[3,128,512]{2,1,0:T(8,128)(2,1)S(1)} collective-permute-done((bf16[3,128,512]{2,1,0:T(8,128)(2,1)}, bf16[3,128,512]{2,1,0:T(8,128)(2,1)S(1)}, u32[]{:S(2)}, u32[]{:S(2)}) %collective-permute-start.7) | collective-permute-done | bytes 393248 | tf_op jit(solution)/shard_map/ppermute | solution.py:285
  74.9 1.0 add_convert_fusion.2
  76.0 6.1 %all-to-all-start.1 = ((bf16[32,16,512]{2,1,0:T(8,128)(2,1)}), bf16[32,16,512]{2,1,0:T(8,128)(2,1)S(1)}, u32[]{:S(2)}, u32[]{:S(2)}) async-start(bf16[32,16,512]{2,1,0:T(8,128)(2,1)} %bitcast.11), calls=%async_computation.1 | async-start | bytes 1048576 | tf_op jit(solution)/shard_map/all_to_all | solution.py:55
  82.2 2.8 %collective-permute-done.9 = bf16[3,128,512]{2,1,0:T(8,128)(2,1)S(1)} collective-permute-done((bf16[3,128,512]{2,1,0:T(8,128)(2,1)S(1)}, bf16[3,128,512]{2,1,0:T(8,128)(2,1)S(1)}, u32[]{:S(2)}, u32[]{:S(2)}) %collective-permute-start.9) | collective-permute-done | bytes 393248 | tf_op jit(solution)/shard_map/ppermute | solution.py:285
  85.3 11.3 %all-to-all-done.1 = bf16[32,16,512]{2,1,0:T(8,128)(2,1)S(1)} async-done(((bf16[32,16,512]{2,1,0:T(8,128)(2,1)}), bf16[32,16,512]{2,1,0:T(8,128)(2,1)S(1)}, u32[]{:S(2)}, u32[]{:S(2)}) %all-to-all-start.1) | async-done | bytes 524320 | tf_op jit(solution)/shard_map/all_to_all | solution.py:55
  97.4 2.1 near.1
  100.3 2.4 %collective-permute-start.5 = (bf16[128,512]{1,0:T(8,128)(2,1)}, bf16[128,512]{1,0:T(8,128)(2,1)S(1)}, u32[]{:S(2)}, u32[]{:S(2)}) collective-permute-start(bf16[128,512]{1,0:T(8,128)(2,1)} %near.1), channel_id=1, source_target_pairs={{0,192},{32,96},{64,0},{96,160},{128,64},{160,224},{192,128},{224,... | collective-permute-start | bytes 393224 | tf_op jit(solution)/shard_map/ppermute | solution.py:288
  102.7 3.2 %collective-permute-done.4 = bf16[128,512]{1,0:T(8,128)(2,1)S(1)} collective-permute-done((bf16[128,512]{1,0:T(8,128)(2,1)}, bf16[128,512]{1,0:T(8,128)(2,1)S(1)}, u32[]{:S(2)}, u32[]{:S(2)}) %collective-permute-start.4) | collective-permute-done | bytes 131104 | tf_op jit(solution)/shard_map/ppermute | solution.py:285
  105.9 2.6 %turn.1.flat_t = bf16[512,1024]{1,0:T(8,128)(2,1)} custom-call(bf16[8,128,512]{2,1,0:T(8,128)(2,1)} %flat.1), custom_call_target="tpu_custom_call" | custom-call | tf_op jit(solution)/shard_map/turn/pallas_call | solution.py:47
  108.4 3.6 %collective-permute-done.6 = bf16[128,512]{1,0:T(8,128)(2,1)S(1)} collective-permute-done((bf16[128,512]{1,0:T(8,128)(2,1)S(1)}, bf16[128,512]{1,0:T(8,128)(2,1)S(1)}, u32[]{:S(2)}, u32[]{:S(2)}) %collective-permute-start.6) | collective-permute-done | bytes 131104 | tf_op jit(solution)/shard_map/ppermute | solution.py:285
  113.0 3.2 %self_grad.1.first = bf16[512,512]{1,0:T(8,128)(2,1)} custom-call(bf16[512,1024]{1,0:T(8,128)(2,1)} %turn.1.flat_t, bf16[5,128,512]{2,1,0:T(8,128)(2,1)} %copy-done.8, bf16[5,128,512]{2,1,0:T(8,128)(2,1)} %copy-done.7), custom_call_target="tpu_custom_call" | custom-call | tf_op jit(solution)/shard_map/self_grad/pallas_call | solution.py:47
  117.0 1.6 slice_bitcast_fusion.3.two_other
  119.3 3.6 %near_grad.1 = (bf16[8,72,256]{2,1,0:T(8,128)(2,1)}, bf16[8,72,256]{2,1,0:T(8,128)(2,1)}, bf16[8,72,256]{2,1,0:T(8,128)(2,1)}, bf16[8,72,256]{2,1,0:T(8,128)(2,1)}) custom-call(bf16[512,1024]{1,0:T(8,128)(2,1)} %turn.1.flat_t, bf16[4,128,512]{2,1,0:T(8,128)(2,1)} %copy-done.2, bf16[4,128,512]{2,1,0:T(8,128)(2,1)} %copy-done.10, ...), custom_call_target="tpu_custom_call" | custom-call | tf_op jit(solution)/shard_map/near_grad/pallas_call | solution.py:47
  123.3 2.9 %collective-permute-start.12 = (bf16[8,72,256]{2,1,0:T(8,128)(2,1)}, bf16[8,72,256]{2,1,0:T(8,128)(2,1)S(1)}, u32[]{:S(2)}, u32[]{:S(2)}) collective-permute-start(bf16[8,72,256]{2,1,0:T(8,128)(2,1)} %get-tuple-element.42), channel_id=1, source_target_pairs={{0,3},{1,0},{2,1},{3,2},{4,7},{5,4},{6,5},{7,6},{8,11},{9,8},{10,9... | collective-permute-start | bytes 884744 | tf_op jit(solution)/shard_map/ppermute | solution.py:297
  126.2 7.5 %collective-permute-done.13 = bf16[8,72,256]{2,1,0:T(8,128)(2,1)S(1)} collective-permute-done((bf16[8,72,256]{2,1,0:T(8,128)(2,1)}, bf16[8,72,256]{2,1,0:T(8,128)(2,1)S(1)}, u32[]{:S(2)}, u32[]{:S(2)}) %collective-permute-start.13) | collective-permute-done | bytes 294944 | tf_op jit(solution)/shard_map/ppermute | solution.py:294
  133.7 1.0 add_convert_fusion.1
  134.9 7.9 %collective-permute-done.14 = bf16[8,72,256]{2,1,0:T(8,128)(2,1)S(1)} collective-permute-done((bf16[8,72,256]{2,1,0:T(8,128)(2,1)S(1)}, bf16[8,72,256]{2,1,0:T(8,128)(2,1)S(1)}, u32[]{:S(2)}, u32[]{:S(2)}) %collective-permute-start.14) | collective-permute-done | bytes 294944 | tf_op jit(solution)/shard_map/ppermute | solution.py:294
  142.8 1.1 add_convert_fusion
  143.9 13.5 %all_to_all.21 = bf16[8,72,256]{2,1,0:T(8,128)(2,1)S(1)} all-to-all(bf16[8,72,256]{2,1,0:T(8,128)(2,1)S(1)} %add_convert_fusion), channel_id=1, replica_groups={{0,4,8,12,16,20,24,28},{1,5,9,13,17,21,25,29},{2,6,10,14,18,22,26,30},{..., dimensions={0} | all-to-all | bytes 589824 | tf_op jit(solution)/shard_map/all_to_all | solution.py:55
  157.4 13.2 %all_to_all.22.b0 = bf16[8,72,256]{2,1,0:T(8,128)(2,1)S(1)} all-to-all(bf16[8,72,256]{2,1,0:T(8,128)(2,1)S(1)} %broadcast_in_dim.10), channel_id=1, replica_groups={{0,4,8,12,16,20,24,28},{1,5,9,13,17,21,25,29},{2,6,10,14,18,22,26,30},{..., dimensions={0} | all-to-all | bytes 589824 | tf_op jit(solution)/shard_map/all_to_all | solution.py:55
  170.7 3.2 %collective-permute-start.16 = (bf16[8,72,256]{2,1,0:T(8,128)(2,1)S(1)}, bf16[8,72,256]{2,1,0:T(8,128)(2,1)S(1)}, u32[]{:S(2)}, u32[]{:S(2)}) collective-permute-start(bf16[8,72,256]{2,1,0:T(8,128)(2,1)S(1)} %all_to_all.22.b0), channel_id=1, source_target_pairs={{0,3},{1,0},{2,1},{3,2},{4,7},{5,4},{6,5},{7,6},{8,11},{9,8},{10,9... | collective-permute-start | bytes 884744 | tf_op jit(solution)/shard_map/ppermute | solution.py:297
  173.9 4.7 %collective-permute-done.15.b1 = bf16[8,72,256]{2,1,0:T(8,128)(2,1)S(1)} collective-permute-done((bf16[8,72,256]{2,1,0:T(8,128)(2,1)S(1)}, bf16[8,72,256]{2,1,0:T(8,128)(2,1)S(1)}, u32[]{:S(2)}, u32[]{:S(2)}) %collective-permute-start.15) | collective-permute-done | bytes 294944 | tf_op jit(solution)/shard_map/ppermute | solution.py:294
  178.6 2.2 %collective-permute-done.16.b2 = bf16[8,72,256]{2,1,0:T(8,128)(2,1)S(1)} collective-permute-done((bf16[8,72,256]{2,1,0:T(8,128)(2,1)S(1)}, bf16[8,72,256]{2,1,0:T(8,128)(2,1)S(1)}, u32[]{:S(2)}, u32[]{:S(2)}) %collective-permute-start.16) | collective-permute-done | bytes 294944 | tf_op jit(solution)/shard_map/ppermute | solution.py:297
  180.8 5.8 %collective-permute-done.17.b3 = bf16[8,72,256]{2,1,0:T(8,128)(2,1)S(1)} collective-permute-done((bf16[8,72,256]{2,1,0:T(8,128)(2,1)S(1)}, bf16[8,72,256]{2,1,0:T(8,128)(2,1)S(1)}, u32[]{:S(2)}, u32[]{:S(2)}) %collective-permute-start.17) | collective-permute-done | bytes 294944 | tf_op jit(solution)/shard_map/ppermute | solution.py:294
  187.3 1.9 chunk.1
  189.2 3.2 %collective-permute-start.19 = (bf16[128,512]{1,0:T(8,128)(2,1)}, bf16[128,512]{1,0:T(8,128)(2,1)S(1)}, u32[]{:S(2)}, u32[]{:S(2)}) collective-permute-start(bf16[128,512]{1,0:T(8,128)(2,1)} %chunk.1), channel_id=1, source_target_pairs={{0,192},{32,96},{64,0},{96,160},{128,64},{160,224},{192,128},{224,... | collective-permute-start | bytes 393224 | tf_op jit(solution)/shard_map/ppermute | solution.py:288
  192.4 3.2 %collective-permute-done.18 = bf16[128,512]{1,0:T(8,128)(2,1)S(1)} collective-permute-done((bf16[128,512]{1,0:T(8,128)(2,1)}, bf16[128,512]{1,0:T(8,128)(2,1)S(1)}, u32[]{:S(2)}, u32[]{:S(2)}) %collective-permute-start.18) | collective-permute-done | bytes 131104 | tf_op jit(solution)/shard_map/ppermute | solution.py:285
  195.6 6.2 %collective-permute-done.20 = bf16[128,512]{1,0:T(8,128)(2,1)S(1)} collective-permute-done((bf16[128,512]{1,0:T(8,128)(2,1)S(1)}, bf16[128,512]{1,0:T(8,128)(2,1)S(1)}, u32[]{:S(2)}, u32[]{:S(2)}) %collective-permute-start.20) | collective-permute-done | bytes 131104 | tf_op jit(solution)/shard_map/ppermute | solution.py:285
  201.7 1.0 pad_maximum_fusion.1.held
  202.8 2.8 %out.1 = bf16[128,512]{1,0:T(8,128)(2,1)} custom-call(bf16[512,512]{1,0:T(8,128)(2,1)} %bitcast.39, bf16[128,512]{1,0:T(8,128)(2,1)} %get-tuple-element.33.hidden, f32[128,128]{1,0:T(8,128)} %get-tuple-element.24.inv, bf16[256,512]{1,0:T(8,128)(2,1)} %get-tuple-element.29.take, bf16[128,128]{1,0:T(8,128)(2,1)} %get-tuple-element.30.own, bf16[1024,512]{1,0:T(8,128)(2,1)} %w_two.3), custom_call_target="tpu_custom_call" | custom-call | tf_op jit(solution)/shard_map/out/pallas_call | solution.py:47
  205.6 2.7 %spread.1 = f32[512,1024]{1,0:T(8,128)} custom-call(bf16[8,72,256]{2,1,0:T(8,128)(2,1)} %copy-done.1, bf16[8,72,256]{2,1,0:T(8,128)(2,1)} %copy-done.4, bf16[8,72,256]{2,1,0:T(8,128)(2,1)} %copy-done.5, bf16[8,72,256]{2,1,0:T(8,128)(2,1)} %copy-done.6), custom_call_target="tpu_custom_call" | custom-call | tf_op jit(solution)/shard_map/spread/pallas_call | solution.py:47
  209.1 2.7 %join.1 = f32[1024,512]{1,0:T(8,128)} custom-call(bf16[4,128,512]{2,1,0:T(8,128)(2,1)} %copy-done.3, bf16[4,128,512]{2,1,0:T(8,128)(2,1)} %copy-done.9), custom_call_target="tpu_custom_call" | custom-call | tf_op jit(solution)/shard_map/join/pallas_call | solution.py:47
  (68 shorter events, 8.7 us)
Async XLA Ops:
  3.9 3.2 %collective-permute-start = (bf16[4,128,1024]{2,1,0:T(8,128)(2,1)}, bf16[4,128,1024]{2,1,0:T(8,128)(2,1)S(1)}, u32[]{:S(2)}, u32[]{:S(2)}) collective-permute-start(bf16[4,128,1024]{2,1,0:T(8,128)(2,1)} %project.3), channel_id=1, source_target_pairs={{0,32},{32,0},{64,96},{96,64},{128,160},{160,128},{192,224},{224,1... | collective-permute-start | bytes 3145736 | tf_op jit(solution)/shard_map/ppermute | solution.py:291
  7.1 13.9 %copy-start.15 = (s32[1,128,10]{1,0,2:T(1,128)S(1)}, s32[1,128,10]{1,0,2:T(1,128)}, u32[]{:S(2)}) copy-start(s32[1,128,10]{1,0,2:T(1,128)} %param.10) | copy-start | bytes 15364
  8.3 8.1 %collective-permute-start.2 = (bf16[128,1024]{1,0:T(8,128)(2,1)S(1)}, bf16[128,1024]{1,0:T(8,128)(2,1)S(1)}, u32[]{:S(2)}, u32[]{:S(2)}) collective-permute-start(bf16[128,1024]{1,0:T(8,128)(2,1)S(1)} %get-tuple-element.45), channel_id=1, source_target_pairs={{0,64},{32,224},{64,128},{96,32},{128,192},{160,96},{192,0},{224,1... | collective-permute-start | bytes 786440 | tf_op jit(solution)/shard_map/ppermute | solution.py:285
  10.0 14.4 %collective-permute-start.1 = (bf16[128,1024]{1,0:T(8,128)(2,1)S(1)}, bf16[128,1024]{1,0:T(8,128)(2,1)S(1)}, u32[]{:S(2)}, u32[]{:S(2)}) collective-permute-start(bf16[128,1024]{1,0:T(8,128)(2,1)S(1)} %get-tuple-element.46), channel_id=1, source_target_pairs={{0,192},{32,96},{64,0},{96,160},{128,64},{160,224},{192,128},{224,... | collective-permute-start | bytes 786440 | tf_op jit(solution)/shard_map/ppermute | solution.py:288
  17.5 8.6 %collective-permute-start.3 = (bf16[128,1024]{1,0:T(8,128)(2,1)S(1)}, bf16[128,1024]{1,0:T(8,128)(2,1)S(1)}, u32[]{:S(2)}, u32[]{:S(2)}) collective-permute-start(bf16[128,1024]{1,0:T(8,128)(2,1)S(1)} %fusion), channel_id=1, source_target_pairs={{0,64},{32,224},{64,128},{96,32},{128,192},{160,96},{192,0},{224,1... | collective-permute-start | bytes 786440 | tf_op jit(solution)/shard_map/ppermute | solution.py:285
  24.4 1.7 copy-start.13
  26.1 0.7 copy-start.14
  62.5 22.5 %copy-start.12 = (bf16[2,128,512]{2,1,0:T(8,128)(2,1)S(1)}, bf16[2,128,512]{2,1,0:T(8,128)(2,1)}, u32[]{:S(2)}) copy-start(bf16[2,128,512]{2,1,0:T(8,128)(2,1)} %get-tuple-element.38) | copy-start | bytes 786436
  62.5 12.3 %collective-permute-start.7 = (bf16[3,128,512]{2,1,0:T(8,128)(2,1)}, bf16[3,128,512]{2,1,0:T(8,128)(2,1)S(1)}, u32[]{:S(2)}, u32[]{:S(2)}) collective-permute-start(bf16[3,128,512]{2,1,0:T(8,128)(2,1)} %get-tuple-element.35), channel_id=1, source_target_pairs={{0,64},{32,224},{64,128},{96,32},{128,192},{160,96},{192,0},{224,1... | collective-permute-start | bytes 1179656 | tf_op jit(solution)/shard_map/ppermute | solution.py:285
  62.6 19.6 %collective-permute-start.8 = (bf16[3,128,512]{2,1,0:T(8,128)(2,1)}, bf16[3,128,512]{2,1,0:T(8,128)(2,1)S(1)}, u32[]{:S(2)}, u32[]{:S(2)}) collective-permute-start(bf16[3,128,512]{2,1,0:T(8,128)(2,1)} %get-tuple-element.36), channel_id=1, source_target_pairs={{0,192},{32,96},{64,0},{96,160},{128,64},{160,224},{192,128},{224,... | collective-permute-start | bytes 1179656 | tf_op jit(solution)/shard_map/ppermute | solution.py:288
  76.0 9.1 %collective-permute-start.9 = (bf16[3,128,512]{2,1,0:T(8,128)(2,1)S(1)}, bf16[3,128,512]{2,1,0:T(8,128)(2,1)S(1)}, u32[]{:S(2)}, u32[]{:S(2)}) collective-permute-start(bf16[3,128,512]{2,1,0:T(8,128)(2,1)S(1)} %pad_maximum_fusion.2), channel_id=1, source_target_pairs={{0,64},{32,224},{64,128},{96,32},{128,192},{160,96},{192,0},{224,1... | collective-permute-start | bytes 1179656 | tf_op jit(solution)/shard_map/ppermute | solution.py:285
  76.0 20.5 %all-to-all-start.1 = ((bf16[32,16,512]{2,1,0:T(8,128)(2,1)}), bf16[32,16,512]{2,1,0:T(8,128)(2,1)S(1)}, u32[]{:S(2)}, u32[]{:S(2)}) async-start(bf16[32,16,512]{2,1,0:T(8,128)(2,1)} %bitcast.11), calls=%async_computation.1 | async-start | bytes 1048576 | tf_op jit(solution)/shard_map/all_to_all | solution.py:55
  85.2 27.0 %copy-start.8 = (bf16[5,128,512]{2,1,0:T(8,128)(2,1)}, bf16[5,128,512]{2,1,0:T(8,128)(2,1)S(1)}, u32[]{:S(2)}) copy-start(bf16[5,128,512]{2,1,0:T(8,128)(2,1)S(1)} %fusion.3.held) | copy-start | bytes 1966084
  85.2 26.9 %collective-permute-start.10 = (bf16[5,128,512]{2,1,0:T(8,128)(2,1)S(1)}, bf16[5,128,512]{2,1,0:T(8,128)(2,1)S(1)}, u32[]{:S(2)}, u32[]{:S(2)}) collective-permute-start(bf16[5,128,512]{2,1,0:T(8,128)(2,1)S(1)} %fusion.3.held), channel_id=1, source_target_pairs={{0,32},{32,0},{64,96},{96,64},{128,160},{160,128},{192,224},{224,1... | collective-permute-start | bytes 1966088 | tf_op jit(solution)/shard_map/ppermute | solution.py:291
  96.6 0.8 copy-start
  99.5 12.6 %copy-start.11 = (bf16[128,512]{1,0:T(8,128)(2,1)S(1)}, bf16[128,512]{1,0:T(8,128)(2,1)}, u32[]{:S(2)}) copy-start(bf16[128,512]{1,0:T(8,128)(2,1)} %near.1) | copy-start | bytes 393220
  99.5 6.4 %collective-permute-start.4 = (bf16[128,512]{1,0:T(8,128)(2,1)}, bf16[128,512]{1,0:T(8,128)(2,1)S(1)}, u32[]{:S(2)}, u32[]{:S(2)}) collective-permute-start(bf16[128,512]{1,0:T(8,128)(2,1)} %near.1), channel_id=1, source_target_pairs={{0,64},{32,224},{64,128},{96,32},{128,192},{160,96},{192,0},{224,1... | collective-permute-start | bytes 393224 | tf_op jit(solution)/shard_map/ppermute | solution.py:285
  100.3 8.1 %collective-permute-start.5 = (bf16[128,512]{1,0:T(8,128)(2,1)}, bf16[128,512]{1,0:T(8,128)(2,1)S(1)}, u32[]{:S(2)}, u32[]{:S(2)}) collective-permute-start(bf16[128,512]{1,0:T(8,128)(2,1)} %near.1), channel_id=1, source_target_pairs={{0,192},{32,96},{64,0},{96,160},{128,64},{160,224},{192,128},{224,... | collective-permute-start | bytes 393224 | tf_op jit(solution)/shard_map/ppermute | solution.py:288
  105.9 6.2 %collective-permute-start.6 = (bf16[128,512]{1,0:T(8,128)(2,1)S(1)}, bf16[128,512]{1,0:T(8,128)(2,1)S(1)}, u32[]{:S(2)}, u32[]{:S(2)}) collective-permute-start(bf16[128,512]{1,0:T(8,128)(2,1)S(1)} %collective-permute-done.4), channel_id=1, source_target_pairs={{0,64},{32,224},{64,128},{96,32},{128,192},{160,96},{192,0},{224,1... | collective-permute-start | bytes 393224 | tf_op jit(solution)/shard_map/ppermute | solution.py:285
  112.1 6.4 %copy-start.2 = (bf16[4,128,512]{2,1,0:T(8,128)(2,1)}, bf16[4,128,512]{2,1,0:T(8,128)(2,1)S(1)}, u32[]{:S(2)}) copy-start(bf16[4,128,512]{2,1,0:T(8,128)(2,1)S(1)} %pad_maximum_fusion.held) | copy-start | bytes 1572868
  112.1 0.9 copy-start.7
  116.2 2.3 %collective-permute-start.11 = (bf16[4,128,512]{2,1,0:T(8,128)(2,1)S(1)}, bf16[4,128,512]{2,1,0:T(8,128)(2,1)S(1)}, u32[]{:S(2)}, u32[]{:S(2)}) collective-permute-start(bf16[4,128,512]{2,1,0:T(8,128)(2,1)S(1)} %pad_maximum_fusion.held), channel_id=1, source_target_pairs={{0,32},{32,0},{64,96},{96,64},{128,160},{160,128},{192,224},{224,1... | collective-permute-start | bytes 1572872 | tf_op jit(solution)/shard_map/ppermute | solution.py:291
  118.5 0.8 copy-start.10
  123.0 10.7 %collective-permute-start.13 = (bf16[8,72,256]{2,1,0:T(8,128)(2,1)}, bf16[8,72,256]{2,1,0:T(8,128)(2,1)S(1)}, u32[]{:S(2)}, u32[]{:S(2)}) collective-permute-start(bf16[8,72,256]{2,1,0:T(8,128)(2,1)} %get-tuple-element.44), channel_id=1, source_target_pairs={{0,1},{1,2},{2,3},{3,0},{4,5},{5,6},{6,7},{7,4},{8,9},{9,10},{10,1... | collective-permute-start | bytes 884744 | tf_op jit(solution)/shard_map/ppermute | solution.py:294
  123.3 11.5 %collective-permute-start.12 = (bf16[8,72,256]{2,1,0:T(8,128)(2,1)}, bf16[8,72,256]{2,1,0:T(8,128)(2,1)S(1)}, u32[]{:S(2)}, u32[]{:S(2)}) collective-permute-start(bf16[8,72,256]{2,1,0:T(8,128)(2,1)} %get-tuple-element.42), channel_id=1, source_target_pairs={{0,3},{1,0},{2,1},{3,2},{4,7},{5,4},{6,5},{7,6},{8,11},{9,8},{10,9... | collective-permute-start | bytes 884744 | tf_op jit(solution)/shard_map/ppermute | solution.py:297
  134.8 8.0 %collective-permute-start.14 = (bf16[8,72,256]{2,1,0:T(8,128)(2,1)S(1)}, bf16[8,72,256]{2,1,0:T(8,128)(2,1)S(1)}, u32[]{:S(2)}, u32[]{:S(2)}) collective-permute-start(bf16[8,72,256]{2,1,0:T(8,128)(2,1)S(1)} %add_convert_fusion.1), channel_id=1, source_target_pairs={{0,1},{1,2},{2,3},{3,0},{4,5},{5,6},{6,7},{7,4},{8,9},{9,10},{10,1... | collective-permute-start | bytes 884744 | tf_op jit(solution)/shard_map/ppermute | solution.py:294
  170.7 15.9 %copy-start.1 = (bf16[8,72,256]{2,1,0:T(8,128)(2,1)}, bf16[8,72,256]{2,1,0:T(8,128)(2,1)S(1)}, u32[]{:S(2)}) copy-start(bf16[8,72,256]{2,1,0:T(8,128)(2,1)S(1)} %all_to_all.22.b0) | copy-start | bytes 884740
  170.7 7.9 %collective-permute-start.15 = (bf16[8,72,256]{2,1,0:T(8,128)(2,1)S(1)}, bf16[8,72,256]{2,1,0:T(8,128)(2,1)S(1)}, u32[]{:S(2)}, u32[]{:S(2)}) collective-permute-start(bf16[8,72,256]{2,1,0:T(8,128)(2,1)S(1)} %all_to_all.22.b0), channel_id=1, source_target_pairs={{0,1},{1,2},{2,3},{3,0},{4,5},{5,6},{6,7},{7,4},{8,9},{9,10},{10,1... | collective-permute-start | bytes 884744 | tf_op jit(solution)/shard_map/ppermute | solution.py:294
  170.7 10.1 %collective-permute-start.16 = (bf16[8,72,256]{2,1,0:T(8,128)(2,1)S(1)}, bf16[8,72,256]{2,1,0:T(8,128)(2,1)S(1)}, u32[]{:S(2)}, u32[]{:S(2)}) collective-permute-start(bf16[8,72,256]{2,1,0:T(8,128)(2,1)S(1)} %all_to_all.22.b0), channel_id=1, source_target_pairs={{0,3},{1,0},{2,1},{3,2},{4,7},{5,4},{6,5},{7,6},{8,11},{9,8},{10,9... | collective-permute-start | bytes 884744 | tf_op jit(solution)/shard_map/ppermute | solution.py:297
  178.6 7.9 %copy-start.4 = (bf16[8,72,256]{2,1,0:T(8,128)(2,1)}, bf16[8,72,256]{2,1,0:T(8,128)(2,1)S(1)}, u32[]{:S(2)}) copy-start(bf16[8,72,256]{2,1,0:T(8,128)(2,1)S(1)} %collective-permute-done.15.b1) | copy-start | bytes 884740
  178.6 7.9 %collective-permute-start.17 = (bf16[8,72,256]{2,1,0:T(8,128)(2,1)S(1)}, bf16[8,72,256]{2,1,0:T(8,128)(2,1)S(1)}, u32[]{:S(2)}, u32[]{:S(2)}) collective-permute-start(bf16[8,72,256]{2,1,0:T(8,128)(2,1)S(1)} %collective-permute-done.15.b1), channel_id=1, source_target_pairs={{0,1},{1,2},{2,3},{3,0},{4,5},{5,6},{6,7},{7,4},{8,9},{9,10},{10,1... | collective-permute-start | bytes 884744 | tf_op jit(solution)/shard_map/ppermute | solution.py:294
  180.8 5.8 %copy-start.5 = (bf16[8,72,256]{2,1,0:T(8,128)(2,1)}, bf16[8,72,256]{2,1,0:T(8,128)(2,1)S(1)}, u32[]{:S(2)}) copy-start(bf16[8,72,256]{2,1,0:T(8,128)(2,1)S(1)} %collective-permute-done.16.b2) | copy-start | bytes 884740
  186.5 0.7 copy-start.6
  189.2 6.4 %collective-permute-start.18 = (bf16[128,512]{1,0:T(8,128)(2,1)}, bf16[128,512]{1,0:T(8,128)(2,1)S(1)}, u32[]{:S(2)}, u32[]{:S(2)}) collective-permute-start(bf16[128,512]{1,0:T(8,128)(2,1)} %chunk.1), channel_id=1, source_target_pairs={{0,64},{32,224},{64,128},{96,32},{128,192},{160,96},{192,0},{224,1... | collective-permute-start | bytes 393224 | tf_op jit(solution)/shard_map/ppermute | solution.py:285
  189.2 6.4 %collective-permute-start.19 = (bf16[128,512]{1,0:T(8,128)(2,1)}, bf16[128,512]{1,0:T(8,128)(2,1)S(1)}, u32[]{:S(2)}, u32[]{:S(2)}) collective-permute-start(bf16[128,512]{1,0:T(8,128)(2,1)} %chunk.1), channel_id=1, source_target_pairs={{0,192},{32,96},{64,0},{96,160},{128,64},{160,224},{192,128},{224,... | collective-permute-start | bytes 393224 | tf_op jit(solution)/shard_map/ppermute | solution.py:288
  195.6 6.2 %collective-permute-start.20 = (bf16[128,512]{1,0:T(8,128)(2,1)S(1)}, bf16[128,512]{1,0:T(8,128)(2,1)S(1)}, u32[]{:S(2)}, u32[]{:S(2)}) collective-permute-start(bf16[128,512]{1,0:T(8,128)(2,1)S(1)} %collective-permute-done.18), channel_id=1, source_target_pairs={{0,64},{32,224},{64,128},{96,32},{128,192},{160,96},{192,0},{224,1... | collective-permute-start | bytes 393224 | tf_op jit(solution)/shard_map/ppermute | solution.py:285
  202.7 5.6 %copy-start.3 = (bf16[4,128,512]{2,1,0:T(8,128)(2,1)}, bf16[4,128,512]{2,1,0:T(8,128)(2,1)S(1)}, u32[]{:S(2)}) copy-start(bf16[4,128,512]{2,1,0:T(8,128)(2,1)S(1)} %pad_maximum_fusion.1.held) | copy-start | bytes 1572868
  202.7 5.6 %collective-permute-start.21 = (bf16[4,128,512]{2,1,0:T(8,128)(2,1)S(1)}, bf16[4,128,512]{2,1,0:T(8,128)(2,1)S(1)}, u32[]{:S(2)}, u32[]{:S(2)}) collective-permute-start(bf16[4,128,512]{2,1,0:T(8,128)(2,1)S(1)} %pad_maximum_fusion.1.held), channel_id=1, source_target_pairs={{0,32},{32,0},{64,96},{96,64},{128,160},{160,128},{192,224},{224,1... | collective-permute-start | bytes 1572872 | tf_op jit(solution)/shard_map/ppermute | solution.py:291
  208.4 0.8 copy-start.9

commit v5 on v4

--- a/solution.py
+++ b/solution.py
@@ -145,7 +145,7 @@
 
 def forward_body(part, got, near, far, grads, inv, give, p_self, p_near, boxes):
     width = grads.shape[1]
-    total = add(part[...], got[...], near[...], far[...])
+    total = add(part[0], got[0], near[...], far[...])
     p_self[...] = total[:, :width]
     mine = total[:, width:].astype(BF16)
     p_near[...] = mine
@@ -198,47 +198,36 @@
     out[...] = (mm(hidden[...], w_two[:width, :]) + mm(agg, w_two[width:, :])).astype(BF16)
 
 
-def grad_of(flat_t, held, other, stack):
-    for k, g in enumerate(places(GET_MINE, False)):
-        stack[g] = held[k]
-    for k, g in enumerate(places(GET_OTHER, True)):
-        stack[g] = other[k]
-    groups, nodes, width = stack.shape
-    return mm(flat_t[...], stack[...].reshape(groups * nodes, width)).astype(BF16)
-
-
-def self_body(flat_t, held, other, out, stack):
-    out[...] = grad_of(flat_t, held, other, stack)
-
-
-def near_grad_body(
-    flat_t, held, other, first, two_mine, two_other, ahead, behind, third, own, stack, boxes
-):
-    width = first.shape[1]
+def grad_body(flat_t, held, other, two, ahead, behind, third, own, stack, boxes):
+    groups, nodes, both = stack.shape
+    width = both // 2
     chips, deep, rows, cut = boxes.shape
-    block = first.shape[0] // chips
+    block = flat_t.shape[0] // chips
     part = block // deep
-    sides = (first[...], grad_of(flat_t, held, other, stack))
-    two = add(two_mine[...], two_other[...]).astype(BF16)
+    ids = places(GET_MINE, False) + places(GET_OTHER, True)
+    for k, g in enumerate(ids):
+        source = held if k < chips else other
+        stack[g, :, :width] = source[k % chips]
+        stack[g, :, width:] = source[chips + k % chips]
+    total = mm(flat_t[...], stack[...].reshape(groups * nodes, both)).astype(BF16)
+    twos = add(two[...], other[2 * chips]).astype(BF16)
     tail = rows - 4 * part
     slab = deep * tail
     for x in range(chips):
         for q in range(4):
-            at = q % 2 * cut
-            piece = sides[q // 2][x * block : (x + 1) * block, at : at + cut]
+            piece = total[x * block : (x + 1) * block, q * cut : (q + 1) * cut]
             boxes[x, :, q * part : (q + 1) * part, :] = piece.reshape(deep, part, cut)
-        piece = two[x % 2 * slab : (x % 2 + 1) * slab, x // 2 * cut : (x // 2 + 1) * cut]
+        piece = twos[x % 2 * slab : (x % 2 + 1) * slab, x // 2 * cut : (x // 2 + 1) * cut]
         boxes[x, :, 4 * part :, :] = piece.reshape(deep, tail, cut)
     for x, target in zip(places_x(SUM_MINE), (ahead, behind, third, own)):
         target[...] = boxes[x]
 
 
 def chunk_body(b0, b1, b2, b3, out, scratch):
-    deep, rows, cut = b0.shape
+    deep, tail, cut = b0.shape
     chips, slab, _ = scratch.shape
-    tail = slab // deep
     for x, block in zip(places_x(GET_MINE), (b0, b1, b2, b3)):
-        scratch[x] = block[:, rows - tail :, :].reshape(slab, cut)
+        scratch[x] = block[...].reshape(slab, cut)
     for x in range(chips):
         at = x % 2 * slab
         out[at : at + slab, x // 2 * cut : (x // 2 + 1) * cut] = scratch[x]
@@ -318,14 +307,26 @@
     flat_t = whole("turn", turn_body, shape((cols, groups * nodes)), features)
     relay = forward(add(mine[0], got[0]).astype(BF16))
     near = backward(add(mine[1], got[1]).astype(BF16))
+    relay, give = lax.optimization_barrier((relay, give))
     far = forward(add(mine[2], got[2], relay).astype(BF16))
+    far, flat_t = lax.optimization_barrier((far, flat_t))
     block = shape((nodes, width))
-    p_self, p_near, boxes = whole(
-        "forward",
+
+    def full(*dims):
+        return pl.BlockSpec(dims, lambda i: (0,) * len(dims))
+
+    last = pl.BlockSpec((1, nodes, 2 * width), lambda i: (CHIPS - 1, 0, 0))
+    p_self, p_near, boxes = pl.pallas_call(
         forward_body,
-        (shape((nodes, width), F32), block, shape((span, width))),
-        mine[3], got[3], near, far, grads, inv, give,
-    )
+        out_shape=(shape((nodes, width), F32), block, shape((span, width))),
+        grid=(1,),
+        in_specs=[
+            last, last, full(nodes, 2 * width), full(nodes, 2 * width), full(nodes, width),
+            full(nodes, nodes), full(span, 2 * nodes),
+        ],
+        out_specs=(full(nodes, width), full(nodes, width), full(span, width)),
+        name="forward",
+    )(mine, got, near, far, grads, inv, give)
     recv = trade(boxes.reshape(parts, 2 * kmax, width)).reshape(span, width)
     rows = 2 * width // groups
     boxes, near_local, hidden, ahead, behind, third, mine = whole(
@@ -347,42 +348,51 @@
 
     relay = forward(ahead)
     near = backward(behind)
-    far = forward(jnp.concatenate([relay[:1], add(third, relay[1:]).astype(BF16)]))
-    sums = add(mine, near[1:], far[1:])
-    held = jnp.stack([ahead[0], relay[0], near[0], far[0], sums[0].astype(BF16)])
+    passed = add(third, relay[1:]).astype(BF16)
+    d_near = whole("near", near_body, block, recv, near_local, take)
+    message = jnp.concatenate([d_near[None], relay[:1], passed])
+    far = forward(message)
+    back = backward(d_near)
+    last = forward(far[0])
+    sums = add(mine, near[1:], far[2:])
+    held = jnp.stack(
+        [ahead[0], relay[0], near[0], far[1], d_near, far[0], back, last, sums[0].astype(BF16)]
+    )
     other = swap(held)
-    stack = pltpu.VMEM((groups, nodes, width), BF16)
-    first = whole("self_grad", self_body, shape((cols, width)), flat_t, held, other, scratch=[stack])
-    two_mine, two_other = sums[1], other[4]
-
-    d_near = whole("near", near_body, block, recv, near_local, take)
-    held, first = lax.optimization_barrier((gather(d_near), first))
-    other = swap(held)
-    out = whole("out", out_body, block, recv, hidden, inv, take, own, w_two)
 
     lot = shape((deep, 9 * cols // parts // 2, width // 2))
     ahead, behind, third, mine = whole(
-        "near_grad",
-        near_grad_body,
+        "grad",
+        grad_body,
         (lot, lot, lot, lot),
-        flat_t, held, other, first, two_mine, two_other,
-        scratch=[stack, pltpu.VMEM((CHIPS, *lot.shape), BF16)],
-    )
+        flat_t, held, other, sums[1],
+        scratch=[
+            pltpu.VMEM((groups, nodes, 2 * width), BF16),
+            pltpu.VMEM((CHIPS, *lot.shape), BF16),
+        ],
+    )
+    out = whole("out", out_body, block, recv, hidden, inv, take, own, w_two)
     relay = x_forward(ahead)
     near = x_backward(behind)
     far = x_forward(add(third, relay).astype(BF16))
+    far, out = lax.optimization_barrier((far, out))
     terms = trade(add(mine, near, far).astype(BF16), lines)
     total = (jnp.sum(terms.astype(F32), axis=0) * scale).astype(BF16)
     total = trade(jnp.broadcast_to(total[None], terms.shape), lines)
-    relay = x_forward(total)
-    near = x_backward(total)
-    lots = (total, relay, near, x_forward(relay))
+
+    def x_gather(lot):
+        one = x_forward(lot)
+        return lot, one, x_backward(lot), x_forward(one)
+
     slab = 2 * width // groups // 2
+    twos = x_gather(total[:, 8 * lot.shape[1] // 9 :, :])
+    ones = x_gather(total)
     chunk = whole(
-        "chunk", chunk_body, block, *lots, scratch=[pltpu.VMEM((CHIPS, slab, width // 2), BF16)]
+        "chunk", chunk_body, block, *twos, scratch=[pltpu.VMEM((CHIPS, slab, width // 2), BF16)]
     )
     held = gather(chunk)
-    one = whole("spread", spread_body, shape((cols, 2 * width), F32), *lots)
+    one = whole("spread", spread_body, shape((cols, 2 * width), F32), *ones)
+    held, one = lax.optimization_barrier((held, one))
     two = whole("join", join_body, shape((2 * width, width), F32), held, swap(held))
     return out[None], one, two
 

time: 216 us -> 208 us (0.963)
  waiting for transfers between devices: 73 us -> 66.2 us
  blocking collectives: 55.7 us -> 59.5 us
  local copies, waits for them, and re-layouts: 11 us -> 8.02 us
  Pallas kernels: 36.8 us -> 34 us
  starting transfers between devices: 27.8 us -> 30.1 us
    all_to_all x1, waiting for transfers between devices: 11.3 us -> 5.28 us  [trade(): lax.all_to_all(boxes, 'dom', split_axis=0, concat_axis=0, axis_index_grou...]
    pallas_call x13 -> x11, Pallas kernels: 36.8 us -> 31.3 us  [whole(): pl.pallas_call(body, out_shape=outs, scratch_shapes=scratch, name=name)]
    ppermute x4 -> x3, waiting for transfers between devices: 0.01 us -> 3.95 us  [swap(): return lax.ppermute(block, 'feat', SWAP)]
    squeeze x4 -> x2, local copies, waits for them, and re-layouts: 4.68 us -> 0.81 us  [the longest x1 0.79 us: on_device(): sums[1]]
    all_to_all x3, blocking collectives: 55.7 us -> 59.5 us  [trade(): lax.all_to_all(boxes, 'dom', split_axis=0, concat_axis=0, axis_index_grou...]
    ppermute x4 -> x6, waiting for transfers between devices: 25.9 us -> 22.6 us  [x_forward(): return lax.ppermute(block, ('feat', 'dom'), x_ahead)]
    pallas_call x0 -> x1, Pallas kernels: none -> 2.61 us  [on_device(): pl.pallas_call(forward_body, out_shape=(shape((nodes, width), F32), block...]
    ppermute x2 -> x3, waiting for transfers between devices: 2.18 us -> 0.01 us  [x_backward(): return lax.ppermute(block, ('feat', 'dom'), x_behind)]
  transfers between devices with their start and end apart: 23 -> 24, of which waited for: 14 -> 15; matrix products, arithmetic and copies ran while one was open for 5% -> 2% of each run, Pallas kernels for 7% -> 7%
where the time goes in v5:
time: 208 us; the launch traced here: 205 us
  waiting for transfers between devices  66.2 us (32%)
  blocking collectives  59.5 us (29%)
  Pallas kernels  34 us (16%)
  starting transfers between devices  30.1 us (14%)
  local copies, waits for them, and re-layouts  8.02 us (4%)
  other arithmetic  6.02 us (3%)
    all_to_all x3, blocking collectives, trade(): lax.all_to_all(boxes, 'dom', split_axis=0, concat_axis=0, axis_index_grou...  59.5 us
    ppermute x7, waiting for transfers between devices, forward(): return lax.ppermute(block, 'feat', y_ahead)  32.6 us
    pallas_call x11, Pallas kernels, whole(): pl.pallas_call(body, out_shape=outs, scratch_shapes=scratch, name=name)  31.3 us
    ppermute x6, waiting for transfers between devices, x_forward(): return lax.ppermute(block, ('feat', 'dom'), x_ahead)  22.6 us
    ppermute x4, starting transfers between devices, backward(): return lax.ppermute(block, 'feat', y_behind)  12.6 us
    unnamed x49, local copies, waits for them, and re-layouts  7.15 us
    ppermute x3, starting transfers between devices, x_backward(): return lax.ppermute(block, ('feat', 'dom'), x_behind)  6.45 us
    all_to_all x1, starting transfers between devices, trade(): lax.all_to_all(boxes, 'dom', split_axis=0, concat_axis=0, axis_index_grou...  5.86 us
  transfers between devices with their start and end apart: 24, of which 15 were waited for; matrix products, arithmetic and copies ran while one was open for 2% of the time, Pallas kernels for 7%

profile of v5, /device:TPU:32, one launch (start us, length us, event | category | flops | bytes accessed | tf_op | source)
XLA Modules:
  0.0 204.8 jit_solution(10501051870811381063)
XLA Ops:
  0.6 3.2 %project.3 = bf16[4,128,1024]{2,1,0:T(8,128)(2,1)} custom-call(bf16[8,128,512]{2,1,0:T(8,128)(2,1)} %flat.1, bf16[512,1024]{1,0:T(8,128)(2,1)} %w.3), custom_call_target="tpu_custom_call" | custom-call | tf_op jit(solution)/shard_map/project/pallas_call | solution.py:47
  3.9 3.2 %project.2.part = bf16[4,128,1024]{2,1,0:T(8,128)(2,1)} custom-call(bf16[8,128,512]{2,1,0:T(8,128)(2,1)} %flat.1, bf16[512,1024]{1,0:T(8,128)(2,1)} %w.3), custom_call_target="tpu_custom_call" | custom-call | tf_op jit(solution)/shard_map/project/pallas_call | solution.py:47
  7.1 1.6 fusion.2
  8.7 1.7 collective-permute-start.1
  11.0 2.0 tables.1
  13.0 3.4 %collective-permute-done.1 = bf16[128,1024]{1,0:T(8,128)(2,1)S(1)} collective-permute-done((bf16[128,1024]{1,0:T(8,128)(2,1)S(1)}, bf16[128,1024]{1,0:T(8,128)(2,1)S(1)}, u32[]{:S(2)}, u32[]{:S(2)}) %collective-permute-start.1) | collective-permute-done | bytes 262176 | tf_op jit(solution)/shard_map/ppermute | solution.py:274
  16.4 1.1 fusion
  17.9 2.9 %collective-permute-start.3 = (bf16[128,1024]{1,0:T(8,128)(2,1)S(1)}, bf16[128,1024]{1,0:T(8,128)(2,1)S(1)}, u32[]{:S(2)}, u32[]{:S(2)}) collective-permute-start(bf16[128,1024]{1,0:T(8,128)(2,1)S(1)} %get-tuple-element.57), channel_id=1, source_target_pairs={{0,192},{32,96},{64,0},{96,160},{128,64},{160,224},{192,128},{224,... | collective-permute-start | bytes 786440 | tf_op jit(solution)/shard_map/ppermute | solution.py:277
  20.8 2.6 %turn.1.flat_t = bf16[512,1024]{1,0:T(8,128)(2,1)} custom-call(bf16[8,128,512]{2,1,0:T(8,128)(2,1)} %flat.1), custom_call_target="tpu_custom_call" | custom-call | tf_op jit(solution)/shard_map/turn/pallas_call | solution.py:47
  23.4 3.4 %collective-permute-done.2.far = bf16[128,1024]{1,0:T(8,128)(2,1)S(1)} collective-permute-done((bf16[128,1024]{1,0:T(8,128)(2,1)S(1)}, bf16[128,1024]{1,0:T(8,128)(2,1)S(1)}, u32[]{:S(2)}, u32[]{:S(2)}) %collective-permute-start.2) | collective-permute-done | bytes 262176 | tf_op jit(solution)/shard_map/ppermute | solution.py:274
  27.6 2.6 %forward.1 = (f32[128,512]{1,0:T(8,128)}, bf16[128,512]{1,0:T(8,128)(2,1)}, bf16[512,512]{1,0:T(8,128)(2,1)}) custom-call(bf16[4,128,1024]{2,1,0:T(8,128)(2,1)} %project.2.part, bf16[4,128,1024]{2,1,0:T(8,128)(2,1)} %copy-done.1, bf16[128,1024]{1,0:T(8,128)(2,1)} %copy-done.15, bf16[128,1024]{1,0:T(8,128)(2,1)} %copy-done.14, bf16[128,512]{1,0:T(8,128)(2,1)} %bitcast.43, ...), custom_call_target="tpu_custom_call" | custom-call | tf_op jit(solution)/shard_map/forward/pallas_call | solution.py:319
  30.2 29.0 %all_to_all.20 = bf16[32,16,512]{2,1,0:T(8,128)(2,1)} all-to-all(bf16[32,16,512]{2,1,0:T(8,128)(2,1)} %bitcast.41), channel_id=1, replica_groups=mesh['feat'=8,'dom'=32] {'dom'}, dimensions={0} | all-to-all | bytes 1048576 | tf_op jit(solution)/shard_map/all_to_all | solution.py:55
  59.2 4.1 %middle.1 = (bf16[512,512]{1,0:T(8,128)(2,1)}, f32[128,512]{1,0:T(8,128)}, bf16[128,512]{1,0:T(8,128)(2,1)}, bf16[3,128,512]{2,1,0:T(8,128)(2,1)}, bf16[3,128,51...) custom-call(bf16[512,512]{1,0:T(8,128)(2,1)} %bitcast.38, ...), custom_call_target="tpu_custom_call" | custom-call | tf_op jit(solution)/shard_map/middle/pallas_call | solution.py:47
  63.3 5.9 %all-to-all-start.1 = ((bf16[32,16,512]{2,1,0:T(8,128)(2,1)}), bf16[32,16,512]{2,1,0:T(8,128)(2,1)S(1)}, u32[]{:S(2)}, u32[]{:S(2)}) async-start(bf16[32,16,512]{2,1,0:T(8,128)(2,1)} %bitcast.40), calls=%async_computation.1 | async-start | bytes 1048576 | tf_op jit(solution)/shard_map/all_to_all | solution.py:55
  69.3 3.2 %collective-permute-start.5 = (bf16[3,128,512]{2,1,0:T(8,128)(2,1)}, bf16[3,128,512]{2,1,0:T(8,128)(2,1)S(1)}, u32[]{:S(2)}, u32[]{:S(2)}) collective-permute-start(bf16[3,128,512]{2,1,0:T(8,128)(2,1)} %get-tuple-element.43), channel_id=1, source_target_pairs={{0,192},{32,96},{64,0},{96,160},{128,64},{160,224},{192,128},{224,... | collective-permute-start | bytes 1179656 | tf_op jit(solution)/shard_map/ppermute | solution.py:277
  72.5 0.9 slice_dynamic-update-slice_fusion.2
  73.4 7.1 %collective-permute-done.4 = bf16[3,128,512]{2,1,0:T(8,128)(2,1)S(1)} collective-permute-done((bf16[3,128,512]{2,1,0:T(8,128)(2,1)}, bf16[3,128,512]{2,1,0:T(8,128)(2,1)S(1)}, u32[]{:S(2)}, u32[]{:S(2)}) %collective-permute-start.4) | collective-permute-done | bytes 393248 | tf_op jit(solution)/shard_map/ppermute | solution.py:274
  80.7 5.3 %all-to-all-done.1 = bf16[32,16,512]{2,1,0:T(8,128)(2,1)S(1)} async-done(((bf16[32,16,512]{2,1,0:T(8,128)(2,1)}), bf16[32,16,512]{2,1,0:T(8,128)(2,1)S(1)}, u32[]{:S(2)}, u32[]{:S(2)}) %all-to-all-start.1) | async-done | bytes 524320 | tf_op jit(solution)/shard_map/all_to_all | solution.py:55
  85.9 0.8 copy-done
  86.8 2.1 %near.1 = bf16[128,512]{1,0:T(8,128)(2,1)} custom-call(bf16[512,512]{1,0:T(8,128)(2,1)} %bitcast.36, f32[128,512]{1,0:T(8,128)} %get-tuple-element.45.near_local, bf16[256,512]{1,0:T(8,128)(2,1)} %get-tuple-element.39.take), custom_call_target="tpu_custom_call" | custom-call | tf_op jit(solution)/shard_map/near/pallas_call | solution.py:47
  88.8 1.0 pad_maximum_fusion
  90.0 3.3 %collective-permute-start.7 = (bf16[128,512]{1,0:T(8,128)(2,1)S(1)}, bf16[128,512]{1,0:T(8,128)(2,1)S(1)}, u32[]{:S(2)}, u32[]{:S(2)}) collective-permute-start(bf16[128,512]{1,0:T(8,128)(2,1)S(1)} %copy-done.6), channel_id=1, source_target_pairs={{0,192},{32,96},{64,0},{96,160},{128,64},{160,224},{192,128},{224,... | collective-permute-start | bytes 393224 | tf_op jit(solution)/shard_map/ppermute | solution.py:277
  93.3 7.1 %collective-permute-done.6 = bf16[4,128,512]{2,1,0:T(8,128)(2,1)S(1)} collective-permute-done((bf16[4,128,512]{2,1,0:T(8,128)(2,1)S(1)}, bf16[4,128,512]{2,1,0:T(8,128)(2,1)S(1)}, u32[]{:S(2)}, u32[]{:S(2)}) %collective-permute-start.6) | collective-permute-done | bytes 524320 | tf_op jit(solution)/shard_map/ppermute | solution.py:274
  100.6 6.0 %collective-permute-done.8 = bf16[128,512]{1,0:T(8,128)(2,1)S(1)} collective-permute-done((bf16[128,512]{1,0:T(8,128)(2,1)S(1)}, bf16[128,512]{1,0:T(8,128)(2,1)S(1)}, u32[]{:S(2)}, u32[]{:S(2)}) %collective-permute-start.8) | collective-permute-done | bytes 131104 | tf_op jit(solution)/shard_map/ppermute | solution.py:274
  107.8 2.0 collective-permute-done.9.other
  109.8 1.0 copy-done.5
  110.8 4.5 %grad.1 = (bf16[8,72,256]{2,1,0:T(8,128)(2,1)}, bf16[8,72,256]{2,1,0:T(8,128)(2,1)}, bf16[8,72,256]{2,1,0:T(8,128)(2,1)}, bf16[8,72,256]{2,1,0:T(8,128)(2,1)}) custom-call(bf16[512,1024]{1,0:T(8,128)(2,1)} %turn.1.flat_t, bf16[9,128,512]{2,1,0:T(8,128)(2,1)} %copy-done.3, bf16[9,128,512]{2,1,0:T(8,128)(2,1)} %copy-done.5, f32[128,512]{1,0:T(8,128)} %slice_bitcast_fusion.two), custom_call_target="tpu_custom_call" | custom-call | tf_op jit(solution)/shard_map/grad/pallas_call | solution.py:47
  115.7 7.8 %collective-permute-done.10 = bf16[8,72,256]{2,1,0:T(8,128)(2,1)S(1)} collective-permute-done((bf16[8,72,256]{2,1,0:T(8,128)(2,1)}, bf16[8,72,256]{2,1,0:T(8,128)(2,1)S(1)}, u32[]{:S(2)}, u32[]{:S(2)}) %collective-permute-start.10) | collective-permute-done | bytes 294944 | tf_op jit(solution)/shard_map/ppermute | solution.py:283
  123.4 1.0 add_convert_fusion.1
  124.6 3.2 %collective-permute-start.12 = (bf16[8,72,256]{2,1,0:T(8,128)(2,1)}, bf16[8,72,256]{2,1,0:T(8,128)(2,1)S(1)}, u32[]{:S(2)}, u32[]{:S(2)}) collective-permute-start(bf16[8,72,256]{2,1,0:T(8,128)(2,1)} %get-tuple-element.53), channel_id=1, source_target_pairs={{0,3},{1,0},{2,1},{3,2},{4,7},{5,4},{6,5},{7,6},{8,11},{9,8},{10,9... | collective-permute-start | bytes 884744 | tf_op jit(solution)/shard_map/ppermute | solution.py:286
  127.8 2.7 %out.1 = bf16[128,512]{1,0:T(8,128)(2,1)} custom-call(bf16[512,512]{1,0:T(8,128)(2,1)} %bitcast.37, bf16[128,512]{1,0:T(8,128)(2,1)} %get-tuple-element.50.hidden, f32[128,128]{1,0:T(8,128)} %get-tuple-element.34.inv, bf16[256,512]{1,0:T(8,128)(2,1)} %get-tuple-element.39.take, bf16[128,128]{1,0:T(8,128)(2,1)} %get-tuple-element.40.own, bf16[1024,512]{1,0:T(8,128)(2,1)} %w_two.3), custom_call_target="tpu_custom_call" | custom-call | tf_op jit(solution)/shard_map/out/pallas_call | solution.py:47
  130.5 4.4 %collective-permute-done.11 = bf16[8,72,256]{2,1,0:T(8,128)(2,1)S(1)} collective-permute-done((bf16[8,72,256]{2,1,0:T(8,128)(2,1)S(1)}, bf16[8,72,256]{2,1,0:T(8,128)(2,1)S(1)}, u32[]{:S(2)}, u32[]{:S(2)}) %collective-permute-start.11) | collective-permute-done | bytes 294944 | tf_op jit(solution)/shard_map/ppermute | solution.py:283
  135.1 15.4 %all_to_all.21 = bf16[8,72,256]{2,1,0:T(8,128)(2,1)S(1)} all-to-all(bf16[8,72,256]{2,1,0:T(8,128)(2,1)S(1)} %add_convert_fusion), channel_id=1, replica_groups={{0,4,8,12,16,20,24,28},{1,5,9,13,17,21,25,29},{2,6,10,14,18,22,26,30},{..., dimensions={0} | all-to-all | bytes 589824 | tf_op jit(solution)/shard_map/all_to_all | solution.py:55
  150.6 15.1 %all_to_all.22.b0 = bf16[8,72,256]{2,1,0:T(8,128)(2,1)S(1)} all-to-all(bf16[8,72,256]{2,1,0:T(8,128)(2,1)S(1)} %broadcast_in_dim.14), channel_id=1, replica_groups={{0,4,8,12,16,20,24,28},{1,5,9,13,17,21,25,29},{2,6,10,14,18,22,26,30},{..., dimensions={0} | all-to-all | bytes 589824 | tf_op jit(solution)/shard_map/all_to_all | solution.py:55
  165.9 3.2 %collective-permute-start.14 = (bf16[8,8,256]{2,1,0:T(8,128)(2,1)S(1)}, bf16[8,8,256]{2,1,0:T(8,128)(2,1)S(1)}, u32[]{:S(2)}, u32[]{:S(2)}) collective-permute-start(bf16[8,8,256]{2,1,0:T(8,128)(2,1)S(1)} %slice.86.b0), channel_id=1, source_target_pairs={{0,3},{1,0},{2,1},{3,2},{4,7},{5,4},{6,5},{7,6},{8,11},{9,8},{10,9... | collective-permute-start | bytes 98312 | tf_op jit(solution)/shard_map/ppermute | solution.py:286
  169.1 5.0 %collective-permute-done.13.b1 = bf16[8,8,256]{2,1,0:T(8,128)(2,1)S(1)} collective-permute-done((bf16[8,8,256]{2,1,0:T(8,128)(2,1)S(1)}, bf16[8,8,256]{2,1,0:T(8,128)(2,1)S(1)}, u32[]{:S(2)}, u32[]{:S(2)}) %collective-permute-start.13) | collective-permute-done | bytes 32800 | tf_op jit(solution)/shard_map/ppermute | solution.py:283
  174.1 5.5 %collective-permute-done.15.b3 = bf16[8,8,256]{2,1,0:T(8,128)(2,1)S(1)} collective-permute-done((bf16[8,8,256]{2,1,0:T(8,128)(2,1)S(1)}, bf16[8,8,256]{2,1,0:T(8,128)(2,1)S(1)}, u32[]{:S(2)}, u32[]{:S(2)}) %collective-permute-start.15) | collective-permute-done | bytes 32800 | tf_op jit(solution)/shard_map/ppermute | solution.py:283
  180.2 1.5 chunk.1
  181.7 2.0 collective-permute-start.21
  183.7 3.2 %collective-permute-start.17 = (bf16[128,512]{1,0:T(8,128)(2,1)}, bf16[128,512]{1,0:T(8,128)(2,1)S(1)}, u32[]{:S(2)}, u32[]{:S(2)}) collective-permute-start(bf16[128,512]{1,0:T(8,128)(2,1)} %chunk.1), channel_id=1, source_target_pairs={{0,192},{32,96},{64,0},{96,160},{128,64},{160,224},{192,128},{224,... | collective-permute-start | bytes 393224 | tf_op jit(solution)/shard_map/ppermute | solution.py:277
  186.9 1.1 collective-permute-done.16
  188.0 1.7 collective-permute-done.17
  189.7 4.5 %collective-permute-done.18 = bf16[128,512]{1,0:T(8,128)(2,1)S(1)} collective-permute-done((bf16[128,512]{1,0:T(8,128)(2,1)S(1)}, bf16[128,512]{1,0:T(8,128)(2,1)S(1)}, u32[]{:S(2)}, u32[]{:S(2)}) %collective-permute-start.18) | collective-permute-done | bytes 131104 | tf_op jit(solution)/shard_map/ppermute | solution.py:274
  194.2 1.0 pad_maximum_fusion.1.held
  196.7 2.7 %spread.1 = f32[512,1024]{1,0:T(8,128)} custom-call(bf16[8,72,256]{2,1,0:T(8,128)(2,1)} %copy-done.4, bf16[8,72,256]{2,1,0:T(8,128)(2,1)} %copy-done.8, bf16[8,72,256]{2,1,0:T(8,128)(2,1)} %copy-done.9, bf16[8,72,256]{2,1,0:T(8,128)(2,1)} %copy-done.10), custom_call_target="tpu_custom_call" | custom-call | tf_op jit(solution)/shard_map/spread/pallas_call | solution.py:47
  199.4 1.9 collective-permute-done.22.other
  201.3 0.8 copy-done.7
  202.1 2.7 %join.1 = f32[1024,512]{1,0:T(8,128)} custom-call(bf16[4,128,512]{2,1,0:T(8,128)(2,1)} %copy-done.2, bf16[4,128,512]{2,1,0:T(8,128)(2,1)} %copy-done.7), custom_call_target="tpu_custom_call" | custom-call | tf_op jit(solution)/shard_map/join/pallas_call | solution.py:47
  (80 shorter events, 6.3 us)
Async XLA Ops:
  3.9 3.2 %collective-permute-start = (bf16[4,128,1024]{2,1,0:T(8,128)(2,1)}, bf16[4,128,1024]{2,1,0:T(8,128)(2,1)S(1)}, u32[]{:S(2)}, u32[]{:S(2)}) collective-permute-start(bf16[4,128,1024]{2,1,0:T(8,128)(2,1)} %project.3), channel_id=1, source_target_pairs={{0,32},{32,0},{64,96},{96,64},{128,160},{160,128},{192,224},{224,1... | collective-permute-start | bytes 3145736 | tf_op jit(solution)/shard_map/ppermute | solution.py:280
  7.1 3.3 %copy-start.20 = (s32[1,128,10]{1,0,2:T(1,128)S(1)}, s32[1,128,10]{1,0,2:T(1,128)}, u32[]{:S(2)}) copy-start(s32[1,128,10]{1,0,2:T(1,128)} %param.10) | copy-start | bytes 15364
  7.1 10.4 %copy-start.1 = (bf16[4,128,1024]{2,1,0:T(8,128)(2,1)}, bf16[4,128,1024]{2,1,0:T(8,128)(2,1)S(1)}, u32[]{:S(2)}) copy-start(bf16[4,128,1024]{2,1,0:T(8,128)(2,1)S(1)} %collective-permute-done.got) | copy-start | bytes 3145732
  8.7 7.7 %collective-permute-start.1 = (bf16[128,1024]{1,0:T(8,128)(2,1)S(1)}, bf16[128,1024]{1,0:T(8,128)(2,1)S(1)}, u32[]{:S(2)}, u32[]{:S(2)}) collective-permute-start(bf16[128,1024]{1,0:T(8,128)(2,1)S(1)} %get-tuple-element.58), channel_id=1, source_target_pairs={{0,64},{32,224},{64,128},{96,32},{128,192},{160,96},{192,0},{224,1... | collective-permute-start | bytes 786440 | tf_op jit(solution)/shard_map/ppermute | solution.py:274
  17.4 9.3 %collective-permute-start.2 = (bf16[128,1024]{1,0:T(8,128)(2,1)S(1)}, bf16[128,1024]{1,0:T(8,128)(2,1)S(1)}, u32[]{:S(2)}, u32[]{:S(2)}) collective-permute-start(bf16[128,1024]{1,0:T(8,128)(2,1)S(1)} %fusion), channel_id=1, source_target_pairs={{0,64},{32,224},{64,128},{96,32},{128,192},{160,96},{192,0},{224,1... | collective-permute-start | bytes 786440 | tf_op jit(solution)/shard_map/ppermute | solution.py:274
  17.9 8.9 %collective-permute-start.3 = (bf16[128,1024]{1,0:T(8,128)(2,1)S(1)}, bf16[128,1024]{1,0:T(8,128)(2,1)S(1)}, u32[]{:S(2)}, u32[]{:S(2)}) collective-permute-start(bf16[128,1024]{1,0:T(8,128)(2,1)S(1)} %get-tuple-element.57), channel_id=1, source_target_pairs={{0,192},{32,96},{64,0},{96,160},{128,64},{160,224},{192,128},{224,... | collective-permute-start | bytes 786440 | tf_op jit(solution)/shard_map/ppermute | solution.py:277
  26.8 0.7 copy-start.14
  26.8 0.8 copy-start.15
  63.3 17.2 %copy-start.13 = (bf16[2,128,512]{2,1,0:T(8,128)(2,1)S(1)}, bf16[2,128,512]{2,1,0:T(8,128)(2,1)}, u32[]{:S(2)}) copy-start(bf16[2,128,512]{2,1,0:T(8,128)(2,1)} %get-tuple-element.46) | copy-start | bytes 786436
  63.3 22.6 %all-to-all-start.1 = ((bf16[32,16,512]{2,1,0:T(8,128)(2,1)}), bf16[32,16,512]{2,1,0:T(8,128)(2,1)S(1)}, u32[]{:S(2)}, u32[]{:S(2)}) async-start(bf16[32,16,512]{2,1,0:T(8,128)(2,1)} %bitcast.40), calls=%async_computation.1 | async-start | bytes 1048576 | tf_op jit(solution)/shard_map/all_to_all | solution.py:55
  69.2 11.4 %collective-permute-start.4 = (bf16[3,128,512]{2,1,0:T(8,128)(2,1)}, bf16[3,128,512]{2,1,0:T(8,128)(2,1)S(1)}, u32[]{:S(2)}, u32[]{:S(2)}) collective-permute-start(bf16[3,128,512]{2,1,0:T(8,128)(2,1)} %get-tuple-element.42), channel_id=1, source_target_pairs={{0,64},{32,224},{64,128},{96,32},{128,192},{160,96},{192,0},{224,1... | collective-permute-start | bytes 1179656 | tf_op jit(solution)/shard_map/ppermute | solution.py:274
  69.3 20.7 %collective-permute-start.5 = (bf16[3,128,512]{2,1,0:T(8,128)(2,1)}, bf16[3,128,512]{2,1,0:T(8,128)(2,1)S(1)}, u32[]{:S(2)}, u32[]{:S(2)}) collective-permute-start(bf16[3,128,512]{2,1,0:T(8,128)(2,1)} %get-tuple-element.43), channel_id=1, source_target_pairs={{0,192},{32,96},{64,0},{96,160},{128,64},{160,224},{192,128},{224,... | collective-permute-start | bytes 1179656 | tf_op jit(solution)/shard_map/ppermute | solution.py:277
  85.9 0.8 copy-start
  88.8 1.2 copy-start.6
  88.8 11.7 %copy-start.12 = (bf16[2,128,512]{2,1,0:T(8,128)(2,1)S(1)}, bf16[2,128,512]{2,1,0:T(8,128)(2,1)}, u32[]{:S(2)}) copy-start(bf16[2,128,512]{2,1,0:T(8,128)(2,1)} %get-tuple-element.47) | copy-start | bytes 786436
  89.9 10.5 %collective-permute-start.6 = (bf16[4,128,512]{2,1,0:T(8,128)(2,1)S(1)}, bf16[4,128,512]{2,1,0:T(8,128)(2,1)S(1)}, u32[]{:S(2)}, u32[]{:S(2)}) collective-permute-start(bf16[4,128,512]{2,1,0:T(8,128)(2,1)S(1)} %pad_maximum_fusion), channel_id=1, source_target_pairs={{0,64},{32,224},{64,128},{96,32},{128,192},{160,96},{192,0},{224,1... | collective-permute-start | bytes 1572872 | tf_op jit(solution)/shard_map/ppermute | solution.py:274
  90.0 10.6 %collective-permute-start.7 = (bf16[128,512]{1,0:T(8,128)(2,1)S(1)}, bf16[128,512]{1,0:T(8,128)(2,1)S(1)}, u32[]{:S(2)}, u32[]{:S(2)}) collective-permute-start(bf16[128,512]{1,0:T(8,128)(2,1)S(1)} %copy-done.6), channel_id=1, source_target_pairs={{0,192},{32,96},{64,0},{96,160},{128,64},{160,224},{192,128},{224,... | collective-permute-start | bytes 393224 | tf_op jit(solution)/shard_map/ppermute | solution.py:277
  100.4 6.3 %collective-permute-start.8 = (bf16[128,512]{1,0:T(8,128)(2,1)S(1)}, bf16[128,512]{1,0:T(8,128)(2,1)S(1)}, u32[]{:S(2)}, u32[]{:S(2)}) collective-permute-start(bf16[128,512]{1,0:T(8,128)(2,1)S(1)} %get-tuple-element.59), channel_id=1, source_target_pairs={{0,64},{32,224},{64,128},{96,32},{128,192},{160,96},{192,0},{224,1... | collective-permute-start | bytes 393224 | tf_op jit(solution)/shard_map/ppermute | solution.py:274
  106.7 3.1 %copy-start.3 = (bf16[9,128,512]{2,1,0:T(8,128)(2,1)}, bf16[9,128,512]{2,1,0:T(8,128)(2,1)S(1)}, u32[]{:S(2)}) copy-start(bf16[9,128,512]{2,1,0:T(8,128)(2,1)S(1)} %fusion.3.held) | copy-start | bytes 3538948
  106.7 3.1 %collective-permute-start.9 = (bf16[9,128,512]{2,1,0:T(8,128)(2,1)S(1)}, bf16[9,128,512]{2,1,0:T(8,128)(2,1)S(1)}, u32[]{:S(2)}, u32[]{:S(2)}) collective-permute-start(bf16[9,128,512]{2,1,0:T(8,128)(2,1)S(1)} %fusion.3.held), channel_id=1, source_target_pairs={{0,32},{32,0},{64,96},{96,64},{128,160},{160,128},{192,224},{224,1... | collective-permute-start | bytes 3538952 | tf_op jit(solution)/shard_map/ppermute | solution.py:280
  109.8 1.0 copy-start.5
  115.3 8.1 %collective-permute-start.10 = (bf16[8,72,256]{2,1,0:T(8,128)(2,1)}, bf16[8,72,256]{2,1,0:T(8,128)(2,1)S(1)}, u32[]{:S(2)}, u32[]{:S(2)}) collective-permute-start(bf16[8,72,256]{2,1,0:T(8,128)(2,1)} %get-tuple-element.49), channel_id=1, source_target_pairs={{0,1},{1,2},{2,3},{3,0},{4,5},{5,6},{6,7},{7,4},{8,9},{9,10},{10,1... | collective-permute-start | bytes 884744 | tf_op jit(solution)/shard_map/ppermute | solution.py:283
  124.5 10.5 %copy-start.11 = (bf16[8,72,256]{2,1,0:T(8,128)(2,1)S(1)}, bf16[8,72,256]{2,1,0:T(8,128)(2,1)}, u32[]{:S(2)}) copy-start(bf16[8,72,256]{2,1,0:T(8,128)(2,1)} %get-tuple-element.52) | copy-start | bytes 884740
  124.5 10.5 %collective-permute-start.11 = (bf16[8,72,256]{2,1,0:T(8,128)(2,1)S(1)}, bf16[8,72,256]{2,1,0:T(8,128)(2,1)S(1)}, u32[]{:S(2)}, u32[]{:S(2)}) collective-permute-start(bf16[8,72,256]{2,1,0:T(8,128)(2,1)S(1)} %add_convert_fusion.1), channel_id=1, source_target_pairs={{0,1},{1,2},{2,3},{3,0},{4,5},{5,6},{6,7},{7,4},{8,9},{9,10},{10,1... | collective-permute-start | bytes 884744 | tf_op jit(solution)/shard_map/ppermute | solution.py:283
  124.6 10.4 %collective-permute-start.12 = (bf16[8,72,256]{2,1,0:T(8,128)(2,1)}, bf16[8,72,256]{2,1,0:T(8,128)(2,1)S(1)}, u32[]{:S(2)}, u32[]{:S(2)}) collective-permute-start(bf16[8,72,256]{2,1,0:T(8,128)(2,1)} %get-tuple-element.53), channel_id=1, source_target_pairs={{0,3},{1,0},{2,1},{3,2},{4,7},{5,4},{6,5},{7,6},{8,11},{9,8},{10,9... | collective-permute-start | bytes 884744 | tf_op jit(solution)/shard_map/ppermute | solution.py:286
  165.7 29.5 %copy-start.4 = (bf16[8,72,256]{2,1,0:T(8,128)(2,1)}, bf16[8,72,256]{2,1,0:T(8,128)(2,1)S(1)}, u32[]{:S(2)}) copy-start(bf16[8,72,256]{2,1,0:T(8,128)(2,1)S(1)} %all_to_all.22.b0) | copy-start | bytes 884740
  165.8 15.9 %collective-permute-start.19 = (bf16[8,72,256]{2,1,0:T(8,128)(2,1)S(1)}, bf16[8,72,256]{2,1,0:T(8,128)(2,1)S(1)}, u32[]{:S(2)}, u32[]{:S(2)}) collective-permute-start(bf16[8,72,256]{2,1,0:T(8,128)(2,1)S(1)} %all_to_all.22.b0), channel_id=1, source_target_pairs={{0,1},{1,2},{2,3},{3,0},{4,5},{5,6},{6,7},{7,4},{8,9},{9,10},{10,1... | collective-permute-start | bytes 884744 | tf_op jit(solution)/shard_map/ppermute | solution.py:283
  165.8 13.8 %copy-start.16 = (bf16[8,8,256]{2,1,0:T(8,128)(2,1)}, bf16[8,8,256]{2,1,0:T(8,128)(2,1)S(1)}, u32[]{:S(2)}) copy-start(bf16[8,8,256]{2,1,0:T(8,128)(2,1)S(1)} %slice.86.b0) | copy-start | bytes 98308
  165.8 8.3 %collective-permute-start.13 = (bf16[8,8,256]{2,1,0:T(8,128)(2,1)S(1)}, bf16[8,8,256]{2,1,0:T(8,128)(2,1)S(1)}, u32[]{:S(2)}, u32[]{:S(2)}) collective-permute-start(bf16[8,8,256]{2,1,0:T(8,128)(2,1)S(1)} %slice.86.b0), channel_id=1, source_target_pairs={{0,1},{1,2},{2,3},{3,0},{4,5},{5,6},{6,7},{7,4},{8,9},{9,10},{10,1... | collective-permute-start | bytes 98312 | tf_op jit(solution)/shard_map/ppermute | solution.py:283
  165.9 8.2 %collective-permute-start.14 = (bf16[8,8,256]{2,1,0:T(8,128)(2,1)S(1)}, bf16[8,8,256]{2,1,0:T(8,128)(2,1)S(1)}, u32[]{:S(2)}, u32[]{:S(2)}) collective-permute-start(bf16[8,8,256]{2,1,0:T(8,128)(2,1)S(1)} %slice.86.b0), channel_id=1, source_target_pairs={{0,3},{1,0},{2,1},{3,2},{4,7},{5,4},{6,5},{7,6},{8,11},{9,8},{10,9... | collective-permute-start | bytes 98312 | tf_op jit(solution)/shard_map/ppermute | solution.py:286
  174.0 5.5 %copy-start.17 = (bf16[8,8,256]{2,1,0:T(8,128)(2,1)}, bf16[8,8,256]{2,1,0:T(8,128)(2,1)S(1)}, u32[]{:S(2)}) copy-start(bf16[8,8,256]{2,1,0:T(8,128)(2,1)S(1)} %collective-permute-done.13.b1) | copy-start | bytes 98308
  174.0 5.5 %collective-permute-start.15 = (bf16[8,8,256]{2,1,0:T(8,128)(2,1)S(1)}, bf16[8,8,256]{2,1,0:T(8,128)(2,1)S(1)}, u32[]{:S(2)}, u32[]{:S(2)}) collective-permute-start(bf16[8,8,256]{2,1,0:T(8,128)(2,1)S(1)} %collective-permute-done.13.b1), channel_id=1, source_target_pairs={{0,1},{1,2},{2,3},{3,0},{4,5},{5,6},{6,7},{7,4},{8,9},{9,10},{10,1... | collective-permute-start | bytes 98312 | tf_op jit(solution)/shard_map/ppermute | solution.py:283
  174.0 5.5 %copy-start.18 = (bf16[8,8,256]{2,1,0:T(8,128)(2,1)}, bf16[8,8,256]{2,1,0:T(8,128)(2,1)S(1)}, u32[]{:S(2)}) copy-start(bf16[8,8,256]{2,1,0:T(8,128)(2,1)S(1)} %collective-permute-done.14.b2) | copy-start | bytes 98308
  179.5 0.6 copy-start.19
  181.6 6.4 %collective-permute-start.16 = (bf16[128,512]{1,0:T(8,128)(2,1)}, bf16[128,512]{1,0:T(8,128)(2,1)S(1)}, u32[]{:S(2)}, u32[]{:S(2)}) collective-permute-start(bf16[128,512]{1,0:T(8,128)(2,1)} %chunk.1), channel_id=1, source_target_pairs={{0,64},{32,224},{64,128},{96,32},{128,192},{160,96},{192,0},{224,1... | collective-permute-start | bytes 393224 | tf_op jit(solution)/shard_map/ppermute | solution.py:274
  181.6 13.6 %collective-permute-start.20 = (bf16[8,72,256]{2,1,0:T(8,128)(2,1)S(1)}, bf16[8,72,256]{2,1,0:T(8,128)(2,1)S(1)}, u32[]{:S(2)}, u32[]{:S(2)}) collective-permute-start(bf16[8,72,256]{2,1,0:T(8,128)(2,1)S(1)} %all_to_all.22.b0), channel_id=1, source_target_pairs={{0,3},{1,0},{2,1},{3,2},{4,7},{5,4},{6,5},{7,6},{8,11},{9,8},{10,9... | collective-permute-start | bytes 884744 | tf_op jit(solution)/shard_map/ppermute | solution.py:286
  181.6 13.6 %copy-start.8 = (bf16[8,72,256]{2,1,0:T(8,128)(2,1)}, bf16[8,72,256]{2,1,0:T(8,128)(2,1)S(1)}, u32[]{:S(2)}) copy-start(bf16[8,72,256]{2,1,0:T(8,128)(2,1)S(1)} %collective-permute-done.19.b1) | copy-start | bytes 884740
  181.7 13.6 %collective-permute-start.21 = (bf16[8,72,256]{2,1,0:T(8,128)(2,1)S(1)}, bf16[8,72,256]{2,1,0:T(8,128)(2,1)S(1)}, u32[]{:S(2)}, u32[]{:S(2)}) collective-permute-start(bf16[8,72,256]{2,1,0:T(8,128)(2,1)S(1)} %collective-permute-done.19.b1), channel_id=1, source_target_pairs={{0,1},{1,2},{2,3},{3,0},{4,5},{5,6},{6,7},{7,4},{8,9},{9,10},{10,1... | collective-permute-start | bytes 884744 | tf_op jit(solution)/shard_map/ppermute | solution.py:283
  183.7 6.1 %collective-permute-start.17 = (bf16[128,512]{1,0:T(8,128)(2,1)}, bf16[128,512]{1,0:T(8,128)(2,1)S(1)}, u32[]{:S(2)}, u32[]{:S(2)}) collective-permute-start(bf16[128,512]{1,0:T(8,128)(2,1)} %chunk.1), channel_id=1, source_target_pairs={{0,192},{32,96},{64,0},{96,160},{128,64},{160,224},{192,128},{224,... | collective-permute-start | bytes 393224 | tf_op jit(solution)/shard_map/ppermute | solution.py:277
  188.0 6.2 %collective-permute-start.18 = (bf16[128,512]{1,0:T(8,128)(2,1)S(1)}, bf16[128,512]{1,0:T(8,128)(2,1)S(1)}, u32[]{:S(2)}, u32[]{:S(2)}) collective-permute-start(bf16[128,512]{1,0:T(8,128)(2,1)S(1)} %collective-permute-done.16), channel_id=1, source_target_pairs={{0,64},{32,224},{64,128},{96,32},{128,192},{160,96},{192,0},{224,1... | collective-permute-start | bytes 393224 | tf_op jit(solution)/shard_map/ppermute | solution.py:274
  195.2 4.2 %copy-start.2 = (bf16[4,128,512]{2,1,0:T(8,128)(2,1)}, bf16[4,128,512]{2,1,0:T(8,128)(2,1)S(1)}, u32[]{:S(2)}) copy-start(bf16[4,128,512]{2,1,0:T(8,128)(2,1)S(1)} %pad_maximum_fusion.1.held) | copy-start | bytes 1572868
  195.2 0.8 copy-start.9
  196.0 0.7 copy-start.10
  199.4 1.9 collective-permute-start.22
  201.3 0.8 copy-start.7

commit v6 on v5

--- a/solution.py
+++ b/solution.py
@@ -143,10 +143,11 @@
     return total
 
 
-def forward_body(part, got, near, far, grads, inv, give, p_self, p_near, boxes):
+def forward_body(part, got, near, far, grads, inv, give, p_self, p_near, boxes, mark):
     width = grads.shape[1]
     total = add(part[0], got[0], near[...], far[...])
     p_self[...] = total[:, :width]
+    mark[...] = total[:8, :128]
     mine = total[:, width:].astype(BF16)
     p_near[...] = mine
     scaled = (grads[...].astype(F32) * inv[:, :1]).astype(BF16)
@@ -154,7 +155,7 @@
 
 
 def middle_body(
-    recv, p_self, p_near, grads, inv, w_two, give, take, own, own_t,
+    recv, p_self, p_near, grads, inv, w_two, give, take, own, own_t, mark,
     boxes, near_local, hidden_out, ahead, behind, third, mine, scratch,
 ):
     nodes, width = grads.shape
@@ -210,27 +211,19 @@
         stack[g, :, :width] = source[k % chips]
         stack[g, :, width:] = source[chips + k % chips]
     total = mm(flat_t[...], stack[...].reshape(groups * nodes, both)).astype(BF16)
-    twos = add(two[...], other[2 * chips]).astype(BF16)
-    tail = rows - 4 * part
-    slab = deep * tail
     for x in range(chips):
         for q in range(4):
             piece = total[x * block : (x + 1) * block, q * cut : (q + 1) * cut]
             boxes[x, :, q * part : (q + 1) * part, :] = piece.reshape(deep, part, cut)
-        piece = twos[x % 2 * slab : (x % 2 + 1) * slab, x // 2 * cut : (x // 2 + 1) * cut]
-        boxes[x, :, 4 * part :, :] = piece.reshape(deep, tail, cut)
     for x, target in zip(places_x(SUM_MINE), (ahead, behind, third, own)):
-        target[...] = boxes[x]
-
-
-def chunk_body(b0, b1, b2, b3, out, scratch):
-    deep, tail, cut = b0.shape
-    chips, slab, _ = scratch.shape
-    for x, block in zip(places_x(GET_MINE), (b0, b1, b2, b3)):
-        scratch[x] = block[...].reshape(slab, cut)
-    for x in range(chips):
-        at = x % 2 * slab
-        out[at : at + slab, x // 2 * cut : (x // 2 + 1) * cut] = scratch[x]
+        target[:, :rows, :] = boxes[x]
+    twos = add(two[...], other[2 * chips]).astype(BF16)
+    tail = (ahead.shape[1] - rows) // 2
+    for k in range(2):
+        piece = twos[:, k * cut : (k + 1) * cut].reshape(deep, tail, cut)
+        for target in (ahead, behind, own):
+            target[:, rows + k * tail : rows + (k + 1) * tail, :] = piece
+    third[:, rows:, :] = jnp.zeros_like(third[:, rows:, :])
 
 
 def spread_body(b0, b1, b2, b3, out):
@@ -316,17 +309,20 @@
         return pl.BlockSpec(dims, lambda i: (0,) * len(dims))
 
     last = pl.BlockSpec((1, nodes, 2 * width), lambda i: (CHIPS - 1, 0, 0))
-    p_self, p_near, boxes = pl.pallas_call(
+    p_self, p_near, boxes, mark = pl.pallas_call(
         forward_body,
-        out_shape=(shape((nodes, width), F32), block, shape((span, width))),
+        out_shape=(
+            shape((nodes, width), F32), block, shape((span, width)), shape((8, 128), F32)
+        ),
         grid=(1,),
         in_specs=[
             last, last, full(nodes, 2 * width), full(nodes, 2 * width), full(nodes, width),
             full(nodes, nodes), full(span, 2 * nodes),
         ],
-        out_specs=(full(nodes, width), full(nodes, width), full(span, width)),
+        out_specs=(full(nodes, width), full(nodes, width), full(span, width), full(8, 128)),
         name="forward",
     )(mine, got, near, far, grads, inv, give)
+    boxes, mark = lax.optimization_barrier((boxes, swap(mark)))
     recv = trade(boxes.reshape(parts, 2 * kmax, width)).reshape(span, width)
     rows = 2 * width // groups
     boxes, near_local, hidden, ahead, behind, third, mine = whole(
@@ -341,26 +337,27 @@
             shape((2, rows, width)),
             shape((2, rows, width)),
         ),
-        recv, p_self, p_near, grads, inv, w_two, give, take, own, own_t,
+        recv, p_self, p_near, grads, inv, w_two, give, take, own, own_t, mark,
         scratch=[pltpu.VMEM((groups, rows, width), BF16)],
     )
     recv = trade(boxes.reshape(parts, 2 * kmax, width)).reshape(span, width)
 
     relay = forward(ahead)
     near = backward(behind)
-    passed = add(third, relay[1:]).astype(BF16)
+    message = jnp.concatenate([relay[:1], add(third, relay[1:]).astype(BF16)])
+    message, recv = lax.optimization_barrier((message, recv))
     d_near = whole("near", near_body, block, recv, near_local, take)
-    message = jnp.concatenate([d_near[None], relay[:1], passed])
+    one = forward(d_near)
+    two = backward(d_near)
     far = forward(message)
-    back = backward(d_near)
-    last = forward(far[0])
-    sums = add(mine, near[1:], far[2:])
+    sums = add(mine, near[1:], far[1:])
     held = jnp.stack(
-        [ahead[0], relay[0], near[0], far[1], d_near, far[0], back, last, sums[0].astype(BF16)]
+        [ahead[0], relay[0], near[0], far[0], d_near, one, two, forward(one), sums[0].astype(BF16)]
     )
     other = swap(held)
 
-    lot = shape((deep, 9 * cols // parts // 2, width // 2))
+    kept = 8 * cols // parts // 2
+    lot = shape((deep, kept + 4 * width // groups // deep, width // 2))
     ahead, behind, third, mine = whole(
         "grad",
         grad_body,
@@ -368,7 +365,7 @@
         flat_t, held, other, sums[1],
         scratch=[
             pltpu.VMEM((groups, nodes, 2 * width), BF16),
-            pltpu.VMEM((CHIPS, *lot.shape), BF16),
+            pltpu.VMEM((CHIPS, deep, kept, width // 2), BF16),
         ],
     )
     out = whole("out", out_body, block, recv, hidden, inv, take, own, w_two)
@@ -376,23 +373,25 @@
     near = x_backward(behind)
     far = x_forward(add(third, relay).astype(BF16))
     far, out = lax.optimization_barrier((far, out))
-    terms = trade(add(mine, near, far).astype(BF16), lines)
+    last_rows = lax.broadcasted_iota(jnp.int32, lot.shape, 1) >= kept
+    terms = add(mine, near, far) + jnp.where(last_rows, relay.astype(F32), 0.0)
+    terms = trade(terms.astype(BF16), lines)
     total = (jnp.sum(terms.astype(F32), axis=0) * scale).astype(BF16)
     total = trade(jnp.broadcast_to(total[None], terms.shape), lines)
-
-    def x_gather(lot):
-        one = x_forward(lot)
-        return lot, one, x_backward(lot), x_forward(one)
-
-    slab = 2 * width // groups // 2
-    twos = x_gather(total[:, 8 * lot.shape[1] // 9 :, :])
-    ones = x_gather(total)
-    chunk = whole(
-        "chunk", chunk_body, block, *twos, scratch=[pltpu.VMEM((CHIPS, slab, width // 2), BF16)]
-    )
-    held = gather(chunk)
-    one = whole("spread", spread_body, shape((cols, 2 * width), F32), *ones)
-    held, one = lax.optimization_barrier((held, one))
+    tail = (lot.shape[1] - kept) // 2
+    chunk = jnp.concatenate(
+        [
+            total[:, kept : kept + tail].reshape(deep * tail, -1),
+            total[:, kept + tail :].reshape(deep * tail, -1),
+        ],
+        axis=1,
+    )
+    mine = total[:, :kept]
+    relay = x_forward(mine)
+    near = x_backward(mine)
+    held, relay = lax.optimization_barrier((gather(chunk), relay))
+    far = x_forward(relay)
+    one = whole("spread", spread_body, shape((cols, 2 * width), F32), mine, relay, near, far)
     two = whole("join", join_body, shape((2 * width, width), F32), held, swap(held))
     return out[None], one, two
 

time: 208 us -> 203 us (0.976)
  blocking collectives: 59.5 us -> 62.7 us
  starting transfers between devices: 30.1 us -> 27.6 us
    ppermute x3 -> x2, waiting for transfers between devices: 0.01 us -> 6.62 us  [x_backward(): return lax.ppermute(block, ('feat', 'dom'), x_behind)]
    ppermute x6 -> x4, waiting for transfers between devices: 22.6 us -> 16.3 us  [x_forward(): return lax.ppermute(block, ('feat', 'dom'), x_ahead)]
    all_to_all x3, blocking collectives: 59.5 us -> 62.7 us  [trade(): lax.all_to_all(boxes, 'dom', split_axis=0, concat_axis=0, axis_index_grou...]
    ppermute x3 -> x2, starting transfers between devices: 6.45 us -> 3.74 us  [x_backward(): return lax.ppermute(block, ('feat', 'dom'), x_behind)]
    ppermute x7 -> x8, waiting for transfers between devices: 32.6 us -> 34.3 us  [forward(): return lax.ppermute(block, 'feat', y_ahead)]
    pallas_call x11 -> x10, Pallas kernels: 31.3 us -> 29.9 us  [whole(): pl.pallas_call(body, out_shape=outs, scratch_shapes=scratch, name=name)]
    unnamed x49 -> x44, local copies, waits for them, and re-layouts: 7.15 us -> 6.67 us
  transfers between devices with their start and end apart: 24 -> 23, of which waited for: 15 -> 14; matrix products, arithmetic and copies ran while one was open for 2% -> 2% of each run, Pallas kernels for 7% -> 8%
where the time goes in v6:
time: 203 us; the launch traced here: 200 us
  waiting for transfers between devices  64.3 us (32%)
  blocking collectives  62.7 us (31%)
  Pallas kernels  32.6 us (16%)
  starting transfers between devices  27.6 us (14%)
  local copies, waits for them, and re-layouts  7.61 us (4%)
  other arithmetic  4.38 us (2%)
    all_to_all x3, blocking collectives, trade(): lax.all_to_all(boxes, 'dom', split_axis=0, concat_axis=0, axis_index_grou...  62.7 us
    ppermute x8, waiting for transfers between devices, forward(): return lax.ppermute(block, 'feat', y_ahead)  34.3 us
    pallas_call x10, Pallas kernels, whole(): pl.pallas_call(body, out_shape=outs, scratch_shapes=scratch, name=name)  29.9 us
    ppermute x4, waiting for transfers between devices, x_forward(): return lax.ppermute(block, ('feat', 'dom'), x_ahead)  16.3 us
    ppermute x4, starting transfers between devices, backward(): return lax.ppermute(block, 'feat', y_behind)  12.7 us
    unnamed x44, local copies, waits for them, and re-layouts  6.67 us
    ppermute x2, waiting for transfers between devices, x_backward(): return lax.ppermute(block, ('feat', 'dom'), x_behind)  6.62 us
    all_to_all x1, starting transfers between devices, trade(): lax.all_to_all(boxes, 'dom', split_axis=0, concat_axis=0, axis_index_grou...  5.39 us
  transfers between devices with their start and end apart: 23, of which 14 were waited for; matrix products, arithmetic and copies ran while one was open for 2% of the time, Pallas kernels for 8%

profile of v6, /device:TPU:32, one launch (start us, length us, event | category | flops | bytes accessed | tf_op | source)
XLA Modules:
  0.0 200.2 jit_solution(9234848231304897100)
XLA Ops:
  0.6 3.2 %project.3 = bf16[4,128,1024]{2,1,0:T(8,128)(2,1)} custom-call(bf16[8,128,512]{2,1,0:T(8,128)(2,1)} %flat.1, bf16[512,1024]{1,0:T(8,128)(2,1)} %w.3), custom_call_target="tpu_custom_call" | custom-call | tf_op jit(solution)/shard_map/project/pallas_call | solution.py:47
  3.9 3.2 %project.2.part = bf16[4,128,1024]{2,1,0:T(8,128)(2,1)} custom-call(bf16[8,128,512]{2,1,0:T(8,128)(2,1)} %flat.1, bf16[512,1024]{1,0:T(8,128)(2,1)} %w.3), custom_call_target="tpu_custom_call" | custom-call | tf_op jit(solution)/shard_map/project/pallas_call | solution.py:47
  7.1 1.6 fusion.5
  8.7 1.7 collective-permute-start.1
  11.0 2.0 tables.1
  12.9 3.4 %collective-permute-done.1 = bf16[128,1024]{1,0:T(8,128)(2,1)S(1)} collective-permute-done((bf16[128,1024]{1,0:T(8,128)(2,1)S(1)}, bf16[128,1024]{1,0:T(8,128)(2,1)S(1)}, u32[]{:S(2)}, u32[]{:S(2)}) %collective-permute-start.1) | collective-permute-done | bytes 262176 | tf_op jit(solution)/shard_map/ppermute | solution.py:267
  16.4 1.1 fusion.3
  17.9 2.9 %collective-permute-start.3 = (bf16[128,1024]{1,0:T(8,128)(2,1)S(1)}, bf16[128,1024]{1,0:T(8,128)(2,1)S(1)}, u32[]{:S(2)}, u32[]{:S(2)}) collective-permute-start(bf16[128,1024]{1,0:T(8,128)(2,1)S(1)} %get-tuple-element.67), channel_id=1, source_target_pairs={{0,192},{32,96},{64,0},{96,160},{128,64},{160,224},{192,128},{224,... | collective-permute-start | bytes 786440 | tf_op jit(solution)/shard_map/ppermute | solution.py:270
  20.8 2.6 %turn.1.flat_t = bf16[512,1024]{1,0:T(8,128)(2,1)} custom-call(bf16[8,128,512]{2,1,0:T(8,128)(2,1)} %flat.1), custom_call_target="tpu_custom_call" | custom-call | tf_op jit(solution)/shard_map/turn/pallas_call | solution.py:47
  23.4 3.4 %collective-permute-done.2.far = bf16[128,1024]{1,0:T(8,128)(2,1)S(1)} collective-permute-done((bf16[128,1024]{1,0:T(8,128)(2,1)S(1)}, bf16[128,1024]{1,0:T(8,128)(2,1)S(1)}, u32[]{:S(2)}, u32[]{:S(2)}) %collective-permute-start.2) | collective-permute-done | bytes 262176 | tf_op jit(solution)/shard_map/ppermute | solution.py:267
  26.8 0.7 copy-done.11
  27.6 2.6 %forward.1 = (f32[128,512]{1,0:T(8,128)}, bf16[128,512]{1,0:T(8,128)(2,1)}, bf16[512,512]{1,0:T(8,128)(2,1)}, f32[8,128]{1,0:T(8,128)}) custom-call(bf16[4,128,1024]{2,1,0:T(8,128)(2,1)} %project.2.part, bf16[4,128,1024]{2,1,0:T(8,128)(2,1)} %copy-done.1, bf16[128,1024]{1,0:T(8,128)(2,1)} %copy-done.12, bf16[128,1024]{1,0:T(8,128)(2,1)} %copy-done.11, ...), custom_call_target="tpu_custom_call" | custom-call | tf_op jit(solution)/shard_map/forward/pallas_call | solution.py:312
  30.2 0.9 collective-permute-start.4
  31.1 1.0 collective-permute-done.4.mark
  32.1 28.9 %all_to_all.20 = bf16[32,16,512]{2,1,0:T(8,128)(2,1)} all-to-all(bf16[32,16,512]{2,1,0:T(8,128)(2,1)} %bitcast.43), channel_id=1, replica_groups=mesh['feat'=8,'dom'=32] {'dom'}, dimensions={0} | all-to-all | bytes 1048576 | tf_op jit(solution)/shard_map/all_to_all | solution.py:55
  61.1 4.2 %middle.1 = (bf16[512,512]{1,0:T(8,128)(2,1)}, f32[128,512]{1,0:T(8,128)}, bf16[128,512]{1,0:T(8,128)(2,1)}, bf16[3,128,512]{2,1,0:T(8,128)(2,1)}, bf16[3,128,51...) custom-call(bf16[512,512]{1,0:T(8,128)(2,1)} %bitcast.41, ...), custom_call_target="tpu_custom_call" | custom-call | tf_op jit(solution)/shard_map/middle/pallas_call | solution.py:47
  65.2 5.4 %all-to-all-start.1 = ((bf16[32,16,512]{2,1,0:T(8,128)(2,1)}), bf16[32,16,512]{2,1,0:T(8,128)(2,1)S(1)}, u32[]{:S(2)}, u32[]{:S(2)}) async-start(bf16[32,16,512]{2,1,0:T(8,128)(2,1)} %bitcast.42), calls=%async_computation.1 | async-start | bytes 1048576 | tf_op jit(solution)/shard_map/all_to_all | solution.py:55
  70.7 3.2 %collective-permute-start.6 = (bf16[3,128,512]{2,1,0:T(8,128)(2,1)}, bf16[3,128,512]{2,1,0:T(8,128)(2,1)S(1)}, u32[]{:S(2)}, u32[]{:S(2)}) collective-permute-start(bf16[3,128,512]{2,1,0:T(8,128)(2,1)} %get-tuple-element.51), channel_id=1, source_target_pairs={{0,192},{32,96},{64,0},{96,160},{128,64},{160,224},{192,128},{224,... | collective-permute-start | bytes 1179656 | tf_op jit(solution)/shard_map/ppermute | solution.py:270
  73.9 0.9 slice_dynamic-update-slice_fusion.2
  74.8 8.2 %collective-permute-done.5 = bf16[3,128,512]{2,1,0:T(8,128)(2,1)S(1)} collective-permute-done((bf16[3,128,512]{2,1,0:T(8,128)(2,1)}, bf16[3,128,512]{2,1,0:T(8,128)(2,1)S(1)}, u32[]{:S(2)}, u32[]{:S(2)}) %collective-permute-start.5) | collective-permute-done | bytes 393248 | tf_op jit(solution)/shard_map/ppermute | solution.py:267
  83.2 4.0 %all-to-all-done.1 = bf16[32,16,512]{2,1,0:T(8,128)(2,1)S(1)} async-done(((bf16[32,16,512]{2,1,0:T(8,128)(2,1)}), bf16[32,16,512]{2,1,0:T(8,128)(2,1)S(1)}, u32[]{:S(2)}, u32[]{:S(2)}) %all-to-all-start.1) | async-done | bytes 524320 | tf_op jit(solution)/shard_map/all_to_all | solution.py:55
  87.3 0.8 copy-done
  88.1 2.1 %near.1 = bf16[128,512]{1,0:T(8,128)(2,1)} custom-call(bf16[512,512]{1,0:T(8,128)(2,1)} %bitcast.39, f32[128,512]{1,0:T(8,128)} %get-tuple-element.56.near_local, bf16[256,512]{1,0:T(8,128)(2,1)} %get-tuple-element.46.take), custom_call_target="tpu_custom_call" | custom-call | tf_op jit(solution)/shard_map/near/pallas_call | solution.py:47
  90.2 3.3 %collective-permute-start.9 = (bf16[128,512]{1,0:T(8,128)(2,1)}, bf16[128,512]{1,0:T(8,128)(2,1)S(1)}, u32[]{:S(2)}, u32[]{:S(2)}) collective-permute-start(bf16[128,512]{1,0:T(8,128)(2,1)} %near.1), channel_id=1, source_target_pairs={{0,192},{32,96},{64,0},{96,160},{128,64},{160,224},{192,128},{224,... | collective-permute-start | bytes 393224 | tf_op jit(solution)/shard_map/ppermute | solution.py:270
  93.5 5.3 %collective-permute-done.8 = bf16[128,512]{1,0:T(8,128)(2,1)S(1)} collective-permute-done((bf16[128,512]{1,0:T(8,128)(2,1)}, bf16[128,512]{1,0:T(8,128)(2,1)S(1)}, u32[]{:S(2)}, u32[]{:S(2)}) %collective-permute-start.8) | collective-permute-done | bytes 131104 | tf_op jit(solution)/shard_map/ppermute | solution.py:267
  98.7 0.9 bitcast_dynamic-update-slice_fusion.3
  99.8 5.1 %collective-permute-done.10 = bf16[128,512]{1,0:T(8,128)(2,1)S(1)} collective-permute-done((bf16[128,512]{1,0:T(8,128)(2,1)S(1)}, bf16[128,512]{1,0:T(8,128)(2,1)S(1)}, u32[]{:S(2)}, u32[]{:S(2)}) %collective-permute-start.10) | collective-permute-done | bytes 131104 | tf_op jit(solution)/shard_map/ppermute | solution.py:267
  105.1 0.8 slice_bitcast_fusion.two
  105.9 2.0 collective-permute-done.11.other
  107.9 1.0 copy-done.4
  108.9 4.6 %grad.1 = (bf16[8,96,256]{2,1,0:T(8,128)(2,1)}, bf16[8,96,256]{2,1,0:T(8,128)(2,1)}, bf16[8,96,256]{2,1,0:T(8,128)(2,1)}, bf16[8,96,256]{2,1,0:T(8,128)(2,1)}) custom-call(bf16[512,1024]{1,0:T(8,128)(2,1)} %turn.1.flat_t, bf16[9,128,512]{2,1,0:T(8,128)(2,1)} %copy-done.3, bf16[9,128,512]{2,1,0:T(8,128)(2,1)} %copy-done.4, f32[128,512]{1,0:T(8,128)} %slice_bitcast_fusion.two), custom_call_target="tpu_custom_call" | custom-call | tf_op jit(solution)/shard_map/grad/pallas_call | solution.py:47
  114.2 8.5 %collective-permute-done.12 = bf16[8,96,256]{2,1,0:T(8,128)(2,1)S(1)} collective-permute-done((bf16[8,96,256]{2,1,0:T(8,128)(2,1)}, bf16[8,96,256]{2,1,0:T(8,128)(2,1)S(1)}, u32[]{:S(2)}, u32[]{:S(2)}) %collective-permute-start.12) | collective-permute-done | bytes 393248 | tf_op jit(solution)/shard_map/ppermute | solution.py:276
  122.7 1.1 fusion
  123.9 3.2 %collective-permute-start.14 = (bf16[8,96,256]{2,1,0:T(8,128)(2,1)S(1)}, bf16[8,96,256]{2,1,0:T(8,128)(2,1)S(1)}, u32[]{:S(2)}, u32[]{:S(2)}) collective-permute-start(bf16[8,96,256]{2,1,0:T(8,128)(2,1)S(1)} %copy-done.17), channel_id=1, source_target_pairs={{0,3},{1,0},{2,1},{3,2},{4,7},{5,4},{6,5},{7,6},{8,11},{9,8},{10,9... | collective-permute-start | bytes 1179656 | tf_op jit(solution)/shard_map/ppermute | solution.py:279
  127.1 2.7 %out.1 = bf16[128,512]{1,0:T(8,128)(2,1)} custom-call(bf16[512,512]{1,0:T(8,128)(2,1)} %bitcast.40, bf16[128,512]{1,0:T(8,128)(2,1)} %get-tuple-element.60.hidden, f32[128,128]{1,0:T(8,128)} %get-tuple-element.39.inv, bf16[256,512]{1,0:T(8,128)(2,1)} %get-tuple-element.46.take, bf16[128,128]{1,0:T(8,128)(2,1)} %get-tuple-element.47.own, bf16[1024,512]{1,0:T(8,128)(2,1)} %w_two.3), custom_call_target="tpu_custom_call" | custom-call | tf_op jit(solution)/shard_map/out/pallas_call | solution.py:47
  129.9 6.6 %collective-permute-done.13 = bf16[8,96,256]{2,1,0:T(8,128)(2,1)S(1)} collective-permute-done((bf16[8,96,256]{2,1,0:T(8,128)(2,1)S(1)}, bf16[8,96,256]{2,1,0:T(8,128)(2,1)S(1)}, u32[]{:S(2)}, u32[]{:S(2)}) %collective-permute-start.13) | collective-permute-done | bytes 393248 | tf_op jit(solution)/shard_map/ppermute | solution.py:276
  136.8 17.8 %all_to_all.21 = bf16[8,96,256]{2,1,0:T(8,128)(2,1)S(1)} all-to-all(bf16[8,96,256]{2,1,0:T(8,128)(2,1)S(1)} %fusion.2), channel_id=1, replica_groups={{0,4,8,12,16,20,24,28},{1,5,9,13,17,21,25,29},{2,6,10,14,18,22,26,30},{..., dimensions={0} | all-to-all | bytes 786432 | tf_op jit(solution)/shard_map/all_to_all | solution.py:55
  154.7 16.0 %all_to_all.22 = bf16[8,96,256]{2,1,0:T(8,128)(2,1)S(1)} all-to-all(bf16[8,96,256]{2,1,0:T(8,128)(2,1)S(1)} %broadcast_in_dim.15), channel_id=1, replica_groups={{0,4,8,12,16,20,24,28},{1,5,9,13,17,21,25,29},{2,6,10,14,18,22,26,30},{..., dimensions={0} | all-to-all | bytes 786432 | tf_op jit(solution)/shard_map/all_to_all | solution.py:55
  171.0 3.3 %collective-permute-start.16 = (bf16[128,512]{1,0:T(8,128)(2,1)S(1)}, bf16[128,512]{1,0:T(8,128)(2,1)S(1)}, u32[]{:S(2)}, u32[]{:S(2)}) collective-permute-start(bf16[128,512]{1,0:T(8,128)(2,1)S(1)} %get-tuple-element.74), channel_id=1, source_target_pairs={{0,192},{32,96},{64,0},{96,160},{128,64},{160,224},{192,128},{224,... | collective-permute-start | bytes 393224 | tf_op jit(solution)/shard_map/ppermute | solution.py:270
  174.2 2.7 %collective-permute-done.15 = bf16[128,512]{1,0:T(8,128)(2,1)S(1)} collective-permute-done((bf16[128,512]{1,0:T(8,128)(2,1)S(1)}, bf16[128,512]{1,0:T(8,128)(2,1)S(1)}, u32[]{:S(2)}, u32[]{:S(2)}) %collective-permute-start.15) | collective-permute-done | bytes 131104 | tf_op jit(solution)/shard_map/ppermute | solution.py:267
  177.0 6.2 %collective-permute-done.17 = bf16[128,512]{1,0:T(8,128)(2,1)S(1)} collective-permute-done((bf16[128,512]{1,0:T(8,128)(2,1)S(1)}, bf16[128,512]{1,0:T(8,128)(2,1)S(1)}, u32[]{:S(2)}, u32[]{:S(2)}) %collective-permute-start.17) | collective-permute-done | bytes 131104 | tf_op jit(solution)/shard_map/ppermute | solution.py:267
  183.9 1.6 collective-permute-start.20
  185.5 6.6 %collective-permute-done.19.b2 = bf16[8,64,256]{2,1,0:T(8,128)(2,1)S(1)} collective-permute-done((bf16[8,64,256]{2,1,0:T(8,128)(2,1)S(1)}, bf16[8,64,256]{2,1,0:T(8,128)(2,1)S(1)}, u32[]{:S(2)}, u32[]{:S(2)}) %collective-permute-start.19) | collective-permute-done | bytes 262176 | tf_op jit(solution)/shard_map/ppermute | solution.py:279
  192.1 1.2 collective-permute-done.20.b3
  193.3 0.7 copy-done.14
  194.0 2.7 %spread.1 = f32[512,1024]{1,0:T(8,128)} custom-call(bf16[8,64,256]{2,1,0:T(8,128)(2,1)} %copy-done.5, bf16[8,64,256]{2,1,0:T(8,128)(2,1)} %copy-done.9, bf16[8,64,256]{2,1,0:T(8,128)(2,1)} %copy-done.13, bf16[8,64,256]{2,1,0:T(8,128)(2,1)} %copy-done.14), custom_call_target="tpu_custom_call" | custom-call | tf_op jit(solution)/shard_map/spread/pallas_call | solution.py:47
  196.7 0.8 copy-done.6
  197.5 2.7 %join.1 = f32[1024,512]{1,0:T(8,128)} custom-call(bf16[4,128,512]{2,1,0:T(8,128)(2,1)} %copy-done.2, bf16[4,128,512]{2,1,0:T(8,128)(2,1)} %copy-done.6), custom_call_target="tpu_custom_call" | custom-call | tf_op jit(solution)/shard_map/join/pallas_call | solution.py:47
  (74 shorter events, 3.7 us)
Async XLA Ops:
  3.9 3.2 %collective-permute-start = (bf16[4,128,1024]{2,1,0:T(8,128)(2,1)}, bf16[4,128,1024]{2,1,0:T(8,128)(2,1)S(1)}, u32[]{:S(2)}, u32[]{:S(2)}) collective-permute-start(bf16[4,128,1024]{2,1,0:T(8,128)(2,1)} %project.3), channel_id=1, source_target_pairs={{0,32},{32,0},{64,96},{96,64},{128,160},{160,128},{192,224},{224,1... | collective-permute-start | bytes 3145736 | tf_op jit(solution)/shard_map/ppermute | solution.py:273
  7.1 3.3 %copy-start.15 = (s32[1,128,10]{1,0,2:T(1,128)S(1)}, s32[1,128,10]{1,0,2:T(1,128)}, u32[]{:S(2)}) copy-start(s32[1,128,10]{1,0,2:T(1,128)} %param.10) | copy-start | bytes 15364
  7.1 10.4 %copy-start.1 = (bf16[4,128,1024]{2,1,0:T(8,128)(2,1)}, bf16[4,128,1024]{2,1,0:T(8,128)(2,1)S(1)}, u32[]{:S(2)}) copy-start(bf16[4,128,1024]{2,1,0:T(8,128)(2,1)S(1)} %collective-permute-done.got) | copy-start | bytes 3145732
  8.7 7.7 %collective-permute-start.1 = (bf16[128,1024]{1,0:T(8,128)(2,1)S(1)}, bf16[128,1024]{1,0:T(8,128)(2,1)S(1)}, u32[]{:S(2)}, u32[]{:S(2)}) collective-permute-start(bf16[128,1024]{1,0:T(8,128)(2,1)S(1)} %get-tuple-element.68), channel_id=1, source_target_pairs={{0,64},{32,224},{64,128},{96,32},{128,192},{160,96},{192,0},{224,1... | collective-permute-start | bytes 786440 | tf_op jit(solution)/shard_map/ppermute | solution.py:267
  17.4 9.3 %collective-permute-start.2 = (bf16[128,1024]{1,0:T(8,128)(2,1)S(1)}, bf16[128,1024]{1,0:T(8,128)(2,1)S(1)}, u32[]{:S(2)}, u32[]{:S(2)}) collective-permute-start(bf16[128,1024]{1,0:T(8,128)(2,1)S(1)} %fusion.3), channel_id=1, source_target_pairs={{0,64},{32,224},{64,128},{96,32},{128,192},{160,96},{192,0},{224,1... | collective-permute-start | bytes 786440 | tf_op jit(solution)/shard_map/ppermute | solution.py:267
  17.9 8.9 %collective-permute-start.3 = (bf16[128,1024]{1,0:T(8,128)(2,1)S(1)}, bf16[128,1024]{1,0:T(8,128)(2,1)S(1)}, u32[]{:S(2)}, u32[]{:S(2)}) collective-permute-start(bf16[128,1024]{1,0:T(8,128)(2,1)S(1)} %get-tuple-element.67), channel_id=1, source_target_pairs={{0,192},{32,96},{64,0},{96,160},{128,64},{160,224},{192,128},{224,... | collective-permute-start | bytes 786440 | tf_op jit(solution)/shard_map/ppermute | solution.py:270
  26.8 0.7 copy-start.11
  26.8 0.8 copy-start.12
  30.2 1.9 collective-permute-start.4
  32.1 28.9 %copy-start.16 = (f32[8,128]{1,0:T(8,128)}, f32[8,128]{1,0:T(8,128)S(1)}, u32[]{:S(2)}) copy-start(f32[8,128]{1,0:T(8,128)S(1)} %collective-permute-done.4.mark) | copy-start | bytes 12292
  65.2 17.9 %copy-start.10 = (bf16[2,128,512]{2,1,0:T(8,128)(2,1)S(1)}, bf16[2,128,512]{2,1,0:T(8,128)(2,1)}, u32[]{:S(2)}) copy-start(bf16[2,128,512]{2,1,0:T(8,128)(2,1)} %get-tuple-element.52) | copy-start | bytes 786436
  65.2 22.0 %all-to-all-start.1 = ((bf16[32,16,512]{2,1,0:T(8,128)(2,1)}), bf16[32,16,512]{2,1,0:T(8,128)(2,1)S(1)}, u32[]{:S(2)}, u32[]{:S(2)}) async-start(bf16[32,16,512]{2,1,0:T(8,128)(2,1)} %bitcast.42), calls=%async_computation.1 | async-start | bytes 1048576 | tf_op jit(solution)/shard_map/all_to_all | solution.py:55
  70.6 12.5 %collective-permute-start.5 = (bf16[3,128,512]{2,1,0:T(8,128)(2,1)}, bf16[3,128,512]{2,1,0:T(8,128)(2,1)S(1)}, u32[]{:S(2)}, u32[]{:S(2)}) collective-permute-start(bf16[3,128,512]{2,1,0:T(8,128)(2,1)} %get-tuple-element.50), channel_id=1, source_target_pairs={{0,64},{32,224},{64,128},{96,32},{128,192},{160,96},{192,0},{224,1... | collective-permute-start | bytes 1179656 | tf_op jit(solution)/shard_map/ppermute | solution.py:267
  70.7 19.4 %collective-permute-start.6 = (bf16[3,128,512]{2,1,0:T(8,128)(2,1)}, bf16[3,128,512]{2,1,0:T(8,128)(2,1)S(1)}, u32[]{:S(2)}, u32[]{:S(2)}) collective-permute-start(bf16[3,128,512]{2,1,0:T(8,128)(2,1)} %get-tuple-element.51), channel_id=1, source_target_pairs={{0,192},{32,96},{64,0},{96,160},{128,64},{160,224},{192,128},{224,... | collective-permute-start | bytes 1179656 | tf_op jit(solution)/shard_map/ppermute | solution.py:270
  83.2 16.4 %copy-start.8 = (bf16[2,128,512]{2,1,0:T(8,128)(2,1)S(1)}, bf16[2,128,512]{2,1,0:T(8,128)(2,1)}, u32[]{:S(2)}) copy-start(bf16[2,128,512]{2,1,0:T(8,128)(2,1)} %get-tuple-element.57) | copy-start | bytes 786436
  87.3 0.8 copy-start
  87.3 11.5 %collective-permute-start.7 = (bf16[3,128,512]{2,1,0:T(8,128)(2,1)S(1)}, bf16[3,128,512]{2,1,0:T(8,128)(2,1)S(1)}, u32[]{:S(2)}, u32[]{:S(2)}) collective-permute-start(bf16[3,128,512]{2,1,0:T(8,128)(2,1)S(1)} %pad_maximum_fusion.1), channel_id=1, source_target_pairs={{0,64},{32,224},{64,128},{96,32},{128,192},{160,96},{192,0},{224,1... | collective-permute-start | bytes 1179656 | tf_op jit(solution)/shard_map/ppermute | solution.py:267
  90.1 8.6 %collective-permute-start.8 = (bf16[128,512]{1,0:T(8,128)(2,1)}, bf16[128,512]{1,0:T(8,128)(2,1)S(1)}, u32[]{:S(2)}, u32[]{:S(2)}) collective-permute-start(bf16[128,512]{1,0:T(8,128)(2,1)} %near.1), channel_id=1, source_target_pairs={{0,64},{32,224},{64,128},{96,32},{128,192},{160,96},{192,0},{224,1... | collective-permute-start | bytes 393224 | tf_op jit(solution)/shard_map/ppermute | solution.py:267
  90.2 9.6 %collective-permute-start.9 = (bf16[128,512]{1,0:T(8,128)(2,1)}, bf16[128,512]{1,0:T(8,128)(2,1)S(1)}, u32[]{:S(2)}, u32[]{:S(2)}) collective-permute-start(bf16[128,512]{1,0:T(8,128)(2,1)} %near.1), channel_id=1, source_target_pairs={{0,192},{32,96},{64,0},{96,160},{128,64},{160,224},{192,128},{224,... | collective-permute-start | bytes 393224 | tf_op jit(solution)/shard_map/ppermute | solution.py:270
  98.7 6.2 %collective-permute-start.10 = (bf16[128,512]{1,0:T(8,128)(2,1)S(1)}, bf16[128,512]{1,0:T(8,128)(2,1)S(1)}, u32[]{:S(2)}, u32[]{:S(2)}) collective-permute-start(bf16[128,512]{1,0:T(8,128)(2,1)S(1)} %collective-permute-done.8), channel_id=1, source_target_pairs={{0,64},{32,224},{64,128},{96,32},{128,192},{160,96},{192,0},{224,1... | collective-permute-start | bytes 393224 | tf_op jit(solution)/shard_map/ppermute | solution.py:267
  104.9 2.9 %copy-start.3 = (bf16[9,128,512]{2,1,0:T(8,128)(2,1)}, bf16[9,128,512]{2,1,0:T(8,128)(2,1)S(1)}, u32[]{:S(2)}) copy-start(bf16[9,128,512]{2,1,0:T(8,128)(2,1)S(1)} %fusion.6.held) | copy-start | bytes 3538948
  105.0 2.9 %collective-permute-start.11 = (bf16[9,128,512]{2,1,0:T(8,128)(2,1)S(1)}, bf16[9,128,512]{2,1,0:T(8,128)(2,1)S(1)}, u32[]{:S(2)}, u32[]{:S(2)}) collective-permute-start(bf16[9,128,512]{2,1,0:T(8,128)(2,1)S(1)} %fusion.6.held), channel_id=1, source_target_pairs={{0,32},{32,0},{64,96},{96,64},{128,160},{160,128},{192,224},{224,1... | collective-permute-start | bytes 3538952 | tf_op jit(solution)/shard_map/ppermute | solution.py:273
  107.9 1.0 copy-start.4
  113.5 10.4 %copy-start.17 = (bf16[8,96,256]{2,1,0:T(8,128)(2,1)S(1)}, bf16[8,96,256]{2,1,0:T(8,128)(2,1)}, u32[]{:S(2)}) copy-start(bf16[8,96,256]{2,1,0:T(8,128)(2,1)} %get-tuple-element.63) | copy-start | bytes 1179652
  113.5 9.2 %collective-permute-start.12 = (bf16[8,96,256]{2,1,0:T(8,128)(2,1)}, bf16[8,96,256]{2,1,0:T(8,128)(2,1)S(1)}, u32[]{:S(2)}, u32[]{:S(2)}) collective-permute-start(bf16[8,96,256]{2,1,0:T(8,128)(2,1)} %get-tuple-element.59), channel_id=1, source_target_pairs={{0,1},{1,2},{2,3},{3,0},{4,5},{5,6},{6,7},{7,4},{8,9},{9,10},{10,1... | collective-permute-start | bytes 1179656 | tf_op jit(solution)/shard_map/ppermute | solution.py:276
  123.8 12.7 %copy-start.7 = (bf16[8,96,256]{2,1,0:T(8,128)(2,1)S(1)}, bf16[8,96,256]{2,1,0:T(8,128)(2,1)}, u32[]{:S(2)}) copy-start(bf16[8,96,256]{2,1,0:T(8,128)(2,1)} %get-tuple-element.62) | copy-start | bytes 1179652
  123.8 12.7 %collective-permute-start.13 = (bf16[8,96,256]{2,1,0:T(8,128)(2,1)S(1)}, bf16[8,96,256]{2,1,0:T(8,128)(2,1)S(1)}, u32[]{:S(2)}, u32[]{:S(2)}) collective-permute-start(bf16[8,96,256]{2,1,0:T(8,128)(2,1)S(1)} %fusion), channel_id=1, source_target_pairs={{0,1},{1,2},{2,3},{3,0},{4,5},{5,6},{6,7},{7,4},{8,9},{9,10},{10,1... | collective-permute-start | bytes 1179656 | tf_op jit(solution)/shard_map/ppermute | solution.py:276
  123.9 12.6 %collective-permute-start.14 = (bf16[8,96,256]{2,1,0:T(8,128)(2,1)S(1)}, bf16[8,96,256]{2,1,0:T(8,128)(2,1)S(1)}, u32[]{:S(2)}, u32[]{:S(2)}) collective-permute-start(bf16[8,96,256]{2,1,0:T(8,128)(2,1)S(1)} %copy-done.17), channel_id=1, source_target_pairs={{0,3},{1,0},{2,1},{3,2},{4,7},{5,4},{6,5},{7,6},{8,11},{9,8},{10,9... | collective-permute-start | bytes 1179656 | tf_op jit(solution)/shard_map/ppermute | solution.py:279
  170.7 6.3 %collective-permute-start.15 = (bf16[128,512]{1,0:T(8,128)(2,1)S(1)}, bf16[128,512]{1,0:T(8,128)(2,1)S(1)}, u32[]{:S(2)}, u32[]{:S(2)}) collective-permute-start(bf16[128,512]{1,0:T(8,128)(2,1)S(1)} %get-tuple-element.74), channel_id=1, source_target_pairs={{0,64},{32,224},{64,128},{96,32},{128,192},{160,96},{192,0},{224,1... | collective-permute-start | bytes 393224 | tf_op jit(solution)/shard_map/ppermute | solution.py:267
  170.8 22.4 %copy-start.5 = (bf16[8,64,256]{2,1,0:T(8,128)(2,1)}, bf16[8,64,256]{2,1,0:T(8,128)(2,1)S(1)}, u32[]{:S(2)}) copy-start(bf16[8,64,256]{2,1,0:T(8,128)(2,1)S(1)} %slice.88.b0) | copy-start | bytes 786436
  170.9 12.4 %collective-permute-start.18 = (bf16[8,64,256]{2,1,0:T(8,128)(2,1)S(1)}, bf16[8,64,256]{2,1,0:T(8,128)(2,1)S(1)}, u32[]{:S(2)}, u32[]{:S(2)}) collective-permute-start(bf16[8,64,256]{2,1,0:T(8,128)(2,1)S(1)} %slice.88.b0), channel_id=1, source_target_pairs={{0,1},{1,2},{2,3},{3,0},{4,5},{5,6},{6,7},{7,4},{8,9},{9,10},{10,1... | collective-permute-start | bytes 786440 | tf_op jit(solution)/shard_map/ppermute | solution.py:276
  171.0 6.0 %collective-permute-start.16 = (bf16[128,512]{1,0:T(8,128)(2,1)S(1)}, bf16[128,512]{1,0:T(8,128)(2,1)S(1)}, u32[]{:S(2)}, u32[]{:S(2)}) collective-permute-start(bf16[128,512]{1,0:T(8,128)(2,1)S(1)} %get-tuple-element.74), channel_id=1, source_target_pairs={{0,192},{32,96},{64,0},{96,160},{128,64},{160,224},{192,128},{224,... | collective-permute-start | bytes 393224 | tf_op jit(solution)/shard_map/ppermute | solution.py:270
  177.0 6.2 %collective-permute-start.17 = (bf16[128,512]{1,0:T(8,128)(2,1)S(1)}, bf16[128,512]{1,0:T(8,128)(2,1)S(1)}, u32[]{:S(2)}, u32[]{:S(2)}) collective-permute-start(bf16[128,512]{1,0:T(8,128)(2,1)S(1)} %collective-permute-done.15), channel_id=1, source_target_pairs={{0,64},{32,224},{64,128},{96,32},{128,192},{160,96},{192,0},{224,1... | collective-permute-start | bytes 393224 | tf_op jit(solution)/shard_map/ppermute | solution.py:267
  183.2 13.4 %copy-start.2 = (bf16[4,128,512]{2,1,0:T(8,128)(2,1)}, bf16[4,128,512]{2,1,0:T(8,128)(2,1)S(1)}, u32[]{:S(2)}) copy-start(bf16[4,128,512]{2,1,0:T(8,128)(2,1)S(1)} %pad_maximum_fusion.held) | copy-start | bytes 1572868
  183.3 10.0 %copy-start.9 = (bf16[8,64,256]{2,1,0:T(8,128)(2,1)}, bf16[8,64,256]{2,1,0:T(8,128)(2,1)S(1)}, u32[]{:S(2)}) copy-start(bf16[8,64,256]{2,1,0:T(8,128)(2,1)S(1)} %collective-permute-done.18.b1) | copy-start | bytes 786436
  183.3 13.4 %collective-permute-start.21 = (bf16[4,128,512]{2,1,0:T(8,128)(2,1)S(1)}, bf16[4,128,512]{2,1,0:T(8,128)(2,1)S(1)}, u32[]{:S(2)}, u32[]{:S(2)}) collective-permute-start(bf16[4,128,512]{2,1,0:T(8,128)(2,1)S(1)} %pad_maximum_fusion.held), channel_id=1, source_target_pairs={{0,32},{32,0},{64,96},{96,64},{128,160},{160,128},{192,224},{224,1... | collective-permute-start | bytes 1572872 | tf_op jit(solution)/shard_map/ppermute | solution.py:273
  183.4 8.7 %collective-permute-start.19 = (bf16[8,64,256]{2,1,0:T(8,128)(2,1)S(1)}, bf16[8,64,256]{2,1,0:T(8,128)(2,1)S(1)}, u32[]{:S(2)}, u32[]{:S(2)}) collective-permute-start(bf16[8,64,256]{2,1,0:T(8,128)(2,1)S(1)} %slice.88.b0), channel_id=1, source_target_pairs={{0,3},{1,0},{2,1},{3,2},{4,7},{5,4},{6,5},{7,6},{8,11},{9,8},{10,9... | collective-permute-start | bytes 786440 | tf_op jit(solution)/shard_map/ppermute | solution.py:279
  183.9 9.4 %collective-permute-start.20 = (bf16[8,64,256]{2,1,0:T(8,128)(2,1)S(1)}, bf16[8,64,256]{2,1,0:T(8,128)(2,1)S(1)}, u32[]{:S(2)}, u32[]{:S(2)}) collective-permute-start(bf16[8,64,256]{2,1,0:T(8,128)(2,1)S(1)} %collective-permute-done.18.b1), channel_id=1, source_target_pairs={{0,1},{1,2},{2,3},{3,0},{4,5},{5,6},{6,7},{7,4},{8,9},{9,10},{10,1... | collective-permute-start | bytes 786440 | tf_op jit(solution)/shard_map/ppermute | solution.py:276
  192.1 1.2 copy-start.13
  193.3 0.7 copy-start.14
  196.7 0.8 copy-start.6

commit v7 on v6

--- a/solution.py
+++ b/solution.py
@@ -43,8 +43,22 @@
     return lax.dot_general(a, b, dims, preferred_element_type=F32)
 
 
-def whole(name, body, outs, *args, scratch=()):
-    return pl.pallas_call(body, out_shape=outs, scratch_shapes=scratch, name=name)(*args)
+def whole(name, body, outs, *args, scratch=(), last=False):
+    many = isinstance(outs, tuple)
+    outs = list(outs) if many else [outs]
+    place = pl.BlockSpec(memory_space=pltpu.VMEM)
+    if not last:
+        outs = [pltpu.VMEM(o.shape, o.dtype) for o in outs]
+    got = pl.pallas_call(
+        body,
+        out_shape=outs,
+        in_specs=[place] * len(args),
+        out_specs=[pl.BlockSpec() if last else place] * len(outs),
+        scratch_shapes=scratch,
+        name=name,
+        compiler_params=pltpu.CompilerParams(vmem_limit_bytes=16 << 20),
+    )(*[pltpu.with_memory_space_constraint(a, pltpu.VMEM) for a in args])
+    return tuple(got) if many else got[0]
 
 
 def shape(dims, kind=BF16):
@@ -143,11 +157,10 @@
     return total
 
 
-def forward_body(part, got, near, far, grads, inv, give, p_self, p_near, boxes, mark):
+def forward_body(part, got, near, far, grads, inv, give, p_self, p_near, boxes):
     width = grads.shape[1]
-    total = add(part[0], got[0], near[...], far[...])
+    total = add(part[3], got[3], near[...], far[...])
     p_self[...] = total[:, :width]
-    mark[...] = total[:8, :128]
     mine = total[:, width:].astype(BF16)
     p_near[...] = mine
     scaled = (grads[...].astype(F32) * inv[:, :1]).astype(BF16)
@@ -155,7 +168,7 @@
 
 
 def middle_body(
-    recv, p_self, p_near, grads, inv, w_two, give, take, own, own_t, mark,
+    recv, p_self, p_near, grads, inv, w_two, give, take, own, own_t,
     boxes, near_local, hidden_out, ahead, behind, third, mine, scratch,
 ):
     nodes, width = grads.shape
@@ -305,24 +318,12 @@
     far, flat_t = lax.optimization_barrier((far, flat_t))
     block = shape((nodes, width))
 
-    def full(*dims):
-        return pl.BlockSpec(dims, lambda i: (0,) * len(dims))
-
-    last = pl.BlockSpec((1, nodes, 2 * width), lambda i: (CHIPS - 1, 0, 0))
-    p_self, p_near, boxes, mark = pl.pallas_call(
+    p_self, p_near, boxes = whole(
+        "forward",
         forward_body,
-        out_shape=(
-            shape((nodes, width), F32), block, shape((span, width)), shape((8, 128), F32)
-        ),
-        grid=(1,),
-        in_specs=[
-            last, last, full(nodes, 2 * width), full(nodes, 2 * width), full(nodes, width),
-            full(nodes, nodes), full(span, 2 * nodes),
-        ],
-        out_specs=(full(nodes, width), full(nodes, width), full(span, width), full(8, 128)),
-        name="forward",
-    )(mine, got, near, far, grads, inv, give)
-    boxes, mark = lax.optimization_barrier((boxes, swap(mark)))
+        (shape((nodes, width), F32), block, shape((span, width))),
+        mine, got, near, far, grads, inv, give,
+    )
     recv = trade(boxes.reshape(parts, 2 * kmax, width)).reshape(span, width)
     rows = 2 * width // groups
     boxes, near_local, hidden, ahead, behind, third, mine = whole(
@@ -337,7 +338,7 @@
             shape((2, rows, width)),
             shape((2, rows, width)),
         ),
-        recv, p_self, p_near, grads, inv, w_two, give, take, own, own_t, mark,
+        recv, p_self, p_near, grads, inv, w_two, give, take, own, own_t,
         scratch=[pltpu.VMEM((groups, rows, width), BF16)],
     )
     recv = trade(boxes.reshape(parts, 2 * kmax, width)).reshape(span, width)
@@ -368,7 +369,7 @@
             pltpu.VMEM((CHIPS, deep, kept, width // 2), BF16),
         ],
     )
-    out = whole("out", out_body, block, recv, hidden, inv, take, own, w_two)
+    out = whole("out", out_body, block, recv, hidden, inv, take, own, w_two, last=True)
     relay = x_forward(ahead)
     near = x_backward(behind)
     far = x_forward(add(third, relay).astype(BF16))
@@ -391,8 +392,8 @@
     near = x_backward(mine)
     held, relay = lax.optimization_barrier((gather(chunk), relay))
     far = x_forward(relay)
-    one = whole("spread", spread_body, shape((cols, 2 * width), F32), mine, relay, near, far)
-    two = whole("join", join_body, shape((2 * width, width), F32), held, swap(held))
+    one = whole("spread", spread_body, shape((cols, 2 * width), F32), mine, relay, near, far, last=True)
+    two = whole("join", join_body, shape((2 * width, width), F32), held, swap(held), last=True)
     return out[None], one, two
 
 

time: 203 us -> 185 us (0.911)
  Pallas kernels: 32.6 us -> 10.5 us
  waiting for transfers between devices: 64.3 us -> 71.1 us
    pallas_call x11, Pallas kernels: 32.6 us -> 10.5 us  [whole(): pl.pallas_call(body, out_shape=outs, in_specs=[place] * len(args), out_sp...]
    ppermute x8, waiting for transfers between devices: 34.3 us -> 37.9 us  [forward(): return lax.ppermute(block, 'feat', y_ahead)]
    unnamed x44 -> x38, local copies, waits for them, and re-layouts: 6.67 us -> 8.81 us
    ppermute x4 -> x3, waiting for transfers between devices: 3.02 us -> 4.69 us  [swap(): return lax.ppermute(block, 'feat', SWAP)]
  transfers between devices with their start and end apart: 23 -> 22, of which waited for: 14 -> 14; matrix products, arithmetic and copies ran while one was open for 2% -> 3% of each run, Pallas kernels for 8% -> 2%
where the time goes in v7:
time: 185 us; the launch traced here: 183 us
  waiting for transfers between devices  71.1 us (38%)
  blocking collectives  62.1 us (34%)
  starting transfers between devices  25.9 us (14%)
  Pallas kernels  10.5 us (6%)
  local copies, waits for them, and re-layouts  9.58 us (5%)
  other arithmetic  2.72 us (1%)
    all_to_all x3, blocking collectives, trade(): lax.all_to_all(boxes, 'dom', split_axis=0, concat_axis=0, axis_index_grou...  62.1 us
    ppermute x8, waiting for transfers between devices, forward(): return lax.ppermute(block, 'feat', y_ahead)  37.9 us
    ppermute x4, waiting for transfers between devices, x_forward(): return lax.ppermute(block, ('feat', 'dom'), x_ahead)  18.1 us
    ppermute x4, starting transfers between devices, backward(): return lax.ppermute(block, 'feat', y_behind)  11.8 us
    pallas_call x11, Pallas kernels, whole(): pl.pallas_call(body, out_shape=outs, in_specs=[place] * len(args), out_sp...  10.5 us
    unnamed x38, local copies, waits for them, and re-layouts  8.81 us
    ppermute x2, waiting for transfers between devices, x_backward(): return lax.ppermute(block, ('feat', 'dom'), x_behind)  6.62 us
    all_to_all x1, starting transfers between devices, trade(): lax.all_to_all(boxes, 'dom', split_axis=0, concat_axis=0, axis_index_grou...  5.53 us
  transfers between devices with their start and end apart: 22, of which 14 were waited for; matrix products, arithmetic and copies ran while one was open for 3% of the time, Pallas kernels for 2%

profile of v7, /device:TPU:32, one launch (start us, length us, event | category | flops | bytes accessed | tf_op | source)
XLA Modules:
  0.0 183.0 jit_solution(5525814348087888724)
XLA Ops:
  0.6 1.2 copy-done
  1.9 1.2 copy-done.2
  3.1 0.7 project.3
  3.9 0.7 project.2.part
  4.7 1.9 %collective-permute-done.got = bf16[4,128,1024]{2,1,0:T(8,128)(2,1)S(1)} collective-permute-done((bf16[4,128,1024]{2,1,0:T(8,128)(2,1)S(1)}, bf16[4,128,1024]{2,1,0:T(8,128)(2,1)S(1)}, u32[]{:S(2)}, u32[]{:S(2)}) %collective-permute-start) | collective-permute-done | bytes 1048608 | tf_op jit(solution)/shard_map/ppermute | solution.py:286
  6.7 1.7 collective-permute-start.1
  8.4 0.6 tables.1
  9.0 5.4 %collective-permute-done.1 = bf16[128,1024]{1,0:T(8,128)(2,1)S(1)} collective-permute-done((bf16[128,1024]{1,0:T(8,128)(2,1)S(1)}, bf16[128,1024]{1,0:T(8,128)(2,1)S(1)}, u32[]{:S(2)}, u32[]{:S(2)}) %collective-permute-start.1) | collective-permute-done | bytes 262176 | tf_op jit(solution)/shard_map/ppermute | solution.py:280
  15.0 2.9 %collective-permute-start.3 = (bf16[128,1024]{1,0:T(8,128)(2,1)S(1)}, bf16[128,1024]{1,0:T(8,128)(2,1)S(1)}, u32[]{:S(2)}, u32[]{:S(2)}) collective-permute-start(bf16[128,1024]{1,0:T(8,128)(2,1)S(1)} %get-tuple-element.61), channel_id=1, source_target_pairs={{0,192},{32,96},{64,0},{96,160},{128,64},{160,224},{192,128},{224,... | collective-permute-start | bytes 786440 | tf_op jit(solution)/shard_map/ppermute | solution.py:283
  18.2 6.1 %collective-permute-done.2.far = bf16[128,1024]{1,0:T(8,128)(2,1)S(1)} collective-permute-done((bf16[128,1024]{1,0:T(8,128)(2,1)S(1)}, bf16[128,1024]{1,0:T(8,128)(2,1)S(1)}, u32[]{:S(2)}, u32[]{:S(2)}) %collective-permute-start.2) | collective-permute-done | bytes 262176 | tf_op jit(solution)/shard_map/ppermute | solution.py:280
  24.3 0.4 forward.1
  24.8 28.7 %all_to_all.20 = bf16[32,16,512]{2,1,0:T(8,128)(2,1)S(1)} all-to-all(bf16[32,16,512]{2,1,0:T(8,128)(2,1)S(1)} %bitcast.42), channel_id=1, replica_groups=mesh['feat'=8,'dom'=32] {'dom'}, dimensions={0} | all-to-all | bytes 1048576 | tf_op jit(solution)/shard_map/all_to_all | solution.py:69
  53.5 1.9 %middle.1 = (bf16[512,512]{1,0:T(8,128)(2,1)}, f32[128,512]{1,0:T(8,128)S(1)}, bf16[128,512]{1,0:T(8,128)(2,1)S(1)}, bf16[3,128,512]{2,1,0:T(8,128)(2,1)S(1)}, b...) custom-call(bf16[512,512]{1,0:T(8,128)(2,1)S(1)} %bitcast.41, ...), custom_call_target="tpu_custom_call" | custom-call | tf_op jit(solution)/shard_map/middle/pallas_call | solution.py:52
  55.3 0.7 copy-done.6
  56.0 0.7 copy-done.8
  56.7 0.7 copy-done.10
  57.4 0.8 copy-done.13
  58.2 5.5 %all-to-all-start.1 = ((bf16[32,16,512]{2,1,0:T(8,128)(2,1)}), bf16[32,16,512]{2,1,0:T(8,128)(2,1)S(1)}, u32[]{:S(2)}, u32[]{:S(2)}) async-start(bf16[32,16,512]{2,1,0:T(8,128)(2,1)} %bitcast.9), calls=%async_computation.1 | async-start | bytes 1048576 | tf_op jit(solution)/shard_map/all_to_all | solution.py:69
  63.8 3.2 %collective-permute-start.5 = (bf16[3,128,512]{2,1,0:T(8,128)(2,1)}, bf16[3,128,512]{2,1,0:T(8,128)(2,1)}, u32[]{:S(2)}, u32[]{:S(2)}) collective-permute-start(bf16[3,128,512]{2,1,0:T(8,128)(2,1)} %copy-done.13), channel_id=1, source_target_pairs={{0,192},{32,96},{64,0},{96,160},{128,64},{160,224},{192,128},{224,... | collective-permute-start | bytes 1179656 | tf_op jit(solution)/shard_map/ppermute | solution.py:283
  67.0 1.6 slice_dynamic-update-slice_fusion.2
  68.6 6.4 %collective-permute-done.4 = bf16[3,128,512]{2,1,0:T(8,128)(2,1)S(1)} collective-permute-done((bf16[3,128,512]{2,1,0:T(8,128)(2,1)}, bf16[3,128,512]{2,1,0:T(8,128)(2,1)S(1)}, u32[]{:S(2)}, u32[]{:S(2)}) %collective-permute-start.4) | collective-permute-done | bytes 393248 | tf_op jit(solution)/shard_map/ppermute | solution.py:280
  75.1 0.7 fusion.9
  75.8 0.8 pad_maximum_fusion.1
  76.6 3.8 %all-to-all-done.1 = bf16[32,16,512]{2,1,0:T(8,128)(2,1)S(1)} async-done(((bf16[32,16,512]{2,1,0:T(8,128)(2,1)}), bf16[32,16,512]{2,1,0:T(8,128)(2,1)S(1)}, u32[]{:S(2)}, u32[]{:S(2)}) %all-to-all-start.1) | async-done | bytes 524320 | tf_op jit(solution)/shard_map/all_to_all | solution.py:69
  80.7 0.9 copy-done.4
  81.7 0.9 slice_dynamic-update-slice_fusion.1
  82.6 2.4 %collective-permute-start.8 = (bf16[128,512]{1,0:T(8,128)(2,1)S(1)}, bf16[128,512]{1,0:T(8,128)(2,1)S(1)}, u32[]{:S(2)}, u32[]{:S(2)}) collective-permute-start(bf16[128,512]{1,0:T(8,128)(2,1)S(1)} %near.1), channel_id=1, source_target_pairs={{0,192},{32,96},{64,0},{96,160},{128,64},{160,224},{192,128},{224,... | collective-permute-start | bytes 393224 | tf_op jit(solution)/shard_map/ppermute | solution.py:283
  85.0 6.0 %collective-permute-done.7 = bf16[128,512]{1,0:T(8,128)(2,1)S(1)} collective-permute-done((bf16[128,512]{1,0:T(8,128)(2,1)S(1)}, bf16[128,512]{1,0:T(8,128)(2,1)S(1)}, u32[]{:S(2)}, u32[]{:S(2)}) %collective-permute-start.7) | collective-permute-done | bytes 131104 | tf_op jit(solution)/shard_map/ppermute | solution.py:280
  91.0 1.0 convert_add_fusion.1
  92.1 5.0 %collective-permute-done.9 = bf16[128,512]{1,0:T(8,128)(2,1)S(1)} collective-permute-done((bf16[128,512]{1,0:T(8,128)(2,1)S(1)}, bf16[128,512]{1,0:T(8,128)(2,1)S(1)}, u32[]{:S(2)}, u32[]{:S(2)}) %collective-permute-start.9) | collective-permute-done | bytes 131104 | tf_op jit(solution)/shard_map/ppermute | solution.py:280
  97.4 2.8 %collective-permute-done.10.other = bf16[9,128,512]{2,1,0:T(8,128)(2,1)S(1)} collective-permute-done((bf16[9,128,512]{2,1,0:T(8,128)(2,1)S(1)}, bf16[9,128,512]{2,1,0:T(8,128)(2,1)S(1)}, u32[]{:S(2)}, u32[]{:S(2)}) %collective-permute-start.10) | collective-permute-done | bytes 1179680 | tf_op jit(solution)/shard_map/ppermute | solution.py:286
  100.2 1.5 grad.1
  101.7 0.5 collective-permute-start.11
  102.2 8.6 %collective-permute-done.11 = bf16[8,96,256]{2,1,0:T(8,128)(2,1)S(1)} collective-permute-done((bf16[8,96,256]{2,1,0:T(8,128)(2,1)S(1)}, bf16[8,96,256]{2,1,0:T(8,128)(2,1)S(1)}, u32[]{:S(2)}, u32[]{:S(2)}) %collective-permute-start.11) | collective-permute-done | bytes 393248 | tf_op jit(solution)/shard_map/ppermute | solution.py:289
  111.0 3.2 %collective-permute-start.13 = (bf16[8,96,256]{2,1,0:T(8,128)(2,1)S(1)}, bf16[8,96,256]{2,1,0:T(8,128)(2,1)S(1)}, u32[]{:S(2)}, u32[]{:S(2)}) collective-permute-start(bf16[8,96,256]{2,1,0:T(8,128)(2,1)S(1)} %get-tuple-element.57), channel_id=1, source_target_pairs={{0,3},{1,0},{2,1},{3,2},{4,7},{5,4},{6,5},{7,6},{8,11},{9,8},{10,9... | collective-permute-start | bytes 1179656 | tf_op jit(solution)/shard_map/ppermute | solution.py:292
  114.2 1.2 out.1
  115.4 8.3 %collective-permute-done.12 = bf16[8,96,256]{2,1,0:T(8,128)(2,1)S(1)} collective-permute-done((bf16[8,96,256]{2,1,0:T(8,128)(2,1)S(1)}, bf16[8,96,256]{2,1,0:T(8,128)(2,1)S(1)}, u32[]{:S(2)}, u32[]{:S(2)}) %collective-permute-start.12) | collective-permute-done | bytes 393248 | tf_op jit(solution)/shard_map/ppermute | solution.py:289
  123.9 17.4 %all_to_all.21 = bf16[8,96,256]{2,1,0:T(8,128)(2,1)S(1)} all-to-all(bf16[8,96,256]{2,1,0:T(8,128)(2,1)S(1)} %fusion.2), channel_id=1, replica_groups={{0,4,8,12,16,20,24,28},{1,5,9,13,17,21,25,29},{2,6,10,14,18,22,26,30},{..., dimensions={0} | all-to-all | bytes 786432 | tf_op jit(solution)/shard_map/all_to_all | solution.py:69
  141.4 16.0 %all_to_all.22 = bf16[8,96,256]{2,1,0:T(8,128)(2,1)S(1)} all-to-all(bf16[8,96,256]{2,1,0:T(8,128)(2,1)S(1)} %broadcast_in_dim.15), channel_id=1, replica_groups={{0,4,8,12,16,20,24,28},{1,5,9,13,17,21,25,29},{2,6,10,14,18,22,26,30},{..., dimensions={0} | all-to-all | bytes 786432 | tf_op jit(solution)/shard_map/all_to_all | solution.py:69
  157.7 3.3 %collective-permute-start.15 = (bf16[128,512]{1,0:T(8,128)(2,1)S(1)}, bf16[128,512]{1,0:T(8,128)(2,1)S(1)}, u32[]{:S(2)}, u32[]{:S(2)}) collective-permute-start(bf16[128,512]{1,0:T(8,128)(2,1)S(1)} %get-tuple-element.68), channel_id=1, source_target_pairs={{0,192},{32,96},{64,0},{96,160},{128,64},{160,224},{192,128},{224,... | collective-permute-start | bytes 393224 | tf_op jit(solution)/shard_map/ppermute | solution.py:283
  160.9 2.8 %collective-permute-done.14 = bf16[128,512]{1,0:T(8,128)(2,1)S(1)} collective-permute-done((bf16[128,512]{1,0:T(8,128)(2,1)S(1)}, bf16[128,512]{1,0:T(8,128)(2,1)S(1)}, u32[]{:S(2)}, u32[]{:S(2)}) %collective-permute-start.14) | collective-permute-done | bytes 131104 | tf_op jit(solution)/shard_map/ppermute | solution.py:280
  163.7 6.2 %collective-permute-done.16 = bf16[128,512]{1,0:T(8,128)(2,1)S(1)} collective-permute-done((bf16[128,512]{1,0:T(8,128)(2,1)S(1)}, bf16[128,512]{1,0:T(8,128)(2,1)S(1)}, u32[]{:S(2)}, u32[]{:S(2)}) %collective-permute-start.16) | collective-permute-done | bytes 131104 | tf_op jit(solution)/shard_map/ppermute | solution.py:280
  170.1 0.5 collective-permute-start.18
  170.5 1.6 collective-permute-start.19
  172.2 6.6 %collective-permute-done.18.b2 = bf16[8,64,256]{2,1,0:T(8,128)(2,1)S(1)} collective-permute-done((bf16[8,64,256]{2,1,0:T(8,128)(2,1)S(1)}, bf16[8,64,256]{2,1,0:T(8,128)(2,1)S(1)}, u32[]{:S(2)}, u32[]{:S(2)}) %collective-permute-start.18) | collective-permute-done | bytes 262176 | tf_op jit(solution)/shard_map/ppermute | solution.py:292
  178.8 1.2 collective-permute-done.19.b3
  180.0 1.5 spread.1
  181.5 1.5 join.1
  (66 shorter events, 2.9 us)
Async XLA Ops:
  0.6 1.2 copy-start
  1.9 1.2 copy-start.2
  3.8 2.7 %collective-permute-start = (bf16[4,128,1024]{2,1,0:T(8,128)(2,1)S(1)}, bf16[4,128,1024]{2,1,0:T(8,128)(2,1)S(1)}, u32[]{:S(2)}, u32[]{:S(2)}) collective-permute-start(bf16[4,128,1024]{2,1,0:T(8,128)(2,1)S(1)} %project.3), channel_id=1, source_target_pairs={{0,32},{32,0},{64,96},{96,64},{128,160},{160,128},{192,224},{224,1... | collective-permute-start | bytes 3145736 | tf_op jit(solution)/shard_map/ppermute | solution.py:286
  4.6 3.8 %copy-start.14 = (s32[1,128,10]{1,0,2:T(1,128)S(1)}, s32[1,128,10]{1,0,2:T(1,128)}, u32[]{:S(2)}) copy-start(s32[1,128,10]{1,0,2:T(1,128)} %param.10) | copy-start | bytes 15364
  4.6 3.8 %copy-start.11 = (s32[1,32,8]{1,2,0:T(8,128)S(1)}, s32[1,32,8]{1,2,0:T(8,128)}, u32[]{:S(2)}) copy-start(s32[1,32,8]{1,2,0:T(8,128)} %param.12) | copy-start | bytes 3076
  4.6 3.8 %copy-start.12 = (s32[1,128]{1,0:T(1,128)S(1)}, s32[1,128]{1,0:T(1,128)}, u32[]{:S(2)}) copy-start(s32[1,128]{1,0:T(1,128)} %deg.1) | copy-start | bytes 1540
  4.7 13.2 %copy-start.1 = (bf16[8,128,512]{2,1,0:T(8,128)(2,1)S(1)}, bf16[8,128,512]{2,1,0:T(8,128)(2,1)}, u32[]{:S(2)}) copy-start(bf16[8,128,512]{2,1,0:T(8,128)(2,1)} %flat.1) | copy-start | bytes 3145732
  6.7 7.7 %collective-permute-start.1 = (bf16[128,1024]{1,0:T(8,128)(2,1)S(1)}, bf16[128,1024]{1,0:T(8,128)(2,1)S(1)}, u32[]{:S(2)}, u32[]{:S(2)}) collective-permute-start(bf16[128,1024]{1,0:T(8,128)(2,1)S(1)} %get-tuple-element.62), channel_id=1, source_target_pairs={{0,64},{32,224},{64,128},{96,32},{128,192},{160,96},{192,0},{224,1... | collective-permute-start | bytes 786440 | tf_op jit(solution)/shard_map/ppermute | solution.py:280
  14.5 9.8 %copy-start.5 = (bf16[1,128,512]{2,1,0:T(8,128)(2,1)S(1)}, bf16[1,128,512]{2,1,0:T(8,128)(2,1)}, u32[]{:S(2)}) copy-start(bf16[1,128,512]{2,1,0:T(8,128)(2,1)} %param.13) | copy-start | bytes 393220
  14.5 9.8 %collective-permute-start.2 = (bf16[128,1024]{1,0:T(8,128)(2,1)S(1)}, bf16[128,1024]{1,0:T(8,128)(2,1)S(1)}, u32[]{:S(2)}, u32[]{:S(2)}) collective-permute-start(bf16[128,1024]{1,0:T(8,128)(2,1)S(1)} %fusion.3), channel_id=1, source_target_pairs={{0,64},{32,224},{64,128},{96,32},{128,192},{160,96},{192,0},{224,1... | collective-permute-start | bytes 786440 | tf_op jit(solution)/shard_map/ppermute | solution.py:280
  15.0 9.3 %collective-permute-start.3 = (bf16[128,1024]{1,0:T(8,128)(2,1)S(1)}, bf16[128,1024]{1,0:T(8,128)(2,1)S(1)}, u32[]{:S(2)}, u32[]{:S(2)}) collective-permute-start(bf16[128,1024]{1,0:T(8,128)(2,1)S(1)} %get-tuple-element.61), channel_id=1, source_target_pairs={{0,192},{32,96},{64,0},{96,160},{128,64},{160,224},{192,128},{224,... | collective-permute-start | bytes 786440 | tf_op jit(solution)/shard_map/ppermute | solution.py:283
  24.8 28.7 %copy-start.3 = (bf16[1024,512]{1,0:T(8,128)(2,1)S(1)}, bf16[1024,512]{1,0:T(8,128)(2,1)}, u32[]{:S(2)}) copy-start(bf16[1024,512]{1,0:T(8,128)(2,1)} %w_two.3) | copy-start | bytes 3145732
  55.3 0.7 copy-start.6
  56.0 0.7 copy-start.8
  56.7 0.7 copy-start.10
  57.4 0.8 copy-start.13
  58.2 22.2 %all-to-all-start.1 = ((bf16[32,16,512]{2,1,0:T(8,128)(2,1)}), bf16[32,16,512]{2,1,0:T(8,128)(2,1)S(1)}, u32[]{:S(2)}, u32[]{:S(2)}) async-start(bf16[32,16,512]{2,1,0:T(8,128)(2,1)} %bitcast.9), calls=%async_computation.1 | async-start | bytes 1048576 | tf_op jit(solution)/shard_map/all_to_all | solution.py:69
  63.7 11.3 %collective-permute-start.4 = (bf16[3,128,512]{2,1,0:T(8,128)(2,1)}, bf16[3,128,512]{2,1,0:T(8,128)(2,1)S(1)}, u32[]{:S(2)}, u32[]{:S(2)}) collective-permute-start(bf16[3,128,512]{2,1,0:T(8,128)(2,1)} %copy-done.10), channel_id=1, source_target_pairs={{0,64},{32,224},{64,128},{96,32},{128,192},{160,96},{192,0},{224,1... | collective-permute-start | bytes 1179656 | tf_op jit(solution)/shard_map/ppermute | solution.py:280
  63.8 16.9 %collective-permute-start.5 = (bf16[3,128,512]{2,1,0:T(8,128)(2,1)}, bf16[3,128,512]{2,1,0:T(8,128)(2,1)}, u32[]{:S(2)}, u32[]{:S(2)}) collective-permute-start(bf16[3,128,512]{2,1,0:T(8,128)(2,1)} %copy-done.13), channel_id=1, source_target_pairs={{0,192},{32,96},{64,0},{96,160},{128,64},{160,224},{192,128},{224,... | collective-permute-start | bytes 1179656 | tf_op jit(solution)/shard_map/ppermute | solution.py:283
  75.1 5.3 %copy-start.7 = (f32[128,512]{1,0:T(8,128)S(1)}, f32[128,512]{1,0:T(8,128)}, u32[]{:S(2)}) copy-start(f32[128,512]{1,0:T(8,128)} %copy-done.6) | copy-start | bytes 786436
  80.4 1.3 copy-start.4
  80.4 10.6 %collective-permute-start.6 = (bf16[3,128,512]{2,1,0:T(8,128)(2,1)}, bf16[3,128,512]{2,1,0:T(8,128)(2,1)S(1)}, u32[]{:S(2)}, u32[]{:S(2)}) collective-permute-start(bf16[3,128,512]{2,1,0:T(8,128)(2,1)} %pad_maximum_fusion.1), channel_id=1, source_target_pairs={{0,64},{32,224},{64,128},{96,32},{128,192},{160,96},{192,0},{224,1... | collective-permute-start | bytes 1179656 | tf_op jit(solution)/shard_map/ppermute | solution.py:280
  80.6 10.4 %collective-permute-start.7 = (bf16[128,512]{1,0:T(8,128)(2,1)S(1)}, bf16[128,512]{1,0:T(8,128)(2,1)S(1)}, u32[]{:S(2)}, u32[]{:S(2)}) collective-permute-start(bf16[128,512]{1,0:T(8,128)(2,1)S(1)} %near.1), channel_id=1, source_target_pairs={{0,64},{32,224},{64,128},{96,32},{128,192},{160,96},{192,0},{224,1... | collective-permute-start | bytes 393224 | tf_op jit(solution)/shard_map/ppermute | solution.py:280
  82.6 9.5 %collective-permute-start.8 = (bf16[128,512]{1,0:T(8,128)(2,1)S(1)}, bf16[128,512]{1,0:T(8,128)(2,1)S(1)}, u32[]{:S(2)}, u32[]{:S(2)}) collective-permute-start(bf16[128,512]{1,0:T(8,128)(2,1)S(1)} %near.1), channel_id=1, source_target_pairs={{0,192},{32,96},{64,0},{96,160},{128,64},{160,224},{192,128},{224,... | collective-permute-start | bytes 393224 | tf_op jit(solution)/shard_map/ppermute | solution.py:283
  91.0 6.2 %collective-permute-start.9 = (bf16[128,512]{1,0:T(8,128)(2,1)S(1)}, bf16[128,512]{1,0:T(8,128)(2,1)S(1)}, u32[]{:S(2)}, u32[]{:S(2)}) collective-permute-start(bf16[128,512]{1,0:T(8,128)(2,1)S(1)} %collective-permute-done.7), channel_id=1, source_target_pairs={{0,64},{32,224},{64,128},{96,32},{128,192},{160,96},{192,0},{224,1... | collective-permute-start | bytes 393224 | tf_op jit(solution)/shard_map/ppermute | solution.py:280
  97.2 2.9 %collective-permute-start.10 = (bf16[9,128,512]{2,1,0:T(8,128)(2,1)S(1)}, bf16[9,128,512]{2,1,0:T(8,128)(2,1)S(1)}, u32[]{:S(2)}, u32[]{:S(2)}) collective-permute-start(bf16[9,128,512]{2,1,0:T(8,128)(2,1)S(1)} %fusion.6.held), channel_id=1, source_target_pairs={{0,32},{32,0},{64,96},{96,64},{128,160},{160,128},{192,224},{224,1... | collective-permute-start | bytes 3538952 | tf_op jit(solution)/shard_map/ppermute | solution.py:286
  101.7 12.5 %copy-start.9 = (bf16[128,512]{1,0:T(8,128)(2,1)S(1)}, bf16[128,512]{1,0:T(8,128)(2,1)}, u32[]{:S(2)}) copy-start(bf16[128,512]{1,0:T(8,128)(2,1)} %copy-done.8) | copy-start | bytes 393220
  101.7 9.1 %collective-permute-start.11 = (bf16[8,96,256]{2,1,0:T(8,128)(2,1)S(1)}, bf16[8,96,256]{2,1,0:T(8,128)(2,1)S(1)}, u32[]{:S(2)}, u32[]{:S(2)}) collective-permute-start(bf16[8,96,256]{2,1,0:T(8,128)(2,1)S(1)} %get-tuple-element.53), channel_id=1, source_target_pairs={{0,1},{1,2},{2,3},{3,0},{4,5},{5,6},{6,7},{7,4},{8,9},{9,10},{10,1... | collective-permute-start | bytes 1179656 | tf_op jit(solution)/shard_map/ppermute | solution.py:289
  110.9 12.7 %collective-permute-start.12 = (bf16[8,96,256]{2,1,0:T(8,128)(2,1)S(1)}, bf16[8,96,256]{2,1,0:T(8,128)(2,1)S(1)}, u32[]{:S(2)}, u32[]{:S(2)}) collective-permute-start(bf16[8,96,256]{2,1,0:T(8,128)(2,1)S(1)} %fusion), channel_id=1, source_target_pairs={{0,1},{1,2},{2,3},{3,0},{4,5},{5,6},{6,7},{7,4},{8,9},{9,10},{10,1... | collective-permute-start | bytes 1179656 | tf_op jit(solution)/shard_map/ppermute | solution.py:289
  111.0 12.6 %collective-permute-start.13 = (bf16[8,96,256]{2,1,0:T(8,128)(2,1)S(1)}, bf16[8,96,256]{2,1,0:T(8,128)(2,1)S(1)}, u32[]{:S(2)}, u32[]{:S(2)}) collective-permute-start(bf16[8,96,256]{2,1,0:T(8,128)(2,1)S(1)} %get-tuple-element.57), channel_id=1, source_target_pairs={{0,3},{1,0},{2,1},{3,2},{4,7},{5,4},{6,5},{7,6},{8,11},{9,8},{10,9... | collective-permute-start | bytes 1179656 | tf_op jit(solution)/shard_map/ppermute | solution.py:292
  157.4 6.3 %collective-permute-start.14 = (bf16[128,512]{1,0:T(8,128)(2,1)S(1)}, bf16[128,512]{1,0:T(8,128)(2,1)S(1)}, u32[]{:S(2)}, u32[]{:S(2)}) collective-permute-start(bf16[128,512]{1,0:T(8,128)(2,1)S(1)} %get-tuple-element.68), channel_id=1, source_target_pairs={{0,64},{32,224},{64,128},{96,32},{128,192},{160,96},{192,0},{224,1... | collective-permute-start | bytes 393224 | tf_op jit(solution)/shard_map/ppermute | solution.py:280
  157.6 12.4 %collective-permute-start.17 = (bf16[8,64,256]{2,1,0:T(8,128)(2,1)S(1)}, bf16[8,64,256]{2,1,0:T(8,128)(2,1)S(1)}, u32[]{:S(2)}, u32[]{:S(2)}) collective-permute-start(bf16[8,64,256]{2,1,0:T(8,128)(2,1)S(1)} %slice.88.b0), channel_id=1, source_target_pairs={{0,1},{1,2},{2,3},{3,0},{4,5},{5,6},{6,7},{7,4},{8,9},{9,10},{10,1... | collective-permute-start | bytes 786440 | tf_op jit(solution)/shard_map/ppermute | solution.py:289
  157.7 6.1 %collective-permute-start.15 = (bf16[128,512]{1,0:T(8,128)(2,1)S(1)}, bf16[128,512]{1,0:T(8,128)(2,1)S(1)}, u32[]{:S(2)}, u32[]{:S(2)}) collective-permute-start(bf16[128,512]{1,0:T(8,128)(2,1)S(1)} %get-tuple-element.68), channel_id=1, source_target_pairs={{0,192},{32,96},{64,0},{96,160},{128,64},{160,224},{192,128},{224,... | collective-permute-start | bytes 393224 | tf_op jit(solution)/shard_map/ppermute | solution.py:283
  163.7 6.2 %collective-permute-start.16 = (bf16[128,512]{1,0:T(8,128)(2,1)S(1)}, bf16[128,512]{1,0:T(8,128)(2,1)S(1)}, u32[]{:S(2)}, u32[]{:S(2)}) collective-permute-start(bf16[128,512]{1,0:T(8,128)(2,1)S(1)} %collective-permute-done.14), channel_id=1, source_target_pairs={{0,64},{32,224},{64,128},{96,32},{128,192},{160,96},{192,0},{224,1... | collective-permute-start | bytes 393224 | tf_op jit(solution)/shard_map/ppermute | solution.py:280
  170.0 11.5 %collective-permute-start.20 = (bf16[4,128,512]{2,1,0:T(8,128)(2,1)S(1)}, bf16[4,128,512]{2,1,0:T(8,128)(2,1)S(1)}, u32[]{:S(2)}, u32[]{:S(2)}) collective-permute-start(bf16[4,128,512]{2,1,0:T(8,128)(2,1)S(1)} %pad_maximum_fusion.held), channel_id=1, source_target_pairs={{0,32},{32,0},{64,96},{96,64},{128,160},{160,128},{192,224},{224,1... | collective-permute-start | bytes 1572872 | tf_op jit(solution)/shard_map/ppermute | solution.py:286
  170.1 8.7 %collective-permute-start.18 = (bf16[8,64,256]{2,1,0:T(8,128)(2,1)S(1)}, bf16[8,64,256]{2,1,0:T(8,128)(2,1)S(1)}, u32[]{:S(2)}, u32[]{:S(2)}) collective-permute-start(bf16[8,64,256]{2,1,0:T(8,128)(2,1)S(1)} %slice.88.b0), channel_id=1, source_target_pairs={{0,3},{1,0},{2,1},{3,2},{4,7},{5,4},{6,5},{7,6},{8,11},{9,8},{10,9... | collective-permute-start | bytes 786440 | tf_op jit(solution)/shard_map/ppermute | solution.py:292
  170.5 9.4 %collective-permute-start.19 = (bf16[8,64,256]{2,1,0:T(8,128)(2,1)S(1)}, bf16[8,64,256]{2,1,0:T(8,128)(2,1)S(1)}, u32[]{:S(2)}, u32[]{:S(2)}) collective-permute-start(bf16[8,64,256]{2,1,0:T(8,128)(2,1)S(1)} %collective-permute-done.17.b1), channel_id=1, source_target_pairs={{0,1},{1,2},{2,3},{3,0},{4,5},{5,6},{6,7},{7,4},{8,9},{9,10},{10,1... | collective-permute-start | bytes 786440 | tf_op jit(solution)/shard_map/ppermute | solution.py:289

commit v8 on v7

--- a/solution.py
+++ b/solution.py
@@ -14,22 +14,19 @@
 TN = (((0,), (0,)), ((), ()))
 
 
-def step(core):
-    return 1 if core == 0 else -1
-
-
-def along_y(sign):
+def beside(at):
+    return at + 1 - 2 * (at % 2), CHIPS - 1 - at
+
+
+def along_y(turn):
     return [
-        (y * 2 + c, (y + sign * step(c)) % CHIPS * 2 + c) for y in range(CHIPS) for c in range(2)
+        (y * 2 + c, beside(y)[(turn + c) % 2] * 2 + c) for y in range(CHIPS) for c in range(2)
     ]
 
 
-def along_x(sign, parts, feats):
-    def device(f, z, x):
-        return f * parts + z * CHIPS + x % CHIPS
-
+def along_x(turn, parts, feats):
     return [
-        (device(f, z, x), device(f, z, x + sign * step(f % 2)))
+        (f * parts + z * CHIPS + x, f * parts + z * CHIPS + beside(x)[(turn + f) % 2])
         for f in range(feats)
         for z in range(parts // CHIPS)
         for x in range(CHIPS)
@@ -43,17 +40,16 @@
     return lax.dot_general(a, b, dims, preferred_element_type=F32)
 
 
-def whole(name, body, outs, *args, scratch=(), last=False):
+def whole(name, body, outs, *args, scratch=(), far=()):
     many = isinstance(outs, tuple)
     outs = list(outs) if many else [outs]
     place = pl.BlockSpec(memory_space=pltpu.VMEM)
-    if not last:
-        outs = [pltpu.VMEM(o.shape, o.dtype) for o in outs]
+    kinds = [o if k in far else pltpu.VMEM(o.shape, o.dtype) for k, o in enumerate(outs)]
     got = pl.pallas_call(
         body,
-        out_shape=outs,
+        out_shape=kinds,
         in_specs=[place] * len(args),
-        out_specs=[pl.BlockSpec() if last else place] * len(outs),
+        out_specs=[pl.BlockSpec() if k in far else place for k in range(len(outs))],
         scratch_shapes=scratch,
         name=name,
         compiler_params=pltpu.CompilerParams(vmem_limit_bytes=16 << 20),
@@ -115,28 +111,29 @@
         out[:, g * nodes : (g + 1) * nodes] = flat[g].T
 
 
-def ring_place(at, turn, offset):
-    o, turned = offset
-    return (at + CHIPS + o * (turn if turned else 1)) % CHIPS
-
-
-def places(offsets, other):
+def around(at, core):
+    left, right = beside(at)
+    first = jnp.where(core == 0, left, right)
+    return at, first, left + right - first, (at + 2) % CHIPS
+
+
+SUM_MINE = (1, 3, 2, 0)
+SUM_OTHER = (2, 3, 1, 0)
+GET_MINE = (0, 1, 2, 3)
+GET_OTHER = (0, 2, 1, 3)
+
+
+def places(order, other):
     feat = lax.axis_index("feat")
-    y, core = feat // 2, feat % 2
+    core = feat % 2
     held = 1 - core if other else core
-    return [ring_place(y, 1 - 2 * core, o) * 2 + held for o in offsets]
-
-
-def places_x(offsets):
-    core = lax.axis_index("feat") % 2
-    x = lax.axis_index("dom") % CHIPS
-    return [ring_place(x, 1 - 2 * core, o) for o in offsets]
-
-
-SUM_MINE = ((2, False), (-1, True), (1, True), (0, False))
-SUM_OTHER = ((2, False), (1, True), (-1, True), (0, False))
-GET_MINE = ((0, False), (-1, True), (1, True), (2, False))
-GET_OTHER = ((0, False), (1, True), (-1, True), (2, False))
+    ring = around(feat // 2, core)
+    return [ring[k] * 2 + held for k in order]
+
+
+def places_x(order):
+    ring = around(lax.axis_index("dom") % CHIPS, lax.axis_index("feat") % 2)
+    return [ring[k] for k in order]
 
 
 def project(flat, w_one, other):
@@ -159,7 +156,7 @@
 
 def forward_body(part, got, near, far, grads, inv, give, p_self, p_near, boxes):
     width = grads.shape[1]
-    total = add(part[3], got[3], near[...], far[...])
+    total = add(part[3], got[3], near[0], far[...])
     p_self[...] = total[:, :width]
     mine = total[:, width:].astype(BF16)
     p_near[...] = mine
@@ -169,7 +166,7 @@
 
 def middle_body(
     recv, p_self, p_near, grads, inv, w_two, give, take, own, own_t,
-    boxes, near_local, hidden_out, ahead, behind, third, mine, scratch,
+    boxes, term_out, hidden_out, first, second, mine, scratch,
 ):
     nodes, width = grads.shape
     scales = inv[:, :1]
@@ -185,24 +182,23 @@
     d_pre = d_hidden * sig * (1.0 + pre * (1.0 - sig))
     term = (d_pre * scales).astype(BF16)
     boxes[...] = mm(give[...], jnp.concatenate([term, hidden], axis=0)).astype(BF16)
-    near_local[...] = mm(own_t[...], term)
+    term_out[...] = term
     half = scratch.shape[0] // 2
     for k, right in enumerate((grad, back)):
         piece = mm(hidden, right, TN).astype(BF16)
         scratch[k * half : (k + 1) * half] = piece.reshape(half, -1, width)
-    ahead[0] = d_pre.astype(BF16)
-    behind[0] = d_pre.astype(BF16)
+    first[0] = d_pre.astype(BF16)
     for k, other in enumerate((True, False)):
-        away, back_to, on_to, here = places(SUM_MINE, other)
-        ahead[1 + k] = scratch[away]
-        behind[1 + k] = scratch[back_to]
-        third[k] = scratch[on_to]
+        partner, opposite, later, here = places(SUM_MINE, other)
+        first[1 + k] = scratch[partner]
+        first[3 + k] = scratch[opposite]
+        second[k] = scratch[later]
         mine[k] = scratch[here]
 
 
-def near_body(recv, near_local, take, out):
+def near_body(recv, term, own_t, take, out):
     nodes = out.shape[0]
-    out[...] = (near_local[...] + mm(take[nodes:, :], recv[...])).astype(BF16)
+    out[...] = (mm(own_t[...], term[...]) + mm(take[nodes:, :], recv[...])).astype(BF16)
 
 
 def out_body(recv, hidden, inv, take, own, w_two, out):
@@ -212,7 +208,7 @@
     out[...] = (mm(hidden[...], w_two[:width, :]) + mm(agg, w_two[width:, :])).astype(BF16)
 
 
-def grad_body(flat_t, held, other, two, ahead, behind, third, own, stack, boxes):
+def grad_body(flat_t, held, other, two, first, second, own, stack, boxes):
     groups, nodes, both = stack.shape
     width = both // 2
     chips, deep, rows, cut = boxes.shape
@@ -228,25 +224,40 @@
         for q in range(4):
             piece = total[x * block : (x + 1) * block, q * cut : (q + 1) * cut]
             boxes[x, :, q * part : (q + 1) * part, :] = piece.reshape(deep, part, cut)
-    for x, target in zip(places_x(SUM_MINE), (ahead, behind, third, own)):
-        target[:, :rows, :] = boxes[x]
+    partner, opposite, later, here = places_x(SUM_MINE)
+    first[:, :rows, :] = boxes[partner]
+    first[:, rows : 2 * rows, :] = boxes[opposite]
+    second[...] = boxes[later]
+    own[:, :rows, :] = boxes[here]
     twos = add(two[...], other[2 * chips]).astype(BF16)
-    tail = (ahead.shape[1] - rows) // 2
+    tail = (own.shape[1] - rows) // 2
     for k in range(2):
         piece = twos[:, k * cut : (k + 1) * cut].reshape(deep, tail, cut)
-        for target in (ahead, behind, own):
-            target[:, rows + k * tail : rows + (k + 1) * tail, :] = piece
-    third[:, rows:, :] = jnp.zeros_like(third[:, rows:, :])
-
-
-def spread_body(b0, b1, b2, b3, out):
-    deep, rows, cut = b0.shape
+        first[:, 2 * rows + k * tail : 2 * rows + (k + 1) * tail, :] = piece
+        own[:, rows + k * tail : rows + (k + 1) * tail, :] = piece
+
+
+def x_pass_body(second, own, got, out):
+    rows = second.shape[1]
+    out[:, :rows, :] = add(second[...], got[:, rows : 2 * rows, :]).astype(BF16)
+    out[:, rows:, :] = add(own[:, rows:, :], got[:, 2 * rows :, :]).astype(BF16)
+
+
+def x_sum_body(own, got, sent, last, out):
+    rows = got.shape[1] - own.shape[1]
+    out[:, :rows, :] = add(own[:, :rows, :], got[:, :rows, :], last[:, :rows, :]).astype(BF16)
+    out[:, rows:, :] = add(sent[:, rows:, :], last[:, rows:, :]).astype(BF16)
+
+
+def spread_body(held, last, out):
+    _, deep, rows, cut = held.shape
     block = out.shape[0] // CHIPS
     part = block // deep
-    for x, held in zip(places_x(GET_MINE), (b0, b1, b2, b3)):
+    for k, x in enumerate(places_x(GET_MINE)):
+        source = held if k < 2 else last
         at = pl.ds(pl.multiple_of(x * block, block), block)
         for q in range(4):
-            piece = held[:, q * part : (q + 1) * part, :].astype(F32)
+            piece = source[k % 2, :, q * part : (q + 1) * part, :].astype(F32)
             out[at, q * cut : (q + 1) * cut] = piece.reshape(block, cut)
 
 
@@ -272,29 +283,18 @@
     span = 2 * sends.size
     grads = grad_out[0]
     scale = 1.0 / math.sqrt(groups * nodes * parts)
-    y_ahead, y_behind = along_y(1), along_y(-1)
-    x_ahead, x_behind = along_x(1, parts, groups), along_x(-1, parts, groups)
+    y_first, y_second = along_y(0), along_y(1)
+    x_first, x_second = along_x(0, parts, groups), along_x(1, parts, groups)
     lines = [[z * CHIPS + x for z in range(deep)] for x in range(CHIPS)]
 
-    def forward(block):
-        return lax.ppermute(block, "feat", y_ahead)
-
-    def backward(block):
-        return lax.ppermute(block, "feat", y_behind)
+    def y_move(block, pairs):
+        return lax.ppermute(block, "feat", pairs)
+
+    def x_move(block, pairs):
+        return lax.ppermute(block, ("feat", "dom"), pairs)
 
     def swap(block):
         return lax.ppermute(block, "feat", SWAP)
-
-    def x_forward(block):
-        return lax.ppermute(block, ("feat", "dom"), x_ahead)
-
-    def x_backward(block):
-        return lax.ppermute(block, ("feat", "dom"), x_behind)
-
-    def gather(block):
-        one = forward(block)
-        two = backward(block)
-        return jnp.stack([block, one, two, forward(one)])
 
     got = swap(project(features, w_one, True))
     mine = project(features, w_one, False)
@@ -311,13 +311,11 @@
         neighbor[0].T, degree, sends.T,
     )
     flat_t = whole("turn", turn_body, shape((cols, groups * nodes)), features)
-    relay = forward(add(mine[0], got[0]).astype(BF16))
-    near = backward(add(mine[1], got[1]).astype(BF16))
-    relay, give = lax.optimization_barrier((relay, give))
-    far = forward(add(mine[2], got[2], relay).astype(BF16))
+    near = y_move(add(mine[:2], got[:2]).astype(BF16), y_first)
+    near, give = lax.optimization_barrier((near, give))
+    far = y_move(add(mine[2], got[2], near[1]).astype(BF16), y_second)
     far, flat_t = lax.optimization_barrier((far, flat_t))
     block = shape((nodes, width))
-
     p_self, p_near, boxes = whole(
         "forward",
         forward_body,
@@ -326,74 +324,79 @@
     )
     recv = trade(boxes.reshape(parts, 2 * kmax, width)).reshape(span, width)
     rows = 2 * width // groups
-    boxes, near_local, hidden, ahead, behind, third, mine = whole(
+    boxes, term, hidden, first, second, mine = whole(
         "middle",
         middle_body,
         (
             shape((span, width)),
-            shape((nodes, width), F32),
             block,
-            shape((3, rows, width)),
-            shape((3, rows, width)),
+            block,
+            shape((5, rows, width)),
             shape((2, rows, width)),
             shape((2, rows, width)),
         ),
         recv, p_self, p_near, grads, inv, w_two, give, take, own, own_t,
         scratch=[pltpu.VMEM((groups, rows, width), BF16)],
+        far=(0, 1, 2, 3, 4, 5),
     )
     recv = trade(boxes.reshape(parts, 2 * kmax, width)).reshape(span, width)
 
-    relay = forward(ahead)
-    near = backward(behind)
-    message = jnp.concatenate([relay[:1], add(third, relay[1:]).astype(BF16)])
+    got = y_move(first, y_first)
+    message = jnp.concatenate([first[:1], got[:1], add(second, got[3:]).astype(BF16)])
     message, recv = lax.optimization_barrier((message, recv))
-    d_near = whole("near", near_body, block, recv, near_local, take)
-    one = forward(d_near)
-    two = backward(d_near)
-    far = forward(message)
-    sums = add(mine, near[1:], far[1:])
-    held = jnp.stack(
-        [ahead[0], relay[0], near[0], far[0], d_near, one, two, forward(one), sums[0].astype(BF16)]
-    )
-    other = swap(held)
+    d_near = whole("near", near_body, block, recv, term, own_t, take)
+    one = y_move(d_near, y_first)
+    last = y_move(message, y_second)
+    sums = add(mine, got[1:3], last[2:])
+    near = jnp.stack([d_near, one])
+    held = jnp.concatenate(
+        [message[:2], last[:2], near, y_move(near, y_second), sums[:1].astype(BF16)]
+    )
 
     kept = 8 * cols // parts // 2
-    lot = shape((deep, kept + 4 * width // groups // deep, width // 2))
-    ahead, behind, third, mine = whole(
+    tail = 4 * width // groups // deep
+    first, second, mine = whole(
         "grad",
         grad_body,
-        (lot, lot, lot, lot),
-        flat_t, held, other, sums[1],
+        (
+            shape((deep, 2 * kept + tail, width // 2)),
+            shape((deep, kept, width // 2)),
+            shape((deep, kept + tail, width // 2)),
+        ),
+        flat_t, held, swap(held), sums[1],
         scratch=[
             pltpu.VMEM((groups, nodes, 2 * width), BF16),
             pltpu.VMEM((CHIPS, deep, kept, width // 2), BF16),
         ],
     )
-    out = whole("out", out_body, block, recv, hidden, inv, take, own, w_two, last=True)
-    relay = x_forward(ahead)
-    near = x_backward(behind)
-    far = x_forward(add(third, relay).astype(BF16))
-    far, out = lax.optimization_barrier((far, out))
-    last_rows = lax.broadcasted_iota(jnp.int32, lot.shape, 1) >= kept
-    terms = add(mine, near, far) + jnp.where(last_rows, relay.astype(F32), 0.0)
-    terms = trade(terms.astype(BF16), lines)
+    out = whole("out", out_body, block, recv, hidden, inv, take, own, w_two, far=(0,))
+    lot = shape((deep, kept + tail, width // 2))
+    got = x_move(first, x_first)
+    sent = whole("x_pass", x_pass_body, lot, second, mine, got)
+    last = x_move(sent, x_second)
+    last, out = lax.optimization_barrier((last, out))
+    terms = trade(whole("x_sum", x_sum_body, lot, mine, got, sent, last), lines)
     total = (jnp.sum(terms.astype(F32), axis=0) * scale).astype(BF16)
     total = trade(jnp.broadcast_to(total[None], terms.shape), lines)
-    tail = (lot.shape[1] - kept) // 2
+    half = kept + tail // 2
     chunk = jnp.concatenate(
-        [
-            total[:, kept : kept + tail].reshape(deep * tail, -1),
-            total[:, kept + tail :].reshape(deep * tail, -1),
-        ],
-        axis=1,
+        [total[:, kept:half].reshape(nodes, -1), total[:, half:].reshape(nodes, -1)], axis=1
     )
     mine = total[:, :kept]
-    relay = x_forward(mine)
-    near = x_backward(mine)
-    held, relay = lax.optimization_barrier((gather(chunk), relay))
-    far = x_forward(relay)
-    one = whole("spread", spread_body, shape((cols, 2 * width), F32), mine, relay, near, far, last=True)
-    two = whole("join", join_body, shape((2 * width, width), F32), held, swap(held), last=True)
+    one_y = y_move(chunk, y_first)
+    one_x = x_move(mine, x_first)
+    one_y, one_x = lax.optimization_barrier((one_y, one_x))
+    held_y = jnp.stack([chunk, one_y])
+    held_y = jnp.concatenate([held_y, y_move(held_y, y_second)])
+    held_x = jnp.stack([mine, one_x])
+    last_x = x_move(held_x, x_second)
+    held_y, last_x = lax.optimization_barrier((held_y, last_x))
+    one = whole(
+        "spread", spread_body, shape((cols, 2 * width), F32), held_x, last_x, far=(0,)
+    )
+    two = whole(
+        "join", join_body, shape((2 * width, width), F32), held_y, swap(held_y), far=(0,)
+    )
     return out[None], one, two
 
 

time: 185 us -> 172 us (0.930)
  blocking collectives: 62.1 us -> 56.4 us
  waiting for transfers between devices: 71.1 us -> 65.8 us
  local copies, waits for them, and re-layouts: 9.58 us -> 6.73 us
    ppermute x18 -> x12, waiting for transfers between devices: 62.6 us -> 51.5 us  [the longest x8 34.8 us: y_move(): return lax.ppermute(block, 'feat', pairs)]
    all_to_all x3, blocking collectives: 62.1 us -> 56.4 us  [trade(): lax.all_to_all(boxes, 'dom', split_axis=0, concat_axis=0, axis_index_grou...]
    all_to_all x1, waiting for transfers between devices: 3.84 us -> 9.11 us  [trade(): lax.all_to_all(boxes, 'dom', split_axis=0, concat_axis=0, axis_index_grou...]
    unnamed x38 -> x32, local copies, waits for them, and re-layouts: 8.81 us -> 4.78 us
    ppermute x18 -> x12, starting transfers between devices: 20.1 us -> 19.2 us  [the longest x8 12.5 us: y_move(): return lax.ppermute(block, 'feat', pairs)]
    pallas_call x11 -> x13, Pallas kernels: 10.5 us -> 11.1 us  [whole(): pl.pallas_call(body, out_shape=kinds, in_specs=[place] * len(args), out_s...]
  transfers between devices with their start and end apart: 22 -> 16, of which waited for: 14 -> 15; matrix products, arithmetic and copies ran while one was open for 3% -> 3% of each run, Pallas kernels for 2% -> 3%
where the time goes in v8:
time: 172 us; the launch traced here: 169 us
  waiting for transfers between devices  65.8 us (38%)
  blocking collectives  56.4 us (33%)
  starting transfers between devices  24.5 us (14%)
  Pallas kernels  11.1 us (6%)
  local copies, waits for them, and re-layouts  6.73 us (4%)
  other arithmetic  3.46 us (2%)
    all_to_all x3, blocking collectives, trade(): lax.all_to_all(boxes, 'dom', split_axis=0, concat_axis=0, axis_index_grou...  56.4 us
    ppermute x8, waiting for transfers between devices, y_move(): return lax.ppermute(block, 'feat', pairs)  34.8 us
    ppermute x4, waiting for transfers between devices, x_move(): return lax.ppermute(block, ('feat', 'dom'), pairs)  16.7 us
    ppermute x8, starting transfers between devices, y_move(): return lax.ppermute(block, 'feat', pairs)  12.5 us
    pallas_call x13, Pallas kernels, whole(): pl.pallas_call(body, out_shape=kinds, in_specs=[place] * len(args), out_s...  11.1 us
    all_to_all x1, waiting for transfers between devices, trade(): lax.all_to_all(boxes, 'dom', split_axis=0, concat_axis=0, axis_index_grou...  9.11 us
    ppermute x4, starting transfers between devices, x_move(): return lax.ppermute(block, ('feat', 'dom'), pairs)  6.66 us
    ppermute x3, waiting for transfers between devices, swap(): return lax.ppermute(block, 'feat', SWAP)  5.12 us
  transfers between devices with their start and end apart: 16, of which 15 were waited for; matrix products, arithmetic and copies ran while one was open for 3% of the time, Pallas kernels for 3%

profile of v8, /device:TPU:32, one launch (start us, length us, event | category | flops | bytes accessed | tf_op | source)
XLA Modules:
  0.0 169.0 jit_solution(5153008086734865598)
XLA Ops:
  0.6 1.2 copy-done
  1.9 1.2 copy-done.2
  3.1 0.7 project.3
  3.9 0.7 project.2.part
  4.7 1.9 %collective-permute-done.got = bf16[4,128,1024]{2,1,0:T(8,128)(2,1)S(1)} collective-permute-done((bf16[4,128,1024]{2,1,0:T(8,128)(2,1)S(1)}, bf16[4,128,1024]{2,1,0:T(8,128)(2,1)S(1)}, u32[]{:S(2)}, u32[]{:S(2)}) %collective-permute-start) | collective-permute-done | bytes 1048608 | tf_op jit(solution)/shard_map/ppermute | solution.py:297
  6.7 1.7 collective-permute-start.1
  8.4 0.6 tables.1
  9.0 7.0 %collective-permute-done.1.near = bf16[2,128,1024]{2,1,0:T(8,128)(2,1)S(1)} collective-permute-done((bf16[2,128,1024]{2,1,0:T(8,128)(2,1)S(1)}, bf16[2,128,1024]{2,1,0:T(8,128)(2,1)S(1)}, u32[]{:S(2)}, u32[]{:S(2)}) %collective-permute-start.1) | collective-permute-done | bytes 524320 | tf_op jit(solution)/shard_map/ppermute | solution.py:291
  16.2 3.1 %collective-permute-start.2 = (bf16[128,1024]{1,0:T(8,128)(2,1)S(1)}, bf16[128,1024]{1,0:T(8,128)(2,1)S(1)}, u32[]{:S(2)}, u32[]{:S(2)}) collective-permute-start(bf16[128,1024]{1,0:T(8,128)(2,1)S(1)} %fusion), channel_id=1, source_target_pairs={{0,192},{32,96},{64,128},{96,32},{128,64},{160,224},{192,0},{224,1... | collective-permute-start | bytes 786440 | tf_op jit(solution)/shard_map/ppermute | solution.py:291
  19.6 4.2 %collective-permute-done.2.far = bf16[128,1024]{1,0:T(8,128)(2,1)S(1)} collective-permute-done((bf16[128,1024]{1,0:T(8,128)(2,1)S(1)}, bf16[128,1024]{1,0:T(8,128)(2,1)S(1)}, u32[]{:S(2)}, u32[]{:S(2)}) %collective-permute-start.2) | collective-permute-done | bytes 262176 | tf_op jit(solution)/shard_map/ppermute | solution.py:291
  23.8 0.4 forward.1
  24.3 26.8 %all_to_all.20 = bf16[32,16,512]{2,1,0:T(8,128)(2,1)S(1)} all-to-all(bf16[32,16,512]{2,1,0:T(8,128)(2,1)S(1)} %bitcast.34), channel_id=1, replica_groups=mesh['feat'=8,'dom'=32] {'dom'}, dimensions={0} | all-to-all | bytes 1048576 | tf_op jit(solution)/shard_map/all_to_all | solution.py:65
  51.1 2.3 %middle.1 = (bf16[512,512]{1,0:T(8,128)(2,1)}, bf16[128,512]{1,0:T(8,128)(2,1)S(1)}, bf16[128,512]{1,0:T(8,128)(2,1)S(1)}, bf16[5,128,512]{2,1,0:T(8,128)(2,1)},...) custom-call(bf16[512,512]{1,0:T(8,128)(2,1)S(1)} %bitcast.32, ...), custom_call_target="tpu_custom_call" | custom-call | tf_op jit(solution)/shard_map/middle/pallas_call | solution.py:48
  53.3 0.7 copy-done.5
  54.0 0.7 copy-done.7
  54.6 0.6 collective-permute-start.3
  55.2 5.1 %all-to-all-start.1 = ((bf16[32,16,512]{2,1,0:T(8,128)(2,1)}), bf16[32,16,512]{2,1,0:T(8,128)(2,1)S(1)}, u32[]{:S(2)}, u32[]{:S(2)}) async-start(bf16[32,16,512]{2,1,0:T(8,128)(2,1)} %bitcast.7), calls=%async_computation.1 | async-start | bytes 1048576 | tf_op jit(solution)/shard_map/all_to_all | solution.py:65
  60.3 0.9 slice.57
  61.3 4.3 %collective-permute-done.3 = bf16[5,128,512]{2,1,0:T(8,128)(2,1)} collective-permute-done((bf16[5,128,512]{2,1,0:T(8,128)(2,1)}, bf16[5,128,512]{2,1,0:T(8,128)(2,1)}, u32[]{:S(2)}, u32[]{:S(2)}) %collective-permute-start.3) | collective-permute-done | bytes 655392 | tf_op jit(solution)/shard_map/ppermute | solution.py:291
  65.5 0.9 slice.73
  66.4 1.0 add_convert_fusion.1
  67.5 0.8 pad_maximum_fusion
  68.3 9.1 %all-to-all-done.1 = bf16[32,16,512]{2,1,0:T(8,128)(2,1)S(1)} async-done(((bf16[32,16,512]{2,1,0:T(8,128)(2,1)}), bf16[32,16,512]{2,1,0:T(8,128)(2,1)S(1)}, u32[]{:S(2)}, u32[]{:S(2)}) %all-to-all-start.1) | async-done | bytes 524320 | tf_op jit(solution)/shard_map/all_to_all | solution.py:65
  77.4 0.4 collective-permute-start.4
  77.8 0.9 copy-done.8
  79.0 0.9 collective-permute-start.5
  79.9 5.3 %collective-permute-done.5 = bf16[128,512]{1,0:T(8,128)(2,1)S(1)} collective-permute-done((bf16[128,512]{1,0:T(8,128)(2,1)S(1)}, bf16[128,512]{1,0:T(8,128)(2,1)S(1)}, u32[]{:S(2)}, u32[]{:S(2)}) %collective-permute-start.5) | collective-permute-done | bytes 131104 | tf_op jit(solution)/shard_map/ppermute | solution.py:291
  85.3 2.9 %collective-permute-start.6 = (bf16[2,128,512]{2,1,0:T(8,128)(2,1)S(1)}, bf16[2,128,512]{2,1,0:T(8,128)(2,1)S(1)}, u32[]{:S(2)}, u32[]{:S(2)}) collective-permute-start(bf16[2,128,512]{2,1,0:T(8,128)(2,1)S(1)} %pad_maximum_fusion.3), channel_id=1, source_target_pairs={{0,192},{32,96},{64,128},{96,32},{128,64},{160,224},{192,0},{224,1... | collective-permute-start | bytes 786440 | tf_op jit(solution)/shard_map/ppermute | solution.py:291
  88.3 1.0 convert_add_fusion
  89.3 3.6 %collective-permute-done.6 = bf16[2,128,512]{2,1,0:T(8,128)(2,1)S(1)} collective-permute-done((bf16[2,128,512]{2,1,0:T(8,128)(2,1)S(1)}, bf16[2,128,512]{2,1,0:T(8,128)(2,1)S(1)}, u32[]{:S(2)}, u32[]{:S(2)}) %collective-permute-start.6) | collective-permute-done | bytes 262176 | tf_op jit(solution)/shard_map/ppermute | solution.py:291
  93.1 2.8 %collective-permute-done.7.other = bf16[9,128,512]{2,1,0:T(8,128)(2,1)S(1)} collective-permute-done((bf16[9,128,512]{2,1,0:T(8,128)(2,1)S(1)}, bf16[9,128,512]{2,1,0:T(8,128)(2,1)S(1)}, u32[]{:S(2)}, u32[]{:S(2)}) %collective-permute-start.7) | collective-permute-done | bytes 1179680 | tf_op jit(solution)/shard_map/ppermute | solution.py:297
  95.9 1.5 grad.1
  97.4 0.9 collective-permute-start.8
  98.3 9.8 %collective-permute-done.8.got = bf16[8,160,256]{2,1,0:T(8,128)(2,1)S(1)} collective-permute-done((bf16[8,160,256]{2,1,0:T(8,128)(2,1)S(1)}, bf16[8,160,256]{2,1,0:T(8,128)(2,1)S(1)}, u32[]{:S(2)}, u32[]{:S(2)}) %collective-permute-start.8) | collective-permute-done | bytes 655392 | tf_op jit(solution)/shard_map/ppermute | solution.py:294
  108.2 1.9 %collective-permute-start.9 = (bf16[8,96,256]{2,1,0:T(8,128)(2,1)S(1)}, bf16[8,96,256]{2,1,0:T(8,128)(2,1)S(1)}, u32[]{:S(2)}, u32[]{:S(2)}) collective-permute-start(bf16[8,96,256]{2,1,0:T(8,128)(2,1)S(1)} %x_pass.1.sent), channel_id=1, source_target_pairs={{0,3},{1,2},{2,1},{3,0},{4,7},{5,6},{6,5},{7,4},{8,11},{9,10},{10,... | collective-permute-start | bytes 1179656 | tf_op jit(solution)/shard_map/ppermute | solution.py:294
  110.2 1.2 out.1
  111.3 6.1 %collective-permute-done.9.last = bf16[8,96,256]{2,1,0:T(8,128)(2,1)S(1)} collective-permute-done((bf16[8,96,256]{2,1,0:T(8,128)(2,1)S(1)}, bf16[8,96,256]{2,1,0:T(8,128)(2,1)S(1)}, u32[]{:S(2)}, u32[]{:S(2)}) %collective-permute-start.9) | collective-permute-done | bytes 393248 | tf_op jit(solution)/shard_map/ppermute | solution.py:294
  117.6 15.6 %all_to_all.21 = bf16[8,96,256]{2,1,0:T(8,128)(2,1)S(1)} all-to-all(bf16[8,96,256]{2,1,0:T(8,128)(2,1)S(1)} %x_sum.1), channel_id=1, replica_groups={{0,4,8,12,16,20,24,28},{1,5,9,13,17,21,25,29},{2,6,10,14,18,22,26,30},{..., dimensions={0} | all-to-all | bytes 786432 | tf_op jit(solution)/shard_map/all_to_all | solution.py:65
  133.3 14.1 %all_to_all.22 = bf16[8,96,256]{2,1,0:T(8,128)(2,1)S(1)} all-to-all(bf16[8,96,256]{2,1,0:T(8,128)(2,1)S(1)} %broadcast_in_dim.10), channel_id=1, replica_groups={{0,4,8,12,16,20,24,28},{1,5,9,13,17,21,25,29},{2,6,10,14,18,22,26,30},{..., dimensions={0} | all-to-all | bytes 786432 | tf_op jit(solution)/shard_map/all_to_all | solution.py:65
  147.4 1.8 %collective-permute-start.11 = (bf16[8,64,256]{2,1,0:T(8,128)(2,1)S(1)}, bf16[8,64,256]{2,1,0:T(8,128)(2,1)S(1)}, u32[]{:S(2)}, u32[]{:S(2)}) collective-permute-start(bf16[8,64,256]{2,1,0:T(8,128)(2,1)S(1)} %get-tuple-element.62), channel_id=1, source_target_pairs={{0,1},{1,0},{2,3},{3,2},{4,5},{5,4},{6,7},{7,6},{8,9},{9,8},{10,11... | collective-permute-start | bytes 786440 | tf_op jit(solution)/shard_map/ppermute | solution.py:294
  149.4 5.6 %collective-permute-done.10 = bf16[128,512]{1,0:T(8,128)(2,1)S(1)} collective-permute-done((bf16[128,512]{1,0:T(8,128)(2,1)S(1)}, bf16[128,512]{1,0:T(8,128)(2,1)S(1)}, u32[]{:S(2)}, u32[]{:S(2)}) %collective-permute-start.10) | collective-permute-done | bytes 131104 | tf_op jit(solution)/shard_map/ppermute | solution.py:291
  155.1 2.0 %collective-permute-start.13 = (bf16[2,8,64,256]{3,2,1,0:T(8,128)(2,1)S(1)}, bf16[2,8,64,256]{3,2,1,0:T(8,128)(2,1)S(1)}, u32[]{:S(2)}, u32[]{:S(2)}) collective-permute-start(bf16[2,8,64,256]{3,2,1,0:T(8,128)(2,1)S(1)} %pad_maximum_fusion.1.held), channel_id=1, source_target_pairs={{0,3},{1,2},{2,1},{3,0},{4,7},{5,6},{6,5},{7,4},{8,11},{9,10},{10,... | collective-permute-start | bytes 1572872 | tf_op jit(solution)/shard_map/ppermute | solution.py:294
  157.2 2.8 %collective-permute-start.12 = (bf16[2,128,512]{2,1,0:T(8,128)(2,1)S(1)}, bf16[2,128,512]{2,1,0:T(8,128)(2,1)S(1)}, u32[]{:S(2)}, u32[]{:S(2)}) collective-permute-start(bf16[2,128,512]{2,1,0:T(8,128)(2,1)S(1)} %pad_maximum_fusion.4), channel_id=1, source_target_pairs={{0,192},{32,96},{64,128},{96,32},{128,64},{160,224},{192,0},{224,1... | collective-permute-start | bytes 786440 | tf_op jit(solution)/shard_map/ppermute | solution.py:291
  160.0 4.8 %collective-permute-done.12 = bf16[2,128,512]{2,1,0:T(8,128)(2,1)S(1)} collective-permute-done((bf16[2,128,512]{2,1,0:T(8,128)(2,1)S(1)}, bf16[2,128,512]{2,1,0:T(8,128)(2,1)S(1)}, u32[]{:S(2)}, u32[]{:S(2)}) %collective-permute-start.12) | collective-permute-done | bytes 262176 | tf_op jit(solution)/shard_map/ppermute | solution.py:291
  164.9 0.7 collective-permute-done.13.last
  165.6 1.5 spread.1
  167.1 0.4 collective-permute-done.14.other
  167.5 1.5 join.1
  (51 shorter events, 2.0 us)
Async XLA Ops:
  0.6 1.2 copy-start
  1.9 1.2 copy-start.2
  3.8 2.7 %collective-permute-start = (bf16[4,128,1024]{2,1,0:T(8,128)(2,1)S(1)}, bf16[4,128,1024]{2,1,0:T(8,128)(2,1)S(1)}, u32[]{:S(2)}, u32[]{:S(2)}) collective-permute-start(bf16[4,128,1024]{2,1,0:T(8,128)(2,1)S(1)} %project.3), channel_id=1, source_target_pairs={{0,32},{32,0},{64,96},{96,64},{128,160},{160,128},{192,224},{224,1... | collective-permute-start | bytes 3145736 | tf_op jit(solution)/shard_map/ppermute | solution.py:297
  4.6 3.8 %copy-start.12 = (s32[1,128,10]{1,0,2:T(1,128)S(1)}, s32[1,128,10]{1,0,2:T(1,128)}, u32[]{:S(2)}) copy-start(s32[1,128,10]{1,0,2:T(1,128)} %param.10) | copy-start | bytes 15364
  4.6 3.8 %copy-start.9 = (s32[1,32,8]{1,2,0:T(8,128)S(1)}, s32[1,32,8]{1,2,0:T(8,128)}, u32[]{:S(2)}) copy-start(s32[1,32,8]{1,2,0:T(8,128)} %param.12) | copy-start | bytes 3076
  4.6 3.8 %copy-start.10 = (s32[1,128]{1,0:T(1,128)S(1)}, s32[1,128]{1,0:T(1,128)}, u32[]{:S(2)}) copy-start(s32[1,128]{1,0:T(1,128)} %deg.1) | copy-start | bytes 1540
  4.7 14.6 %copy-start.1 = (bf16[8,128,512]{2,1,0:T(8,128)(2,1)S(1)}, bf16[8,128,512]{2,1,0:T(8,128)(2,1)}, u32[]{:S(2)}) copy-start(bf16[8,128,512]{2,1,0:T(8,128)(2,1)} %flat.1) | copy-start | bytes 3145732
  6.7 9.3 %collective-permute-start.1 = (bf16[2,128,1024]{2,1,0:T(8,128)(2,1)S(1)}, bf16[2,128,1024]{2,1,0:T(8,128)(2,1)S(1)}, u32[]{:S(2)}, u32[]{:S(2)}) collective-permute-start(bf16[2,128,1024]{2,1,0:T(8,128)(2,1)S(1)} %add_convert_fusion), channel_id=1, source_target_pairs={{0,64},{32,224},{64,0},{96,160},{128,192},{160,96},{192,128},{224,... | collective-permute-start | bytes 1572872 | tf_op jit(solution)/shard_map/ppermute | solution.py:291
  16.1 7.7 %copy-start.4 = (bf16[1,128,512]{2,1,0:T(8,128)(2,1)S(1)}, bf16[1,128,512]{2,1,0:T(8,128)(2,1)}, u32[]{:S(2)}) copy-start(bf16[1,128,512]{2,1,0:T(8,128)(2,1)} %param.13) | copy-start | bytes 393220
  16.2 7.7 %collective-permute-start.2 = (bf16[128,1024]{1,0:T(8,128)(2,1)S(1)}, bf16[128,1024]{1,0:T(8,128)(2,1)S(1)}, u32[]{:S(2)}, u32[]{:S(2)}) collective-permute-start(bf16[128,1024]{1,0:T(8,128)(2,1)S(1)} %fusion), channel_id=1, source_target_pairs={{0,192},{32,96},{64,128},{96,32},{128,64},{160,224},{192,0},{224,1... | collective-permute-start | bytes 786440 | tf_op jit(solution)/shard_map/ppermute | solution.py:291
  24.3 26.8 %copy-start.3 = (bf16[1024,512]{1,0:T(8,128)(2,1)S(1)}, bf16[1024,512]{1,0:T(8,128)(2,1)}, u32[]{:S(2)}) copy-start(bf16[1024,512]{1,0:T(8,128)(2,1)} %w_two.3) | copy-start | bytes 3145732
  53.3 0.7 copy-start.5
  54.0 0.7 copy-start.7
  54.6 10.9 %collective-permute-start.3 = (bf16[5,128,512]{2,1,0:T(8,128)(2,1)}, bf16[5,128,512]{2,1,0:T(8,128)(2,1)}, u32[]{:S(2)}, u32[]{:S(2)}) collective-permute-start(bf16[5,128,512]{2,1,0:T(8,128)(2,1)} %get-tuple-element.44), channel_id=1, source_target_pairs={{0,64},{32,224},{64,0},{96,160},{128,192},{160,96},{192,128},{224,... | collective-permute-start | bytes 1966088 | tf_op jit(solution)/shard_map/ppermute | solution.py:291
  55.2 22.2 %all-to-all-start.1 = ((bf16[32,16,512]{2,1,0:T(8,128)(2,1)}), bf16[32,16,512]{2,1,0:T(8,128)(2,1)S(1)}, u32[]{:S(2)}, u32[]{:S(2)}) async-start(bf16[32,16,512]{2,1,0:T(8,128)(2,1)} %bitcast.7), calls=%async_computation.1 | async-start | bytes 1048576 | tf_op jit(solution)/shard_map/all_to_all | solution.py:65
  77.4 10.8 %collective-permute-start.4 = (bf16[4,128,512]{2,1,0:T(8,128)(2,1)}, bf16[4,128,512]{2,1,0:T(8,128)(2,1)S(1)}, u32[]{:S(2)}, u32[]{:S(2)}) collective-permute-start(bf16[4,128,512]{2,1,0:T(8,128)(2,1)} %pad_maximum_fusion), channel_id=1, source_target_pairs={{0,192},{32,96},{64,128},{96,32},{128,64},{160,224},{192,0},{224,1... | collective-permute-start | bytes 1572872 | tf_op jit(solution)/shard_map/ppermute | solution.py:291
  77.8 0.9 copy-start.8
  78.7 1.2 copy-start.11
  79.0 6.2 %collective-permute-start.5 = (bf16[128,512]{1,0:T(8,128)(2,1)S(1)}, bf16[128,512]{1,0:T(8,128)(2,1)S(1)}, u32[]{:S(2)}, u32[]{:S(2)}) collective-permute-start(bf16[128,512]{1,0:T(8,128)(2,1)S(1)} %near.1), channel_id=1, source_target_pairs={{0,64},{32,224},{64,0},{96,160},{128,192},{160,96},{192,128},{224,... | collective-permute-start | bytes 393224 | tf_op jit(solution)/shard_map/ppermute | solution.py:291
  85.3 7.7 %collective-permute-start.6 = (bf16[2,128,512]{2,1,0:T(8,128)(2,1)S(1)}, bf16[2,128,512]{2,1,0:T(8,128)(2,1)S(1)}, u32[]{:S(2)}, u32[]{:S(2)}) collective-permute-start(bf16[2,128,512]{2,1,0:T(8,128)(2,1)S(1)} %pad_maximum_fusion.3), channel_id=1, source_target_pairs={{0,192},{32,96},{64,128},{96,32},{128,64},{160,224},{192,0},{224,1... | collective-permute-start | bytes 786440 | tf_op jit(solution)/shard_map/ppermute | solution.py:291
  93.0 2.9 %collective-permute-start.7 = (bf16[9,128,512]{2,1,0:T(8,128)(2,1)S(1)}, bf16[9,128,512]{2,1,0:T(8,128)(2,1)S(1)}, u32[]{:S(2)}, u32[]{:S(2)}) collective-permute-start(bf16[9,128,512]{2,1,0:T(8,128)(2,1)S(1)} %fusion.1.held), channel_id=1, source_target_pairs={{0,32},{32,0},{64,96},{96,64},{128,160},{160,128},{192,224},{224,1... | collective-permute-start | bytes 3538952 | tf_op jit(solution)/shard_map/ppermute | solution.py:297
  97.4 12.7 %copy-start.6 = (bf16[128,512]{1,0:T(8,128)(2,1)S(1)}, bf16[128,512]{1,0:T(8,128)(2,1)}, u32[]{:S(2)}) copy-start(bf16[128,512]{1,0:T(8,128)(2,1)} %copy-done.5) | copy-start | bytes 393220
  97.4 10.7 %collective-permute-start.8 = (bf16[8,160,256]{2,1,0:T(8,128)(2,1)S(1)}, bf16[8,160,256]{2,1,0:T(8,128)(2,1)S(1)}, u32[]{:S(2)}, u32[]{:S(2)}) collective-permute-start(bf16[8,160,256]{2,1,0:T(8,128)(2,1)S(1)} %get-tuple-element.53), channel_id=1, source_target_pairs={{0,1},{1,0},{2,3},{3,2},{4,5},{5,4},{6,7},{7,6},{8,9},{9,8},{10,11... | collective-permute-start | bytes 1966088 | tf_op jit(solution)/shard_map/ppermute | solution.py:294
  108.2 9.3 %collective-permute-start.9 = (bf16[8,96,256]{2,1,0:T(8,128)(2,1)S(1)}, bf16[8,96,256]{2,1,0:T(8,128)(2,1)S(1)}, u32[]{:S(2)}, u32[]{:S(2)}) collective-permute-start(bf16[8,96,256]{2,1,0:T(8,128)(2,1)S(1)} %x_pass.1.sent), channel_id=1, source_target_pairs={{0,3},{1,2},{2,1},{3,0},{4,7},{5,6},{6,5},{7,4},{8,11},{9,10},{10,... | collective-permute-start | bytes 1179656 | tf_op jit(solution)/shard_map/ppermute | solution.py:294
  147.4 7.6 %collective-permute-start.11 = (bf16[8,64,256]{2,1,0:T(8,128)(2,1)S(1)}, bf16[8,64,256]{2,1,0:T(8,128)(2,1)S(1)}, u32[]{:S(2)}, u32[]{:S(2)}) collective-permute-start(bf16[8,64,256]{2,1,0:T(8,128)(2,1)S(1)} %get-tuple-element.62), channel_id=1, source_target_pairs={{0,1},{1,0},{2,3},{3,2},{4,5},{5,4},{6,7},{7,6},{8,9},{9,8},{10,11... | collective-permute-start | bytes 786440 | tf_op jit(solution)/shard_map/ppermute | solution.py:294
  149.3 5.7 %collective-permute-start.10 = (bf16[128,512]{1,0:T(8,128)(2,1)S(1)}, bf16[128,512]{1,0:T(8,128)(2,1)S(1)}, u32[]{:S(2)}, u32[]{:S(2)}) collective-permute-start(bf16[128,512]{1,0:T(8,128)(2,1)S(1)} %get-tuple-element.66), channel_id=1, source_target_pairs={{0,64},{32,224},{64,0},{96,160},{128,192},{160,96},{192,128},{224,... | collective-permute-start | bytes 393224 | tf_op jit(solution)/shard_map/ppermute | solution.py:291
  155.1 10.5 %collective-permute-start.13 = (bf16[2,8,64,256]{3,2,1,0:T(8,128)(2,1)S(1)}, bf16[2,8,64,256]{3,2,1,0:T(8,128)(2,1)S(1)}, u32[]{:S(2)}, u32[]{:S(2)}) collective-permute-start(bf16[2,8,64,256]{3,2,1,0:T(8,128)(2,1)S(1)} %pad_maximum_fusion.1.held), channel_id=1, source_target_pairs={{0,3},{1,2},{2,1},{3,0},{4,7},{5,6},{6,5},{7,4},{8,11},{9,10},{10,... | collective-permute-start | bytes 1572872 | tf_op jit(solution)/shard_map/ppermute | solution.py:294
  157.2 7.7 %collective-permute-start.12 = (bf16[2,128,512]{2,1,0:T(8,128)(2,1)S(1)}, bf16[2,128,512]{2,1,0:T(8,128)(2,1)S(1)}, u32[]{:S(2)}, u32[]{:S(2)}) collective-permute-start(bf16[2,128,512]{2,1,0:T(8,128)(2,1)S(1)} %pad_maximum_fusion.4), channel_id=1, source_target_pairs={{0,192},{32,96},{64,128},{96,32},{128,64},{160,224},{192,0},{224,1... | collective-permute-start | bytes 786440 | tf_op jit(solution)/shard_map/ppermute | solution.py:291
  165.6 1.9 %collective-permute-start.14 = (bf16[4,128,512]{2,1,0:T(8,128)(2,1)S(1)}, bf16[4,128,512]{2,1,0:T(8,128)(2,1)S(1)}, u32[]{:S(2)}, u32[]{:S(2)}) collective-permute-start(bf16[4,128,512]{2,1,0:T(8,128)(2,1)S(1)} %pad_maximum_fusion.2.held), channel_id=1, source_target_pairs={{0,32},{32,0},{64,96},{96,64},{128,160},{160,128},{192,224},{224,1... | collective-permute-start | bytes 1572872 | tf_op jit(solution)/shard_map/ppermute | solution.py:297

commit v9 on v8

--- a/solution.py
+++ b/solution.py
@@ -40,20 +40,31 @@
     return lax.dot_general(a, b, dims, preferred_element_type=F32)
 
 
-def whole(name, body, outs, *args, scratch=(), far=()):
+def whole(name, body, outs, *args, scratch=(), far=(), kept=(), raw=()):
     many = isinstance(outs, tuple)
     outs = list(outs) if many else [outs]
     place = pl.BlockSpec(memory_space=pltpu.VMEM)
-    kinds = [o if k in far else pltpu.VMEM(o.shape, o.dtype) for k, o in enumerate(outs)]
+    kinds = [
+        o if k in far else (pltpu.HBM if k in kept else pltpu.VMEM)(o.shape, o.dtype)
+        for k, o in enumerate(outs)
+    ]
+    anywhere = pl.BlockSpec(memory_space=pltpu.HBM)
     got = pl.pallas_call(
         body,
         out_shape=kinds,
-        in_specs=[place] * len(args),
-        out_specs=[pl.BlockSpec() if k in far else place for k in range(len(outs))],
+        in_specs=[anywhere if k in raw else place for k in range(len(args))],
+        out_specs=[
+            pl.BlockSpec() if k in far or k in kept else place for k in range(len(outs))
+        ],
         scratch_shapes=scratch,
         name=name,
         compiler_params=pltpu.CompilerParams(vmem_limit_bytes=16 << 20),
-    )(*[pltpu.with_memory_space_constraint(a, pltpu.VMEM) for a in args])
+    )(
+        *[
+            pltpu.with_memory_space_constraint(a, pltpu.HBM if k in raw else pltpu.VMEM)
+            for k, a in enumerate(args)
+        ]
+    )
     return tuple(got) if many else got[0]
 
 
@@ -138,13 +149,47 @@
 
 def project(flat, w_one, other):
     groups, nodes, cols = flat.shape
-
-    def body(rows, w, out):
+    width = w_one.shape[1]
+    cut = width // 4
+    held = pltpu.VMEM((CHIPS, nodes, cols), BF16)
+    sems = pltpu.SemaphoreType.DMA((2, CHIPS))
+    picks = shape((CHIPS, nodes, width))
+
+    def fetch(rows, mine, sem):
         ids = places(SUM_OTHER if other else SUM_MINE, other)
-        picked = jnp.concatenate([rows[g] for g in ids], axis=0)
+        moves = [
+            pltpu.make_async_copy(rows.at[g], mine.at[k], sem.at[0, k]) for k, g in enumerate(ids)
+        ]
+        for move in moves:
+            move.start()
+        return moves
+
+    def other_body(rows, w, out, w_out, mine, sem):
+        moves = fetch(rows, mine, sem)
+        cuts = [slice(k * cut, (k + 1) * cut) for k in range(4)]
+        loads = [
+            pltpu.make_async_copy(w.at[:, c], w_out.at[:, c], sem.at[1, k])
+            for k, c in enumerate(cuts)
+        ]
+        for load in loads:
+            load.start()
+        for move in moves:
+            move.wait()
+        picked = mine[...].reshape(CHIPS * nodes, cols)
+        for load, c in zip(loads, cuts):
+            load.wait()
+            out[:, :, c] = mm(picked, w_out[:, c]).astype(BF16).reshape(CHIPS, nodes, cut)
+
+    def mine_body(rows, w, out, mine, sem):
+        for move in fetch(rows, mine, sem):
+            move.wait()
+        picked = mine[...].reshape(CHIPS * nodes, cols)
         out[...] = mm(picked, w[...]).astype(BF16).reshape(out.shape)
 
-    return whole("project", body, shape((CHIPS, nodes, w_one.shape[1])), flat, w_one)
+    if other:
+        outs = (picks, shape(w_one.shape))
+        return whole("project", other_body, outs, flat, w_one, scratch=[held, sems], raw=(0, 1))
+    return whole("project", mine_body, picks, flat, w_one, scratch=[held, sems], raw=(0,))
 
 
 def add(*terms):
@@ -296,7 +341,8 @@
     def swap(block):
         return lax.ppermute(block, "feat", SWAP)
 
-    got = swap(project(features, w_one, True))
+    theirs, w_one = project(features, w_one, True)
+    got = swap(theirs)
     mine = project(features, w_one, False)
     give, take, own, own_t, inv = whole(
         "tables",
@@ -337,7 +383,8 @@
         ),
         recv, p_self, p_near, grads, inv, w_two, give, take, own, own_t,
         scratch=[pltpu.VMEM((groups, rows, width), BF16)],
-        far=(0, 1, 2, 3, 4, 5),
+        far=(0, 3, 4, 5),
+        kept=(1, 2),
     )
     recv = trade(boxes.reshape(parts, 2 * kmax, width)).reshape(span, width)
 
@@ -390,7 +437,6 @@
     held_y = jnp.concatenate([held_y, y_move(held_y, y_second)])
     held_x = jnp.stack([mine, one_x])
     last_x = x_move(held_x, x_second)
-    held_y, last_x = lax.optimization_barrier((held_y, last_x))
     one = whole(
         "spread", spread_body, shape((cols, 2 * width), F32), held_x, last_x, far=(0,)
     )

time: 172 us -> 171 us (level); the launches traced: 169 us -> 171 us
  local copies, waits for them, and re-layouts: 6.73 us -> 2.98 us
  Pallas kernels: 11.1 us -> 14.6 us
  waiting for transfers between devices: 65.8 us -> 67.8 us
    ppermute x4, waiting for transfers between devices: 16.7 us -> 21.5 us  [x_move(): return lax.ppermute(block, ('feat', 'dom'), pairs)]
    unnamed x32 -> x24, local copies, waits for them, and re-layouts: 4.78 us -> 1.03 us
    pallas_call x13, Pallas kernels: 11.1 us -> 14.6 us  [whole(): pl.pallas_call(body, out_shape=kinds, in_specs=[anywhere if k in raw else...]
  transfers between devices with their start and end apart: 16 -> 16, of which waited for: 15 -> 13; matrix products, arithmetic and copies ran while one was open for 3% -> 3% of each run, Pallas kernels for 3% -> 3%
where the time goes in v9:
time: 171 us
  waiting for transfers between devices  67.8 us (40%)
  blocking collectives  56.4 us (33%)
  starting transfers between devices  24.4 us (14%)
  Pallas kernels  14.6 us (9%)
  other arithmetic  3.46 us (2%)
  local copies, waits for them, and re-layouts  2.98 us (2%)
    all_to_all x3, blocking collectives, trade(): lax.all_to_all(boxes, 'dom', split_axis=0, concat_axis=0, axis_index_grou...  56.4 us
    ppermute x8, waiting for transfers between devices, y_move(): return lax.ppermute(block, 'feat', pairs)  33.7 us
    ppermute x4, waiting for transfers between devices, x_move(): return lax.ppermute(block, ('feat', 'dom'), pairs)  21.5 us
    pallas_call x13, Pallas kernels, whole(): pl.pallas_call(body, out_shape=kinds, in_specs=[anywhere if k in raw else...  14.6 us
    ppermute x8, starting transfers between devices, y_move(): return lax.ppermute(block, 'feat', pairs)  12.5 us
    all_to_all x1, waiting for transfers between devices, trade(): lax.all_to_all(boxes, 'dom', split_axis=0, concat_axis=0, axis_index_grou...  9.11 us
    ppermute x4, starting transfers between devices, x_move(): return lax.ppermute(block, ('feat', 'dom'), pairs)  6.47 us
    all_to_all x1, starting transfers between devices, trade(): lax.all_to_all(boxes, 'dom', split_axis=0, concat_axis=0, axis_index_grou...  5.12 us
  transfers between devices with their start and end apart: 16, of which 13 were waited for; matrix products, arithmetic and copies ran while one was open for 3% of the time, Pallas kernels for 3%

profile of v9, /device:TPU:32, one launch (start us, length us, event | category | flops | bytes accessed | tf_op | source)
XLA Modules:
  0.0 170.6 jit_solution(15630232926597873248)
XLA Ops:
  0.6 3.0 %project.2 = (bf16[4,128,1024]{2,1,0:T(8,128)(2,1)S(1)}, bf16[512,1024]{1,0:T(8,128)(2,1)S(1)}) custom-call(bf16[8,128,512]{2,1,0:T(8,128)(2,1)} %flat.1, bf16[512,1024]{1,0:T(8,128)(2,1)} %w.1), custom_call_target="tpu_custom_call" | custom-call | tf_op jit(solution)/shard_map/project/pallas_call | solution.py:52
  3.7 1.9 %project.3.part = bf16[4,128,1024]{2,1,0:T(8,128)(2,1)S(1)} custom-call(bf16[8,128,512]{2,1,0:T(8,128)(2,1)} %flat.1, bf16[512,1024]{1,0:T(8,128)(2,1)S(1)} %get-tuple-element.32.w), custom_call_target="tpu_custom_call" | custom-call | tf_op jit(solution)/shard_map/project/pallas_call | solution.py:52
  5.7 0.7 collective-permute-done.got
  6.4 0.2 add_convert_fusion
  6.6 1.7 collective-permute-start.1
  8.3 0.6 tables.1
  8.8 7.0 %collective-permute-done.1.near = bf16[2,128,1024]{2,1,0:T(8,128)(2,1)S(1)} collective-permute-done((bf16[2,128,1024]{2,1,0:T(8,128)(2,1)S(1)}, bf16[2,128,1024]{2,1,0:T(8,128)(2,1)S(1)}, u32[]{:S(2)}, u32[]{:S(2)}) %collective-permute-start.1) | collective-permute-done | bytes 524320 | tf_op jit(solution)/shard_map/ppermute | solution.py:336
  15.9 0.1 fusion
  16.0 3.1 %collective-permute-start.2 = (bf16[128,1024]{1,0:T(8,128)(2,1)S(1)}, bf16[128,1024]{1,0:T(8,128)(2,1)S(1)}, u32[]{:S(2)}, u32[]{:S(2)}) collective-permute-start(bf16[128,1024]{1,0:T(8,128)(2,1)S(1)} %fusion), channel_id=1, source_target_pairs={{0,192},{32,96},{64,128},{96,32},{128,64},{160,224},{192,0},{224,1... | collective-permute-start | bytes 786440 | tf_op jit(solution)/shard_map/ppermute | solution.py:336
  19.1 0.4 turn.1.flat_t
  19.5 4.2 %collective-permute-done.2.far = bf16[128,1024]{1,0:T(8,128)(2,1)S(1)} collective-permute-done((bf16[128,1024]{1,0:T(8,128)(2,1)S(1)}, bf16[128,1024]{1,0:T(8,128)(2,1)S(1)}, u32[]{:S(2)}, u32[]{:S(2)}) %collective-permute-start.2) | collective-permute-done | bytes 262176 | tf_op jit(solution)/shard_map/ppermute | solution.py:336
  23.7 0.4 forward.1
  24.1 26.8 %all_to_all.20 = bf16[32,16,512]{2,1,0:T(8,128)(2,1)S(1)} all-to-all(bf16[32,16,512]{2,1,0:T(8,128)(2,1)S(1)} %bitcast.34), channel_id=1, replica_groups=mesh['feat'=8,'dom'=32] {'dom'}, dimensions={0} | all-to-all | bytes 1048576 | tf_op jit(solution)/shard_map/all_to_all | solution.py:76
  50.9 2.2 %middle.1 = (bf16[512,512]{1,0:T(8,128)(2,1)}, bf16[128,512]{1,0:T(8,128)(2,1)}, bf16[128,512]{1,0:T(8,128)(2,1)}, bf16[5,128,512]{2,1,0:T(8,128)(2,1)}, bf16[2,...) custom-call(bf16[512,512]{1,0:T(8,128)(2,1)S(1)} %bitcast.32, f32[128,512]{1,0:T(8,128)S(1)} %get-tuple-element.41.p_self, ...), custom_call_target="tpu_custom_call" | custom-call | tf_op jit(solution)/shard_map/middle/pallas_call | solution.py:52
  53.1 0.6 collective-permute-start.3
  53.7 5.1 %all-to-all-start.1 = ((bf16[32,16,512]{2,1,0:T(8,128)(2,1)}), bf16[32,16,512]{2,1,0:T(8,128)(2,1)S(1)}, u32[]{:S(2)}, u32[]{:S(2)}) async-start(bf16[32,16,512]{2,1,0:T(8,128)(2,1)} %bitcast.7), calls=%async_computation.1 | async-start | bytes 1048576 | tf_op jit(solution)/shard_map/all_to_all | solution.py:76
  58.9 0.9 slice.57
  59.8 4.3 %collective-permute-done.3 = bf16[5,128,512]{2,1,0:T(8,128)(2,1)} collective-permute-done((bf16[5,128,512]{2,1,0:T(8,128)(2,1)}, bf16[5,128,512]{2,1,0:T(8,128)(2,1)}, u32[]{:S(2)}, u32[]{:S(2)}) %collective-permute-start.3) | collective-permute-done | bytes 655392 | tf_op jit(solution)/shard_map/ppermute | solution.py:336
  64.0 0.9 slice.73
  65.0 1.0 add_convert_fusion.1
  66.0 0.8 pad_maximum_fusion
  66.8 9.1 %all-to-all-done.1 = bf16[32,16,512]{2,1,0:T(8,128)(2,1)S(1)} async-done(((bf16[32,16,512]{2,1,0:T(8,128)(2,1)}), bf16[32,16,512]{2,1,0:T(8,128)(2,1)S(1)}, u32[]{:S(2)}, u32[]{:S(2)}) %all-to-all-start.1) | async-done | bytes 524320 | tf_op jit(solution)/shard_map/all_to_all | solution.py:76
  75.9 0.4 collective-permute-start.4
  76.3 0.9 copy-done.4
  77.2 0.3 near.1
  77.5 0.9 collective-permute-start.5
  78.5 5.3 %collective-permute-done.5 = bf16[128,512]{1,0:T(8,128)(2,1)S(1)} collective-permute-done((bf16[128,512]{1,0:T(8,128)(2,1)S(1)}, bf16[128,512]{1,0:T(8,128)(2,1)S(1)}, u32[]{:S(2)}, u32[]{:S(2)}) %collective-permute-start.5) | collective-permute-done | bytes 131104 | tf_op jit(solution)/shard_map/ppermute | solution.py:336
  83.8 2.9 %collective-permute-start.6 = (bf16[2,128,512]{2,1,0:T(8,128)(2,1)S(1)}, bf16[2,128,512]{2,1,0:T(8,128)(2,1)S(1)}, u32[]{:S(2)}, u32[]{:S(2)}) collective-permute-start(bf16[2,128,512]{2,1,0:T(8,128)(2,1)S(1)} %pad_maximum_fusion.3), channel_id=1, source_target_pairs={{0,192},{32,96},{64,128},{96,32},{128,64},{160,224},{192,0},{224,1... | collective-permute-start | bytes 786440 | tf_op jit(solution)/shard_map/ppermute | solution.py:336
  86.8 1.0 convert_add_fusion
  87.8 3.6 %collective-permute-done.6 = bf16[2,128,512]{2,1,0:T(8,128)(2,1)S(1)} collective-permute-done((bf16[2,128,512]{2,1,0:T(8,128)(2,1)S(1)}, bf16[2,128,512]{2,1,0:T(8,128)(2,1)S(1)}, u32[]{:S(2)}, u32[]{:S(2)}) %collective-permute-start.6) | collective-permute-done | bytes 262176 | tf_op jit(solution)/shard_map/ppermute | solution.py:336
  91.6 2.8 %collective-permute-done.7.other = bf16[9,128,512]{2,1,0:T(8,128)(2,1)S(1)} collective-permute-done((bf16[9,128,512]{2,1,0:T(8,128)(2,1)S(1)}, bf16[9,128,512]{2,1,0:T(8,128)(2,1)S(1)}, u32[]{:S(2)}, u32[]{:S(2)}) %collective-permute-start.7) | collective-permute-done | bytes 1179680 | tf_op jit(solution)/shard_map/ppermute | solution.py:342
  94.4 1.5 grad.1
  96.0 0.9 collective-permute-start.8
  96.8 9.8 %collective-permute-done.8.got = bf16[8,160,256]{2,1,0:T(8,128)(2,1)S(1)} collective-permute-done((bf16[8,160,256]{2,1,0:T(8,128)(2,1)S(1)}, bf16[8,160,256]{2,1,0:T(8,128)(2,1)S(1)}, u32[]{:S(2)}, u32[]{:S(2)}) %collective-permute-start.8) | collective-permute-done | bytes 655392 | tf_op jit(solution)/shard_map/ppermute | solution.py:339
  106.7 1.9 %collective-permute-start.9 = (bf16[8,96,256]{2,1,0:T(8,128)(2,1)S(1)}, bf16[8,96,256]{2,1,0:T(8,128)(2,1)S(1)}, u32[]{:S(2)}, u32[]{:S(2)}) collective-permute-start(bf16[8,96,256]{2,1,0:T(8,128)(2,1)S(1)} %x_pass.1.sent), channel_id=1, source_target_pairs={{0,3},{1,2},{2,1},{3,0},{4,7},{5,6},{6,5},{7,4},{8,11},{9,10},{10,... | collective-permute-start | bytes 1179656 | tf_op jit(solution)/shard_map/ppermute | solution.py:339
  108.7 1.2 out.1
  109.8 6.1 %collective-permute-done.9.last = bf16[8,96,256]{2,1,0:T(8,128)(2,1)S(1)} collective-permute-done((bf16[8,96,256]{2,1,0:T(8,128)(2,1)S(1)}, bf16[8,96,256]{2,1,0:T(8,128)(2,1)S(1)}, u32[]{:S(2)}, u32[]{:S(2)}) %collective-permute-start.9) | collective-permute-done | bytes 393248 | tf_op jit(solution)/shard_map/ppermute | solution.py:339
  116.0 0.1 x_sum.1
  116.1 15.6 %all_to_all.21 = bf16[8,96,256]{2,1,0:T(8,128)(2,1)S(1)} all-to-all(bf16[8,96,256]{2,1,0:T(8,128)(2,1)S(1)} %x_sum.1), channel_id=1, replica_groups={{0,4,8,12,16,20,24,28},{1,5,9,13,17,21,25,29},{2,6,10,14,18,22,26,30},{..., dimensions={0} | all-to-all | bytes 786432 | tf_op jit(solution)/shard_map/all_to_all | solution.py:76
  131.8 14.1 %all_to_all.22 = bf16[8,96,256]{2,1,0:T(8,128)(2,1)S(1)} all-to-all(bf16[8,96,256]{2,1,0:T(8,128)(2,1)S(1)} %broadcast_in_dim.10), channel_id=1, replica_groups={{0,4,8,12,16,20,24,28},{1,5,9,13,17,21,25,29},{2,6,10,14,18,22,26,30},{..., dimensions={0} | all-to-all | bytes 786432 | tf_op jit(solution)/shard_map/all_to_all | solution.py:76
  145.9 1.8 %collective-permute-start.11 = (bf16[8,64,256]{2,1,0:T(8,128)(2,1)S(1)}, bf16[8,64,256]{2,1,0:T(8,128)(2,1)S(1)}, u32[]{:S(2)}, u32[]{:S(2)}) collective-permute-start(bf16[8,64,256]{2,1,0:T(8,128)(2,1)S(1)} %get-tuple-element.62), channel_id=1, source_target_pairs={{0,1},{1,0},{2,3},{3,2},{4,5},{5,4},{6,7},{7,6},{8,9},{9,8},{10,11... | collective-permute-start | bytes 786440 | tf_op jit(solution)/shard_map/ppermute | solution.py:339
  147.9 6.4 %collective-permute-done.10 = bf16[128,512]{1,0:T(8,128)(2,1)S(1)} collective-permute-done((bf16[128,512]{1,0:T(8,128)(2,1)S(1)}, bf16[128,512]{1,0:T(8,128)(2,1)S(1)}, u32[]{:S(2)}, u32[]{:S(2)}) %collective-permute-start.10) | collective-permute-done | bytes 131104 | tf_op jit(solution)/shard_map/ppermute | solution.py:336
  154.3 2.8 %collective-permute-start.13 = (bf16[2,128,512]{2,1,0:T(8,128)(2,1)S(1)}, bf16[2,128,512]{2,1,0:T(8,128)(2,1)S(1)}, u32[]{:S(2)}, u32[]{:S(2)}) collective-permute-start(bf16[2,128,512]{2,1,0:T(8,128)(2,1)S(1)} %pad_maximum_fusion.4), channel_id=1, source_target_pairs={{0,192},{32,96},{64,128},{96,32},{128,64},{160,224},{192,0},{224,1... | collective-permute-start | bytes 786440 | tf_op jit(solution)/shard_map/ppermute | solution.py:336
  157.2 1.8 %collective-permute-start.12 = (bf16[2,8,64,256]{3,2,1,0:T(8,128)(2,1)S(1)}, bf16[2,8,64,256]{3,2,1,0:T(8,128)(2,1)S(1)}, u32[]{:S(2)}, u32[]{:S(2)}) collective-permute-start(bf16[2,8,64,256]{3,2,1,0:T(8,128)(2,1)S(1)} %pad_maximum_fusion.1.held), channel_id=1, source_target_pairs={{0,3},{1,2},{2,1},{3,0},{4,7},{5,6},{6,5},{7,4},{8,11},{9,10},{10,... | collective-permute-start | bytes 1572872 | tf_op jit(solution)/shard_map/ppermute | solution.py:339
  159.0 3.0 %collective-permute-done.13 = bf16[2,128,512]{2,1,0:T(8,128)(2,1)S(1)} collective-permute-done((bf16[2,128,512]{2,1,0:T(8,128)(2,1)S(1)}, bf16[2,128,512]{2,1,0:T(8,128)(2,1)S(1)}, u32[]{:S(2)}, u32[]{:S(2)}) %collective-permute-start.13) | collective-permute-done | bytes 262176 | tf_op jit(solution)/shard_map/ppermute | solution.py:336
  162.1 5.5 %collective-permute-done.12.last = bf16[2,8,64,256]{3,2,1,0:T(8,128)(2,1)S(1)} collective-permute-done((bf16[2,8,64,256]{3,2,1,0:T(8,128)(2,1)S(1)}, bf16[2,8,64,256]{3,2,1,0:T(8,128)(2,1)S(1)}, u32[]{:S(2)}, u32[]{:S(2)}) %collective-permute-start.12) | collective-permute-done | bytes 524320 | tf_op jit(solution)/shard_map/ppermute | solution.py:339
  167.6 1.5 spread.1
  169.1 1.5 join.1
  (43 shorter events, 1.0 us)
Async XLA Ops:
  3.6 2.7 %collective-permute-start = (bf16[4,128,1024]{2,1,0:T(8,128)(2,1)S(1)}, bf16[4,128,1024]{2,1,0:T(8,128)(2,1)S(1)}, u32[]{:S(2)}, u32[]{:S(2)}) collective-permute-start(bf16[4,128,1024]{2,1,0:T(8,128)(2,1)S(1)} %get-tuple-element.33), channel_id=1, source_target_pairs={{0,32},{32,0},{64,96},{96,64},{128,160},{160,128},{192,224},{224,1... | collective-permute-start | bytes 3145736 | tf_op jit(solution)/shard_map/ppermute | solution.py:342
  5.6 2.6 %copy-start.8 = (s32[1,128,10]{1,0,2:T(1,128)S(1)}, s32[1,128,10]{1,0,2:T(1,128)}, u32[]{:S(2)}) copy-start(s32[1,128,10]{1,0,2:T(1,128)} %param.10) | copy-start | bytes 15364
  5.7 2.6 %copy-start.5 = (s32[1,32,8]{1,2,0:T(8,128)S(1)}, s32[1,32,8]{1,2,0:T(8,128)}, u32[]{:S(2)}) copy-start(s32[1,32,8]{1,2,0:T(8,128)} %param.12) | copy-start | bytes 3076
  5.7 2.6 %copy-start.6 = (s32[1,128]{1,0:T(1,128)S(1)}, s32[1,128]{1,0:T(1,128)}, u32[]{:S(2)}) copy-start(s32[1,128]{1,0:T(1,128)} %deg.1) | copy-start | bytes 1540
  5.7 13.4 %copy-start = (bf16[8,128,512]{2,1,0:T(8,128)(2,1)S(1)}, bf16[8,128,512]{2,1,0:T(8,128)(2,1)}, u32[]{:S(2)}) copy-start(bf16[8,128,512]{2,1,0:T(8,128)(2,1)} %flat.1) | copy-start | bytes 3145732
  6.6 9.3 %collective-permute-start.1 = (bf16[2,128,1024]{2,1,0:T(8,128)(2,1)S(1)}, bf16[2,128,1024]{2,1,0:T(8,128)(2,1)S(1)}, u32[]{:S(2)}, u32[]{:S(2)}) collective-permute-start(bf16[2,128,1024]{2,1,0:T(8,128)(2,1)S(1)} %add_convert_fusion), channel_id=1, source_target_pairs={{0,64},{32,224},{64,0},{96,160},{128,192},{160,96},{192,128},{224,... | collective-permute-start | bytes 1572872 | tf_op jit(solution)/shard_map/ppermute | solution.py:336
  16.0 7.7 %copy-start.2 = (bf16[1,128,512]{2,1,0:T(8,128)(2,1)S(1)}, bf16[1,128,512]{2,1,0:T(8,128)(2,1)}, u32[]{:S(2)}) copy-start(bf16[1,128,512]{2,1,0:T(8,128)(2,1)} %param.13) | copy-start | bytes 393220
  16.0 7.7 %collective-permute-start.2 = (bf16[128,1024]{1,0:T(8,128)(2,1)S(1)}, bf16[128,1024]{1,0:T(8,128)(2,1)S(1)}, u32[]{:S(2)}, u32[]{:S(2)}) collective-permute-start(bf16[128,1024]{1,0:T(8,128)(2,1)S(1)} %fusion), channel_id=1, source_target_pairs={{0,192},{32,96},{64,128},{96,32},{128,64},{160,224},{192,0},{224,1... | collective-permute-start | bytes 786440 | tf_op jit(solution)/shard_map/ppermute | solution.py:336
  24.1 26.8 %copy-start.1 = (bf16[1024,512]{1,0:T(8,128)(2,1)S(1)}, bf16[1024,512]{1,0:T(8,128)(2,1)}, u32[]{:S(2)}) copy-start(bf16[1024,512]{1,0:T(8,128)(2,1)} %w_two.3) | copy-start | bytes 3145732
  53.1 10.9 %collective-permute-start.3 = (bf16[5,128,512]{2,1,0:T(8,128)(2,1)}, bf16[5,128,512]{2,1,0:T(8,128)(2,1)}, u32[]{:S(2)}, u32[]{:S(2)}) collective-permute-start(bf16[5,128,512]{2,1,0:T(8,128)(2,1)} %get-tuple-element.46), channel_id=1, source_target_pairs={{0,64},{32,224},{64,0},{96,160},{128,192},{160,96},{192,128},{224,... | collective-permute-start | bytes 1966088 | tf_op jit(solution)/shard_map/ppermute | solution.py:336
  53.7 22.2 %all-to-all-start.1 = ((bf16[32,16,512]{2,1,0:T(8,128)(2,1)}), bf16[32,16,512]{2,1,0:T(8,128)(2,1)S(1)}, u32[]{:S(2)}, u32[]{:S(2)}) async-start(bf16[32,16,512]{2,1,0:T(8,128)(2,1)} %bitcast.7), calls=%async_computation.1 | async-start | bytes 1048576 | tf_op jit(solution)/shard_map/all_to_all | solution.py:76
  75.9 10.8 %collective-permute-start.4 = (bf16[4,128,512]{2,1,0:T(8,128)(2,1)}, bf16[4,128,512]{2,1,0:T(8,128)(2,1)S(1)}, u32[]{:S(2)}, u32[]{:S(2)}) collective-permute-start(bf16[4,128,512]{2,1,0:T(8,128)(2,1)} %pad_maximum_fusion), channel_id=1, source_target_pairs={{0,192},{32,96},{64,128},{96,32},{128,64},{160,224},{192,0},{224,1... | collective-permute-start | bytes 1572872 | tf_op jit(solution)/shard_map/ppermute | solution.py:336
  76.3 0.9 copy-start.4
  77.2 1.2 copy-start.7
  77.5 6.2 %collective-permute-start.5 = (bf16[128,512]{1,0:T(8,128)(2,1)S(1)}, bf16[128,512]{1,0:T(8,128)(2,1)S(1)}, u32[]{:S(2)}, u32[]{:S(2)}) collective-permute-start(bf16[128,512]{1,0:T(8,128)(2,1)S(1)} %near.1), channel_id=1, source_target_pairs={{0,64},{32,224},{64,0},{96,160},{128,192},{160,96},{192,128},{224,... | collective-permute-start | bytes 393224 | tf_op jit(solution)/shard_map/ppermute | solution.py:336
  83.8 7.7 %collective-permute-start.6 = (bf16[2,128,512]{2,1,0:T(8,128)(2,1)S(1)}, bf16[2,128,512]{2,1,0:T(8,128)(2,1)S(1)}, u32[]{:S(2)}, u32[]{:S(2)}) collective-permute-start(bf16[2,128,512]{2,1,0:T(8,128)(2,1)S(1)} %pad_maximum_fusion.3), channel_id=1, source_target_pairs={{0,192},{32,96},{64,128},{96,32},{128,64},{160,224},{192,0},{224,1... | collective-permute-start | bytes 786440 | tf_op jit(solution)/shard_map/ppermute | solution.py:336
  91.5 2.9 %collective-permute-start.7 = (bf16[9,128,512]{2,1,0:T(8,128)(2,1)S(1)}, bf16[9,128,512]{2,1,0:T(8,128)(2,1)S(1)}, u32[]{:S(2)}, u32[]{:S(2)}) collective-permute-start(bf16[9,128,512]{2,1,0:T(8,128)(2,1)S(1)} %fusion.1.held), channel_id=1, source_target_pairs={{0,32},{32,0},{64,96},{96,64},{128,160},{160,128},{192,224},{224,1... | collective-permute-start | bytes 3538952 | tf_op jit(solution)/shard_map/ppermute | solution.py:342
  96.0 12.7 %copy-start.3 = (bf16[128,512]{1,0:T(8,128)(2,1)S(1)}, bf16[128,512]{1,0:T(8,128)(2,1)}, u32[]{:S(2)}) copy-start(bf16[128,512]{1,0:T(8,128)(2,1)} %get-tuple-element.56.hidden) | copy-start | bytes 393220
  96.0 10.7 %collective-permute-start.8 = (bf16[8,160,256]{2,1,0:T(8,128)(2,1)S(1)}, bf16[8,160,256]{2,1,0:T(8,128)(2,1)S(1)}, u32[]{:S(2)}, u32[]{:S(2)}) collective-permute-start(bf16[8,160,256]{2,1,0:T(8,128)(2,1)S(1)} %get-tuple-element.55), channel_id=1, source_target_pairs={{0,1},{1,0},{2,3},{3,2},{4,5},{5,4},{6,7},{7,6},{8,9},{9,8},{10,11... | collective-permute-start | bytes 1966088 | tf_op jit(solution)/shard_map/ppermute | solution.py:339
  106.7 9.3 %collective-permute-start.9 = (bf16[8,96,256]{2,1,0:T(8,128)(2,1)S(1)}, bf16[8,96,256]{2,1,0:T(8,128)(2,1)S(1)}, u32[]{:S(2)}, u32[]{:S(2)}) collective-permute-start(bf16[8,96,256]{2,1,0:T(8,128)(2,1)S(1)} %x_pass.1.sent), channel_id=1, source_target_pairs={{0,3},{1,2},{2,1},{3,0},{4,7},{5,6},{6,5},{7,4},{8,11},{9,10},{10,... | collective-permute-start | bytes 1179656 | tf_op jit(solution)/shard_map/ppermute | solution.py:339
  145.9 8.3 %collective-permute-start.11 = (bf16[8,64,256]{2,1,0:T(8,128)(2,1)S(1)}, bf16[8,64,256]{2,1,0:T(8,128)(2,1)S(1)}, u32[]{:S(2)}, u32[]{:S(2)}) collective-permute-start(bf16[8,64,256]{2,1,0:T(8,128)(2,1)S(1)} %get-tuple-element.62), channel_id=1, source_target_pairs={{0,1},{1,0},{2,3},{3,2},{4,5},{5,4},{6,7},{7,6},{8,9},{9,8},{10,11... | collective-permute-start | bytes 786440 | tf_op jit(solution)/shard_map/ppermute | solution.py:339
  147.8 6.5 %collective-permute-start.10 = (bf16[128,512]{1,0:T(8,128)(2,1)S(1)}, bf16[128,512]{1,0:T(8,128)(2,1)S(1)}, u32[]{:S(2)}, u32[]{:S(2)}) collective-permute-start(bf16[128,512]{1,0:T(8,128)(2,1)S(1)} %get-tuple-element.66), channel_id=1, source_target_pairs={{0,64},{32,224},{64,0},{96,160},{128,192},{160,96},{192,128},{224,... | collective-permute-start | bytes 393224 | tf_op jit(solution)/shard_map/ppermute | solution.py:336
  154.3 7.7 %collective-permute-start.13 = (bf16[2,128,512]{2,1,0:T(8,128)(2,1)S(1)}, bf16[2,128,512]{2,1,0:T(8,128)(2,1)S(1)}, u32[]{:S(2)}, u32[]{:S(2)}) collective-permute-start(bf16[2,128,512]{2,1,0:T(8,128)(2,1)S(1)} %pad_maximum_fusion.4), channel_id=1, source_target_pairs={{0,192},{32,96},{64,128},{96,32},{128,64},{160,224},{192,0},{224,1... | collective-permute-start | bytes 786440 | tf_op jit(solution)/shard_map/ppermute | solution.py:336
  157.2 10.5 %collective-permute-start.12 = (bf16[2,8,64,256]{3,2,1,0:T(8,128)(2,1)S(1)}, bf16[2,8,64,256]{3,2,1,0:T(8,128)(2,1)S(1)}, u32[]{:S(2)}, u32[]{:S(2)}) collective-permute-start(bf16[2,8,64,256]{3,2,1,0:T(8,128)(2,1)S(1)} %pad_maximum_fusion.1.held), channel_id=1, source_target_pairs={{0,3},{1,2},{2,1},{3,0},{4,7},{5,6},{6,5},{7,4},{8,11},{9,10},{10,... | collective-permute-start | bytes 1572872 | tf_op jit(solution)/shard_map/ppermute | solution.py:339
  162.0 7.1 %collective-permute-start.14 = (bf16[4,128,512]{2,1,0:T(8,128)(2,1)S(1)}, bf16[4,128,512]{2,1,0:T(8,128)(2,1)S(1)}, u32[]{:S(2)}, u32[]{:S(2)}) collective-permute-start(bf16[4,128,512]{2,1,0:T(8,128)(2,1)S(1)} %pad_maximum_fusion.2.held), channel_id=1, source_target_pairs={{0,32},{32,0},{64,96},{96,64},{128,160},{160,128},{192,224},{224,1... | collective-permute-start | bytes 1572872 | tf_op jit(solution)/shard_map/ppermute | solution.py:342

commit v10 on v9

--- a/solution.py
+++ b/solution.py
@@ -78,42 +78,36 @@
     )
 
 
-def tables_body(nbr_t, deg, sends_t, give, take, own, own_t, inv):
+def tables_body(
+    nbr_t, deg, sends_t, grads, pick, mean, back, home, own, own_t, inv, boxes
+):
     fan, nodes = nbr_t.shape
     kmax, parts = sends_t.shape
-    span = 2 * kmax * parts
-    r = lax.broadcasted_iota(jnp.int32, (span, nodes), 0)
-    j = r % (2 * kmax)
-    entry = nodes + r // (2 * kmax) * kmax + j
-    leave = jnp.where(j < kmax, entry, -2)
-    arrive = jnp.where(j >= kmax, entry - kmax, -2)
-    row = lax.broadcasted_iota(jnp.int32, (nodes, nodes), 0)
-    leave_sum = jnp.zeros((span, nodes), F32)
-    arrive_sum = jnp.zeros((span, nodes), F32)
-    own_sum = jnp.zeros((nodes, nodes), F32)
+    span = kmax * parts
+    entry = lax.broadcasted_iota(jnp.int32, (nodes + span, nodes), 0)
+    count = jnp.zeros((nodes + span, nodes), F32)
     for s in range(fan):
         used = jnp.where(s < deg[...], nbr_t[s : s + 1, :], -1)
-        leave_sum += jnp.where(leave == used, 1.0, 0.0)
-        arrive_sum += jnp.where(arrive == used, 1.0, 0.0)
-        own_sum += jnp.where(row == used, 1.0, 0.0)
-    own_t[...] = own_sum.astype(BF16)
-    own[...] = own_sum.T.astype(BF16)
+        count += jnp.where(entry == used, 1.0, 0.0)
+    own_t[...] = count[:nodes].astype(BF16)
+    own[...] = count[:nodes].T.astype(BF16)
+    back[...] = count[nodes:].astype(BF16)
+    mean[...] = count[nodes:].T.astype(BF16)
     part = lax.broadcasted_iota(jnp.int32, (parts, span), 0)
     lane = lax.broadcasted_iota(jnp.int32, (parts, span), 1)
-    spread = jnp.where(lane // (2 * kmax) == part, 1.0, 0.0).astype(BF16)
+    spread = jnp.where(lane // kmax == part, 1.0, 0.0).astype(BF16)
     ids = mm(sends_t[...].astype(F32).astype(BF16), spread)
     slot = lax.broadcasted_iota(jnp.int32, (kmax, span), 0)
-    at = lax.broadcasted_iota(jnp.int32, (kmax, span), 1) % (2 * kmax)
-    back_id = jnp.sum(jnp.where(slot == at, ids + 1.0, 0.0), axis=0, keepdims=True) - 1.0
-    pick_id = jnp.sum(jnp.where(slot + kmax == at, ids + 1.0, 0.0), axis=0, keepdims=True) - 1.0
+    at = lax.broadcasted_iota(jnp.int32, (kmax, span), 1) % kmax
+    sent = jnp.sum(jnp.where(slot == at, ids, 0.0), axis=0, keepdims=True)
     node = lax.broadcasted_iota(jnp.int32, (nodes, span), 0).astype(F32)
-    home = jnp.where(node == back_id, 1.0, 0.0)
-    pick = jnp.where(node == pick_id, 1.0, 0.0)
-    give[:, :nodes] = leave_sum.astype(BF16)
-    give[:, nodes:] = pick.T.astype(BF16)
-    take[:nodes, :] = arrive_sum.T.astype(BF16)
-    take[nodes:, :] = home.astype(BF16)
-    inv[...] = jnp.broadcast_to(1.0 / deg[...].astype(F32), (nodes, nodes)).T
+    chosen = jnp.where(node == sent, 1.0, 0.0)
+    home[...] = chosen.astype(BF16)
+    pick[...] = chosen.T.astype(BF16)
+    scales = jnp.broadcast_to(1.0 / deg[...].astype(F32), (nodes, nodes)).T
+    inv[...] = scales
+    scaled = (grads[...].astype(F32) * scales[:, :1]).astype(BF16)
+    boxes[...] = mm(count[nodes:].astype(BF16), scaled).astype(BF16)
 
 
 def turn_body(flat, out):
@@ -199,34 +193,33 @@
     return total
 
 
-def forward_body(part, got, near, far, grads, inv, give, p_self, p_near, boxes):
-    width = grads.shape[1]
+def forward_body(part, got, near, far, pick, p_self, p_near, boxes):
+    width = p_near.shape[1]
     total = add(part[3], got[3], near[0], far[...])
     p_self[...] = total[:, :width]
     mine = total[:, width:].astype(BF16)
     p_near[...] = mine
-    scaled = (grads[...].astype(F32) * inv[:, :1]).astype(BF16)
-    boxes[...] = mm(give[...], jnp.concatenate([scaled, mine], axis=0)).astype(BF16)
+    boxes[...] = mm(pick[...], mine).astype(BF16)
 
 
 def middle_body(
-    recv, p_self, p_near, grads, inv, w_two, give, take, own, own_t,
-    boxes, term_out, hidden_out, first, second, mine, scratch,
+    recv, recv_back, p_self, p_near, grads, inv, w_two, pick, mean, back_t, home, own, own_t,
+    boxes, hidden_boxes, term_out, hidden_out, first, second, mine, scratch,
 ):
     nodes, width = grads.shape
     scales = inv[:, :1]
-    both = mm(take[...], recv[...])
     grad = grads[...]
     scaled = (grad.astype(F32) * scales).astype(BF16)
-    pre = p_self[...] + scales * (both[:nodes] + mm(own[...], p_near[...]))
-    back = (both[nodes:] + mm(own_t[...], scaled)).astype(BF16)
+    pre = p_self[...] + scales * (mm(mean[...], recv[...]) + mm(own[...], p_near[...]))
+    back = (mm(home[...], recv_back[...]) + mm(own_t[...], scaled)).astype(BF16)
     d_hidden = mm(grad, w_two[:width, :], NT) + mm(back, w_two[width:, :], NT)
     sig = jax.nn.sigmoid(pre)
     hidden = (pre * sig).astype(BF16)
     hidden_out[...] = hidden
     d_pre = d_hidden * sig * (1.0 + pre * (1.0 - sig))
     term = (d_pre * scales).astype(BF16)
-    boxes[...] = mm(give[...], jnp.concatenate([term, hidden], axis=0)).astype(BF16)
+    boxes[...] = mm(back_t[...], term).astype(BF16)
+    hidden_boxes[...] = mm(pick[...], hidden).astype(BF16)
     term_out[...] = term
     half = scratch.shape[0] // 2
     for k, right in enumerate((grad, back)):
@@ -241,14 +234,13 @@
         mine[k] = scratch[here]
 
 
-def near_body(recv, term, own_t, take, out):
-    nodes = out.shape[0]
-    out[...] = (mm(own_t[...], term[...]) + mm(take[nodes:, :], recv[...])).astype(BF16)
-
-
-def out_body(recv, hidden, inv, take, own, w_two, out):
-    nodes, width = hidden.shape
-    total = mm(take[:nodes, :], recv[...]) + mm(own[...], hidden[...])
+def near_body(recv, term, own_t, home, out):
+    out[...] = (mm(own_t[...], term[...]) + mm(home[...], recv[...])).astype(BF16)
+
+
+def out_body(recv, hidden, inv, mean, own, w_two, out):
+    width = hidden.shape[1]
+    total = mm(mean[...], recv[...]) + mm(own[...], hidden[...])
     agg = (inv[:, :1] * total).astype(BF16)
     out[...] = (mm(hidden[...], w_two[:width, :]) + mm(agg, w_two[width:, :])).astype(BF16)
 
@@ -325,7 +317,7 @@
     deep = parts // CHIPS
     sends = send_rows[0]
     kmax = sends.shape[1]
-    span = 2 * sends.size
+    span = sends.size
     grads = grad_out[0]
     scale = 1.0 / math.sqrt(groups * nodes * parts)
     y_first, y_second = along_y(0), along_y(1)
@@ -344,54 +336,65 @@
     theirs, w_one = project(features, w_one, True)
     got = swap(theirs)
     mine = project(features, w_one, False)
-    give, take, own, own_t, inv = whole(
+    block = shape((nodes, width))
+    lot = shape((span, width))
+    pick, mean, back_t, home, own, own_t, inv, boxes = whole(
         "tables",
         tables_body,
         (
-            shape((span, 2 * nodes)),
-            shape((2 * nodes, span)),
+            shape((span, nodes)),
+            shape((nodes, span)),
+            shape((span, nodes)),
+            shape((nodes, span)),
             shape((nodes, nodes)),
             shape((nodes, nodes)),
             shape((nodes, nodes), F32),
+            lot,
         ),
-        neighbor[0].T, degree, sends.T,
-    )
+        neighbor[0].T, degree, sends.T, grads,
+    )
+
+    def exchange(boxes):
+        return trade(boxes.reshape(parts, kmax, width)).reshape(span, width)
+
+    recv_back = exchange(boxes)
     flat_t = whole("turn", turn_body, shape((cols, groups * nodes)), features)
     near = y_move(add(mine[:2], got[:2]).astype(BF16), y_first)
-    near, give = lax.optimization_barrier((near, give))
+    near, pick = lax.optimization_barrier((near, pick))
     far = y_move(add(mine[2], got[2], near[1]).astype(BF16), y_second)
-    far, flat_t = lax.optimization_barrier((far, flat_t))
-    block = shape((nodes, width))
+    far, flat_t, recv_back = lax.optimization_barrier((far, flat_t, recv_back))
     p_self, p_near, boxes = whole(
         "forward",
         forward_body,
-        (shape((nodes, width), F32), block, shape((span, width))),
-        mine, got, near, far, grads, inv, give,
-    )
-    recv = trade(boxes.reshape(parts, 2 * kmax, width)).reshape(span, width)
+        (shape((nodes, width), F32), block, lot),
+        mine, got, near, far, pick,
+    )
+    recv = exchange(boxes)
     rows = 2 * width // groups
-    boxes, term, hidden, first, second, mine = whole(
+    boxes, hidden_boxes, term, hidden, first, second, mine = whole(
         "middle",
         middle_body,
         (
-            shape((span, width)),
+            lot,
+            lot,
             block,
             block,
             shape((5, rows, width)),
             shape((2, rows, width)),
             shape((2, rows, width)),
         ),
-        recv, p_self, p_near, grads, inv, w_two, give, take, own, own_t,
+        recv, recv_back, p_self, p_near, grads, inv, w_two, pick, mean, back_t, home, own, own_t,
         scratch=[pltpu.VMEM((groups, rows, width), BF16)],
-        far=(0, 3, 4, 5),
-        kept=(1, 2),
-    )
-    recv = trade(boxes.reshape(parts, 2 * kmax, width)).reshape(span, width)
+        far=(0, 4, 5, 6),
+        kept=(1, 2, 3),
+    )
+    recv = exchange(boxes)
 
     got = y_move(first, y_first)
     message = jnp.concatenate([first[:1], got[:1], add(second, got[3:]).astype(BF16)])
     message, recv = lax.optimization_barrier((message, recv))
-    d_near = whole("near", near_body, block, recv, term, own_t, take)
+    hidden_boxes, message = lax.optimization_barrier((hidden_boxes, message))
+    d_near = whole("near", near_body, block, recv, term, own_t, home)
     one = y_move(d_near, y_first)
     last = y_move(message, y_second)
     sums = add(mine, got[1:3], last[2:])
@@ -399,6 +402,8 @@
     held = jnp.concatenate(
         [message[:2], last[:2], near, y_move(near, y_second), sums[:1].astype(BF16)]
     )
+
+    recv = exchange(hidden_boxes)
 
     kept = 8 * cols // parts // 2
     tail = 4 * width // groups // deep
@@ -416,7 +421,7 @@
             pltpu.VMEM((CHIPS, deep, kept, width // 2), BF16),
         ],
     )
-    out = whole("out", out_body, block, recv, hidden, inv, take, own, w_two, far=(0,))
+    out = whole("out", out_body, block, recv, hidden, inv, mean, own, w_two, far=(0,))
     lot = shape((deep, kept + tail, width // 2))
     got = x_move(first, x_first)
     sent = whole("x_pass", x_pass_body, lot, second, mine, got)

time: 171 us -> 177 us (1.035)
  waiting for transfers between devices: 67.8 us -> 56.8 us
  starting transfers between devices: 24.4 us -> 34.6 us
  local copies, waits for them, and re-layouts: 2.98 us -> 12.2 us
  blocking collectives: 56.4 us -> 49 us
  other arithmetic: 3.46 us -> 6.06 us
    all_to_all x1 -> x3, starting transfers between devices: 5.12 us -> 21.4 us  [trade(): lax.all_to_all(boxes, 'dom', split_axis=0, concat_axis=0, axis_index_grou...]
    ppermute x8, waiting for transfers between devices: 33.7 us -> 23 us  [y_move(): return lax.ppermute(block, 'feat', pairs)]
    unnamed x24 -> x68, local copies, waits for them, and re-layouts: 1.03 us -> 10.3 us
    ppermute x4, waiting for transfers between devices: 21.5 us -> 12.8 us  [x_move(): return lax.ppermute(block, ('feat', 'dom'), pairs)]
    all_to_all x1 -> x3, waiting for transfers between devices: 9.11 us -> 17.5 us  [trade(): lax.all_to_all(boxes, 'dom', split_axis=0, concat_axis=0, axis_index_grou...]
    all_to_all x3, blocking collectives: 56.4 us -> 49 us  [trade(): lax.all_to_all(boxes, 'dom', split_axis=0, concat_axis=0, axis_index_grou...]
    ppermute x4, starting transfers between devices: 6.47 us -> 2.88 us  [x_move(): return lax.ppermute(block, ('feat', 'dom'), pairs)]
    ppermute x8, starting transfers between devices: 12.5 us -> 10 us  [y_move(): return lax.ppermute(block, 'feat', pairs)]
  transfers between devices with their start and end apart: 16 -> 18, of which waited for: 13 -> 15; matrix products, arithmetic and copies ran while one was open for 3% -> 4% of each run, Pallas kernels for 3% -> 3%
where the time goes in v10:
time: 177 us; the launch traced here: 176 us
  waiting for transfers between devices  56.8 us (32%)
  blocking collectives  49 us (28%)
  starting transfers between devices  34.6 us (20%)
  Pallas kernels  16.3 us (9%)
  local copies, waits for them, and re-layouts  12.2 us (7%)
  other arithmetic  6.06 us (3%)
    all_to_all x3, blocking collectives, trade(): lax.all_to_all(boxes, 'dom', split_axis=0, concat_axis=0, axis_index_grou...  49 us
    ppermute x8, waiting for transfers between devices, y_move(): return lax.ppermute(block, 'feat', pairs)  23 us
    all_to_all x3, starting transfers between devices, trade(): lax.all_to_all(boxes, 'dom', split_axis=0, concat_axis=0, axis_index_grou...  21.4 us
    all_to_all x3, waiting for transfers between devices, trade(): lax.all_to_all(boxes, 'dom', split_axis=0, concat_axis=0, axis_index_grou...  17.5 us
    pallas_call x13, Pallas kernels, whole(): pl.pallas_call(body, out_shape=kinds, in_specs=[anywhere if k in raw else...  16.3 us
    ppermute x4, waiting for transfers between devices, x_move(): return lax.ppermute(block, ('feat', 'dom'), pairs)  12.8 us
    unnamed x68, local copies, waits for them, and re-layouts  10.3 us
    ppermute x8, starting transfers between devices, y_move(): return lax.ppermute(block, 'feat', pairs)  10 us
  transfers between devices with their start and end apart: 18, of which 15 were waited for; matrix products, arithmetic and copies ran while one was open for 4% of the time, Pallas kernels for 3%

profile of v10, /device:TPU:32, one launch (start us, length us, event | category | flops | bytes accessed | tf_op | source)
XLA Modules:
  0.0 176.0 jit_solution(16155841189804295138)
XLA Ops:
  0.6 3.0 %project.2 = (bf16[4,128,1024]{2,1,0:T(8,128)(2,1)S(1)}, bf16[512,1024]{1,0:T(8,128)(2,1)S(1)}) custom-call(bf16[8,128,512]{2,1,0:T(8,128)(2,1)} %flat.1, bf16[512,1024]{1,0:T(8,128)(2,1)} %w.1), custom_call_target="tpu_custom_call" | custom-call | tf_op jit(solution)/shard_map/project/pallas_call | solution.py:52
  3.7 1.9 %project.3.part = bf16[4,128,1024]{2,1,0:T(8,128)(2,1)S(1)} custom-call(bf16[8,128,512]{2,1,0:T(8,128)(2,1)} %flat.1, bf16[512,1024]{1,0:T(8,128)(2,1)S(1)} %get-tuple-element.39.w), custom_call_target="tpu_custom_call" | custom-call | tf_op jit(solution)/shard_map/project/pallas_call | solution.py:52
  5.7 0.7 collective-permute-done.got
  6.4 1.1 add_convert_fusion
  7.5 1.6 collective-permute-start.1
  9.6 0.6 copy-done.5
  13.9 0.7 copy-done.11
  14.6 11.2 %all-to-all-start = ((bf16[32,8,512]{2,1,0:T(8,128)(2,1)}), bf16[32,8,512]{2,1,0:T(8,128)(2,1)S(1)}, u32[]{:S(2)}, u32[]{:S(2)}) async-start(bf16[32,8,512]{2,1,0:T(8,128)(2,1)} %bitcast.42), calls=%async_computation | async-start | bytes 524288 | tf_op jit(solution)/shard_map/all_to_all | solution.py:76
  25.8 1.8 %fusion = bf16[128,1024]{1,0:T(8,128)(2,1)} fusion(bf16[4,128,1024]{2,1,0:T(8,128)(2,1)S(1)} %collective-permute-done.got, bf16[4,128,1024]{2,1,0:T(8,128)(2,1)S(1)} %project.3.part, bf16[2,128,1024]{2,1,0:T(8,128)(2,1)} %collective-permute-done.1.near), kind=kLoop, calls=%fused_computation.8 | loop fusion | flops 786432 | bytes 1048576 | tf_op jit(solution)/shard_map/convert_element_type | solution.py:364
  27.6 2.2 %collective-permute-start.2 = (bf16[128,1024]{1,0:T(8,128)(2,1)}, bf16[128,1024]{1,0:T(8,128)(2,1)}, u32[]{:S(2)}, u32[]{:S(2)}) collective-permute-start(bf16[128,1024]{1,0:T(8,128)(2,1)} %fusion), channel_id=1, source_target_pairs={{0,192},{32,96},{64,128},{96,32},{128,64},{160,224},{192,0},{224,1... | collective-permute-start | bytes 786440 | tf_op jit(solution)/shard_map/ppermute | solution.py:328
  30.1 8.7 %all-to-all-done = bf16[32,8,512]{2,1,0:T(8,128)(2,1)S(1)} async-done(((bf16[32,8,512]{2,1,0:T(8,128)(2,1)}), bf16[32,8,512]{2,1,0:T(8,128)(2,1)S(1)}, u32[]{:S(2)}, u32[]{:S(2)}) %all-to-all-start) | async-done | bytes 262176 | tf_op jit(solution)/shard_map/all_to_all | solution.py:76
  38.8 1.2 copy-done.3
  40.0 0.8 copy-done.9
  40.9 1.6 forward.1
  42.5 17.2 %all_to_all.30 = bf16[32,8,512]{2,1,0:T(8,128)(2,1)S(1)} all-to-all(bf16[32,8,512]{2,1,0:T(8,128)(2,1)S(1)} %bitcast.43), channel_id=1, replica_groups=mesh['feat'=8,'dom'=32] {'dom'}, dimensions={0} | all-to-all | bytes 524288 | tf_op jit(solution)/shard_map/all_to_all | solution.py:76
  59.7 2.1 %middle.1 = (bf16[256,512]{1,0:T(8,128)(2,1)S(1)}, bf16[256,512]{1,0:T(8,128)(2,1)}, bf16[128,512]{1,0:T(8,128)(2,1)}, bf16[128,512]{1,0:T(8,128)(2,1)}, bf16[5,...) custom-call(bf16[256,512]{1,0:T(8,128)(2,1)S(1)} %bitcast.36, ...), custom_call_target="tpu_custom_call" | custom-call | tf_op jit(solution)/shard_map/middle/pallas_call | solution.py:52
  62.6 4.9 %all-to-all-start.2 = ((bf16[32,8,512]{2,1,0:T(8,128)(2,1)}), bf16[32,8,512]{2,1,0:T(8,128)(2,1)S(1)}, u32[]{:S(2)}, u32[]{:S(2)}) async-start(bf16[32,8,512]{2,1,0:T(8,128)(2,1)} %bitcast.41), calls=%async_computation.2 | async-start | bytes 524288 | tf_op jit(solution)/shard_map/all_to_all | solution.py:76
  67.5 1.0 slice.57
  68.5 4.3 %collective-permute-done.3 = bf16[5,128,512]{2,1,0:T(8,128)(2,1)} collective-permute-done((bf16[5,128,512]{2,1,0:T(8,128)(2,1)}, bf16[5,128,512]{2,1,0:T(8,128)(2,1)}, u32[]{:S(2)}, u32[]{:S(2)}) %collective-permute-start.3) | collective-permute-done | bytes 655392 | tf_op jit(solution)/shard_map/ppermute | solution.py:328
  72.8 0.9 slice.73
  73.7 1.0 add_convert_fusion.1
  74.7 0.8 pad_maximum_fusion
  75.6 2.7 %all-to-all-done.2 = bf16[32,8,512]{2,1,0:T(8,128)(2,1)S(1)} async-done(((bf16[32,8,512]{2,1,0:T(8,128)(2,1)}), bf16[32,8,512]{2,1,0:T(8,128)(2,1)S(1)}, u32[]{:S(2)}, u32[]{:S(2)}) %all-to-all-start.2) | async-done | bytes 262176 | tf_op jit(solution)/shard_map/all_to_all | solution.py:76
  78.3 1.7 collective-permute-start.4
  80.2 0.8 collective-permute-start.5
  81.0 1.0 slice_dynamic-update-slice_fusion.1
  82.0 4.6 %collective-permute-done.5 = bf16[128,512]{1,0:T(8,128)(2,1)S(1)} collective-permute-done((bf16[128,512]{1,0:T(8,128)(2,1)S(1)}, bf16[128,512]{1,0:T(8,128)(2,1)S(1)}, u32[]{:S(2)}, u32[]{:S(2)}) %collective-permute-start.5) | collective-permute-done | bytes 131104 | tf_op jit(solution)/shard_map/ppermute | solution.py:328
  86.6 1.7 collective-permute-start.6
  88.9 1.0 convert_add_fusion
  90.0 4.3 %collective-permute-done.6 = bf16[2,128,512]{2,1,0:T(8,128)(2,1)S(1)} collective-permute-done((bf16[2,128,512]{2,1,0:T(8,128)(2,1)S(1)}, bf16[2,128,512]{2,1,0:T(8,128)(2,1)S(1)}, u32[]{:S(2)}, u32[]{:S(2)}) %collective-permute-start.6) | collective-permute-done | bytes 262176 | tf_op jit(solution)/shard_map/ppermute | solution.py:328
  94.4 2.8 %collective-permute-done.7.other = bf16[9,128,512]{2,1,0:T(8,128)(2,1)S(1)} collective-permute-done((bf16[9,128,512]{2,1,0:T(8,128)(2,1)S(1)}, bf16[9,128,512]{2,1,0:T(8,128)(2,1)S(1)}, u32[]{:S(2)}, u32[]{:S(2)}) %collective-permute-start.7) | collective-permute-done | bytes 1179680 | tf_op jit(solution)/shard_map/ppermute | solution.py:334
  97.2 2.3 %grad.1 = (bf16[8,160,256]{2,1,0:T(8,128)(2,1)}, bf16[8,64,256]{2,1,0:T(8,128)(2,1)S(1)}, bf16[8,96,256]{2,1,0:T(8,128)(2,1)S(1)}) custom-call(bf16[512,1024]{1,0:T(8,128)(2,1)S(1)} %turn.1.flat_t, bf16[9,128,512]{2,1,0:T(8,128)(2,1)S(1)} %fusion.1.held, bf16[9,128,512]{2,1,0:T(8,128)(2,1)S(1)} %collective-permute-done.7.other, ...), custom_call_target="tpu_custom_call" | custom-call | tf_op jit(solution)/shard_map/grad/pallas_call | solution.py:52
  100.0 5.4 %all-to-all-start.3 = ((bf16[32,8,512]{2,1,0:T(8,128)(2,1)}), bf16[32,8,512]{2,1,0:T(8,128)(2,1)S(1)}, u32[]{:S(2)}, u32[]{:S(2)}) async-start(bf16[32,8,512]{2,1,0:T(8,128)(2,1)} %bitcast.49), calls=%async_computation.3 | async-start | bytes 524288 | tf_op jit(solution)/shard_map/all_to_all | solution.py:76
  105.4 6.4 %collective-permute-done.8.got = bf16[8,160,256]{2,1,0:T(8,128)(2,1)S(1)} collective-permute-done((bf16[8,160,256]{2,1,0:T(8,128)(2,1)}, bf16[8,160,256]{2,1,0:T(8,128)(2,1)S(1)}, u32[]{:S(2)}, u32[]{:S(2)}) %collective-permute-start.8) | collective-permute-done | bytes 655392 | tf_op jit(solution)/shard_map/ppermute | solution.py:331
  112.2 6.1 %all-to-all-done.3 = bf16[32,8,512]{2,1,0:T(8,128)(2,1)S(1)} async-done(((bf16[32,8,512]{2,1,0:T(8,128)(2,1)}), bf16[32,8,512]{2,1,0:T(8,128)(2,1)S(1)}, u32[]{:S(2)}, u32[]{:S(2)}) %all-to-all-start.3) | async-done | bytes 262176 | tf_op jit(solution)/shard_map/all_to_all | solution.py:76
  118.3 0.8 copy-done.20
  119.1 0.9 copy-done.25
  120.0 1.1 out.1
  121.4 16.2 %all_to_all.31 = bf16[8,96,256]{2,1,0:T(8,128)(2,1)S(1)} all-to-all(bf16[8,96,256]{2,1,0:T(8,128)(2,1)S(1)} %x_sum.1), channel_id=1, replica_groups={{0,4,8,12,16,20,24,28},{1,5,9,13,17,21,25,29},{2,6,10,14,18,22,26,30},{..., dimensions={0} | all-to-all | bytes 786432 | tf_op jit(solution)/shard_map/all_to_all | solution.py:76
  137.7 15.6 %all_to_all.32 = bf16[8,96,256]{2,1,0:T(8,128)(2,1)S(1)} all-to-all(bf16[8,96,256]{2,1,0:T(8,128)(2,1)S(1)} %broadcast_in_dim.10), channel_id=1, replica_groups={{0,4,8,12,16,20,24,28},{1,5,9,13,17,21,25,29},{2,6,10,14,18,22,26,30},{..., dimensions={0} | all-to-all | bytes 786432 | tf_op jit(solution)/shard_map/all_to_all | solution.py:76
  153.8 5.1 %collective-permute-done.10 = bf16[128,512]{1,0:T(8,128)(2,1)S(1)} collective-permute-done((bf16[128,512]{1,0:T(8,128)(2,1)S(1)}, bf16[128,512]{1,0:T(8,128)(2,1)S(1)}, u32[]{:S(2)}, u32[]{:S(2)}) %collective-permute-start.10) | collective-permute-done | bytes 131104 | tf_op jit(solution)/shard_map/ppermute | solution.py:328
  158.8 2.0 %collective-permute-done.11 = bf16[8,64,256]{2,1,0:T(8,128)(2,1)S(1)} collective-permute-done((bf16[8,64,256]{2,1,0:T(8,128)(2,1)S(1)}, bf16[8,64,256]{2,1,0:T(8,128)(2,1)S(1)}, u32[]{:S(2)}, u32[]{:S(2)}) %collective-permute-start.11) | collective-permute-done | bytes 262176 | tf_op jit(solution)/shard_map/ppermute | solution.py:331
  160.8 1.6 collective-permute-start.13
  162.5 1.8 %collective-permute-start.12 = (bf16[2,8,64,256]{3,2,1,0:T(8,128)(2,1)S(1)}, bf16[2,8,64,256]{3,2,1,0:T(8,128)(2,1)S(1)}, u32[]{:S(2)}, u32[]{:S(2)}) collective-permute-start(bf16[2,8,64,256]{3,2,1,0:T(8,128)(2,1)S(1)} %pad_maximum_fusion.1.held), channel_id=1, source_target_pairs={{0,3},{1,2},{2,1},{3,0},{4,7},{5,6},{6,5},{7,4},{8,11},{9,10},{10,... | collective-permute-start | bytes 1572872 | tf_op jit(solution)/shard_map/ppermute | solution.py:331
  164.3 4.2 %collective-permute-done.13 = bf16[2,128,512]{2,1,0:T(8,128)(2,1)S(1)} collective-permute-done((bf16[2,128,512]{2,1,0:T(8,128)(2,1)S(1)}, bf16[2,128,512]{2,1,0:T(8,128)(2,1)S(1)}, u32[]{:S(2)}, u32[]{:S(2)}) %collective-permute-start.13) | collective-permute-done | bytes 262176 | tf_op jit(solution)/shard_map/ppermute | solution.py:328
  168.7 4.3 %collective-permute-done.12.last = bf16[2,8,64,256]{3,2,1,0:T(8,128)(2,1)S(1)} collective-permute-done((bf16[2,8,64,256]{3,2,1,0:T(8,128)(2,1)S(1)}, bf16[2,8,64,256]{3,2,1,0:T(8,128)(2,1)S(1)}, u32[]{:S(2)}, u32[]{:S(2)}) %collective-permute-start.12) | collective-permute-done | bytes 524320 | tf_op jit(solution)/shard_map/ppermute | solution.py:331
  173.0 1.5 spread.1
  174.5 1.5 join.1
  (91 shorter events, 8.3 us)
Async XLA Ops:
  3.6 2.7 %collective-permute-start = (bf16[4,128,1024]{2,1,0:T(8,128)(2,1)S(1)}, bf16[4,128,1024]{2,1,0:T(8,128)(2,1)S(1)}, u32[]{:S(2)}, u32[]{:S(2)}) collective-permute-start(bf16[4,128,1024]{2,1,0:T(8,128)(2,1)S(1)} %get-tuple-element.40), channel_id=1, source_target_pairs={{0,32},{32,0},{64,96},{96,64},{128,160},{160,128},{192,224},{224,1... | collective-permute-start | bytes 3145736 | tf_op jit(solution)/shard_map/ppermute | solution.py:334
  5.6 3.5 %copy-start.30 = (s32[1,128,10]{1,0,2:T(1,128)S(1)}, s32[1,128,10]{1,0,2:T(1,128)}, u32[]{:S(2)}) copy-start(s32[1,128,10]{1,0,2:T(1,128)} %param.10) | copy-start | bytes 15364
  5.7 3.4 %copy-start.4 = (bf16[1,128,512]{2,1,0:T(8,128)(2,1)S(1)}, bf16[1,128,512]{2,1,0:T(8,128)(2,1)}, u32[]{:S(2)}) copy-start(bf16[1,128,512]{2,1,0:T(8,128)(2,1)} %param.13) | copy-start | bytes 393220
  5.7 3.4 %copy-start.28 = (s32[1,32,8]{1,2,0:T(8,128)S(1)}, s32[1,32,8]{1,2,0:T(8,128)}, u32[]{:S(2)}) copy-start(s32[1,32,8]{1,2,0:T(8,128)} %param.12) | copy-start | bytes 3076
  5.7 3.4 %copy-start.29 = (s32[1,128]{1,0:T(1,128)S(1)}, s32[1,128]{1,0:T(1,128)}, u32[]{:S(2)}) copy-start(s32[1,128]{1,0:T(1,128)} %deg.1) | copy-start | bytes 1540
  6.4 21.2 %copy-start.2 = (bf16[4,128,1024]{2,1,0:T(8,128)(2,1)}, bf16[4,128,1024]{2,1,0:T(8,128)(2,1)S(1)}, u32[]{:S(2)}) copy-start(bf16[4,128,1024]{2,1,0:T(8,128)(2,1)S(1)} %collective-permute-done.got) | copy-start | bytes 3145732
  7.5 22.3 %copy-start = (bf16[8,128,512]{2,1,0:T(8,128)(2,1)S(1)}, bf16[8,128,512]{2,1,0:T(8,128)(2,1)}, u32[]{:S(2)}) copy-start(bf16[8,128,512]{2,1,0:T(8,128)(2,1)} %flat.1) | copy-start | bytes 3145732
  7.5 18.3 %collective-permute-start.1 = (bf16[2,128,1024]{2,1,0:T(8,128)(2,1)}, bf16[2,128,1024]{2,1,0:T(8,128)(2,1)}, u32[]{:S(2)}, u32[]{:S(2)}) collective-permute-start(bf16[2,128,1024]{2,1,0:T(8,128)(2,1)} %add_convert_fusion), channel_id=1, source_target_pairs={{0,64},{32,224},{64,0},{96,160},{128,192},{160,96},{192,128},{224,... | collective-permute-start | bytes 1572872 | tf_op jit(solution)/shard_map/ppermute | solution.py:328
  9.6 0.6 copy-start.5
  10.2 0.6 copy-start.8
  10.9 0.6 copy-start.12
  11.5 0.6 copy-start.15
  12.1 0.6 copy-start.18
  13.3 0.6 copy-start.26
  13.9 0.7 copy-start.11
  14.6 24.2 %all-to-all-start = ((bf16[32,8,512]{2,1,0:T(8,128)(2,1)}), bf16[32,8,512]{2,1,0:T(8,128)(2,1)S(1)}, u32[]{:S(2)}, u32[]{:S(2)}) async-start(bf16[32,8,512]{2,1,0:T(8,128)(2,1)} %bitcast.42), calls=%async_computation | async-start | bytes 524288 | tf_op jit(solution)/shard_map/all_to_all | solution.py:76
  27.6 11.2 %collective-permute-start.2 = (bf16[128,1024]{1,0:T(8,128)(2,1)}, bf16[128,1024]{1,0:T(8,128)(2,1)}, u32[]{:S(2)}, u32[]{:S(2)}) collective-permute-start(bf16[128,1024]{1,0:T(8,128)(2,1)} %fusion), channel_id=1, source_target_pairs={{0,192},{32,96},{64,128},{96,32},{128,64},{160,224},{192,0},{224,1... | collective-permute-start | bytes 786440 | tf_op jit(solution)/shard_map/ppermute | solution.py:328
  38.8 1.2 copy-start.3
  40.0 0.8 copy-start.9
  40.9 18.8 %copy-start.1 = (bf16[1024,512]{1,0:T(8,128)(2,1)S(1)}, bf16[1024,512]{1,0:T(8,128)(2,1)}, u32[]{:S(2)}) copy-start(bf16[1024,512]{1,0:T(8,128)(2,1)} %w_two.3) | copy-start | bytes 3145732
  40.9 18.8 %copy-start.6 = (bf16[128,256]{1,0:T(8,128)(2,1)S(1)}, bf16[128,256]{1,0:T(8,128)(2,1)}, u32[]{:S(2)}) copy-start(bf16[128,256]{1,0:T(8,128)(2,1)} %copy-done.5) | copy-start | bytes 196612
  40.9 18.8 %copy-start.13 = (bf16[128,256]{1,0:T(8,128)(2,1)S(1)}, bf16[128,256]{1,0:T(8,128)(2,1)}, u32[]{:S(2)}) copy-start(bf16[128,256]{1,0:T(8,128)(2,1)} %copy-done.12) | copy-start | bytes 196612
  40.9 18.8 %copy-start.16 = (f32[128,128]{1,0:T(8,128)S(1)}, f32[128,128]{1,0:T(8,128)}, u32[]{:S(2)}) copy-start(f32[128,128]{1,0:T(8,128)} %copy-done.15) | copy-start | bytes 196612
  40.9 18.8 %copy-start.19 = (bf16[128,128]{1,0:T(8,128)(2,1)S(1)}, bf16[128,128]{1,0:T(8,128)(2,1)}, u32[]{:S(2)}) copy-start(bf16[128,128]{1,0:T(8,128)(2,1)} %copy-done.18) | copy-start | bytes 98308
  40.9 18.8 %copy-start.22 = (bf16[128,128]{1,0:T(8,128)(2,1)S(1)}, bf16[128,128]{1,0:T(8,128)(2,1)}, u32[]{:S(2)}) copy-start(bf16[128,128]{1,0:T(8,128)(2,1)} %copy-done.21) | copy-start | bytes 98308
  40.9 18.8 %copy-start.27 = (bf16[256,128]{1,0:T(8,128)(2,1)S(1)}, bf16[256,128]{1,0:T(8,128)(2,1)}, u32[]{:S(2)}) copy-start(bf16[256,128]{1,0:T(8,128)(2,1)} %copy-done.26) | copy-start | bytes 196612
  61.9 0.7 copy-start.10
  61.9 10.9 %collective-permute-start.3 = (bf16[5,128,512]{2,1,0:T(8,128)(2,1)}, bf16[5,128,512]{2,1,0:T(8,128)(2,1)}, u32[]{:S(2)}, u32[]{:S(2)}) collective-permute-start(bf16[5,128,512]{2,1,0:T(8,128)(2,1)} %get-tuple-element.58), channel_id=1, source_target_pairs={{0,64},{32,224},{64,0},{96,160},{128,192},{160,96},{192,128},{224,... | collective-permute-start | bytes 1966088 | tf_op jit(solution)/shard_map/ppermute | solution.py:328
  62.6 15.7 %all-to-all-start.2 = ((bf16[32,8,512]{2,1,0:T(8,128)(2,1)}), bf16[32,8,512]{2,1,0:T(8,128)(2,1)S(1)}, u32[]{:S(2)}, u32[]{:S(2)}) async-start(bf16[32,8,512]{2,1,0:T(8,128)(2,1)} %bitcast.41), calls=%async_computation.2 | async-start | bytes 524288 | tf_op jit(solution)/shard_map/all_to_all | solution.py:76
  67.5 12.5 %copy-start.7 = (bf16[128,256]{1,0:T(8,128)(2,1)S(1)}, bf16[128,256]{1,0:T(8,128)(2,1)}, u32[]{:S(2)}) copy-start(bf16[128,256]{1,0:T(8,128)(2,1)} %copy-done.5) | copy-start | bytes 196612
  67.5 12.5 %copy-start.23 = (bf16[128,128]{1,0:T(8,128)(2,1)S(1)}, bf16[128,128]{1,0:T(8,128)(2,1)}, u32[]{:S(2)}) copy-start(bf16[128,128]{1,0:T(8,128)(2,1)} %copy-done.21) | copy-start | bytes 98308
  67.5 12.5 %copy-start.24 = (bf16[128,512]{1,0:T(8,128)(2,1)S(1)}, bf16[128,512]{1,0:T(8,128)(2,1)}, u32[]{:S(2)}) copy-start(bf16[128,512]{1,0:T(8,128)(2,1)} %get-tuple-element.64.term) | copy-start | bytes 393220
  78.3 10.6 %collective-permute-start.4 = (bf16[4,128,512]{2,1,0:T(8,128)(2,1)}, bf16[4,128,512]{2,1,0:T(8,128)(2,1)S(1)}, u32[]{:S(2)}, u32[]{:S(2)}) collective-permute-start(bf16[4,128,512]{2,1,0:T(8,128)(2,1)} %pad_maximum_fusion), channel_id=1, source_target_pairs={{0,192},{32,96},{64,128},{96,32},{128,64},{160,224},{192,0},{224,1... | collective-permute-start | bytes 1572872 | tf_op jit(solution)/shard_map/ppermute | solution.py:328
  80.2 6.4 %collective-permute-start.5 = (bf16[128,512]{1,0:T(8,128)(2,1)S(1)}, bf16[128,512]{1,0:T(8,128)(2,1)S(1)}, u32[]{:S(2)}, u32[]{:S(2)}) collective-permute-start(bf16[128,512]{1,0:T(8,128)(2,1)S(1)} %near.1), channel_id=1, source_target_pairs={{0,64},{32,224},{64,0},{96,160},{128,192},{160,96},{192,128},{224,... | collective-permute-start | bytes 393224 | tf_op jit(solution)/shard_map/ppermute | solution.py:328
  86.6 7.7 %collective-permute-start.6 = (bf16[2,128,512]{2,1,0:T(8,128)(2,1)S(1)}, bf16[2,128,512]{2,1,0:T(8,128)(2,1)S(1)}, u32[]{:S(2)}, u32[]{:S(2)}) collective-permute-start(bf16[2,128,512]{2,1,0:T(8,128)(2,1)S(1)} %pad_maximum_fusion.3), channel_id=1, source_target_pairs={{0,192},{32,96},{64,128},{96,32},{128,64},{160,224},{192,0},{224,1... | collective-permute-start | bytes 786440 | tf_op jit(solution)/shard_map/ppermute | solution.py:328
  94.3 2.9 %collective-permute-start.7 = (bf16[9,128,512]{2,1,0:T(8,128)(2,1)S(1)}, bf16[9,128,512]{2,1,0:T(8,128)(2,1)S(1)}, u32[]{:S(2)}, u32[]{:S(2)}) collective-permute-start(bf16[9,128,512]{2,1,0:T(8,128)(2,1)S(1)} %fusion.1.held), channel_id=1, source_target_pairs={{0,32},{32,0},{64,96},{96,64},{128,160},{160,128},{192,224},{224,1... | collective-permute-start | bytes 3538952 | tf_op jit(solution)/shard_map/ppermute | solution.py:334
  99.6 18.7 %copy-start.14 = (bf16[128,256]{1,0:T(8,128)(2,1)S(1)}, bf16[128,256]{1,0:T(8,128)(2,1)}, u32[]{:S(2)}) copy-start(bf16[128,256]{1,0:T(8,128)(2,1)} %copy-done.12) | copy-start | bytes 196612
  99.6 18.7 %copy-start.17 = (f32[128,128]{1,0:T(8,128)S(1)}, f32[128,128]{1,0:T(8,128)}, u32[]{:S(2)}) copy-start(f32[128,128]{1,0:T(8,128)} %copy-done.15) | copy-start | bytes 196612
  99.6 12.2 %collective-permute-start.8 = (bf16[8,160,256]{2,1,0:T(8,128)(2,1)}, bf16[8,160,256]{2,1,0:T(8,128)(2,1)S(1)}, u32[]{:S(2)}, u32[]{:S(2)}) collective-permute-start(bf16[8,160,256]{2,1,0:T(8,128)(2,1)} %get-tuple-element.68), channel_id=1, source_target_pairs={{0,1},{1,0},{2,3},{3,2},{4,5},{5,4},{6,7},{7,6},{8,9},{9,8},{10,11... | collective-permute-start | bytes 1966088 | tf_op jit(solution)/shard_map/ppermute | solution.py:331
  100.0 18.3 %all-to-all-start.3 = ((bf16[32,8,512]{2,1,0:T(8,128)(2,1)}), bf16[32,8,512]{2,1,0:T(8,128)(2,1)S(1)}, u32[]{:S(2)}, u32[]{:S(2)}) async-start(bf16[32,8,512]{2,1,0:T(8,128)(2,1)} %bitcast.49), calls=%async_computation.3 | async-start | bytes 524288 | tf_op jit(solution)/shard_map/all_to_all | solution.py:76
  111.9 9.3 %collective-permute-start.9 = (bf16[8,96,256]{2,1,0:T(8,128)(2,1)S(1)}, bf16[8,96,256]{2,1,0:T(8,128)(2,1)S(1)}, u32[]{:S(2)}, u32[]{:S(2)}) collective-permute-start(bf16[8,96,256]{2,1,0:T(8,128)(2,1)S(1)} %x_pass.1.sent), channel_id=1, source_target_pairs={{0,3},{1,2},{2,1},{3,0},{4,7},{5,6},{6,5},{7,4},{8,11},{9,10},{10,... | collective-permute-start | bytes 1179656 | tf_op jit(solution)/shard_map/ppermute | solution.py:331
  118.3 0.8 copy-start.20
  119.1 0.9 copy-start.25
  153.3 7.5 %collective-permute-start.11 = (bf16[8,64,256]{2,1,0:T(8,128)(2,1)S(1)}, bf16[8,64,256]{2,1,0:T(8,128)(2,1)S(1)}, u32[]{:S(2)}, u32[]{:S(2)}) collective-permute-start(bf16[8,64,256]{2,1,0:T(8,128)(2,1)S(1)} %get-tuple-element.76), channel_id=1, source_target_pairs={{0,1},{1,0},{2,3},{3,2},{4,5},{5,4},{6,7},{7,6},{8,9},{9,8},{10,11... | collective-permute-start | bytes 786440 | tf_op jit(solution)/shard_map/ppermute | solution.py:331
  153.7 5.2 %collective-permute-start.10 = (bf16[128,512]{1,0:T(8,128)(2,1)S(1)}, bf16[128,512]{1,0:T(8,128)(2,1)S(1)}, u32[]{:S(2)}, u32[]{:S(2)}) collective-permute-start(bf16[128,512]{1,0:T(8,128)(2,1)S(1)} %get-tuple-element.80), channel_id=1, source_target_pairs={{0,64},{32,224},{64,0},{96,160},{128,192},{160,96},{192,128},{224,... | collective-permute-start | bytes 393224 | tf_op jit(solution)/shard_map/ppermute | solution.py:328
  160.8 7.7 %collective-permute-start.13 = (bf16[2,128,512]{2,1,0:T(8,128)(2,1)S(1)}, bf16[2,128,512]{2,1,0:T(8,128)(2,1)S(1)}, u32[]{:S(2)}, u32[]{:S(2)}) collective-permute-start(bf16[2,128,512]{2,1,0:T(8,128)(2,1)S(1)} %pad_maximum_fusion.4), channel_id=1, source_target_pairs={{0,192},{32,96},{64,128},{96,32},{128,64},{160,224},{192,0},{224,1... | collective-permute-start | bytes 786440 | tf_op jit(solution)/shard_map/ppermute | solution.py:328
  162.5 10.5 %collective-permute-start.12 = (bf16[2,8,64,256]{3,2,1,0:T(8,128)(2,1)S(1)}, bf16[2,8,64,256]{3,2,1,0:T(8,128)(2,1)S(1)}, u32[]{:S(2)}, u32[]{:S(2)}) collective-permute-start(bf16[2,8,64,256]{3,2,1,0:T(8,128)(2,1)S(1)} %pad_maximum_fusion.1.held), channel_id=1, source_target_pairs={{0,3},{1,2},{2,1},{3,0},{4,7},{5,6},{6,5},{7,4},{8,11},{9,10},{10,... | collective-permute-start | bytes 1572872 | tf_op jit(solution)/shard_map/ppermute | solution.py:331
  168.6 5.9 %collective-permute-start.14 = (bf16[4,128,512]{2,1,0:T(8,128)(2,1)S(1)}, bf16[4,128,512]{2,1,0:T(8,128)(2,1)S(1)}, u32[]{:S(2)}, u32[]{:S(2)}) collective-permute-start(bf16[4,128,512]{2,1,0:T(8,128)(2,1)S(1)} %pad_maximum_fusion.2.held), channel_id=1, source_target_pairs={{0,32},{32,0},{64,96},{96,64},{128,160},{160,128},{192,224},{224,1... | collective-permute-start | bytes 1572872 | tf_op jit(solution)/shard_map/ppermute | solution.py:334
  (1 other events, 0.6 us)

commit v11 on v9

--- a/solution.py
+++ b/solution.py
@@ -40,7 +40,7 @@
     return lax.dot_general(a, b, dims, preferred_element_type=F32)
 
 
-def whole(name, body, outs, *args, scratch=(), far=(), kept=(), raw=()):
+def whole(name, body, outs, *args, scratch=(), far=(), kept=(), raw=(), load=()):
     many = isinstance(outs, tuple)
     outs = list(outs) if many else [outs]
     place = pl.BlockSpec(memory_space=pltpu.VMEM)
@@ -52,7 +52,10 @@
     got = pl.pallas_call(
         body,
         out_shape=kinds,
-        in_specs=[anywhere if k in raw else place for k in range(len(args))],
+        in_specs=[
+            anywhere if k in raw else pl.BlockSpec() if k in load else place
+            for k in range(len(args))
+        ],
         out_specs=[
             pl.BlockSpec() if k in far or k in kept else place for k in range(len(outs))
         ],
@@ -61,7 +64,9 @@
         compiler_params=pltpu.CompilerParams(vmem_limit_bytes=16 << 20),
     )(
         *[
-            pltpu.with_memory_space_constraint(a, pltpu.HBM if k in raw else pltpu.VMEM)
+            pltpu.with_memory_space_constraint(
+                a, pltpu.HBM if k in raw or k in load else pltpu.VMEM
+            )
             for k, a in enumerate(args)
         ]
     )
@@ -78,7 +83,9 @@
     )
 
 
-def tables_body(nbr_t, deg, sends_t, give, take, own, own_t, inv):
+def tables_body(
+    nbr_t, deg, sends_t, give, take, own, own_t, inv, pick_out, mean, back, home_out
+):
     fan, nodes = nbr_t.shape
     kmax, parts = sends_t.shape
     span = 2 * kmax * parts
@@ -87,17 +94,20 @@
     entry = nodes + r // (2 * kmax) * kmax + j
     leave = jnp.where(j < kmax, entry, -2)
     arrive = jnp.where(j >= kmax, entry - kmax, -2)
-    row = lax.broadcasted_iota(jnp.int32, (nodes, nodes), 0)
+    half = span // 2
+    row = lax.broadcasted_iota(jnp.int32, (nodes + half, nodes), 0)
     leave_sum = jnp.zeros((span, nodes), F32)
     arrive_sum = jnp.zeros((span, nodes), F32)
-    own_sum = jnp.zeros((nodes, nodes), F32)
+    own_sum = jnp.zeros((nodes + half, nodes), F32)
     for s in range(fan):
         used = jnp.where(s < deg[...], nbr_t[s : s + 1, :], -1)
         leave_sum += jnp.where(leave == used, 1.0, 0.0)
         arrive_sum += jnp.where(arrive == used, 1.0, 0.0)
         own_sum += jnp.where(row == used, 1.0, 0.0)
-    own_t[...] = own_sum.astype(BF16)
-    own[...] = own_sum.T.astype(BF16)
+    own_t[...] = own_sum[:nodes].astype(BF16)
+    own[...] = own_sum[:nodes].T.astype(BF16)
+    back[...] = own_sum[nodes:].astype(BF16)
+    mean[...] = own_sum[nodes:].T.astype(BF16)
     part = lax.broadcasted_iota(jnp.int32, (parts, span), 0)
     lane = lax.broadcasted_iota(jnp.int32, (parts, span), 1)
     spread = jnp.where(lane // (2 * kmax) == part, 1.0, 0.0).astype(BF16)
@@ -114,6 +124,16 @@
     take[:nodes, :] = arrive_sum.T.astype(BF16)
     take[nodes:, :] = home.astype(BF16)
     inv[...] = jnp.broadcast_to(1.0 / deg[...].astype(F32), (nodes, nodes)).T
+    part = lax.broadcasted_iota(jnp.int32, (parts, half), 0)
+    lane = lax.broadcasted_iota(jnp.int32, (parts, half), 1)
+    spread = jnp.where(lane // kmax == part, 1.0, 0.0).astype(BF16)
+    ids = mm(sends_t[...].astype(F32).astype(BF16), spread)
+    slot = lax.broadcasted_iota(jnp.int32, (kmax, half), 0)
+    sent = jnp.sum(jnp.where(slot == lane[:kmax] % kmax, ids, 0.0), axis=0, keepdims=True)
+    node = lax.broadcasted_iota(jnp.int32, (nodes, half), 0).astype(F32)
+    chosen = jnp.where(node == sent, 1.0, 0.0)
+    home_out[...] = chosen.astype(BF16)
+    pick_out[...] = chosen.T.astype(BF16)
 
 
 def turn_body(flat, out):
@@ -210,8 +230,8 @@
 
 
 def middle_body(
-    recv, p_self, p_near, grads, inv, w_two, give, take, own, own_t,
-    boxes, term_out, hidden_out, first, second, mine, scratch,
+    recv, p_self, p_near, grads, inv, w_two, pick, back_t, take, own, own_t,
+    boxes, hidden_boxes, term_out, hidden_out, first, second, mine, scratch,
 ):
     nodes, width = grads.shape
     scales = inv[:, :1]
@@ -226,7 +246,8 @@
     hidden_out[...] = hidden
     d_pre = d_hidden * sig * (1.0 + pre * (1.0 - sig))
     term = (d_pre * scales).astype(BF16)
-    boxes[...] = mm(give[...], jnp.concatenate([term, hidden], axis=0)).astype(BF16)
+    boxes[...] = mm(back_t[...], term).astype(BF16)
+    hidden_boxes[...] = mm(pick[...], hidden).astype(BF16)
     term_out[...] = term
     half = scratch.shape[0] // 2
     for k, right in enumerate((grad, back)):
@@ -241,14 +262,13 @@
         mine[k] = scratch[here]
 
 
-def near_body(recv, term, own_t, take, out):
-    nodes = out.shape[0]
-    out[...] = (mm(own_t[...], term[...]) + mm(take[nodes:, :], recv[...])).astype(BF16)
-
-
-def out_body(recv, hidden, inv, take, own, w_two, out):
-    nodes, width = hidden.shape
-    total = mm(take[:nodes, :], recv[...]) + mm(own[...], hidden[...])
+def near_body(recv, term, own_t, home, out):
+    out[...] = (mm(own_t[...], term[...]) + mm(home[...], recv[...])).astype(BF16)
+
+
+def out_body(recv, hidden, inv, mean, own, w_two, out):
+    width = hidden.shape[1]
+    total = mm(mean[...], recv[...]) + mm(own[...], hidden[...])
     agg = (inv[:, :1] * total).astype(BF16)
     out[...] = (mm(hidden[...], w_two[:width, :]) + mm(agg, w_two[width:, :])).astype(BF16)
 
@@ -344,7 +364,7 @@
     theirs, w_one = project(features, w_one, True)
     got = swap(theirs)
     mine = project(features, w_one, False)
-    give, take, own, own_t, inv = whole(
+    give, take, own, own_t, inv, pick, mean, back_t, home = whole(
         "tables",
         tables_body,
         (
@@ -353,6 +373,10 @@
             shape((nodes, nodes)),
             shape((nodes, nodes)),
             shape((nodes, nodes), F32),
+            shape((span // 2, nodes)),
+            shape((nodes, span // 2)),
+            shape((span // 2, nodes)),
+            shape((nodes, span // 2)),
         ),
         neighbor[0].T, degree, sends.T,
     )
@@ -370,28 +394,35 @@
     )
     recv = trade(boxes.reshape(parts, 2 * kmax, width)).reshape(span, width)
     rows = 2 * width // groups
-    boxes, term, hidden, first, second, mine = whole(
+    lot = shape((span // 2, width))
+    boxes, hidden_boxes, term, hidden, first, second, mine = whole(
         "middle",
         middle_body,
         (
-            shape((span, width)),
+            lot,
+            lot,
             block,
             block,
             shape((5, rows, width)),
             shape((2, rows, width)),
             shape((2, rows, width)),
         ),
-        recv, p_self, p_near, grads, inv, w_two, give, take, own, own_t,
+        recv, p_self, p_near, grads, inv, w_two, pick, back_t, take, own, own_t,
         scratch=[pltpu.VMEM((groups, rows, width), BF16)],
-        far=(0, 3, 4, 5),
-        kept=(1, 2),
-    )
-    recv = trade(boxes.reshape(parts, 2 * kmax, width)).reshape(span, width)
+        far=(0, 4, 5, 6),
+        kept=(1, 2, 3),
+    )
+
+    def exchange(boxes):
+        return trade(boxes.reshape(parts, kmax, width)).reshape(span // 2, width)
+
+    recv = exchange(boxes)
 
     got = y_move(first, y_first)
     message = jnp.concatenate([first[:1], got[:1], add(second, got[3:]).astype(BF16)])
     message, recv = lax.optimization_barrier((message, recv))
-    d_near = whole("near", near_body, block, recv, term, own_t, take)
+    hidden_boxes, message = lax.optimization_barrier((hidden_boxes, message))
+    d_near = whole("near", near_body, block, recv, term, own_t, home)
     one = y_move(d_near, y_first)
     last = y_move(message, y_second)
     sums = add(mine, got[1:3], last[2:])
@@ -399,6 +430,8 @@
     held = jnp.concatenate(
         [message[:2], last[:2], near, y_move(near, y_second), sums[:1].astype(BF16)]
     )
+
+    recv = exchange(hidden_boxes)
 
     kept = 8 * cols // parts // 2
     tail = 4 * width // groups // deep
@@ -416,13 +449,12 @@
             pltpu.VMEM((CHIPS, deep, kept, width // 2), BF16),
         ],
     )
-    out = whole("out", out_body, block, recv, hidden, inv, take, own, w_two, far=(0,))
     lot = shape((deep, kept + tail, width // 2))
     got = x_move(first, x_first)
     sent = whole("x_pass", x_pass_body, lot, second, mine, got)
     last = x_move(sent, x_second)
-    last, out = lax.optimization_barrier((last, out))
-    terms = trade(whole("x_sum", x_sum_body, lot, mine, got, sent, last), lines)
+    last, recv = lax.optimization_barrier((last, recv))
+    terms = trade(whole("x_sum", x_sum_body, lot, mine, got, sent, last, load=(3,)), lines)
     total = (jnp.sum(terms.astype(F32), axis=0) * scale).astype(BF16)
     total = trade(jnp.broadcast_to(total[None], terms.shape), lines)
     half = kept + tail // 2
@@ -432,9 +464,11 @@
     mine = total[:, :kept]
     one_y = y_move(chunk, y_first)
     one_x = x_move(mine, x_first)
+    out = whole("out", out_body, block, recv, hidden, inv, mean, own, w_two, far=(0,))
     one_y, one_x = lax.optimization_barrier((one_y, one_x))
     held_y = jnp.stack([chunk, one_y])
     held_y = jnp.concatenate([held_y, y_move(held_y, y_second)])
+    held_y, out = lax.optimization_barrier((held_y, out))
     held_x = jnp.stack([mine, one_x])
     last_x = x_move(held_x, x_second)
     one = whole(

time: 171 us -> 170 us (level)
  waiting for transfers between devices: 67.8 us -> 59.2 us
  starting transfers between devices: 24.4 us -> 29.2 us
  Pallas kernels: 14.6 us -> 16.5 us
    ppermute x4, waiting for transfers between devices: 21.5 us -> 15.4 us  [x_move(): return lax.ppermute(block, ('feat', 'dom'), pairs)]
    all_to_all x1 -> x2, starting transfers between devices: 5.12 us -> 10.5 us  [trade(): lax.all_to_all(boxes, 'dom', split_axis=0, concat_axis=0, axis_index_grou...]
    ppermute x8, waiting for transfers between devices: 33.7 us -> 30 us  [y_move(): return lax.ppermute(block, 'feat', pairs)]
    pallas_call x13, Pallas kernels: 14.6 us -> 16.5 us  [whole(): pl.pallas_call(body, out_shape=kinds, in_specs=[anywhere if k in raw else...]
    all_to_all x1 -> x2, waiting for transfers between devices: 9.11 us -> 10.3 us  [trade(): lax.all_to_all(boxes, 'dom', split_axis=0, concat_axis=0, axis_index_grou...]
  transfers between devices with their start and end apart: 16 -> 17, of which waited for: 13 -> 15; matrix products, arithmetic and copies ran while one was open for 3% -> 4% of each run, Pallas kernels for 3% -> 4%
where the time goes in v11:
time: 170 us; the launch traced here: 168 us
  waiting for transfers between devices  59.2 us (35%)
  blocking collectives  55.5 us (33%)
  starting transfers between devices  29.2 us (17%)
  Pallas kernels  16.5 us (10%)
  local copies, waits for them, and re-layouts  3.67 us (2%)
  other arithmetic  3.46 us (2%)
    all_to_all x3, blocking collectives, trade(): lax.all_to_all(boxes, 'dom', split_axis=0, concat_axis=0, axis_index_grou...  55.5 us
    ppermute x8, waiting for transfers between devices, y_move(): return lax.ppermute(block, 'feat', pairs)  30 us
    pallas_call x13, Pallas kernels, whole(): pl.pallas_call(body, out_shape=kinds, in_specs=[anywhere if k in raw else...  16.5 us
    ppermute x4, waiting for transfers between devices, x_move(): return lax.ppermute(block, ('feat', 'dom'), pairs)  15.4 us
    ppermute x8, starting transfers between devices, y_move(): return lax.ppermute(block, 'feat', pairs)  11.4 us
    all_to_all x2, starting transfers between devices, trade(): lax.all_to_all(boxes, 'dom', split_axis=0, concat_axis=0, axis_index_grou...  10.5 us
    all_to_all x2, waiting for transfers between devices, trade(): lax.all_to_all(boxes, 'dom', split_axis=0, concat_axis=0, axis_index_grou...  10.3 us
    ppermute x4, starting transfers between devices, x_move(): return lax.ppermute(block, ('feat', 'dom'), pairs)  7.01 us
  transfers between devices with their start and end apart: 17, of which 15 were waited for; matrix products, arithmetic and copies ran while one was open for 4% of the time, Pallas kernels for 4%

profile of v11, /device:TPU:32, one launch (start us, length us, event | category | flops | bytes accessed | tf_op | source)
XLA Modules:
  0.0 168.4 jit_solution(16428517192686725725)
XLA Ops:
  0.6 3.0 %project.2 = (bf16[4,128,1024]{2,1,0:T(8,128)(2,1)S(1)}, bf16[512,1024]{1,0:T(8,128)(2,1)S(1)}) custom-call(bf16[8,128,512]{2,1,0:T(8,128)(2,1)} %flat.1, bf16[512,1024]{1,0:T(8,128)(2,1)} %w.1), custom_call_target="tpu_custom_call" | custom-call | tf_op jit(solution)/shard_map/project/pallas_call | solution.py:52
  3.7 1.9 %project.3.part = bf16[4,128,1024]{2,1,0:T(8,128)(2,1)S(1)} custom-call(bf16[8,128,512]{2,1,0:T(8,128)(2,1)} %flat.1, bf16[512,1024]{1,0:T(8,128)(2,1)S(1)} %get-tuple-element.41.w), custom_call_target="tpu_custom_call" | custom-call | tf_op jit(solution)/shard_map/project/pallas_call | solution.py:52
  5.7 0.7 collective-permute-done.got
  6.6 1.7 collective-permute-start.1
  8.3 0.7 tables.1
  9.0 0.6 copy-done.5
  9.6 6.2 %collective-permute-done.1.near = bf16[2,128,1024]{2,1,0:T(8,128)(2,1)S(1)} collective-permute-done((bf16[2,128,1024]{2,1,0:T(8,128)(2,1)S(1)}, bf16[2,128,1024]{2,1,0:T(8,128)(2,1)S(1)}, u32[]{:S(2)}, u32[]{:S(2)}) %collective-permute-start.1) | collective-permute-done | bytes 524320 | tf_op jit(solution)/shard_map/ppermute | solution.py:356
  16.0 3.1 %collective-permute-start.2 = (bf16[128,1024]{1,0:T(8,128)(2,1)S(1)}, bf16[128,1024]{1,0:T(8,128)(2,1)S(1)}, u32[]{:S(2)}, u32[]{:S(2)}) collective-permute-start(bf16[128,1024]{1,0:T(8,128)(2,1)S(1)} %fusion), channel_id=1, source_target_pairs={{0,192},{32,96},{64,128},{96,32},{128,64},{160,224},{192,0},{224,1... | collective-permute-start | bytes 786440 | tf_op jit(solution)/shard_map/ppermute | solution.py:356
  19.1 0.4 turn.1.flat_t
  19.5 4.2 %collective-permute-done.2.far = bf16[128,1024]{1,0:T(8,128)(2,1)S(1)} collective-permute-done((bf16[128,1024]{1,0:T(8,128)(2,1)S(1)}, bf16[128,1024]{1,0:T(8,128)(2,1)S(1)}, u32[]{:S(2)}, u32[]{:S(2)}) %collective-permute-start.2) | collective-permute-done | bytes 262176 | tf_op jit(solution)/shard_map/ppermute | solution.py:356
  23.7 0.4 forward.1
  24.1 26.8 %all_to_all.25 = bf16[32,16,512]{2,1,0:T(8,128)(2,1)S(1)} all-to-all(bf16[32,16,512]{2,1,0:T(8,128)(2,1)S(1)} %bitcast.38), channel_id=1, replica_groups=mesh['feat'=8,'dom'=32] {'dom'}, dimensions={0} | all-to-all | bytes 1048576 | tf_op jit(solution)/shard_map/all_to_all | solution.py:81
  50.9 2.2 %middle.1 = (bf16[256,512]{1,0:T(8,128)(2,1)}, bf16[256,512]{1,0:T(8,128)(2,1)}, bf16[128,512]{1,0:T(8,128)(2,1)}, bf16[128,512]{1,0:T(8,128)(2,1)}, bf16[5,128,...) custom-call(bf16[512,512]{1,0:T(8,128)(2,1)S(1)} %bitcast.32, ...), custom_call_target="tpu_custom_call" | custom-call | tf_op jit(solution)/shard_map/middle/pallas_call | solution.py:52
  53.1 0.6 collective-permute-start.3
  53.7 5.1 %all-to-all-start.1 = ((bf16[32,8,512]{2,1,0:T(8,128)(2,1)}), bf16[32,8,512]{2,1,0:T(8,128)(2,1)S(1)}, u32[]{:S(2)}, u32[]{:S(2)}) async-start(bf16[32,8,512]{2,1,0:T(8,128)(2,1)} %bitcast.7), calls=%async_computation.1 | async-start | bytes 524288 | tf_op jit(solution)/shard_map/all_to_all | solution.py:81
  58.9 1.0 slice.57
  59.8 4.2 %collective-permute-done.3 = bf16[5,128,512]{2,1,0:T(8,128)(2,1)} collective-permute-done((bf16[5,128,512]{2,1,0:T(8,128)(2,1)}, bf16[5,128,512]{2,1,0:T(8,128)(2,1)}, u32[]{:S(2)}, u32[]{:S(2)}) %collective-permute-start.3) | collective-permute-done | bytes 655392 | tf_op jit(solution)/shard_map/ppermute | solution.py:356
  64.0 0.9 slice.73
  64.9 1.0 add_convert_fusion.1
  66.0 0.8 pad_maximum_fusion
  66.8 4.1 %all-to-all-done.1 = bf16[32,8,512]{2,1,0:T(8,128)(2,1)S(1)} async-done(((bf16[32,8,512]{2,1,0:T(8,128)(2,1)}), bf16[32,8,512]{2,1,0:T(8,128)(2,1)S(1)}, u32[]{:S(2)}, u32[]{:S(2)}) %all-to-all-start.1) | async-done | bytes 262176 | tf_op jit(solution)/shard_map/all_to_all | solution.py:81
  70.9 1.4 collective-permute-start.4
  72.5 1.2 collective-permute-start.5
  73.8 1.0 slice_dynamic-update-slice_fusion.1
  74.7 4.3 %collective-permute-done.5 = bf16[128,512]{1,0:T(8,128)(2,1)S(1)} collective-permute-done((bf16[128,512]{1,0:T(8,128)(2,1)S(1)}, bf16[128,512]{1,0:T(8,128)(2,1)S(1)}, u32[]{:S(2)}, u32[]{:S(2)}) %collective-permute-start.5) | collective-permute-done | bytes 131104 | tf_op jit(solution)/shard_map/ppermute | solution.py:356
  79.1 1.8 %collective-permute-start.6 = (bf16[2,128,512]{2,1,0:T(8,128)(2,1)S(1)}, bf16[2,128,512]{2,1,0:T(8,128)(2,1)S(1)}, u32[]{:S(2)}, u32[]{:S(2)}) collective-permute-start(bf16[2,128,512]{2,1,0:T(8,128)(2,1)S(1)} %pad_maximum_fusion.3), channel_id=1, source_target_pairs={{0,192},{32,96},{64,128},{96,32},{128,64},{160,224},{192,0},{224,1... | collective-permute-start | bytes 786440 | tf_op jit(solution)/shard_map/ppermute | solution.py:356
  80.8 0.6 collective-permute-done.4
  81.5 1.0 convert_add_fusion
  82.6 4.2 %collective-permute-done.6 = bf16[2,128,512]{2,1,0:T(8,128)(2,1)S(1)} collective-permute-done((bf16[2,128,512]{2,1,0:T(8,128)(2,1)S(1)}, bf16[2,128,512]{2,1,0:T(8,128)(2,1)S(1)}, u32[]{:S(2)}, u32[]{:S(2)}) %collective-permute-start.6) | collective-permute-done | bytes 262176 | tf_op jit(solution)/shard_map/ppermute | solution.py:356
  86.9 2.8 %collective-permute-done.7.other = bf16[9,128,512]{2,1,0:T(8,128)(2,1)S(1)} collective-permute-done((bf16[9,128,512]{2,1,0:T(8,128)(2,1)S(1)}, bf16[9,128,512]{2,1,0:T(8,128)(2,1)S(1)}, u32[]{:S(2)}, u32[]{:S(2)}) %collective-permute-start.7) | collective-permute-done | bytes 1179680 | tf_op jit(solution)/shard_map/ppermute | solution.py:362
  89.7 2.3 %grad.1 = (bf16[8,160,256]{2,1,0:T(8,128)(2,1)}, bf16[8,64,256]{2,1,0:T(8,128)(2,1)S(1)}, bf16[8,96,256]{2,1,0:T(8,128)(2,1)S(1)}) custom-call(bf16[512,1024]{1,0:T(8,128)(2,1)S(1)} %turn.1.flat_t, bf16[9,128,512]{2,1,0:T(8,128)(2,1)S(1)} %fusion.1.held, bf16[9,128,512]{2,1,0:T(8,128)(2,1)S(1)} %collective-permute-done.7.other, ...), custom_call_target="tpu_custom_call" | custom-call | tf_op jit(solution)/shard_map/grad/pallas_call | solution.py:52
  92.1 0.6 collective-permute-start.8
  92.7 5.4 %all-to-all-start.2 = ((bf16[32,8,512]{2,1,0:T(8,128)(2,1)}), bf16[32,8,512]{2,1,0:T(8,128)(2,1)S(1)}, u32[]{:S(2)}, u32[]{:S(2)}) async-start(bf16[32,8,512]{2,1,0:T(8,128)(2,1)} %bitcast.12), calls=%async_computation.2 | async-start | bytes 524288 | tf_op jit(solution)/shard_map/all_to_all | solution.py:81
  98.0 6.2 %collective-permute-done.8.got = bf16[8,160,256]{2,1,0:T(8,128)(2,1)S(1)} collective-permute-done((bf16[8,160,256]{2,1,0:T(8,128)(2,1)}, bf16[8,160,256]{2,1,0:T(8,128)(2,1)S(1)}, u32[]{:S(2)}, u32[]{:S(2)}) %collective-permute-start.8) | collective-permute-done | bytes 655392 | tf_op jit(solution)/shard_map/ppermute | solution.py:359
  104.6 6.3 %all-to-all-done.2 = bf16[32,8,512]{2,1,0:T(8,128)(2,1)S(1)} async-done(((bf16[32,8,512]{2,1,0:T(8,128)(2,1)}), bf16[32,8,512]{2,1,0:T(8,128)(2,1)S(1)}, u32[]{:S(2)}, u32[]{:S(2)}) %all-to-all-start.2) | async-done | bytes 262176 | tf_op jit(solution)/shard_map/all_to_all | solution.py:81
  110.9 3.0 %collective-permute-done.9.last = bf16[8,96,256]{2,1,0:T(8,128)(2,1)} collective-permute-done((bf16[8,96,256]{2,1,0:T(8,128)(2,1)S(1)}, bf16[8,96,256]{2,1,0:T(8,128)(2,1)}, u32[]{:S(2)}, u32[]{:S(2)}) %collective-permute-start.9) | collective-permute-done | bytes 393248 | tf_op jit(solution)/shard_map/ppermute | solution.py:359
  113.9 1.1 x_sum.1
  115.0 14.6 %all_to_all.26 = bf16[8,96,256]{2,1,0:T(8,128)(2,1)S(1)} all-to-all(bf16[8,96,256]{2,1,0:T(8,128)(2,1)S(1)} %x_sum.1), channel_id=1, replica_groups={{0,4,8,12,16,20,24,28},{1,5,9,13,17,21,25,29},{2,6,10,14,18,22,26,30},{..., dimensions={0} | all-to-all | bytes 786432 | tf_op jit(solution)/shard_map/all_to_all | solution.py:81
  129.7 14.1 %all_to_all.27 = bf16[8,96,256]{2,1,0:T(8,128)(2,1)S(1)} all-to-all(bf16[8,96,256]{2,1,0:T(8,128)(2,1)S(1)} %broadcast_in_dim.4), channel_id=1, replica_groups={{0,4,8,12,16,20,24,28},{1,5,9,13,17,21,25,29},{2,6,10,14,18,22,26,30},{..., dimensions={0} | all-to-all | bytes 786432 | tf_op jit(solution)/shard_map/all_to_all | solution.py:81
  143.9 2.1 %collective-permute-start.11 = (bf16[8,64,256]{2,1,0:T(8,128)(2,1)S(1)}, bf16[8,64,256]{2,1,0:T(8,128)(2,1)S(1)}, u32[]{:S(2)}, u32[]{:S(2)}) collective-permute-start(bf16[8,64,256]{2,1,0:T(8,128)(2,1)S(1)} %get-tuple-element.80), channel_id=1, source_target_pairs={{0,1},{1,0},{2,3},{3,2},{4,5},{5,4},{6,7},{7,6},{8,9},{9,8},{10,11... | collective-permute-start | bytes 786440 | tf_op jit(solution)/shard_map/ppermute | solution.py:359
  146.1 5.3 %collective-permute-done.10 = bf16[128,512]{1,0:T(8,128)(2,1)S(1)} collective-permute-done((bf16[128,512]{1,0:T(8,128)(2,1)S(1)}, bf16[128,512]{1,0:T(8,128)(2,1)S(1)}, u32[]{:S(2)}, u32[]{:S(2)}) %collective-permute-start.10) | collective-permute-done | bytes 131104 | tf_op jit(solution)/shard_map/ppermute | solution.py:356
  151.5 1.5 collective-permute-start.12
  153.0 1.1 out.1
  154.2 4.1 %collective-permute-start.13 = (bf16[2,8,64,256]{3,2,1,0:T(8,128)(2,1)S(1)}, bf16[2,8,64,256]{3,2,1,0:T(8,128)(2,1)S(1)}, u32[]{:S(2)}, u32[]{:S(2)}) collective-permute-start(bf16[2,8,64,256]{3,2,1,0:T(8,128)(2,1)S(1)} %pad_maximum_fusion.2.held), channel_id=1, source_target_pairs={{0,3},{1,2},{2,1},{3,0},{4,7},{5,6},{6,5},{7,4},{8,11},{9,10},{10,... | collective-permute-start | bytes 1572872 | tf_op jit(solution)/shard_map/ppermute | solution.py:359
  158.3 0.9 collective-permute-done.12
  159.3 6.1 %collective-permute-done.13.last = bf16[2,8,64,256]{3,2,1,0:T(8,128)(2,1)S(1)} collective-permute-done((bf16[2,8,64,256]{3,2,1,0:T(8,128)(2,1)S(1)}, bf16[2,8,64,256]{3,2,1,0:T(8,128)(2,1)S(1)}, u32[]{:S(2)}, u32[]{:S(2)}) %collective-permute-start.13) | collective-permute-done | bytes 524320 | tf_op jit(solution)/shard_map/ppermute | solution.py:359
  165.5 1.5 spread.1
  166.9 1.5 join.1
  (47 shorter events, 1.7 us)
Async XLA Ops:
  3.6 2.7 %collective-permute-start = (bf16[4,128,1024]{2,1,0:T(8,128)(2,1)S(1)}, bf16[4,128,1024]{2,1,0:T(8,128)(2,1)S(1)}, u32[]{:S(2)}, u32[]{:S(2)}) collective-permute-start(bf16[4,128,1024]{2,1,0:T(8,128)(2,1)S(1)} %get-tuple-element.42), channel_id=1, source_target_pairs={{0,32},{32,0},{64,96},{96,64},{128,160},{160,128},{192,224},{224,1... | collective-permute-start | bytes 3145736 | tf_op jit(solution)/shard_map/ppermute | solution.py:362
  5.6 2.6 %copy-start.9 = (s32[1,128,10]{1,0,2:T(1,128)S(1)}, s32[1,128,10]{1,0,2:T(1,128)}, u32[]{:S(2)}) copy-start(s32[1,128,10]{1,0,2:T(1,128)} %param.10) | copy-start | bytes 15364
  5.7 2.6 %copy-start.7 = (s32[1,32,8]{1,2,0:T(8,128)S(1)}, s32[1,32,8]{1,2,0:T(8,128)}, u32[]{:S(2)}) copy-start(s32[1,32,8]{1,2,0:T(8,128)} %param.12) | copy-start | bytes 3076
  5.7 2.6 %copy-start.8 = (s32[1,128]{1,0:T(1,128)S(1)}, s32[1,128]{1,0:T(1,128)}, u32[]{:S(2)}) copy-start(s32[1,128]{1,0:T(1,128)} %deg.1) | copy-start | bytes 1540
  5.7 13.4 %copy-start = (bf16[8,128,512]{2,1,0:T(8,128)(2,1)S(1)}, bf16[8,128,512]{2,1,0:T(8,128)(2,1)}, u32[]{:S(2)}) copy-start(bf16[8,128,512]{2,1,0:T(8,128)(2,1)} %flat.1) | copy-start | bytes 3145732
  6.6 9.3 %collective-permute-start.1 = (bf16[2,128,1024]{2,1,0:T(8,128)(2,1)S(1)}, bf16[2,128,1024]{2,1,0:T(8,128)(2,1)S(1)}, u32[]{:S(2)}, u32[]{:S(2)}) collective-permute-start(bf16[2,128,1024]{2,1,0:T(8,128)(2,1)S(1)} %add_convert_fusion), channel_id=1, source_target_pairs={{0,64},{32,224},{64,0},{96,160},{128,192},{160,96},{192,128},{224,... | collective-permute-start | bytes 1572872 | tf_op jit(solution)/shard_map/ppermute | solution.py:356
  9.0 0.6 copy-start.5
  16.0 7.7 %copy-start.2 = (bf16[1,128,512]{2,1,0:T(8,128)(2,1)S(1)}, bf16[1,128,512]{2,1,0:T(8,128)(2,1)}, u32[]{:S(2)}) copy-start(bf16[1,128,512]{2,1,0:T(8,128)(2,1)} %param.13) | copy-start | bytes 393220
  16.0 7.7 %collective-permute-start.2 = (bf16[128,1024]{1,0:T(8,128)(2,1)S(1)}, bf16[128,1024]{1,0:T(8,128)(2,1)S(1)}, u32[]{:S(2)}, u32[]{:S(2)}) collective-permute-start(bf16[128,1024]{1,0:T(8,128)(2,1)S(1)} %fusion), channel_id=1, source_target_pairs={{0,192},{32,96},{64,128},{96,32},{128,64},{160,224},{192,0},{224,1... | collective-permute-start | bytes 786440 | tf_op jit(solution)/shard_map/ppermute | solution.py:356
  24.1 26.8 %copy-start.1 = (bf16[1024,512]{1,0:T(8,128)(2,1)S(1)}, bf16[1024,512]{1,0:T(8,128)(2,1)}, u32[]{:S(2)}) copy-start(bf16[1024,512]{1,0:T(8,128)(2,1)} %w_two.3) | copy-start | bytes 3145732
  53.1 10.9 %collective-permute-start.3 = (bf16[5,128,512]{2,1,0:T(8,128)(2,1)}, bf16[5,128,512]{2,1,0:T(8,128)(2,1)}, u32[]{:S(2)}, u32[]{:S(2)}) collective-permute-start(bf16[5,128,512]{2,1,0:T(8,128)(2,1)} %get-tuple-element.58), channel_id=1, source_target_pairs={{0,64},{32,224},{64,0},{96,160},{128,192},{160,96},{192,128},{224,... | collective-permute-start | bytes 1966088 | tf_op jit(solution)/shard_map/ppermute | solution.py:356
  53.7 17.1 %all-to-all-start.1 = ((bf16[32,8,512]{2,1,0:T(8,128)(2,1)}), bf16[32,8,512]{2,1,0:T(8,128)(2,1)S(1)}, u32[]{:S(2)}, u32[]{:S(2)}) async-start(bf16[32,8,512]{2,1,0:T(8,128)(2,1)} %bitcast.7), calls=%async_computation.1 | async-start | bytes 524288 | tf_op jit(solution)/shard_map/all_to_all | solution.py:81
  58.9 13.4 %copy-start.3 = (bf16[128,512]{1,0:T(8,128)(2,1)S(1)}, bf16[128,512]{1,0:T(8,128)(2,1)}, u32[]{:S(2)}) copy-start(bf16[128,512]{1,0:T(8,128)(2,1)} %get-tuple-element.64.term) | copy-start | bytes 393220
  70.9 10.6 %collective-permute-start.4 = (bf16[4,128,512]{2,1,0:T(8,128)(2,1)}, bf16[4,128,512]{2,1,0:T(8,128)(2,1)S(1)}, u32[]{:S(2)}, u32[]{:S(2)}) collective-permute-start(bf16[4,128,512]{2,1,0:T(8,128)(2,1)} %pad_maximum_fusion), channel_id=1, source_target_pairs={{0,192},{32,96},{64,128},{96,32},{128,64},{160,224},{192,0},{224,1... | collective-permute-start | bytes 1572872 | tf_op jit(solution)/shard_map/ppermute | solution.py:356
  72.5 6.5 %collective-permute-start.5 = (bf16[128,512]{1,0:T(8,128)(2,1)S(1)}, bf16[128,512]{1,0:T(8,128)(2,1)S(1)}, u32[]{:S(2)}, u32[]{:S(2)}) collective-permute-start(bf16[128,512]{1,0:T(8,128)(2,1)S(1)} %near.1), channel_id=1, source_target_pairs={{0,64},{32,224},{64,0},{96,160},{128,192},{160,96},{192,128},{224,... | collective-permute-start | bytes 393224 | tf_op jit(solution)/shard_map/ppermute | solution.py:356
  79.1 7.7 %collective-permute-start.6 = (bf16[2,128,512]{2,1,0:T(8,128)(2,1)S(1)}, bf16[2,128,512]{2,1,0:T(8,128)(2,1)S(1)}, u32[]{:S(2)}, u32[]{:S(2)}) collective-permute-start(bf16[2,128,512]{2,1,0:T(8,128)(2,1)S(1)} %pad_maximum_fusion.3), channel_id=1, source_target_pairs={{0,192},{32,96},{64,128},{96,32},{128,64},{160,224},{192,0},{224,1... | collective-permute-start | bytes 786440 | tf_op jit(solution)/shard_map/ppermute | solution.py:356
  86.8 2.9 %collective-permute-start.7 = (bf16[9,128,512]{2,1,0:T(8,128)(2,1)S(1)}, bf16[9,128,512]{2,1,0:T(8,128)(2,1)S(1)}, u32[]{:S(2)}, u32[]{:S(2)}) collective-permute-start(bf16[9,128,512]{2,1,0:T(8,128)(2,1)S(1)} %fusion.1.held), channel_id=1, source_target_pairs={{0,32},{32,0},{64,96},{96,64},{128,160},{160,128},{192,224},{224,1... | collective-permute-start | bytes 3538952 | tf_op jit(solution)/shard_map/ppermute | solution.py:362
  92.1 12.2 %collective-permute-start.8 = (bf16[8,160,256]{2,1,0:T(8,128)(2,1)}, bf16[8,160,256]{2,1,0:T(8,128)(2,1)S(1)}, u32[]{:S(2)}, u32[]{:S(2)}) collective-permute-start(bf16[8,160,256]{2,1,0:T(8,128)(2,1)} %get-tuple-element.68), channel_id=1, source_target_pairs={{0,1},{1,0},{2,3},{3,2},{4,5},{5,4},{6,7},{7,6},{8,9},{9,8},{10,11... | collective-permute-start | bytes 1966088 | tf_op jit(solution)/shard_map/ppermute | solution.py:359
  92.7 18.2 %all-to-all-start.2 = ((bf16[32,8,512]{2,1,0:T(8,128)(2,1)}), bf16[32,8,512]{2,1,0:T(8,128)(2,1)S(1)}, u32[]{:S(2)}, u32[]{:S(2)}) async-start(bf16[32,8,512]{2,1,0:T(8,128)(2,1)} %bitcast.12), calls=%async_computation.2 | async-start | bytes 524288 | tf_op jit(solution)/shard_map/all_to_all | solution.py:81
  104.4 9.5 %collective-permute-start.9 = (bf16[8,96,256]{2,1,0:T(8,128)(2,1)S(1)}, bf16[8,96,256]{2,1,0:T(8,128)(2,1)}, u32[]{:S(2)}, u32[]{:S(2)}) collective-permute-start(bf16[8,96,256]{2,1,0:T(8,128)(2,1)S(1)} %x_pass.1.sent), channel_id=1, source_target_pairs={{0,3},{1,2},{2,1},{3,0},{4,7},{5,6},{6,5},{7,4},{8,11},{9,10},{10,... | collective-permute-start | bytes 1179656 | tf_op jit(solution)/shard_map/ppermute | solution.py:359
  143.8 9.2 %copy-start.4 = (bf16[128,512]{1,0:T(8,128)(2,1)S(1)}, bf16[128,512]{1,0:T(8,128)(2,1)}, u32[]{:S(2)}) copy-start(bf16[128,512]{1,0:T(8,128)(2,1)} %get-tuple-element.74.hidden) | copy-start | bytes 393220
  143.8 9.2 %copy-start.6 = (bf16[128,256]{1,0:T(8,128)(2,1)S(1)}, bf16[128,256]{1,0:T(8,128)(2,1)}, u32[]{:S(2)}) copy-start(bf16[128,256]{1,0:T(8,128)(2,1)} %copy-done.5) | copy-start | bytes 196612
  143.9 7.6 %collective-permute-start.11 = (bf16[8,64,256]{2,1,0:T(8,128)(2,1)S(1)}, bf16[8,64,256]{2,1,0:T(8,128)(2,1)S(1)}, u32[]{:S(2)}, u32[]{:S(2)}) collective-permute-start(bf16[8,64,256]{2,1,0:T(8,128)(2,1)S(1)} %get-tuple-element.80), channel_id=1, source_target_pairs={{0,1},{1,0},{2,3},{3,2},{4,5},{5,4},{6,7},{7,6},{8,9},{9,8},{10,11... | collective-permute-start | bytes 786440 | tf_op jit(solution)/shard_map/ppermute | solution.py:359
  146.0 5.4 %collective-permute-start.10 = (bf16[128,512]{1,0:T(8,128)(2,1)S(1)}, bf16[128,512]{1,0:T(8,128)(2,1)S(1)}, u32[]{:S(2)}, u32[]{:S(2)}) collective-permute-start(bf16[128,512]{1,0:T(8,128)(2,1)S(1)} %get-tuple-element.84), channel_id=1, source_target_pairs={{0,64},{32,224},{64,0},{96,160},{128,192},{160,96},{192,128},{224,... | collective-permute-start | bytes 393224 | tf_op jit(solution)/shard_map/ppermute | solution.py:356
  151.5 7.7 %collective-permute-start.12 = (bf16[2,128,512]{2,1,0:T(8,128)(2,1)S(1)}, bf16[2,128,512]{2,1,0:T(8,128)(2,1)S(1)}, u32[]{:S(2)}, u32[]{:S(2)}) collective-permute-start(bf16[2,128,512]{2,1,0:T(8,128)(2,1)S(1)} %pad_maximum_fusion.4), channel_id=1, source_target_pairs={{0,192},{32,96},{64,128},{96,32},{128,64},{160,224},{192,0},{224,1... | collective-permute-start | bytes 786440 | tf_op jit(solution)/shard_map/ppermute | solution.py:356
  154.2 11.3 %collective-permute-start.13 = (bf16[2,8,64,256]{3,2,1,0:T(8,128)(2,1)S(1)}, bf16[2,8,64,256]{3,2,1,0:T(8,128)(2,1)S(1)}, u32[]{:S(2)}, u32[]{:S(2)}) collective-permute-start(bf16[2,8,64,256]{3,2,1,0:T(8,128)(2,1)S(1)} %pad_maximum_fusion.2.held), channel_id=1, source_target_pairs={{0,3},{1,2},{2,1},{3,0},{4,7},{5,6},{6,5},{7,4},{8,11},{9,10},{10,... | collective-permute-start | bytes 1572872 | tf_op jit(solution)/shard_map/ppermute | solution.py:359
  159.2 7.7 %collective-permute-start.14 = (bf16[4,128,512]{2,1,0:T(8,128)(2,1)S(1)}, bf16[4,128,512]{2,1,0:T(8,128)(2,1)S(1)}, u32[]{:S(2)}, u32[]{:S(2)}) collective-permute-start(bf16[4,128,512]{2,1,0:T(8,128)(2,1)S(1)} %pad_maximum_fusion.1.held), channel_id=1, source_target_pairs={{0,32},{32,0},{64,96},{96,64},{128,160},{160,128},{192,224},{224,1... | collective-permute-start | bytes 1572872 | tf_op jit(solution)/shard_map/ppermute | solution.py:362

commit v12 on v11

--- a/solution.py
+++ b/solution.py
@@ -170,7 +170,6 @@
 def project(flat, w_one, other):
     groups, nodes, cols = flat.shape
     width = w_one.shape[1]
-    cut = width // 4
     held = pltpu.VMEM((CHIPS, nodes, cols), BF16)
     sems = pltpu.SemaphoreType.DMA((2, CHIPS))
     picks = shape((CHIPS, nodes, width))
@@ -186,19 +185,25 @@
 
     def other_body(rows, w, out, w_out, mine, sem):
         moves = fetch(rows, mine, sem)
-        cuts = [slice(k * cut, (k + 1) * cut) for k in range(4)]
+        depth = cols // CHIPS
         loads = [
-            pltpu.make_async_copy(w.at[:, c], w_out.at[:, c], sem.at[1, k])
-            for k, c in enumerate(cuts)
+            pltpu.make_async_copy(w.at[c], w_out.at[c], sem.at[1, k])
+            for k, c in enumerate([pl.ds(k * depth, depth) for k in range(CHIPS)])
         ]
         for load in loads:
             load.start()
         for move in moves:
             move.wait()
+        half = cols // 2
         picked = mine[...].reshape(CHIPS * nodes, cols)
-        for load, c in zip(loads, cuts):
-            load.wait()
-            out[:, :, c] = mm(picked, w_out[:, c]).astype(BF16).reshape(CHIPS, nodes, cut)
+        total = None
+        for k in range(2):
+            for load in loads[2 * k : 2 * k + 2]:
+                load.wait()
+            at = slice(k * half, (k + 1) * half)
+            term = mm(picked[:, at], w_out[at, :])
+            total = term if total is None else total + term
+        out[...] = total.astype(BF16).reshape(out.shape)
 
     def mine_body(rows, w, out, mine, sem):
         for move in fetch(rows, mine, sem):
@@ -465,10 +470,9 @@
     one_y = y_move(chunk, y_first)
     one_x = x_move(mine, x_first)
     out = whole("out", out_body, block, recv, hidden, inv, mean, own, w_two, far=(0,))
-    one_y, one_x = lax.optimization_barrier((one_y, one_x))
+    one_y, one_x, out = lax.optimization_barrier((one_y, one_x, out))
     held_y = jnp.stack([chunk, one_y])
     held_y = jnp.concatenate([held_y, y_move(held_y, y_second)])
-    held_y, out = lax.optimization_barrier((held_y, out))
     held_x = jnp.stack([mine, one_x])
     last_x = x_move(held_x, x_second)
     one = whole(

time: 170 us -> 168 us (0.988)
  no operation moved by 1% of the time
where the time goes in v12:
time: 168 us; the launch traced here: 166 us
  waiting for transfers between devices  57.8 us (34%)
  blocking collectives  55.7 us (33%)
  starting transfers between devices  29 us (17%)
  Pallas kernels  15.8 us (9%)
  local copies, waits for them, and re-layouts  3.68 us (2%)
  other arithmetic  3.46 us (2%)
    all_to_all x3, blocking collectives, trade(): lax.all_to_all(boxes, 'dom', split_axis=0, concat_axis=0, axis_index_grou...  55.7 us
    ppermute x8, waiting for transfers between devices, y_move(): return lax.ppermute(block, 'feat', pairs)  29.5 us
    pallas_call x13, Pallas kernels, whole(): pl.pallas_call(body, out_shape=kinds, in_specs=[anywhere if k in raw else...  15.8 us
    ppermute x4, waiting for transfers between devices, x_move(): return lax.ppermute(block, ('feat', 'dom'), pairs)  14.7 us
    ppermute x8, starting transfers between devices, y_move(): return lax.ppermute(block, 'feat', pairs)  11.5 us
    all_to_all x2, starting transfers between devices, trade(): lax.all_to_all(boxes, 'dom', split_axis=0, concat_axis=0, axis_index_grou...  10.3 us
    all_to_all x2, waiting for transfers between devices, trade(): lax.all_to_all(boxes, 'dom', split_axis=0, concat_axis=0, axis_index_grou...  10.2 us
    ppermute x4, starting transfers between devices, x_move(): return lax.ppermute(block, ('feat', 'dom'), pairs)  6.88 us
  transfers between devices with their start and end apart: 17, of which 15 were waited for; matrix products, arithmetic and copies ran while one was open for 4% of the time, Pallas kernels for 4%

profile of v12, /device:TPU:32, one launch (start us, length us, event | category | flops | bytes accessed | tf_op | source)
XLA Modules:
  0.0 166.5 jit_solution(9439579041557843196)
XLA Ops:
  0.6 2.3 %project.2 = (bf16[4,128,1024]{2,1,0:T(8,128)(2,1)S(1)}, bf16[512,1024]{1,0:T(8,128)(2,1)S(1)}) custom-call(bf16[8,128,512]{2,1,0:T(8,128)(2,1)} %flat.1, bf16[512,1024]{1,0:T(8,128)(2,1)} %w.1), custom_call_target="tpu_custom_call" | custom-call | tf_op jit(solution)/shard_map/project/pallas_call | solution.py:52
  3.0 1.9 %project.3.part = bf16[4,128,1024]{2,1,0:T(8,128)(2,1)S(1)} custom-call(bf16[8,128,512]{2,1,0:T(8,128)(2,1)} %flat.1, bf16[512,1024]{1,0:T(8,128)(2,1)S(1)} %get-tuple-element.40.w), custom_call_target="tpu_custom_call" | custom-call | tf_op jit(solution)/shard_map/project/pallas_call | solution.py:52
  5.0 0.7 collective-permute-done.got
  5.8 1.7 collective-permute-start.1
  7.5 0.7 tables.1
  8.3 0.6 copy-done.5
  8.9 6.2 %collective-permute-done.1.near = bf16[2,128,1024]{2,1,0:T(8,128)(2,1)S(1)} collective-permute-done((bf16[2,128,1024]{2,1,0:T(8,128)(2,1)S(1)}, bf16[2,128,1024]{2,1,0:T(8,128)(2,1)S(1)}, u32[]{:S(2)}, u32[]{:S(2)}) %collective-permute-start.1) | collective-permute-done | bytes 524320 | tf_op jit(solution)/shard_map/ppermute | solution.py:361
  15.2 3.1 %collective-permute-start.2 = (bf16[128,1024]{1,0:T(8,128)(2,1)S(1)}, bf16[128,1024]{1,0:T(8,128)(2,1)S(1)}, u32[]{:S(2)}, u32[]{:S(2)}) collective-permute-start(bf16[128,1024]{1,0:T(8,128)(2,1)S(1)} %fusion), channel_id=1, source_target_pairs={{0,192},{32,96},{64,128},{96,32},{128,64},{160,224},{192,0},{224,1... | collective-permute-start | bytes 786440 | tf_op jit(solution)/shard_map/ppermute | solution.py:361
  18.4 0.4 turn.1.flat_t
  18.7 4.2 %collective-permute-done.2.far = bf16[128,1024]{1,0:T(8,128)(2,1)S(1)} collective-permute-done((bf16[128,1024]{1,0:T(8,128)(2,1)S(1)}, bf16[128,1024]{1,0:T(8,128)(2,1)S(1)}, u32[]{:S(2)}, u32[]{:S(2)}) %collective-permute-start.2) | collective-permute-done | bytes 262176 | tf_op jit(solution)/shard_map/ppermute | solution.py:361
  22.9 0.5 forward.1
  23.4 26.8 %all_to_all.25 = bf16[32,16,512]{2,1,0:T(8,128)(2,1)S(1)} all-to-all(bf16[32,16,512]{2,1,0:T(8,128)(2,1)S(1)} %bitcast.38), channel_id=1, replica_groups=mesh['feat'=8,'dom'=32] {'dom'}, dimensions={0} | all-to-all | bytes 1048576 | tf_op jit(solution)/shard_map/all_to_all | solution.py:81
  50.2 2.2 %middle.1 = (bf16[256,512]{1,0:T(8,128)(2,1)}, bf16[256,512]{1,0:T(8,128)(2,1)}, bf16[128,512]{1,0:T(8,128)(2,1)}, bf16[128,512]{1,0:T(8,128)(2,1)}, bf16[5,128,...) custom-call(bf16[512,512]{1,0:T(8,128)(2,1)S(1)} %bitcast.32, ...), custom_call_target="tpu_custom_call" | custom-call | tf_op jit(solution)/shard_map/middle/pallas_call | solution.py:52
  52.4 0.6 collective-permute-start.3
  53.0 5.1 %all-to-all-start.1 = ((bf16[32,8,512]{2,1,0:T(8,128)(2,1)}), bf16[32,8,512]{2,1,0:T(8,128)(2,1)S(1)}, u32[]{:S(2)}, u32[]{:S(2)}) async-start(bf16[32,8,512]{2,1,0:T(8,128)(2,1)} %bitcast.7), calls=%async_computation.1 | async-start | bytes 524288 | tf_op jit(solution)/shard_map/all_to_all | solution.py:81
  58.1 1.0 slice.57
  59.1 4.2 %collective-permute-done.3 = bf16[5,128,512]{2,1,0:T(8,128)(2,1)} collective-permute-done((bf16[5,128,512]{2,1,0:T(8,128)(2,1)}, bf16[5,128,512]{2,1,0:T(8,128)(2,1)}, u32[]{:S(2)}, u32[]{:S(2)}) %collective-permute-start.3) | collective-permute-done | bytes 655392 | tf_op jit(solution)/shard_map/ppermute | solution.py:361
  63.3 0.9 slice.73
  64.2 1.0 add_convert_fusion.1
  65.2 0.8 pad_maximum_fusion
  66.1 4.1 %all-to-all-done.1 = bf16[32,8,512]{2,1,0:T(8,128)(2,1)S(1)} async-done(((bf16[32,8,512]{2,1,0:T(8,128)(2,1)}), bf16[32,8,512]{2,1,0:T(8,128)(2,1)S(1)}, u32[]{:S(2)}, u32[]{:S(2)}) %all-to-all-start.1) | async-done | bytes 262176 | tf_op jit(solution)/shard_map/all_to_all | solution.py:81
  70.1 1.4 collective-permute-start.4
  71.8 1.2 collective-permute-start.5
  73.0 1.0 slice_dynamic-update-slice_fusion.1
  74.0 4.3 %collective-permute-done.5 = bf16[128,512]{1,0:T(8,128)(2,1)S(1)} collective-permute-done((bf16[128,512]{1,0:T(8,128)(2,1)S(1)}, bf16[128,512]{1,0:T(8,128)(2,1)S(1)}, u32[]{:S(2)}, u32[]{:S(2)}) %collective-permute-start.5) | collective-permute-done | bytes 131104 | tf_op jit(solution)/shard_map/ppermute | solution.py:361
  78.3 1.8 %collective-permute-start.6 = (bf16[2,128,512]{2,1,0:T(8,128)(2,1)S(1)}, bf16[2,128,512]{2,1,0:T(8,128)(2,1)S(1)}, u32[]{:S(2)}, u32[]{:S(2)}) collective-permute-start(bf16[2,128,512]{2,1,0:T(8,128)(2,1)S(1)} %pad_maximum_fusion.3), channel_id=1, source_target_pairs={{0,192},{32,96},{64,128},{96,32},{128,64},{160,224},{192,0},{224,1... | collective-permute-start | bytes 786440 | tf_op jit(solution)/shard_map/ppermute | solution.py:361
  80.1 0.6 collective-permute-done.4
  80.8 1.0 convert_add_fusion
  81.8 4.2 %collective-permute-done.6 = bf16[2,128,512]{2,1,0:T(8,128)(2,1)S(1)} collective-permute-done((bf16[2,128,512]{2,1,0:T(8,128)(2,1)S(1)}, bf16[2,128,512]{2,1,0:T(8,128)(2,1)S(1)}, u32[]{:S(2)}, u32[]{:S(2)}) %collective-permute-start.6) | collective-permute-done | bytes 262176 | tf_op jit(solution)/shard_map/ppermute | solution.py:361
  86.2 2.8 %collective-permute-done.7.other = bf16[9,128,512]{2,1,0:T(8,128)(2,1)S(1)} collective-permute-done((bf16[9,128,512]{2,1,0:T(8,128)(2,1)S(1)}, bf16[9,128,512]{2,1,0:T(8,128)(2,1)S(1)}, u32[]{:S(2)}, u32[]{:S(2)}) %collective-permute-start.7) | collective-permute-done | bytes 1179680 | tf_op jit(solution)/shard_map/ppermute | solution.py:367
  89.0 2.3 %grad.1 = (bf16[8,160,256]{2,1,0:T(8,128)(2,1)}, bf16[8,64,256]{2,1,0:T(8,128)(2,1)S(1)}, bf16[8,96,256]{2,1,0:T(8,128)(2,1)S(1)}) custom-call(bf16[512,1024]{1,0:T(8,128)(2,1)S(1)} %turn.1.flat_t, bf16[9,128,512]{2,1,0:T(8,128)(2,1)S(1)} %fusion.1.held, bf16[9,128,512]{2,1,0:T(8,128)(2,1)S(1)} %collective-permute-done.7.other, ...), custom_call_target="tpu_custom_call" | custom-call | tf_op jit(solution)/shard_map/grad/pallas_call | solution.py:52
  91.3 0.6 collective-permute-start.8
  91.9 5.2 %all-to-all-start.2 = ((bf16[32,8,512]{2,1,0:T(8,128)(2,1)}), bf16[32,8,512]{2,1,0:T(8,128)(2,1)S(1)}, u32[]{:S(2)}, u32[]{:S(2)}) async-start(bf16[32,8,512]{2,1,0:T(8,128)(2,1)} %bitcast.12), calls=%async_computation.2 | async-start | bytes 524288 | tf_op jit(solution)/shard_map/all_to_all | solution.py:81
  97.1 6.4 %collective-permute-done.8.got = bf16[8,160,256]{2,1,0:T(8,128)(2,1)S(1)} collective-permute-done((bf16[8,160,256]{2,1,0:T(8,128)(2,1)}, bf16[8,160,256]{2,1,0:T(8,128)(2,1)S(1)}, u32[]{:S(2)}, u32[]{:S(2)}) %collective-permute-start.8) | collective-permute-done | bytes 655392 | tf_op jit(solution)/shard_map/ppermute | solution.py:364
  104.0 6.1 %all-to-all-done.2 = bf16[32,8,512]{2,1,0:T(8,128)(2,1)S(1)} async-done(((bf16[32,8,512]{2,1,0:T(8,128)(2,1)}), bf16[32,8,512]{2,1,0:T(8,128)(2,1)S(1)}, u32[]{:S(2)}, u32[]{:S(2)}) %all-to-all-start.2) | async-done | bytes 262176 | tf_op jit(solution)/shard_map/all_to_all | solution.py:81
  110.1 3.0 %collective-permute-done.9.last = bf16[8,96,256]{2,1,0:T(8,128)(2,1)} collective-permute-done((bf16[8,96,256]{2,1,0:T(8,128)(2,1)S(1)}, bf16[8,96,256]{2,1,0:T(8,128)(2,1)}, u32[]{:S(2)}, u32[]{:S(2)}) %collective-permute-start.9) | collective-permute-done | bytes 393248 | tf_op jit(solution)/shard_map/ppermute | solution.py:364
  113.1 1.1 x_sum.1
  114.2 14.7 %all_to_all.26 = bf16[8,96,256]{2,1,0:T(8,128)(2,1)S(1)} all-to-all(bf16[8,96,256]{2,1,0:T(8,128)(2,1)S(1)} %x_sum.1), channel_id=1, replica_groups={{0,4,8,12,16,20,24,28},{1,5,9,13,17,21,25,29},{2,6,10,14,18,22,26,30},{..., dimensions={0} | all-to-all | bytes 786432 | tf_op jit(solution)/shard_map/all_to_all | solution.py:81
  129.1 14.2 %all_to_all.27 = bf16[8,96,256]{2,1,0:T(8,128)(2,1)S(1)} all-to-all(bf16[8,96,256]{2,1,0:T(8,128)(2,1)S(1)} %broadcast_in_dim.4), channel_id=1, replica_groups={{0,4,8,12,16,20,24,28},{1,5,9,13,17,21,25,29},{2,6,10,14,18,22,26,30},{..., dimensions={0} | all-to-all | bytes 786432 | tf_op jit(solution)/shard_map/all_to_all | solution.py:81
  143.3 1.9 %collective-permute-start.11 = (bf16[8,64,256]{2,1,0:T(8,128)(2,1)S(1)}, bf16[8,64,256]{2,1,0:T(8,128)(2,1)S(1)}, u32[]{:S(2)}, u32[]{:S(2)}) collective-permute-start(bf16[8,64,256]{2,1,0:T(8,128)(2,1)S(1)} %get-tuple-element.78), channel_id=1, source_target_pairs={{0,1},{1,0},{2,3},{3,2},{4,5},{5,4},{6,7},{7,6},{8,9},{9,8},{10,11... | collective-permute-start | bytes 786440 | tf_op jit(solution)/shard_map/ppermute | solution.py:364
  145.4 1.1 out.1
  146.5 4.0 %collective-permute-done.10 = bf16[128,512]{1,0:T(8,128)(2,1)S(1)} collective-permute-done((bf16[128,512]{1,0:T(8,128)(2,1)S(1)}, bf16[128,512]{1,0:T(8,128)(2,1)S(1)}, u32[]{:S(2)}, u32[]{:S(2)}) %collective-permute-start.10) | collective-permute-done | bytes 131104 | tf_op jit(solution)/shard_map/ppermute | solution.py:361
  150.5 1.7 %collective-permute-start.13 = (bf16[2,128,512]{2,1,0:T(8,128)(2,1)S(1)}, bf16[2,128,512]{2,1,0:T(8,128)(2,1)S(1)}, u32[]{:S(2)}, u32[]{:S(2)}) collective-permute-start(bf16[2,128,512]{2,1,0:T(8,128)(2,1)S(1)} %pad_maximum_fusion.4), channel_id=1, source_target_pairs={{0,192},{32,96},{64,128},{96,32},{128,64},{160,224},{192,0},{224,1... | collective-permute-start | bytes 786440 | tf_op jit(solution)/shard_map/ppermute | solution.py:361
  152.2 4.1 %collective-permute-start.12 = (bf16[2,8,64,256]{3,2,1,0:T(8,128)(2,1)S(1)}, bf16[2,8,64,256]{3,2,1,0:T(8,128)(2,1)S(1)}, u32[]{:S(2)}, u32[]{:S(2)}) collective-permute-start(bf16[2,8,64,256]{3,2,1,0:T(8,128)(2,1)S(1)} %pad_maximum_fusion.1.held), channel_id=1, source_target_pairs={{0,3},{1,2},{2,1},{3,0},{4,7},{5,6},{6,5},{7,4},{8,11},{9,10},{10,... | collective-permute-start | bytes 1572872 | tf_op jit(solution)/shard_map/ppermute | solution.py:364
  156.4 1.8 %collective-permute-done.13 = bf16[2,128,512]{2,1,0:T(8,128)(2,1)S(1)} collective-permute-done((bf16[2,128,512]{2,1,0:T(8,128)(2,1)S(1)}, bf16[2,128,512]{2,1,0:T(8,128)(2,1)S(1)}, u32[]{:S(2)}, u32[]{:S(2)}) %collective-permute-start.13) | collective-permute-done | bytes 262176 | tf_op jit(solution)/shard_map/ppermute | solution.py:361
  158.3 5.2 %collective-permute-done.12.last = bf16[2,8,64,256]{3,2,1,0:T(8,128)(2,1)S(1)} collective-permute-done((bf16[2,8,64,256]{3,2,1,0:T(8,128)(2,1)S(1)}, bf16[2,8,64,256]{3,2,1,0:T(8,128)(2,1)S(1)}, u32[]{:S(2)}, u32[]{:S(2)}) %collective-permute-start.12) | collective-permute-done | bytes 524320 | tf_op jit(solution)/shard_map/ppermute | solution.py:364
  163.5 1.5 spread.1
  165.0 1.5 join.1
  (47 shorter events, 1.8 us)
Async XLA Ops:
  2.9 2.7 %collective-permute-start = (bf16[4,128,1024]{2,1,0:T(8,128)(2,1)S(1)}, bf16[4,128,1024]{2,1,0:T(8,128)(2,1)S(1)}, u32[]{:S(2)}, u32[]{:S(2)}) collective-permute-start(bf16[4,128,1024]{2,1,0:T(8,128)(2,1)S(1)} %get-tuple-element.41), channel_id=1, source_target_pairs={{0,32},{32,0},{64,96},{96,64},{128,160},{160,128},{192,224},{224,1... | collective-permute-start | bytes 3145736 | tf_op jit(solution)/shard_map/ppermute | solution.py:367
  4.9 2.6 %copy-start.9 = (s32[1,128,10]{1,0,2:T(1,128)S(1)}, s32[1,128,10]{1,0,2:T(1,128)}, u32[]{:S(2)}) copy-start(s32[1,128,10]{1,0,2:T(1,128)} %param.10) | copy-start | bytes 15364
  4.9 2.6 %copy-start.7 = (s32[1,32,8]{1,2,0:T(8,128)S(1)}, s32[1,32,8]{1,2,0:T(8,128)}, u32[]{:S(2)}) copy-start(s32[1,32,8]{1,2,0:T(8,128)} %param.12) | copy-start | bytes 3076
  4.9 2.6 %copy-start.8 = (s32[1,128]{1,0:T(1,128)S(1)}, s32[1,128]{1,0:T(1,128)}, u32[]{:S(2)}) copy-start(s32[1,128]{1,0:T(1,128)} %deg.1) | copy-start | bytes 1540
  4.9 13.4 %copy-start = (bf16[8,128,512]{2,1,0:T(8,128)(2,1)S(1)}, bf16[8,128,512]{2,1,0:T(8,128)(2,1)}, u32[]{:S(2)}) copy-start(bf16[8,128,512]{2,1,0:T(8,128)(2,1)} %flat.1) | copy-start | bytes 3145732
  5.8 9.3 %collective-permute-start.1 = (bf16[2,128,1024]{2,1,0:T(8,128)(2,1)S(1)}, bf16[2,128,1024]{2,1,0:T(8,128)(2,1)S(1)}, u32[]{:S(2)}, u32[]{:S(2)}) collective-permute-start(bf16[2,128,1024]{2,1,0:T(8,128)(2,1)S(1)} %add_convert_fusion), channel_id=1, source_target_pairs={{0,64},{32,224},{64,0},{96,160},{128,192},{160,96},{192,128},{224,... | collective-permute-start | bytes 1572872 | tf_op jit(solution)/shard_map/ppermute | solution.py:361
  8.2 0.6 copy-start.5
  15.2 7.7 %copy-start.2 = (bf16[1,128,512]{2,1,0:T(8,128)(2,1)S(1)}, bf16[1,128,512]{2,1,0:T(8,128)(2,1)}, u32[]{:S(2)}) copy-start(bf16[1,128,512]{2,1,0:T(8,128)(2,1)} %param.13) | copy-start | bytes 393220
  15.2 7.7 %collective-permute-start.2 = (bf16[128,1024]{1,0:T(8,128)(2,1)S(1)}, bf16[128,1024]{1,0:T(8,128)(2,1)S(1)}, u32[]{:S(2)}, u32[]{:S(2)}) collective-permute-start(bf16[128,1024]{1,0:T(8,128)(2,1)S(1)} %fusion), channel_id=1, source_target_pairs={{0,192},{32,96},{64,128},{96,32},{128,64},{160,224},{192,0},{224,1... | collective-permute-start | bytes 786440 | tf_op jit(solution)/shard_map/ppermute | solution.py:361
  23.4 26.8 %copy-start.1 = (bf16[1024,512]{1,0:T(8,128)(2,1)S(1)}, bf16[1024,512]{1,0:T(8,128)(2,1)}, u32[]{:S(2)}) copy-start(bf16[1024,512]{1,0:T(8,128)(2,1)} %w_two.3) | copy-start | bytes 3145732
  52.4 10.9 %collective-permute-start.3 = (bf16[5,128,512]{2,1,0:T(8,128)(2,1)}, bf16[5,128,512]{2,1,0:T(8,128)(2,1)}, u32[]{:S(2)}, u32[]{:S(2)}) collective-permute-start(bf16[5,128,512]{2,1,0:T(8,128)(2,1)} %get-tuple-element.57), channel_id=1, source_target_pairs={{0,64},{32,224},{64,0},{96,160},{128,192},{160,96},{192,128},{224,... | collective-permute-start | bytes 1966088 | tf_op jit(solution)/shard_map/ppermute | solution.py:361
  53.0 17.2 %all-to-all-start.1 = ((bf16[32,8,512]{2,1,0:T(8,128)(2,1)}), bf16[32,8,512]{2,1,0:T(8,128)(2,1)S(1)}, u32[]{:S(2)}, u32[]{:S(2)}) async-start(bf16[32,8,512]{2,1,0:T(8,128)(2,1)} %bitcast.7), calls=%async_computation.1 | async-start | bytes 524288 | tf_op jit(solution)/shard_map/all_to_all | solution.py:81
  58.1 13.4 %copy-start.3 = (bf16[128,512]{1,0:T(8,128)(2,1)S(1)}, bf16[128,512]{1,0:T(8,128)(2,1)}, u32[]{:S(2)}) copy-start(bf16[128,512]{1,0:T(8,128)(2,1)} %get-tuple-element.63.term) | copy-start | bytes 393220
  70.1 10.6 %collective-permute-start.4 = (bf16[4,128,512]{2,1,0:T(8,128)(2,1)}, bf16[4,128,512]{2,1,0:T(8,128)(2,1)S(1)}, u32[]{:S(2)}, u32[]{:S(2)}) collective-permute-start(bf16[4,128,512]{2,1,0:T(8,128)(2,1)} %pad_maximum_fusion), channel_id=1, source_target_pairs={{0,192},{32,96},{64,128},{96,32},{128,64},{160,224},{192,0},{224,1... | collective-permute-start | bytes 1572872 | tf_op jit(solution)/shard_map/ppermute | solution.py:361
  71.8 6.5 %collective-permute-start.5 = (bf16[128,512]{1,0:T(8,128)(2,1)S(1)}, bf16[128,512]{1,0:T(8,128)(2,1)S(1)}, u32[]{:S(2)}, u32[]{:S(2)}) collective-permute-start(bf16[128,512]{1,0:T(8,128)(2,1)S(1)} %near.1), channel_id=1, source_target_pairs={{0,64},{32,224},{64,0},{96,160},{128,192},{160,96},{192,128},{224,... | collective-permute-start | bytes 393224 | tf_op jit(solution)/shard_map/ppermute | solution.py:361
  78.3 7.7 %collective-permute-start.6 = (bf16[2,128,512]{2,1,0:T(8,128)(2,1)S(1)}, bf16[2,128,512]{2,1,0:T(8,128)(2,1)S(1)}, u32[]{:S(2)}, u32[]{:S(2)}) collective-permute-start(bf16[2,128,512]{2,1,0:T(8,128)(2,1)S(1)} %pad_maximum_fusion.3), channel_id=1, source_target_pairs={{0,192},{32,96},{64,128},{96,32},{128,64},{160,224},{192,0},{224,1... | collective-permute-start | bytes 786440 | tf_op jit(solution)/shard_map/ppermute | solution.py:361
  86.1 2.9 %collective-permute-start.7 = (bf16[9,128,512]{2,1,0:T(8,128)(2,1)S(1)}, bf16[9,128,512]{2,1,0:T(8,128)(2,1)S(1)}, u32[]{:S(2)}, u32[]{:S(2)}) collective-permute-start(bf16[9,128,512]{2,1,0:T(8,128)(2,1)S(1)} %fusion.1.held), channel_id=1, source_target_pairs={{0,32},{32,0},{64,96},{96,64},{128,160},{160,128},{192,224},{224,1... | collective-permute-start | bytes 3538952 | tf_op jit(solution)/shard_map/ppermute | solution.py:367
  91.3 12.2 %collective-permute-start.8 = (bf16[8,160,256]{2,1,0:T(8,128)(2,1)}, bf16[8,160,256]{2,1,0:T(8,128)(2,1)S(1)}, u32[]{:S(2)}, u32[]{:S(2)}) collective-permute-start(bf16[8,160,256]{2,1,0:T(8,128)(2,1)} %get-tuple-element.67), channel_id=1, source_target_pairs={{0,1},{1,0},{2,3},{3,2},{4,5},{5,4},{6,7},{7,6},{8,9},{9,8},{10,11... | collective-permute-start | bytes 1966088 | tf_op jit(solution)/shard_map/ppermute | solution.py:364
  91.9 18.1 %all-to-all-start.2 = ((bf16[32,8,512]{2,1,0:T(8,128)(2,1)}), bf16[32,8,512]{2,1,0:T(8,128)(2,1)S(1)}, u32[]{:S(2)}, u32[]{:S(2)}) async-start(bf16[32,8,512]{2,1,0:T(8,128)(2,1)} %bitcast.12), calls=%async_computation.2 | async-start | bytes 524288 | tf_op jit(solution)/shard_map/all_to_all | solution.py:81
  103.7 9.4 %collective-permute-start.9 = (bf16[8,96,256]{2,1,0:T(8,128)(2,1)S(1)}, bf16[8,96,256]{2,1,0:T(8,128)(2,1)}, u32[]{:S(2)}, u32[]{:S(2)}) collective-permute-start(bf16[8,96,256]{2,1,0:T(8,128)(2,1)S(1)} %x_pass.1.sent), channel_id=1, source_target_pairs={{0,3},{1,2},{2,1},{3,0},{4,7},{5,6},{6,5},{7,4},{8,11},{9,10},{10,... | collective-permute-start | bytes 1179656 | tf_op jit(solution)/shard_map/ppermute | solution.py:364
  129.0 16.3 %copy-start.4 = (bf16[128,512]{1,0:T(8,128)(2,1)S(1)}, bf16[128,512]{1,0:T(8,128)(2,1)}, u32[]{:S(2)}) copy-start(bf16[128,512]{1,0:T(8,128)(2,1)} %get-tuple-element.72.hidden) | copy-start | bytes 393220
  129.0 16.3 %copy-start.6 = (bf16[128,256]{1,0:T(8,128)(2,1)S(1)}, bf16[128,256]{1,0:T(8,128)(2,1)}, u32[]{:S(2)}) copy-start(bf16[128,256]{1,0:T(8,128)(2,1)} %copy-done.5) | copy-start | bytes 196612
  143.3 7.1 %collective-permute-start.11 = (bf16[8,64,256]{2,1,0:T(8,128)(2,1)S(1)}, bf16[8,64,256]{2,1,0:T(8,128)(2,1)S(1)}, u32[]{:S(2)}, u32[]{:S(2)}) collective-permute-start(bf16[8,64,256]{2,1,0:T(8,128)(2,1)S(1)} %get-tuple-element.78), channel_id=1, source_target_pairs={{0,1},{1,0},{2,3},{3,2},{4,5},{5,4},{6,7},{7,6},{8,9},{9,8},{10,11... | collective-permute-start | bytes 786440 | tf_op jit(solution)/shard_map/ppermute | solution.py:364
  145.3 5.2 %collective-permute-start.10 = (bf16[128,512]{1,0:T(8,128)(2,1)S(1)}, bf16[128,512]{1,0:T(8,128)(2,1)S(1)}, u32[]{:S(2)}, u32[]{:S(2)}) collective-permute-start(bf16[128,512]{1,0:T(8,128)(2,1)S(1)} %get-tuple-element.82), channel_id=1, source_target_pairs={{0,64},{32,224},{64,0},{96,160},{128,192},{160,96},{192,128},{224,... | collective-permute-start | bytes 393224 | tf_op jit(solution)/shard_map/ppermute | solution.py:361
  150.5 7.7 %collective-permute-start.13 = (bf16[2,128,512]{2,1,0:T(8,128)(2,1)S(1)}, bf16[2,128,512]{2,1,0:T(8,128)(2,1)S(1)}, u32[]{:S(2)}, u32[]{:S(2)}) collective-permute-start(bf16[2,128,512]{2,1,0:T(8,128)(2,1)S(1)} %pad_maximum_fusion.4), channel_id=1, source_target_pairs={{0,192},{32,96},{64,128},{96,32},{128,64},{160,224},{192,0},{224,1... | collective-permute-start | bytes 786440 | tf_op jit(solution)/shard_map/ppermute | solution.py:361
  152.2 11.3 %collective-permute-start.12 = (bf16[2,8,64,256]{3,2,1,0:T(8,128)(2,1)S(1)}, bf16[2,8,64,256]{3,2,1,0:T(8,128)(2,1)S(1)}, u32[]{:S(2)}, u32[]{:S(2)}) collective-permute-start(bf16[2,8,64,256]{3,2,1,0:T(8,128)(2,1)S(1)} %pad_maximum_fusion.1.held), channel_id=1, source_target_pairs={{0,3},{1,2},{2,1},{3,0},{4,7},{5,6},{6,5},{7,4},{8,11},{9,10},{10,... | collective-permute-start | bytes 1572872 | tf_op jit(solution)/shard_map/ppermute | solution.py:364
  158.2 6.8 %collective-permute-start.14 = (bf16[4,128,512]{2,1,0:T(8,128)(2,1)S(1)}, bf16[4,128,512]{2,1,0:T(8,128)(2,1)S(1)}, u32[]{:S(2)}, u32[]{:S(2)}) collective-permute-start(bf16[4,128,512]{2,1,0:T(8,128)(2,1)S(1)} %pad_maximum_fusion.2.held), channel_id=1, source_target_pairs={{0,32},{32,0},{64,96},{96,64},{128,160},{160,128},{192,224},{224,1... | collective-permute-start | bytes 1572872 | tf_op jit(solution)/shard_map/ppermute | solution.py:367
